TPU v7x, 32 devices: a whole 2x2x4 slice. The times are simulated.
32 devices in a mesh: var: 8 (over y, x, core), head: 4 (over z).
Axes of the slice: x: 2, y: 2, z: 4, core: 2. Of those that a mesh axis runs over, the one named last changes fastest.
Arguments:
- series: float32 [1024, 8192], P('var', 'head'), may hold values from -48 to 48
- emb_weight: float32 [8192, 512], P('head'), as said below
- emb_bias: float32 [512], replicated, may hold values from -3 to 3
- q_weight: float32 [512, 512], P(None, 'head'), may hold values from -0.75 to 0.75
- k_weight: float32 [512, 512], P(None, 'head'), may hold values from -0.25 to 0.25
- v_weight: float32 [512, 512], P(None, 'head'), may hold values from -0.25 to 0.25
- out_weight: float32 [512, 512], P('head'), may hold values from -0.25 to 0.25
- norm1_gain: float32 [512], replicated, may hold values from 0.1 to 1.9
- norm1_bias: float32 [512], replicated, may hold values from -3 to 3
- ffn_in: float32 [512, 2048], P(None, 'head'), may hold values from -0.25 to 0.25
- ffn_out: float32 [2048, 512], P('head'), may hold values from -0.1875 to 0.1875
- norm2_gain: float32 [512], replicated, may hold values from 0.1 to 1.9
- norm2_bias: float32 [512], replicated, may hold values from -3 to 3
Outputs:
- final: float32 [512, 1024], P('head', 'var')
Inputs may be any that keep to these rules, and one draw needn't show every extreme that they name: `emb_weight`: every entry lies within 12 / sqrt(8192) in magnitude, and some entry reaches that bound.
All inputs are finite; a program needn't handle non-finite values.
Results may differ from a plain program's by a relative error of at most 0.0003.
Values sent between devices are 32-bit elements; how exact they have to be, the bound alone decides.
No kernel may reach another device: no remote copies, remote signals or barrier semaphores. Data moves between devices by JAX's collectives and lax.ppermute only.
A program may use at most 64 MiB of HBM per device.

v0:
```python
import math

import jax
import jax.numpy as jnp
from jax import lax
from jax.sharding import PartitionSpec as P

DH = 64


HIGH = lax.Precision.HIGHEST


def product(first_op, second_op):
    return jnp.dot(first_op, second_op, precision=HIGH, preferred_element_type=jnp.float32)


def project_cols(weight, stream):
    return lax.dot_general(
        weight, stream, (((0,), (1,)), ((), ())), precision=HIGH, preferred_element_type=jnp.float32
    )


def layer_norm(stream, scale_gain, shift_bias):
    centre = jnp.mean(stream, axis=-1, keepdims=True)
    spread = stream - centre
    variance = jnp.mean(spread * spread, axis=-1, keepdims=True)
    return spread * lax.rsqrt(variance + 1e-05) * scale_gain + shift_bias


def fold_keys(state, pieces, queries, local_heads):
    key_piece, value_piece = pieces
    piece_len = key_piece.shape[1]
    block_count = max(1, piece_len // 1024)
    while piece_len % block_count:
        block_count += 1
    block_len = piece_len // block_count
    score_scale = 1.0 / math.sqrt(DH)

    def advance(block_num, carry):
        run_max, run_sum, run_acc = carry
        key_block = lax.dynamic_slice_in_dim(
            key_piece, block_num * block_len, block_len, 1
        ).reshape(local_heads, DH, block_len)
        value_block = lax.dynamic_slice_in_dim(
            value_piece, block_num * block_len, block_len, 1
        ).reshape(local_heads, DH, block_len)
        scores = (
            jnp.einsum(
                "hdk,hdq->hkq",
                key_block,
                queries,
                precision=HIGH,
                preferred_element_type=jnp.float32,
            )
            * score_scale
        )
        new_max = jnp.maximum(run_max, jnp.max(scores, axis=1))
        weights = jnp.exp(scores - new_max[:, None, :])
        rescale = jnp.exp(run_max - new_max)
        new_sum = run_sum * rescale + jnp.sum(weights, axis=1)
        new_acc = run_acc * rescale[:, None, :] + jnp.einsum(
            "hdk,hkq->hdq", value_block, weights, precision=HIGH, preferred_element_type=jnp.float32
        )
        return (new_max, new_sum, new_acc)

    return lax.fori_loop(0, block_count, advance, state)


def on_device(
    series,
    emb_weight,
    emb_bias,
    q_weight,
    k_weight,
    v_weight,
    out_weight,
    norm1_gain,
    norm1_bias,
    ffn_in,
    ffn_out,
    norm2_gain,
    norm2_bias,
):
    head_count = lax.axis_size("head")
    head_pos = lax.axis_index("head")
    model_width = emb_bias.shape[0]
    col_count = model_width // head_count
    col_start = head_pos * col_count
    partial_emb = product(series, emb_weight)
    embedded = lax.psum(partial_emb, "head") + emb_bias
    query_count = embedded.shape[0]
    local_heads = q_weight.shape[1] // DH
    queries = project_cols(q_weight, embedded).reshape(local_heads, DH, query_count)
    key_t = project_cols(k_weight, embedded)
    value_t = project_cols(v_weight, embedded)
    start_state = (
        jnp.full((local_heads, query_count), -1e30, jnp.float32),
        jnp.zeros((local_heads, query_count), jnp.float32),
        jnp.zeros((local_heads, DH, query_count), jnp.float32),
    )
    state = fold_keys(
        start_state,
        (
            lax.all_gather(key_t, "var", axis=1, tiled=True),
            lax.all_gather(value_t, "var", axis=1, tiled=True),
        ),
        queries,
        local_heads,
    )
    run_max, run_sum, run_acc = state
    mixed_t = (run_acc / run_sum[:, None, :]).reshape(local_heads * DH, query_count)
    partial_out = lax.dot_general(
        mixed_t,
        out_weight,
        (((0,), (0,)), ((), ())),
        precision=HIGH,
        preferred_element_type=jnp.float32,
    )
    attention = lax.psum(partial_out, "head")
    normed = layer_norm(embedded + attention, norm1_gain, norm1_bias)
    hidden = jax.nn.gelu(product(normed, ffn_in), approximate=False)
    ffn_t = lax.psum_scatter(
        lax.dot_general(
            ffn_out,
            hidden,
            (((0,), (1,)), ((), ())),
            precision=HIGH,
            preferred_element_type=jnp.float32,
        ),
        "head",
        scatter_dimension=0,
        tiled=True,
    )
    resid_t = lax.dynamic_slice_in_dim(normed, col_start, col_count, 1).T + ffn_t
    col_sums = lax.psum((jnp.sum(resid_t, axis=0), jnp.sum(resid_t * resid_t, axis=0)), "head")
    centre = col_sums[0] / model_width
    variance = col_sums[1] / model_width - centre * centre
    gain_part = lax.dynamic_slice_in_dim(norm2_gain, col_start, col_count)
    bias_part = lax.dynamic_slice_in_dim(norm2_bias, col_start, col_count)
    return (resid_t - centre[None, :]) * lax.rsqrt(variance[None, :] + 1e-05) * gain_part[
        :, None
    ] + bias_part[:, None]


def solution(mesh):
    return jax.shard_map(
        on_device,
        mesh=mesh,
        in_specs=(
            P("var", "head"),
            P("head", None),
            P(),
            P(None, "head"),
            P(None, "head"),
            P(None, "head"),
            P("head", None),
            P(),
            P(),
            P(None, "head"),
            P("head", None),
            P(),
            P(),
        ),
        out_specs=P("head", "var"),
        check_vma=False,
    )
```

profile of v0, /device:TPU:0, one launch (start us, length us, event | category | flops | bytes accessed | tf_op | source)
XLA Modules:
  0.0 158.4 jit_solution(4958936107451321450)
XLA Ops:
  6.5 0.0 copy-start
  6.5 0.0 copy-start.5
  6.5 0.0 copy-start.2
  6.5 0.0 copy-start.3
  6.5 0.0 all-reduce.4.cloned.1.call-start
  6.6 1.2 copy-done
  7.8 5.3 %fusion.132 = f32[128,512]{1,0:T(8,128)} fusion(f32[128,2048]{1,0:T(8,128)S(1)} %copy-done, f32[2048,512]{1,0:T(8,128)} %param.14), kind=kOutput, calls=%fused_computation.155 | convolution fusion | flops 1610612736 | bytes 5505024 | tf_op jit(solution)/shard_map/dot_general | solution.py:15
  13.1 0.0 copy-start.4
  13.1 0.0 all-reduce.4.cloned.1.call-update
  13.1 0.0 all-reduce.6.cloned.1.call-start
  13.2 38.4 %all-reduce.4.cloned.1.call-done = f32[128,512]{1,0:T(8,128)} async-done(((f32[128,512]{1,0:T(8,128)}), f32[128,512]{1,0:T(8,128)}) %all-reduce.4.cloned.1.call-update) | async-done | bytes 262160 | tf_op jit(solution)/shard_map/psum | solution.py:91
  51.6 0.0 copy-done.5
  51.6 0.0 copy-done.2
  51.6 0.0 copy-start.1
  51.6 1.4 convolution_bitcast_fusion.2
  53.0 9.8 %all_gather.6 = f32[128,1024]{0,1:T(8,128)S(1)} all-gather(f32[128,128]{0,1:T(8,128)S(1)} %convolution_bitcast_fusion.2), channel_id=1, replica_groups=mesh['var'=8,'head'=4] {'var'}, dimensions={1}, use_global_device_ids=true | all-gather | bytes 589824 | tf_op jit(solution)/shard_map/all_gather | solution.py:105
  62.8 0.2 copy.17
  63.0 0.0 copy-done.3
  63.1 1.5 fusion.62
  64.6 0.0 copy-start.6
  64.6 0.0 copy-start.7
  64.6 1.8 %fusion.131 = (f32[2,128]{1,0:T(2,128)S(1)}, f32[2,1024,128]{2,1,0:T(8,128)S(1)}) fusion(f32[2,64,1024]{2,1,0:T(8,128)S(1)} %bitcast.29, f32[2,64,128]{2,1,0:T(8,128)S(1)} %bitcast.31), kind=kOutput, calls=%fused_computation.154 | convolution fusion | flops 201850624 | bytes 1639424 | tf_op jit(solution)/shard_map/while/body/eval_jaxpr/hdk,hdq->hkq/dot_general | solution.py:49
  66.5 0.2 fusion.1
  66.6 0.0 copy-done.4
  66.6 0.0 copy-done.1
  66.6 0.4 convolution_bitcast_fusion.1
  67.0 9.8 %all_gather.7 = f32[128,1024]{0,1:T(8,128)S(1)} all-gather(f32[128,128]{0,1:T(8,128)S(1)} %convolution_bitcast_fusion.1), channel_id=1, replica_groups=mesh['var'=8,'head'=4] {'var'}, dimensions={1}, use_global_device_ids=true | all-gather | bytes 589824 | tf_op jit(solution)/shard_map/all_gather | solution.py:106
  76.9 0.2 copy.18
  77.1 0.9 fusion
  77.9 2.1 %fusion.133 = f32[128,512]{1,0:T(8,128)} fusion(f32[128,128]{1,0:T(8,128)S(1)} %bitcast.30, f32[128,512]{1,0:T(8,128)} %param.19), kind=kOutput, calls=%fused_computation.156 | convolution fusion | flops 100663296 | bytes 589824 | tf_op jit(solution)/shard_map/dot_general | solution.py:113
  80.0 0.0 all-reduce.6.cloned.1.call-update
  80.0 0.0 reduce-scatter.2.cloned.1.call-start
  80.1 34.6 %all-reduce.6.cloned.1.call-done = f32[128,512]{1,0:T(8,128)} async-done(((f32[128,512]{1,0:T(8,128)}), f32[128,512]{1,0:T(8,128)}) %all-reduce.6.cloned.1.call-update) | async-done | bytes 262160 | tf_op jit(solution)/shard_map/psum | solution.py:120
  114.7 1.1 fusion.130
  115.8 0.2 multiply_reduce_fusion
  116.0 0.0 copy-done.6
  116.0 0.0 copy-done.7
  116.0 0.1 multiply_add_fusion
  116.1 1.9 %fusion.134 = f32[128,512]{1,0:T(8,128)S(1)} fusion(f32[128,512]{1,0:T(8,128)S(1)} %multiply_add_fusion, f32[512,512]{1,0:T(8,128)} %param.22), kind=kOutput, calls=%fused_computation.157 | convolution fusion | flops 402653184 | bytes 1572864 | tf_op jit(solution)/shard_map/dot_general | solution.py:15
  118.1 3.2 %convolution_bitcast_fusion = f32[512,128]{0,1:T(8,128)} fusion(f32[512,512]{1,0:T(8,128)} %param.23, f32[128,512]{1,0:T(8,128)S(1)} %fusion.134), kind=kOutput, calls=%fused_computation.1 | convolution fusion | flops 406847488 | bytes 1572864 | tf_op jit(solution)/shard_map/dot_general | solution.py:124
  121.3 0.0 reduce-scatter.2.cloned.1.call-update
  121.3 0.8 dynamic_slice.14
  122.1 0.8 dynamic_slice.15
  122.8 18.5 %reduce-scatter.2.cloned.1.call-done = f32[128,128]{0,1:T(8,128)} async-done(((f32[512,128]{0,1:T(8,128)}), f32[128,128]{0,1:T(8,128)}) %reduce-scatter.2.cloned.1.call-update) | async-done | bytes 65552 | tf_op jit(solution)/shard_map/reduce_scatter | solution.py:123
  141.3 1.0 fusion.129
  142.3 8.8 %all-reduce = (f32[128]{0:T(128)S(1)}, f32[128]{0:T(128)S(1)}) all-reduce(f32[128]{0:T(128)S(1)} %get-tuple-element.20, f32[128]{0:T(128)S(1)} %get-tuple-element.19), channel_id=1, replica_groups=mesh['var'=8,'head'=4] {'head'}, use_global_device_ids=true, to_apply=%region_10.0 | all-reduce | flops 256 | bytes 2048 | tf_op jit(solution)/shard_map/psum | solution.py:136
  151.1 0.1 multiply_add_fusion.1
  151.2 0.7 copy.19
  (5 shorter events, 0.0 us)
Async XLA Ops:
  6.5 1.2 copy-start
  6.5 45.1 %copy-start.5 = (f32[512]{0:T(512)S(1)}, f32[512]{0:T(512)}, u32[]{:S(2)}) copy-start(f32[512]{0:T(512)} %param.15) | copy-start | bytes 6148
  6.5 45.1 %copy-start.2 = (f32[512,128]{1,0:T(8,128)S(1)}, f32[512,128]{1,0:T(8,128)}, u32[]{:S(2)}) copy-start(f32[512,128]{1,0:T(8,128)} %param.17) | copy-start | bytes 786436
  6.5 56.5 %copy-start.3 = (f32[512,128]{1,0:T(8,128)S(1)}, f32[512,128]{1,0:T(8,128)}, u32[]{:S(2)}) copy-start(f32[512,128]{1,0:T(8,128)} %param.16) | copy-start | bytes 786436
  6.5 45.1 %all-reduce.4.cloned.1.call-start = ((), (), s32[]{:S(2)}) async-start(), calls=%async_computation.1 | async-start | bytes 524288 | tf_op jit(solution)/shard_map/psum | solution.py:91
  13.1 53.5 %copy-start.4 = (f32[512,128]{1,0:T(8,128)S(1)}, f32[512,128]{1,0:T(8,128)}, u32[]{:S(2)}) copy-start(f32[512,128]{1,0:T(8,128)} %param.18) | copy-start | bytes 786436
  13.1 101.6 %all-reduce.6.cloned.1.call-start = ((), (), s32[]{:S(2)}) async-start(), calls=%async_computation.2 | async-start | bytes 524288 | tf_op jit(solution)/shard_map/psum | solution.py:120
  51.6 15.0 %copy-start.1 = (f32[128,512]{1,0:T(8,128)S(1)}, f32[128,512]{1,0:T(8,128)}, u32[]{:S(2)}) copy-start(f32[128,512]{1,0:T(8,128)} %all-reduce.4.cloned.1.call-done) | copy-start | bytes 786436
  64.6 51.4 %copy-start.6 = (f32[512]{0:T(512)S(1)}, f32[512]{0:T(512)}, u32[]{:S(2)}) copy-start(f32[512]{0:T(512)} %param.21) | copy-start | bytes 6148
  64.6 51.4 %copy-start.7 = (f32[512]{0:T(512)S(1)}, f32[512]{0:T(512)}, u32[]{:S(2)}) copy-start(f32[512]{0:T(512)} %param.20) | copy-start | bytes 6148
  80.0 61.3 %reduce-scatter.2.cloned.1.call-start = ((), (), s32[]{:S(2)}) async-start(), calls=%async_computation.3 | async-start | bytes 327680 | tf_op jit(solution)/shard_map/reduce_scatter | solution.py:123
Sparse Core Ops, SparseCore 0:
  13.2 38.3 all-reduce.3
  80.1 34.5 all-reduce.5
  121.4 19.8 reduce-scatter.1
where the time goes:
time: 159 us; the launch traced here: 158 us
  waiting for transfers between devices  91.6 us (58%)
  blocking collectives  28.4 us (18%)
  matrix products  18.6 us (12%)
  between operations  13.3 us (8%)
  local copies, waits for them, and re-layouts  3.84 us (2%)
  other arithmetic  2.62 us (2%)
    psum x1, waiting for transfers between devices, on_device(): embedded = lax.psum(partial_emb, 'head') + emb_bias  38.4 us
    psum x1, waiting for transfers between devices, on_device(): attention = lax.psum(partial_out, 'head')  34.6 us
    reduce_scatter x1, waiting for transfers between devices, on_device(): lax.psum_scatter(lax.dot_general(ffn_out, hidden, (((0,), (1,)), ((), ())...  18.5 us
    all_gather x1, blocking collectives, on_device(): lax.all_gather(key_t, 'var', axis=1, tiled=True)  9.81 us
    all_gather x1, blocking collectives, on_device(): lax.all_gather(value_t, 'var', axis=1, tiled=True)  9.81 us
    psum x1, blocking collectives, on_device(): lax.psum((jnp.sum(resid_t, axis=0), jnp.sum(resid_t * resid_t, axis=0)),...  8.75 us
    dot_general x2, matrix products, product(): jnp.dot(first_op, second_op, precision=HIGH, preferred_element_type=jnp.f...  7.26 us
    dot_general x3, matrix products, project_cols(): lax.dot_general(weight, stream, (((0,), (1,)), ((), ())), precision=HIGH,...  3.35 us
  transfers between devices with their start and end apart: 3, of which 3 were waited for; matrix products, arithmetic and copies ran while one was open for 1% of the time, Pallas kernels for 0%

commit v1 on v0

v1 whole, which is shorter than its diff:
```python
import functools
import math

import jax
import jax.numpy as jnp
from jax import lax
from jax.experimental import pallas as pl
from jax.experimental.pallas import tpu as pltpu
from jax.sharding import PartitionSpec as P

DH = 64
EPS = 1e-05
F32 = jnp.float32
BF16 = jnp.bfloat16
MIB = 1 << 20


def split(x):
    hi = x.astype(BF16)
    return hi, (x - hi.astype(F32)).astype(BF16)


def mm(a, b, dims):
    return lax.dot_general(a, b, (dims, ((), ())), preferred_element_type=F32)


def dot3(a, b, dims=((1,), (0,))):
    a_hi, a_lo = split(a)
    b_hi, b_lo = split(b)
    rows = a.shape[0]
    first = mm(jnp.concatenate([a_hi, a_lo], 0), b_hi, dims)
    return first[:rows] + (first[rows:] + mm(a_hi, b_lo, dims))


def butterfly(blocks, pos):
    count = len(blocks)
    out = list(blocks)
    bit = 1
    while bit < count:
        take = (pos & bit) != 0
        out = [jnp.where(take, out[j ^ bit], out[j]) for j in range(count)]
        bit *= 2
    return out


def columns(x, count):
    width = x.shape[1] // count
    return [x[:, j * width : (j + 1) * width] for j in range(count)]


def call(body, outs, name, scratch=(), limit=12, grid=None, in_specs=None, out_specs=None, flops=0, nbytes=0):
    kwargs = {}
    if grid is not None:
        kwargs = dict(grid=grid, in_specs=in_specs, out_specs=out_specs)
    return pl.pallas_call(
        body,
        out_shape=outs,
        scratch_shapes=list(scratch),
        name=name,
        compiler_params=pltpu.CompilerParams(vmem_limit_bytes=limit * MIB),
        cost_estimate=pl.CostEstimate(flops=flops, bytes_accessed=nbytes, transcendentals=0),
        **kwargs,
    )


def shape(*dims):
    return jax.ShapeDtypeStruct(dims, F32)


def embed_kernel(count, x_ref, w_ref, *rest):
    outs, acc = rest[:count], rest[count]
    step = pl.program_id(0)
    pos = lax.axis_index("head")
    part = dot3(x_ref[...], w_ref[...])

    @pl.when(step == 0)
    def _():
        acc[...] = part

    @pl.when(step > 0)
    def _():
        acc[...] += part

    @pl.when(step == pl.num_programs(0) - 1)
    def _():
        for ref, block in zip(outs, butterfly(columns(acc[...], count), pos)):
            ref[...] = block


def embed_reduce_kernel(count, *refs):
    pos = lax.axis_index("head")
    parts, bias, out = refs[:count], refs[count], refs[count + 1]
    total = parts[0][...]
    for part in parts[1:]:
        total = total + part[...]
    out[...] = total + bias[pos]


def rows_of(weight, block, width):
    return weight[pl.ds(pl.multiple_of(block * width, width), width), :]


def project_kernel(count, scale, *refs):
    pos = lax.axis_index("head")
    blocks, weights, out = refs[:count], refs[count:-1], refs[-1]
    width = blocks[0].shape[1]
    stream = jnp.concatenate([block[...] for block in blocks], 1)
    at = 0
    for weight in weights:
        ordered = jnp.concatenate([rows_of(weight, pos ^ k, width) for k in range(count)], 0)
        result = dot3(stream, ordered)
        out[:, at : at + result.shape[1]] = result * scale if scale != 1.0 else result
        at += result.shape[1]


def attend_kernel(q_ref, *refs):
    pieces, out = refs[:-1], refs[-1]
    heads_width = q_ref.shape[1]
    for head in range(heads_width // DH):
        cols = slice(head * DH, (head + 1) * DH)
        vcols = slice(heads_width + head * DH, heads_width + (head + 1) * DH)
        query = q_ref[:, cols]
        keys = jnp.concatenate([piece[:, cols] for piece in pieces], 0)
        values = jnp.concatenate([piece[:, vcols] for piece in pieces], 0)
        scores = dot3(query, keys, ((1,), (1,)))
        top = jnp.max(scores, axis=1, keepdims=True)
        weights = jnp.exp(scores - top)
        total = jnp.sum(weights, axis=1, keepdims=True)
        out[:, cols] = dot3(weights, values) / total


def normalise(x, gain, bias):
    centre = jnp.mean(x, axis=-1, keepdims=True)
    spread = x - centre
    variance = jnp.mean(spread * spread, axis=-1, keepdims=True)
    return spread * lax.rsqrt(variance + EPS) * gain + bias


def gelu(v):
    return 0.5 * v * (1.0 + lax.erf(v * (1.0 / math.sqrt(2.0))))


def post_kernel(count, *refs):
    pos = lax.axis_index("head")
    mixed, owts, emb = refs[:count], refs[count : 2 * count], refs[2 * count : 3 * count]
    gain, bias, w_in, w_out = refs[3 * count : 3 * count + 4]
    outs = refs[3 * count + 4 :]
    stream = jnp.concatenate([m[...] for m in mixed], 1)
    weight = jnp.concatenate([w[...] for w in owts], 0)
    attention = dot3(stream, weight)
    embedded = jnp.concatenate(butterfly([e[...] for e in emb], pos), 1)
    normed = normalise(embedded + attention, gain[...], bias[...])
    hidden = gelu(dot3(normed, w_in[...]))
    partial = butterfly(columns(dot3(hidden, w_out[...]), count), pos)
    mine = butterfly(columns(normed, count), pos)[0]
    outs[0][...] = mine + partial[0]
    for ref, block in zip(outs[1:], partial[1:]):
        ref[...] = block


def stats_kernel(count, *refs):
    parts, out, stats = refs[:count], refs[count], refs[count + 1]
    total = parts[0][...]
    for part in parts[1:]:
        total = total + part[...]
    flipped = total.T
    centre = jnp.mean(flipped, axis=0, keepdims=True)
    spread = flipped - centre
    out[...] = flipped
    stats[...] = jnp.concatenate([centre, jnp.sum(spread * spread, axis=0, keepdims=True)], 0)


def final_kernel(count, x_ref, *refs):
    pos = lax.axis_index("head")
    stats, gain, bias, out = refs[:count], refs[count], refs[count + 1], refs[count + 2]
    width = x_ref.shape[0]
    centres = [s[0:1, :] for s in stats]
    centre = sum(centres[1:], centres[0]) * (1.0 / count)
    square = sum((s[1:2, :] for s in stats[1:]), stats[0][1:2, :])
    for each in centres:
        square = square + width * (each - centre) * (each - centre)
    scale = lax.rsqrt(square * (1.0 / (count * width)) + EPS)
    pair = jnp.concatenate([gain[pos], bias[pos], jnp.zeros((6, width), F32)], 0).T
    out[...] = (x_ref[...] - centre) * scale * pair[:, 0:1] + pair[:, 1:2]


def send(x, axis, offset):
    size = lax.axis_size(axis)
    return lax.ppermute(x, axis, [(i, i ^ offset) for i in range(size)])


def spread_out(x, axis):
    return [x] + [send(x, axis, k) for k in range(1, lax.axis_size(axis))]


def gather_pieces(piece):
    size = lax.axis_size("var")
    if size > 8:
        return [lax.all_gather(piece, "var", axis=0, tiled=True)]
    far = [piece] + [send(piece, "var", k) for k in range(2, size, 2)]
    return far + [send(each, "var", 1) for each in far]


def on_device(
    series, emb_weight, emb_bias, q_weight, k_weight, v_weight, out_weight,
    norm1_gain, norm1_bias, ffn_in, ffn_out, norm2_gain, norm2_bias,
):
    n = lax.axis_size("head")
    rows, depth = series.shape
    model = emb_weight.shape[1]
    width = model // n
    heads_width = q_weight.shape[1]
    block = shape(rows, width)

    chunk = math.gcd(depth, 512)
    parts = call(
        functools.partial(embed_kernel, n), [block] * n, "embed",
        scratch=[pltpu.VMEM((rows, model), F32)],
        grid=(depth // chunk,),
        in_specs=[
            pl.BlockSpec((rows, chunk), lambda i: (0, i)),
            pl.BlockSpec((chunk, model), lambda i: (i, 0)),
        ],
        out_specs=[pl.BlockSpec((rows, width), lambda i: (0, 0))] * n,
        flops=6 * rows * depth * model, nbytes=4 * depth * (rows + model),
    )(series, emb_weight)
    got = [parts[0]] + [send(parts[k], "head", k) for k in range(1, n)]
    mine = call(functools.partial(embed_reduce_kernel, n), block, "embed_sum")(
        *got, emb_bias.reshape(n, 1, width)
    )
    emb = spread_out(mine, "head")
    pair = call(functools.partial(project_kernel, n, 1.0), shape(rows, 2 * heads_width), "project_kv")(
        *emb, k_weight, v_weight
    )
    queries = call(
        functools.partial(project_kernel, n, 1.0 / math.sqrt(DH)), shape(rows, heads_width), "project_q"
    )(*emb, q_weight)
    pieces = gather_pieces(pair)
    late_weight, _ = lax.optimization_barrier((out_weight, pair))
    owts = spread_out(late_weight, "head")
    mixed = call(attend_kernel, shape(rows, heads_width), "attend", limit=16)(queries, *pieces)
    mixes = spread_out(mixed, "head")
    partial = call(functools.partial(post_kernel, n), [block] * n, "post", limit=16)(
        *mixes, *owts, *emb, norm1_gain[None, :], norm1_bias[None, :], ffn_in, ffn_out
    )
    got = [partial[0]] + [send(partial[k], "head", k) for k in range(1, n)]
    flipped, stats = call(
        functools.partial(stats_kernel, n), [shape(width, rows), shape(2, rows)], "stats"
    )(*got)
    return call(functools.partial(final_kernel, n), shape(width, rows), "final")(
        flipped, *spread_out(stats, "head"), norm2_gain.reshape(n, 1, width), norm2_bias.reshape(n, 1, width)
    )


def solution(mesh):
    return jax.shard_map(
        on_device,
        mesh=mesh,
        in_specs=(
            P("var", "head"), P("head", None), P(), P(None, "head"), P(None, "head"), P(None, "head"),
            P("head", None), P(), P(), P(None, "head"), P("head", None), P(), P(),
        ),
        out_specs=P("head", "var"),
        check_vma=False,
    )
```

time: 159 us -> 80.6 us (0.51)
  waiting for transfers between devices: 91.6 us -> 30.5 us
  starting transfers between devices: 0.12 us -> 40 us
  blocking collectives: 28.4 us -> 0 us
  matrix products: 18.6 us -> 0 us
  between operations: 13.3 us -> 0.16 us
  Pallas kernels: 0 us -> 6.32 us
  other arithmetic: 2.62 us -> 0 us
    psum x2 -> x0, waiting for transfers between devices: 73.1 us -> none  [the longest x1 38.4 us: on_device(): embedded = lax.psum(partial_emb, 'head') + emb_bias]
    ppermute x0 -> x25, starting transfers between devices: none -> 40 us  [send(): return lax.ppermute(x, axis, [(i, i ^ offset) for i in range(size)])]
    ppermute x0 -> x25, waiting for transfers between devices: none -> 30.5 us  [send(): return lax.ppermute(x, axis, [(i, i ^ offset) for i in range(size)])]
    all_gather x2 -> x0, blocking collectives: 19.6 us -> none  [the longest x1 9.81 us: on_device(): lax.all_gather(key_t, 'var', axis=1, tiled=True)]
    dot_general x9 -> x0, matrix products: 18.6 us -> none  [the longest x2 7.26 us: product(): jnp.dot(first_op, second_op, precision=HIGH, preferred_element_type=jnp.f...]
    reduce_scatter x1 -> x0, waiting for transfers between devices: 18.5 us -> none  [on_device(): lax.psum_scatter(lax.dot_general(ffn_out, hidden, (((0,), (1,)), ((), ())...]
    psum x1 -> x0, blocking collectives: 8.75 us -> none  [on_device(): lax.psum((jnp.sum(resid_t, axis=0), jnp.sum(resid_t * resid_t, axis=0)),...]
    pallas_call x0 -> x8, Pallas kernels: none -> 6.32 us  [the longest x1 1.8 us: on_device(): call(functools.partial(embed_kernel, n), [block] * n, 'embed', scratch=[p...]
  transfers between devices with their start and end apart: 3 -> 25, of which waited for: 3 -> 15; matrix products, arithmetic and copies ran while one was open for 1% -> 0% of each run, Pallas kernels for 0% -> 2%
where the time goes in v1:
time: 80.6 us; the launch traced here: 80.5 us
  starting transfers between devices  40 us (50%)
  waiting for transfers between devices  30.5 us (38%)
  Pallas kernels  6.32 us (8%)
  local copies, waits for them, and re-layouts  3.46 us (4%)
    ppermute x25, starting transfers between devices, send(): return lax.ppermute(x, axis, [(i, i ^ offset) for i in range(size)])  40 us
    ppermute x25, waiting for transfers between devices, send(): return lax.ppermute(x, axis, [(i, i ^ offset) for i in range(size)])  30.5 us
    unnamed x26, local copies, waits for them, and re-layouts  3.46 us
    pallas_call x1, Pallas kernels, on_device(): call(functools.partial(embed_kernel, n), [block] * n, 'embed', scratch=[p...  1.8 us
  transfers between devices with their start and end apart: 25, of which 15 were waited for; matrix products, arithmetic and copies ran while one was open for 0% of the time, Pallas kernels for 2%

profile of v1, /device:TPU:0, one launch (start us, length us, event | category | flops | bytes accessed | tf_op | source)
XLA Modules:
  0.0 80.5 jit_solution(7391546762464103918)
XLA Ops:
  0.0 2.2 %copy-done = f32[2048,512]{1,0:T(8,128)S(1)} copy-done((f32[2048,512]{1,0:T(8,128)S(1)}, f32[2048,512]{1,0:T(8,128)}, u32[]{:S(2)}) %copy-start) | copy-done | bytes 4194328
  2.2 1.2 %copy-done.1 = f32[128,2048]{1,0:T(8,128)S(1)} copy-done((f32[128,2048]{1,0:T(8,128)S(1)}, f32[128,2048]{1,0:T(8,128)}, u32[]{:S(2)}) %copy-start.1) | copy-done | bytes 1048600
  3.5 1.8 %embed.1 = (f32[128,128]{1,0:T(8,128)S(1)}, f32[128,128]{1,0:T(8,128)S(1)}, f32[128,128]{1,0:T(8,128)S(1)}, f32[128,128]{1,0:T(8,128)S(1)}) custom-call(f32[128,2048]{1,0:T(8,128)S(1)} %copy-done.1, f32[2048,512]{1,0:T(8,128)S(1)} %copy-done), custom_call_target="tpu_custom_call" | custom-call | flops 805306368 | bytes 5242880 | tf_op jit(solution)/shard_map/embed/pallas_call | solution.py:216
  5.3 0.0 copy-start.11
  5.3 0.0 copy-start.12
  5.3 3.1 %collective-permute-start = (f32[128,128]{1,0:T(8,128)S(1)}, f32[128,128]{1,0:T(8,128)S(1)}, u32[]{:S(2)}, u32[]{:S(2)}) collective-permute-start(f32[128,128]{1,0:T(8,128)S(1)} %get-tuple-element.17), channel_id=1, source_target_pairs={{0,1},{1,0},{2,3},{3,2},{4,5},{5,4},{6,7},{7,6},{8,9},{9,8},{10,11... | collective-permute-start | bytes 196616 | tf_op jit(solution)/shard_map/ppermute | solution.py:189
  8.4 2.6 %collective-permute-start.1 = (f32[128,128]{1,0:T(8,128)S(1)}, f32[128,128]{1,0:T(8,128)S(1)}, u32[]{:S(2)}, u32[]{:S(2)}) collective-permute-start(f32[128,128]{1,0:T(8,128)S(1)} %get-tuple-element.18), channel_id=1, source_target_pairs={{0,2},{1,3},{2,0},{3,1},{4,6},{5,7},{6,4},{7,5},{8,10},{9,11},{10,... | collective-permute-start | bytes 196616 | tf_op jit(solution)/shard_map/ppermute | solution.py:189
  11.0 0.0 collective-permute-done.refs_1_
  11.0 4.7 %collective-permute-done.1.refs_2_ = f32[128,128]{1,0:T(8,128)S(1)} collective-permute-done((f32[128,128]{1,0:T(8,128)S(1)}, f32[128,128]{1,0:T(8,128)S(1)}, u32[]{:S(2)}, u32[]{:S(2)}) %collective-permute-start.1) | collective-permute-done | bytes 65568 | tf_op jit(solution)/shard_map/ppermute | solution.py:189
  15.7 1.4 %collective-permute-done.2.refs_3_ = f32[128,128]{1,0:T(8,128)S(1)} collective-permute-done((f32[128,128]{1,0:T(8,128)S(1)}, f32[128,128]{1,0:T(8,128)S(1)}, u32[]{:S(2)}, u32[]{:S(2)}) %collective-permute-start.2) | collective-permute-done | bytes 65568 | tf_op jit(solution)/shard_map/ppermute | solution.py:189
  17.1 1.8 %collective-permute-start.5 = (f32[128,128]{1,0:T(8,128)S(1)}, f32[128,128]{1,0:T(8,128)S(1)}, u32[]{:S(2)}, u32[]{:S(2)}) collective-permute-start(f32[128,128]{1,0:T(8,128)S(1)} %embed_sum.1.refs_0_.refs_8_), channel_id=1, source_target_pairs={{0,3},{1,2},{2,1},{3,0},{4,7},{5,6},{6,5},{7,4},{8,11},{9,10},{10,... | collective-permute-start | bytes 196616 | tf_op jit(solution)/shard_map/ppermute | solution.py:189
  19.0 0.0 collective-permute-start.4
  19.0 2.6 %collective-permute-start.3 = (f32[128,128]{1,0:T(8,128)S(1)}, f32[128,128]{1,0:T(8,128)S(1)}, u32[]{:S(2)}, u32[]{:S(2)}) collective-permute-start(f32[128,128]{1,0:T(8,128)S(1)} %embed_sum.1.refs_0_.refs_8_), channel_id=1, source_target_pairs={{0,1},{1,0},{2,3},{3,2},{4,5},{5,4},{6,7},{7,6},{8,9},{9,8},{10,11... | collective-permute-start | bytes 196616 | tf_op jit(solution)/shard_map/ppermute | solution.py:189
  21.6 1.7 %collective-permute-done.5.refs_3_.refs_11_ = f32[128,128]{1,0:T(8,128)S(1)} collective-permute-done((f32[128,128]{1,0:T(8,128)S(1)}, f32[128,128]{1,0:T(8,128)S(1)}, u32[]{:S(2)}, u32[]{:S(2)}) %collective-permute-start.5) | collective-permute-done | bytes 65568 | tf_op jit(solution)/shard_map/ppermute | solution.py:189
  23.2 1.4 %collective-permute-done.4.refs_2_.refs_10_ = f32[128,128]{1,0:T(8,128)S(1)} collective-permute-done((f32[128,128]{1,0:T(8,128)S(1)}, f32[128,128]{1,0:T(8,128)S(1)}, u32[]{:S(2)}, u32[]{:S(2)}) %collective-permute-start.4) | collective-permute-done | bytes 65568 | tf_op jit(solution)/shard_map/ppermute | solution.py:189
  24.6 0.0 collective-permute-done.3.refs_1_.refs_9_
  24.6 0.4 project_kv.1.refs_0_
  25.0 2.5 %collective-permute-start.8 = (f32[128,256]{1,0:T(8,128)S(1)}, f32[128,256]{1,0:T(8,128)S(1)}, u32[]{:S(2)}, u32[]{:S(2)}) collective-permute-start(f32[128,256]{1,0:T(8,128)S(1)} %project_kv.1.refs_0_), channel_id=1, source_target_pairs={{0,24},{4,28},{8,16},{12,20},{16,8},{20,12},{24,0},{28,4},{1,25},{... | collective-permute-start | bytes 393224 | tf_op jit(solution)/shard_map/ppermute | solution.py:189
  27.6 0.5 collective-permute-start.7
  28.1 0.5 collective-permute-start.6
  28.6 2.5 %collective-permute-done.8.refs_3_ = f32[128,256]{1,0:T(8,128)S(1)} collective-permute-done((f32[128,256]{1,0:T(8,128)S(1)}, f32[128,256]{1,0:T(8,128)S(1)}, u32[]{:S(2)}, u32[]{:S(2)}) %collective-permute-start.8) | collective-permute-done | bytes 131104 | tf_op jit(solution)/shard_map/ppermute | solution.py:189
  31.1 2.0 %collective-permute-start.18 = (f32[128,512]{1,0:T(8,128)S(1)}, f32[128,512]{1,0:T(8,128)S(1)}, u32[]{:S(2)}, u32[]{:S(2)}) collective-permute-start(f32[128,512]{1,0:T(8,128)S(1)} %copy-done.6), channel_id=1, source_target_pairs={{0,3},{1,2},{2,1},{3,0},{4,7},{5,6},{6,5},{7,4},{8,11},{9,10},{10,... | collective-permute-start | bytes 786440 | tf_op jit(solution)/shard_map/ppermute | solution.py:189
  33.1 0.6 collective-permute-start.17
  33.8 1.8 %collective-permute-start.16 = (f32[128,512]{1,0:T(8,128)S(1)}, f32[128,512]{1,0:T(8,128)S(1)}, u32[]{:S(2)}, u32[]{:S(2)}) collective-permute-start(f32[128,512]{1,0:T(8,128)S(1)} %copy-done.6), channel_id=1, source_target_pairs={{0,1},{1,0},{2,3},{3,2},{4,5},{5,4},{6,7},{7,6},{8,9},{9,8},{10,11... | collective-permute-start | bytes 786440 | tf_op jit(solution)/shard_map/ppermute | solution.py:189
  35.6 0.5 collective-permute-start.10
  36.1 0.3 project_q.1.q_ref
  36.3 0.6 collective-permute-done.11.refs_6_
  36.9 0.2 collective-permute-done.10.refs_5_
  37.1 1.6 %attend.1.refs_0_ = f32[128,128]{1,0:T(8,128)S(1)} custom-call(f32[128,128]{1,0:T(8,128)S(1)} %project_q.1.q_ref, f32[128,256]{1,0:T(8,128)S(1)} %project_kv.1.refs_0_, f32[128,256]{1,0:T(8,128)S(1)} %collective-permute-done.6.refs_1_, f32[128,256]{1,0:T(8,128)S(1)} %collective-permute-done.7.refs_2_, f32[128,256]{1,0:T(8,128)S(1)} %collective-permute-done.8.refs_3_, ...), custom_call_target="tpu_custom_call" | custom-call | tf_op jit(solution)/shard_map/attend/pallas_call | solution.py:241
  38.6 2.0 %collective-permute-start.15 = (f32[128,128]{1,0:T(8,128)S(1)}, f32[128,128]{1,0:T(8,128)S(1)}, u32[]{:S(2)}, u32[]{:S(2)}) collective-permute-start(f32[128,128]{1,0:T(8,128)S(1)} %attend.1.refs_0_), channel_id=1, source_target_pairs={{0,3},{1,2},{2,1},{3,0},{4,7},{5,6},{6,5},{7,4},{8,11},{9,10},{10,... | collective-permute-start | bytes 196616 | tf_op jit(solution)/shard_map/ppermute | solution.py:189
  40.7 1.6 %collective-permute-done.18.refs_7_ = f32[128,512]{1,0:T(8,128)S(1)} collective-permute-done((f32[128,512]{1,0:T(8,128)S(1)}, f32[128,512]{1,0:T(8,128)S(1)}, u32[]{:S(2)}, u32[]{:S(2)}) %collective-permute-start.18) | collective-permute-done | bytes 262176 | tf_op jit(solution)/shard_map/ppermute | solution.py:189
  42.3 10.5 %collective-permute-start.13 = (f32[128,128]{1,0:T(8,128)S(1)}, f32[128,128]{1,0:T(8,128)S(1)}, u32[]{:S(2)}, u32[]{:S(2)}) collective-permute-start(f32[128,128]{1,0:T(8,128)S(1)} %attend.1.refs_0_), channel_id=1, source_target_pairs={{0,1},{1,0},{2,3},{3,2},{4,5},{5,4},{6,7},{7,6},{8,9},{9,8},{10,11... | collective-permute-start | bytes 196616 | tf_op jit(solution)/shard_map/ppermute | solution.py:189
  52.7 7.9 %collective-permute-done.17.refs_6_ = f32[128,512]{1,0:T(8,128)S(1)} collective-permute-done((f32[128,512]{1,0:T(8,128)S(1)}, f32[128,512]{1,0:T(8,128)S(1)}, u32[]{:S(2)}, u32[]{:S(2)}) %collective-permute-start.17) | collective-permute-done | bytes 262176 | tf_op jit(solution)/shard_map/ppermute | solution.py:189
  60.6 2.3 %collective-permute-done.14.refs_2_ = f32[128,128]{1,0:T(8,128)S(1)} collective-permute-done((f32[128,128]{1,0:T(8,128)S(1)}, f32[128,128]{1,0:T(8,128)S(1)}, u32[]{:S(2)}, u32[]{:S(2)}) %collective-permute-start.14) | collective-permute-done | bytes 65568 | tf_op jit(solution)/shard_map/ppermute | solution.py:189
  63.0 1.3 %post.1 = (f32[128,128]{1,0:T(8,128)S(1)}, f32[128,128]{1,0:T(8,128)S(1)}, f32[128,128]{1,0:T(8,128)S(1)}, f32[128,128]{1,0:T(8,128)S(1)}) custom-call(f32[128,128]{1,0:T(8,128)S(1)} %attend.1.refs_0_, f32[128,128]{1,0:T(8,128)S(1)} %collective-permute-done.13.refs_1_, f32[128,128]{1,0:T(8,128)S(1)} %collective-permute-done.14.refs_2_, ...), custom_call_target="tpu_custom_call" | custom-call | tf_op jit(solution)/shard_map/post/pallas_call | solution.py:243
  64.3 0.1 collective-permute-start.19
  64.4 2.3 %collective-permute-start.20 = (f32[128,128]{1,0:T(8,128)S(1)}, f32[128,128]{1,0:T(8,128)S(1)}, u32[]{:S(2)}, u32[]{:S(2)}) collective-permute-start(f32[128,128]{1,0:T(8,128)S(1)} %get-tuple-element.23), channel_id=1, source_target_pairs={{0,2},{1,3},{2,0},{3,1},{4,6},{5,7},{6,4},{7,5},{8,10},{9,11},{10,... | collective-permute-start | bytes 196616 | tf_op jit(solution)/shard_map/ppermute | solution.py:189
  66.7 2.0 %collective-permute-start.21 = (f32[128,128]{1,0:T(8,128)S(1)}, f32[128,128]{1,0:T(8,128)S(1)}, u32[]{:S(2)}, u32[]{:S(2)}) collective-permute-start(f32[128,128]{1,0:T(8,128)S(1)} %get-tuple-element.24), channel_id=1, source_target_pairs={{0,3},{1,2},{2,1},{3,0},{4,7},{5,6},{6,5},{7,4},{8,11},{9,10},{10,... | collective-permute-start | bytes 196616 | tf_op jit(solution)/shard_map/ppermute | solution.py:189
  68.7 0.2 collective-permute-done.19.refs_1_
  69.0 2.8 %collective-permute-done.20.refs_2_ = f32[128,128]{1,0:T(8,128)S(1)} collective-permute-done((f32[128,128]{1,0:T(8,128)S(1)}, f32[128,128]{1,0:T(8,128)S(1)}, u32[]{:S(2)}, u32[]{:S(2)}) %collective-permute-start.20) | collective-permute-done | bytes 65568 | tf_op jit(solution)/shard_map/ppermute | solution.py:189
  71.8 1.0 %collective-permute-done.21.refs_3_ = f32[128,128]{1,0:T(8,128)S(1)} collective-permute-done((f32[128,128]{1,0:T(8,128)S(1)}, f32[128,128]{1,0:T(8,128)S(1)}, u32[]{:S(2)}, u32[]{:S(2)}) %collective-permute-start.21) | collective-permute-done | bytes 65568 | tf_op jit(solution)/shard_map/ppermute | solution.py:189
  72.8 0.1 stats.1
  72.9 2.2 %collective-permute-start.24 = (f32[2,128]{1,0:T(2,128)S(1)}, f32[2,128]{1,0:T(2,128)S(1)}, u32[]{:S(2)}, u32[]{:S(2)}) collective-permute-start(f32[2,128]{1,0:T(2,128)S(1)} %get-tuple-element.26.refs_0_), channel_id=1, source_target_pairs={{0,3},{1,2},{2,1},{3,0},{4,7},{5,6},{6,5},{7,4},{8,11},{9,10},{10,... | collective-permute-start | bytes 3080 | tf_op jit(solution)/shard_map/ppermute | solution.py:189
  75.1 0.3 collective-permute-start.23
  75.4 1.9 %collective-permute-start.22 = (f32[2,128]{1,0:T(2,128)S(1)}, f32[2,128]{1,0:T(2,128)S(1)}, u32[]{:S(2)}, u32[]{:S(2)}) collective-permute-start(f32[2,128]{1,0:T(2,128)S(1)} %get-tuple-element.26.refs_0_), channel_id=1, source_target_pairs={{0,1},{1,0},{2,3},{3,2},{4,5},{5,4},{6,7},{7,6},{8,9},{9,8},{10,11... | collective-permute-start | bytes 3080 | tf_op jit(solution)/shard_map/ppermute | solution.py:189
  77.4 1.0 %collective-permute-done.24.refs_3_ = f32[2,128]{1,0:T(2,128)S(1)} collective-permute-done((f32[2,128]{1,0:T(2,128)S(1)}, f32[2,128]{1,0:T(2,128)S(1)}, u32[]{:S(2)}, u32[]{:S(2)}) %collective-permute-start.24) | collective-permute-done | bytes 1056 | tf_op jit(solution)/shard_map/ppermute | solution.py:189
  78.3 1.2 %collective-permute-done.23.refs_2_ = f32[2,128]{1,0:T(2,128)S(1)} collective-permute-done((f32[2,128]{1,0:T(2,128)S(1)}, f32[2,128]{1,0:T(2,128)S(1)}, u32[]{:S(2)}, u32[]{:S(2)}) %collective-permute-start.23) | collective-permute-done | bytes 1056 | tf_op jit(solution)/shard_map/ppermute | solution.py:189
  79.6 0.8 %final.1 = f32[128,128]{1,0:T(8,128)} custom-call(f32[128,128]{1,0:T(8,128)S(1)} %get-tuple-element.25.x_ref, f32[2,128]{1,0:T(2,128)S(1)} %get-tuple-element.26.refs_0_, f32[2,128]{1,0:T(2,128)S(1)} %collective-permute-done.22.refs_1_, f32[2,128]{1,0:T(2,128)S(1)} %collective-permute-done.23.refs_2_, f32[2,128]{1,0:T(2,128)S(1)} %collective-permute-done.24.refs_3_, ...), custom_call_target="tpu_custom_call" | custom-call | tf_op jit(solution)/shard_map/final/pallas_call | solution.py:250
  (36 shorter events, 0.1 us)
Async XLA Ops:
  0.0 2.2 %copy-start = (f32[2048,512]{1,0:T(8,128)S(1)}, f32[2048,512]{1,0:T(8,128)}, u32[]{:S(2)}) copy-start(f32[2048,512]{1,0:T(8,128)} %w_ref.1) | copy-start | bytes 12582916
  2.2 1.2 %copy-start.1 = (f32[128,2048]{1,0:T(8,128)S(1)}, f32[128,2048]{1,0:T(8,128)}, u32[]{:S(2)}) copy-start(f32[128,2048]{1,0:T(8,128)} %x_ref.1) | copy-start | bytes 3145732
  3.4 13.7 %copy-start.8 = (f32[512]{0:T(512)S(1)}, f32[512]{0:T(512)}, u32[]{:S(2)}) copy-start(f32[512]{0:T(512)} %param.15) | copy-start | bytes 6148
  3.4 21.2 %copy-start.4 = (f32[512,128]{1,0:T(8,128)S(1)}, f32[512,128]{1,0:T(8,128)}, u32[]{:S(2)}) copy-start(f32[512,128]{1,0:T(8,128)} %refs_4_.3) | copy-start | bytes 786436
  3.4 21.2 %copy-start.5 = (f32[512,128]{1,0:T(8,128)S(1)}, f32[512,128]{1,0:T(8,128)}, u32[]{:S(2)}) copy-start(f32[512,128]{1,0:T(8,128)} %refs_5_.1) | copy-start | bytes 786436
  3.4 27.7 %copy-start.6 = (f32[128,512]{1,0:T(8,128)S(1)}, f32[128,512]{1,0:T(8,128)}, u32[]{:S(2)}) copy-start(f32[128,512]{1,0:T(8,128)} %refs_4_.4) | copy-start | bytes 786436
  3.4 32.6 %copy-start.7 = (f32[512,128]{1,0:T(8,128)S(1)}, f32[512,128]{1,0:T(8,128)}, u32[]{:S(2)}) copy-start(f32[512,128]{1,0:T(8,128)} %refs_4_.2) | copy-start | bytes 786436
  3.4 59.5 %copy-start.2 = (f32[512,512]{1,0:T(8,128)S(1)}, f32[512,512]{1,0:T(8,128)}, u32[]{:S(2)}) copy-start(f32[512,512]{1,0:T(8,128)} %refs_14_.1) | copy-start | bytes 3145732
  3.4 59.5 %copy-start.3 = (f32[512,512]{1,0:T(8,128)S(1)}, f32[512,512]{1,0:T(8,128)}, u32[]{:S(2)}) copy-start(f32[512,512]{1,0:T(8,128)} %refs_15_.1) | copy-start | bytes 3145732
  3.5 59.5 %copy-start.9 = (f32[512]{0:T(512)S(1)}, f32[512]{0:T(512)}, u32[]{:S(2)}) copy-start(f32[512]{0:T(512)} %param.20) | copy-start | bytes 6148
  3.5 59.5 %copy-start.10 = (f32[512]{0:T(512)S(1)}, f32[512]{0:T(512)}, u32[]{:S(2)}) copy-start(f32[512]{0:T(512)} %param.21) | copy-start | bytes 6148
  5.3 74.3 %copy-start.11 = (f32[512]{0:T(512)S(1)}, f32[512]{0:T(512)}, u32[]{:S(2)}) copy-start(f32[512]{0:T(512)} %param.24) | copy-start | bytes 6148
  5.3 74.3 %copy-start.12 = (f32[512]{0:T(512)S(1)}, f32[512]{0:T(512)}, u32[]{:S(2)}) copy-start(f32[512]{0:T(512)} %param.25) | copy-start | bytes 6148
  5.3 5.7 %collective-permute-start = (f32[128,128]{1,0:T(8,128)S(1)}, f32[128,128]{1,0:T(8,128)S(1)}, u32[]{:S(2)}, u32[]{:S(2)}) collective-permute-start(f32[128,128]{1,0:T(8,128)S(1)} %get-tuple-element.17), channel_id=1, source_target_pairs={{0,1},{1,0},{2,3},{3,2},{4,5},{5,4},{6,7},{7,6},{8,9},{9,8},{10,11... | collective-permute-start | bytes 196616 | tf_op jit(solution)/shard_map/ppermute | solution.py:189
  8.4 7.3 %collective-permute-start.1 = (f32[128,128]{1,0:T(8,128)S(1)}, f32[128,128]{1,0:T(8,128)S(1)}, u32[]{:S(2)}, u32[]{:S(2)}) collective-permute-start(f32[128,128]{1,0:T(8,128)S(1)} %get-tuple-element.18), channel_id=1, source_target_pairs={{0,2},{1,3},{2,0},{3,1},{4,6},{5,7},{6,4},{7,5},{8,10},{9,11},{10,... | collective-permute-start | bytes 196616 | tf_op jit(solution)/shard_map/ppermute | solution.py:189
  11.0 6.1 %collective-permute-start.2 = (f32[128,128]{1,0:T(8,128)S(1)}, f32[128,128]{1,0:T(8,128)S(1)}, u32[]{:S(2)}, u32[]{:S(2)}) collective-permute-start(f32[128,128]{1,0:T(8,128)S(1)} %get-tuple-element.19), channel_id=1, source_target_pairs={{0,3},{1,2},{2,1},{3,0},{4,7},{5,6},{6,5},{7,4},{8,11},{9,10},{10,... | collective-permute-start | bytes 196616 | tf_op jit(solution)/shard_map/ppermute | solution.py:189
  17.1 6.1 %collective-permute-start.5 = (f32[128,128]{1,0:T(8,128)S(1)}, f32[128,128]{1,0:T(8,128)S(1)}, u32[]{:S(2)}, u32[]{:S(2)}) collective-permute-start(f32[128,128]{1,0:T(8,128)S(1)} %embed_sum.1.refs_0_.refs_8_), channel_id=1, source_target_pairs={{0,3},{1,2},{2,1},{3,0},{4,7},{5,6},{6,5},{7,4},{8,11},{9,10},{10,... | collective-permute-start | bytes 196616 | tf_op jit(solution)/shard_map/ppermute | solution.py:189
  19.0 5.7 %collective-permute-start.4 = (f32[128,128]{1,0:T(8,128)S(1)}, f32[128,128]{1,0:T(8,128)S(1)}, u32[]{:S(2)}, u32[]{:S(2)}) collective-permute-start(f32[128,128]{1,0:T(8,128)S(1)} %embed_sum.1.refs_0_.refs_8_), channel_id=1, source_target_pairs={{0,2},{1,3},{2,0},{3,1},{4,6},{5,7},{6,4},{7,5},{8,10},{9,11},{10,... | collective-permute-start | bytes 196616 | tf_op jit(solution)/shard_map/ppermute | solution.py:189
  19.0 5.7 %collective-permute-start.3 = (f32[128,128]{1,0:T(8,128)S(1)}, f32[128,128]{1,0:T(8,128)S(1)}, u32[]{:S(2)}, u32[]{:S(2)}) collective-permute-start(f32[128,128]{1,0:T(8,128)S(1)} %embed_sum.1.refs_0_.refs_8_), channel_id=1, source_target_pairs={{0,1},{1,0},{2,3},{3,2},{4,5},{5,4},{6,7},{7,6},{8,9},{9,8},{10,11... | collective-permute-start | bytes 196616 | tf_op jit(solution)/shard_map/ppermute | solution.py:189
  25.0 6.1 %collective-permute-start.8 = (f32[128,256]{1,0:T(8,128)S(1)}, f32[128,256]{1,0:T(8,128)S(1)}, u32[]{:S(2)}, u32[]{:S(2)}) collective-permute-start(f32[128,256]{1,0:T(8,128)S(1)} %project_kv.1.refs_0_), channel_id=1, source_target_pairs={{0,24},{4,28},{8,16},{12,20},{16,8},{20,12},{24,0},{28,4},{1,25},{... | collective-permute-start | bytes 393224 | tf_op jit(solution)/shard_map/ppermute | solution.py:189
  27.5 5.6 %collective-permute-start.9 = (f32[128,256]{1,0:T(8,128)S(1)}, f32[128,256]{1,0:T(8,128)S(1)}, u32[]{:S(2)}, u32[]{:S(2)}) collective-permute-start(f32[128,256]{1,0:T(8,128)S(1)} %project_kv.1.refs_0_), channel_id=1, source_target_pairs={{0,4},{4,0},{8,12},{12,8},{16,20},{20,16},{24,28},{28,24},{1,5},{5... | collective-permute-start | bytes 393224 | tf_op jit(solution)/shard_map/ppermute | solution.py:189
  27.6 6.2 %collective-permute-start.7 = (f32[128,256]{1,0:T(8,128)S(1)}, f32[128,256]{1,0:T(8,128)S(1)}, u32[]{:S(2)}, u32[]{:S(2)}) collective-permute-start(f32[128,256]{1,0:T(8,128)S(1)} %project_kv.1.refs_0_), channel_id=1, source_target_pairs={{0,16},{4,20},{8,24},{12,28},{16,0},{20,4},{24,8},{28,12},{1,17},{... | collective-permute-start | bytes 393224 | tf_op jit(solution)/shard_map/ppermute | solution.py:189
  28.1 7.5 %collective-permute-start.6 = (f32[128,256]{1,0:T(8,128)S(1)}, f32[128,256]{1,0:T(8,128)S(1)}, u32[]{:S(2)}, u32[]{:S(2)}) collective-permute-start(f32[128,256]{1,0:T(8,128)S(1)} %project_kv.1.refs_0_), channel_id=1, source_target_pairs={{0,8},{4,12},{8,0},{12,4},{16,24},{20,28},{24,16},{28,20},{1,9},{5... | collective-permute-start | bytes 393224 | tf_op jit(solution)/shard_map/ppermute | solution.py:189
  31.1 4.4 %collective-permute-start.12 = (f32[128,256]{1,0:T(8,128)S(1)}, f32[128,256]{1,0:T(8,128)S(1)}, u32[]{:S(2)}, u32[]{:S(2)}) collective-permute-start(f32[128,256]{1,0:T(8,128)S(1)} %collective-permute-done.8.refs_3_), channel_id=1, source_target_pairs={{0,4},{4,0},{8,12},{12,8},{16,20},{20,16},{24,28},{28,24},{1,5},{5... | collective-permute-start | bytes 393224 | tf_op jit(solution)/shard_map/ppermute | solution.py:189
  31.1 11.1 %collective-permute-start.18 = (f32[128,512]{1,0:T(8,128)S(1)}, f32[128,512]{1,0:T(8,128)S(1)}, u32[]{:S(2)}, u32[]{:S(2)}) collective-permute-start(f32[128,512]{1,0:T(8,128)S(1)} %copy-done.6), channel_id=1, source_target_pairs={{0,3},{1,2},{2,1},{3,0},{4,7},{5,6},{6,5},{7,4},{8,11},{9,10},{10,... | collective-permute-start | bytes 786440 | tf_op jit(solution)/shard_map/ppermute | solution.py:189
  33.1 27.5 %collective-permute-start.17 = (f32[128,512]{1,0:T(8,128)S(1)}, f32[128,512]{1,0:T(8,128)S(1)}, u32[]{:S(2)}, u32[]{:S(2)}) collective-permute-start(f32[128,512]{1,0:T(8,128)S(1)} %copy-done.6), channel_id=1, source_target_pairs={{0,2},{1,3},{2,0},{3,1},{4,6},{5,7},{6,4},{7,5},{8,10},{9,11},{10,... | collective-permute-start | bytes 786440 | tf_op jit(solution)/shard_map/ppermute | solution.py:189
  33.8 26.8 %collective-permute-start.16 = (f32[128,512]{1,0:T(8,128)S(1)}, f32[128,512]{1,0:T(8,128)S(1)}, u32[]{:S(2)}, u32[]{:S(2)}) collective-permute-start(f32[128,512]{1,0:T(8,128)S(1)} %copy-done.6), channel_id=1, source_target_pairs={{0,1},{1,0},{2,3},{3,2},{4,5},{5,4},{6,7},{7,6},{8,9},{9,8},{10,11... | collective-permute-start | bytes 786440 | tf_op jit(solution)/shard_map/ppermute | solution.py:189
  35.5 1.3 %collective-permute-start.11 = (f32[128,256]{1,0:T(8,128)S(1)}, f32[128,256]{1,0:T(8,128)S(1)}, u32[]{:S(2)}, u32[]{:S(2)}) collective-permute-start(f32[128,256]{1,0:T(8,128)S(1)} %collective-permute-done.7.refs_2_), channel_id=1, source_target_pairs={{0,4},{4,0},{8,12},{12,8},{16,20},{20,16},{24,28},{28,24},{1,5},{5... | collective-permute-start | bytes 393224 | tf_op jit(solution)/shard_map/ppermute | solution.py:189
  35.6 1.5 %collective-permute-start.10 = (f32[128,256]{1,0:T(8,128)S(1)}, f32[128,256]{1,0:T(8,128)S(1)}, u32[]{:S(2)}, u32[]{:S(2)}) collective-permute-start(f32[128,256]{1,0:T(8,128)S(1)} %collective-permute-done.6.refs_1_), channel_id=1, source_target_pairs={{0,4},{4,0},{8,12},{12,8},{16,20},{20,16},{24,28},{28,24},{1,5},{5... | collective-permute-start | bytes 393224 | tf_op jit(solution)/shard_map/ppermute | solution.py:189
  38.6 22.0 %collective-permute-start.15 = (f32[128,128]{1,0:T(8,128)S(1)}, f32[128,128]{1,0:T(8,128)S(1)}, u32[]{:S(2)}, u32[]{:S(2)}) collective-permute-start(f32[128,128]{1,0:T(8,128)S(1)} %attend.1.refs_0_), channel_id=1, source_target_pairs={{0,3},{1,2},{2,1},{3,0},{4,7},{5,6},{6,5},{7,4},{8,11},{9,10},{10,... | collective-permute-start | bytes 196616 | tf_op jit(solution)/shard_map/ppermute | solution.py:189
  40.7 22.3 %collective-permute-start.14 = (f32[128,128]{1,0:T(8,128)S(1)}, f32[128,128]{1,0:T(8,128)S(1)}, u32[]{:S(2)}, u32[]{:S(2)}) collective-permute-start(f32[128,128]{1,0:T(8,128)S(1)} %attend.1.refs_0_), channel_id=1, source_target_pairs={{0,2},{1,3},{2,0},{3,1},{4,6},{5,7},{6,4},{7,5},{8,10},{9,11},{10,... | collective-permute-start | bytes 196616 | tf_op jit(solution)/shard_map/ppermute | solution.py:189
  42.3 20.7 %collective-permute-start.13 = (f32[128,128]{1,0:T(8,128)S(1)}, f32[128,128]{1,0:T(8,128)S(1)}, u32[]{:S(2)}, u32[]{:S(2)}) collective-permute-start(f32[128,128]{1,0:T(8,128)S(1)} %attend.1.refs_0_), channel_id=1, source_target_pairs={{0,1},{1,0},{2,3},{3,2},{4,5},{5,4},{6,7},{7,6},{8,9},{9,8},{10,11... | collective-permute-start | bytes 196616 | tf_op jit(solution)/shard_map/ppermute | solution.py:189
  64.3 4.7 %collective-permute-start.19 = (f32[128,128]{1,0:T(8,128)S(1)}, f32[128,128]{1,0:T(8,128)S(1)}, u32[]{:S(2)}, u32[]{:S(2)}) collective-permute-start(f32[128,128]{1,0:T(8,128)S(1)} %get-tuple-element.22), channel_id=1, source_target_pairs={{0,1},{1,0},{2,3},{3,2},{4,5},{5,4},{6,7},{7,6},{8,9},{9,8},{10,11... | collective-permute-start | bytes 196616 | tf_op jit(solution)/shard_map/ppermute | solution.py:189
  64.4 7.4 %collective-permute-start.20 = (f32[128,128]{1,0:T(8,128)S(1)}, f32[128,128]{1,0:T(8,128)S(1)}, u32[]{:S(2)}, u32[]{:S(2)}) collective-permute-start(f32[128,128]{1,0:T(8,128)S(1)} %get-tuple-element.23), channel_id=1, source_target_pairs={{0,2},{1,3},{2,0},{3,1},{4,6},{5,7},{6,4},{7,5},{8,10},{9,11},{10,... | collective-permute-start | bytes 196616 | tf_op jit(solution)/shard_map/ppermute | solution.py:189
  66.7 6.1 %collective-permute-start.21 = (f32[128,128]{1,0:T(8,128)S(1)}, f32[128,128]{1,0:T(8,128)S(1)}, u32[]{:S(2)}, u32[]{:S(2)}) collective-permute-start(f32[128,128]{1,0:T(8,128)S(1)} %get-tuple-element.24), channel_id=1, source_target_pairs={{0,3},{1,2},{2,1},{3,0},{4,7},{5,6},{6,5},{7,4},{8,11},{9,10},{10,... | collective-permute-start | bytes 196616 | tf_op jit(solution)/shard_map/ppermute | solution.py:189
  72.9 5.4 %collective-permute-start.24 = (f32[2,128]{1,0:T(2,128)S(1)}, f32[2,128]{1,0:T(2,128)S(1)}, u32[]{:S(2)}, u32[]{:S(2)}) collective-permute-start(f32[2,128]{1,0:T(2,128)S(1)} %get-tuple-element.26.refs_0_), channel_id=1, source_target_pairs={{0,3},{1,2},{2,1},{3,0},{4,7},{5,6},{6,5},{7,4},{8,11},{9,10},{10,... | collective-permute-start | bytes 3080 | tf_op jit(solution)/shard_map/ppermute | solution.py:189
  75.1 4.5 %collective-permute-start.23 = (f32[2,128]{1,0:T(2,128)S(1)}, f32[2,128]{1,0:T(2,128)S(1)}, u32[]{:S(2)}, u32[]{:S(2)}) collective-permute-start(f32[2,128]{1,0:T(2,128)S(1)} %get-tuple-element.26.refs_0_), channel_id=1, source_target_pairs={{0,2},{1,3},{2,0},{3,1},{4,6},{5,7},{6,4},{7,5},{8,10},{9,11},{10,... | collective-permute-start | bytes 3080 | tf_op jit(solution)/shard_map/ppermute | solution.py:189
  75.4 4.2 %collective-permute-start.22 = (f32[2,128]{1,0:T(2,128)S(1)}, f32[2,128]{1,0:T(2,128)S(1)}, u32[]{:S(2)}, u32[]{:S(2)}) collective-permute-start(f32[2,128]{1,0:T(2,128)S(1)} %get-tuple-element.26.refs_0_), channel_id=1, source_target_pairs={{0,1},{1,0},{2,3},{3,2},{4,5},{5,4},{6,7},{7,6},{8,9},{9,8},{10,11... | collective-permute-start | bytes 3080 | tf_op jit(solution)/shard_map/ppermute | solution.py:189

commit v2 on v1

--- a/solution.py
+++ b/solution.py
@@ -7,6 +7,7 @@
 from jax.experimental import pallas as pl
 from jax.experimental.pallas import tpu as pltpu
 from jax.sharding import PartitionSpec as P
+
 
 DH = 64
 EPS = 1e-05
@@ -48,7 +49,7 @@
     return [x[:, j * width : (j + 1) * width] for j in range(count)]
 
 
-def call(body, outs, name, scratch=(), limit=12, grid=None, in_specs=None, out_specs=None, flops=0, nbytes=0):
+def call(body, outs, scratch=(), limit=12, grid=None, in_specs=None, out_specs=None, flops=0, nbytes=0):
     kwargs = {}
     if grid is not None:
         kwargs = dict(grid=grid, in_specs=in_specs, out_specs=out_specs)
@@ -56,7 +57,6 @@
         body,
         out_shape=outs,
         scratch_shapes=list(scratch),
-        name=name,
         compiler_params=pltpu.CompilerParams(vmem_limit_bytes=limit * MIB),
         cost_estimate=pl.CostEstimate(flops=flops, bytes_accessed=nbytes, transcendentals=0),
         **kwargs,
@@ -67,24 +67,75 @@
     return jax.ShapeDtypeStruct(dims, F32)
 
 
-def embed_kernel(count, x_ref, w_ref, *rest):
-    outs, acc = rest[:count], rest[count]
-    step = pl.program_id(0)
-    pos = lax.axis_index("head")
-    part = dot3(x_ref[...], w_ref[...])
-
-    @pl.when(step == 0)
-    def _():
-        acc[...] = part
-
-    @pl.when(step > 0)
-    def _():
-        acc[...] += part
-
-    @pl.when(step == pl.num_programs(0) - 1)
-    def _():
-        for ref, block in zip(outs, butterfly(columns(acc[...], count), pos)):
-            ref[...] = block
+def embed_kernel(count, far, x_hbm, w_hbm, *rest):
+    outs, (x_buf, w_buf, sems) = rest[: count // 2], rest[count // 2 :]
+    pos = lax.axis_index("head")
+    half = w_hbm.shape[1] // 2
+    side = pos // (count // 2)
+    side = 1 - side if far else side
+    cols = pl.ds(pl.multiple_of(side * half, half), half)
+    steps, step = w_buf.shape[0], w_buf.shape[1]
+    copies = []
+    for at in range(steps):
+        span = pl.ds(at * step, step)
+        copies.append(
+            (
+                pltpu.make_async_copy(x_hbm.at[:, span], x_buf.at[at], sems.at[0, at]),
+                pltpu.make_async_copy(w_hbm.at[span, cols], w_buf.at[at], sems.at[1, at]),
+            )
+        )
+        for copy in copies[-1]:
+            copy.start()
+    total = None
+    for at in range(steps):
+        for copy in copies[at]:
+            copy.wait()
+        part = dot3(x_buf[at], w_buf[at])
+        total = part if total is None else total + part
+    for ref, block in zip(outs, butterfly(columns(total, count // 2), pos)):
+        ref[...] = block
+
+
+def embed_half(count, far, series, emb_weight):
+    rows, depth = series.shape
+    half = emb_weight.shape[1] // 2
+    step = math.gcd(depth, 256)
+    steps = depth // step
+    hbm = pl.BlockSpec(memory_space=pltpu.HBM)
+    return pl.pallas_call(
+        functools.partial(embed_kernel, count, far),
+        out_shape=[shape(rows, 2 * half // count)] * (count // 2),
+        in_specs=[hbm, hbm],
+        scratch_shapes=[
+            pltpu.VMEM((steps, rows, step), F32),
+            pltpu.VMEM((steps, step, half), F32),
+            pltpu.SemaphoreType.DMA((2, steps)),
+        ],
+        name="embed_far" if far else "embed_near",
+        compiler_params=pltpu.CompilerParams(vmem_limit_bytes=(127 if far else 121) * MIB // 2),
+        cost_estimate=pl.CostEstimate(flops=6 * rows * depth * half, bytes_accessed=4 * depth * half, transcendentals=0),
+    )(series, emb_weight)
+
+
+def piece_of(index, bits):
+    return sum(((index >> bit) & 1) << at for at, bit in enumerate(bits))
+
+
+def cut_kernel(bits, w_ref, out):
+    part = piece_of(lax.axis_index("var"), bits)
+    size = out.shape[0]
+    out[...] = w_ref[pl.ds(pl.multiple_of(part * size, size), size), :]
+
+
+def order_kernel(bits, own_ref, rest_ref, out):
+    me = piece_of(lax.axis_index("var"), bits)
+    rows = own_ref.shape[0]
+    size = rows >> len(bits)
+    out[0:rows, :] = own_ref[...]
+    for apart in range(1 << len(bits)):
+        for k in range(rest_ref.shape[1]):
+            start = pl.multiple_of((k + 1) * rows + (me ^ apart) * size, size)
+            out[pl.ds(start, size), :] = rest_ref[apart, k]
 
 
 def embed_reduce_kernel(count, *refs):
@@ -142,12 +193,11 @@
 
 def post_kernel(count, *refs):
     pos = lax.axis_index("head")
-    mixed, owts, emb = refs[:count], refs[count : 2 * count], refs[2 * count : 3 * count]
-    gain, bias, w_in, w_out = refs[3 * count : 3 * count + 4]
-    outs = refs[3 * count + 4 :]
+    mixed, emb = refs[:count], refs[count : 2 * count]
+    weight, gain, bias, w_in, w_out = refs[2 * count : 2 * count + 5]
+    outs = refs[2 * count + 5 :]
     stream = jnp.concatenate([m[...] for m in mixed], 1)
-    weight = jnp.concatenate([w[...] for w in owts], 0)
-    attention = dot3(stream, weight)
+    attention = dot3(stream, weight[...])
     embedded = jnp.concatenate(butterfly([e[...] for e in emb], pos), 1)
     normed = normalise(embedded + attention, gain[...], bias[...])
     hidden = gelu(dot3(normed, w_in[...]))
@@ -193,6 +243,10 @@
     return [x] + [send(x, axis, k) for k in range(1, lax.axis_size(axis))]
 
 
+def hand_out(parts, axis):
+    return [parts[0]] + [send(parts[k], axis, k) for k in range(1, lax.axis_size(axis))]
+
+
 def gather_pieces(piece):
     size = lax.axis_size("var")
     if size > 8:
@@ -206,48 +260,39 @@
     norm1_gain, norm1_bias, ffn_in, ffn_out, norm2_gain, norm2_bias,
 ):
     n = lax.axis_size("head")
-    rows, depth = series.shape
+    rows, _ = series.shape
     model = emb_weight.shape[1]
     width = model // n
     heads_width = q_weight.shape[1]
     block = shape(rows, width)
 
-    chunk = math.gcd(depth, 512)
-    parts = call(
-        functools.partial(embed_kernel, n), [block] * n, "embed",
-        scratch=[pltpu.VMEM((rows, model), F32)],
-        grid=(depth // chunk,),
-        in_specs=[
-            pl.BlockSpec((rows, chunk), lambda i: (0, i)),
-            pl.BlockSpec((chunk, model), lambda i: (i, 0)),
-        ],
-        out_specs=[pl.BlockSpec((rows, width), lambda i: (0, 0))] * n,
-        flops=6 * rows * depth * model, nbytes=4 * depth * (rows + model),
-    )(series, emb_weight)
-    got = [parts[0]] + [send(parts[k], "head", k) for k in range(1, n)]
-    mine = call(functools.partial(embed_reduce_kernel, n), block, "embed_sum")(
+    var_bits = lax.axis_size("var").bit_length() - 1
+    bits = [var_bits - 1, 0]
+    far = embed_half(n, True, series, emb_weight)
+    near = embed_half(n, False, series, emb_weight)
+    parts = [*near, *far]
+    got = hand_out(parts, "head")
+    cut = call(functools.partial(cut_kernel, bits), shape(heads_width >> len(bits), model))(out_weight)
+    rest = jnp.stack(spread_out(cut, "head")[1:])[None]
+    mine = call(functools.partial(embed_reduce_kernel, n), block)(
         *got, emb_bias.reshape(n, 1, width)
     )
     emb = spread_out(mine, "head")
-    pair = call(functools.partial(project_kernel, n, 1.0), shape(rows, 2 * heads_width), "project_kv")(
-        *emb, k_weight, v_weight
-    )
-    queries = call(
-        functools.partial(project_kernel, n, 1.0 / math.sqrt(DH)), shape(rows, heads_width), "project_q"
-    )(*emb, q_weight)
+    for bit in bits:
+        rest = jnp.concatenate([rest, send(rest, "var", 1 << bit)], 0)
+    pair = call(functools.partial(project_kernel, n, 1.0), shape(rows, 2 * heads_width))(*emb, k_weight, v_weight)
+    queries = call(functools.partial(project_kernel, n, 1.0 / math.sqrt(DH)), shape(rows, heads_width))(*emb, q_weight)
     pieces = gather_pieces(pair)
-    late_weight, _ = lax.optimization_barrier((out_weight, pair))
-    owts = spread_out(late_weight, "head")
-    mixed = call(attend_kernel, shape(rows, heads_width), "attend", limit=16)(queries, *pieces)
+    order = functools.partial(order_kernel, bits)
+    whole_out = call(order, shape(n * heads_width, model))(out_weight, rest)
+    mixed = call(attend_kernel, shape(rows, heads_width), limit=16)(queries, *pieces)
     mixes = spread_out(mixed, "head")
-    partial = call(functools.partial(post_kernel, n), [block] * n, "post", limit=16)(
-        *mixes, *owts, *emb, norm1_gain[None, :], norm1_bias[None, :], ffn_in, ffn_out
-    )
-    got = [partial[0]] + [send(partial[k], "head", k) for k in range(1, n)]
-    flipped, stats = call(
-        functools.partial(stats_kernel, n), [shape(width, rows), shape(2, rows)], "stats"
-    )(*got)
-    return call(functools.partial(final_kernel, n), shape(width, rows), "final")(
+    partial = call(functools.partial(post_kernel, n), [block] * n, limit=16)(
+        *mixes, *emb, whole_out, norm1_gain[None, :], norm1_bias[None, :], ffn_in, ffn_out
+    )
+    got = hand_out(partial, "head")
+    flipped, stats = call(functools.partial(stats_kernel, n), [shape(width, rows), shape(2, rows)])(*got)
+    return call(functools.partial(final_kernel, n), shape(width, rows))(
         flipped, *spread_out(stats, "head"), norm2_gain.reshape(n, 1, width), norm2_bias.reshape(n, 1, width)
     )
 

time: 80.6 us -> 75 us (0.931)
  starting transfers between devices: 40 us -> 32.3 us
  Pallas kernels: 6.32 us -> 11.7 us
  waiting for transfers between devices: 30.5 us -> 28.5 us
  local copies, waits for them, and re-layouts: 3.46 us -> 1.85 us
    ppermute x25 -> x27, starting transfers between devices: 40 us -> 32.3 us  [send(): return lax.ppermute(x, axis, [(i, i ^ offset) for i in range(size)])]
    pallas_call x5 -> x8, Pallas kernels: 5.53 us -> 11 us  [the longest x2 7.16 us: embed_half(): pl.pallas_call(functools.partial(embed_kernel, count, far), out_shape=[sh...]
    ppermute x25 -> x27, waiting for transfers between devices: 30.5 us -> 28.5 us  [send(): return lax.ppermute(x, axis, [(i, i ^ offset) for i in range(size)])]
    unnamed x26, local copies, waits for them, and re-layouts: 3.46 us -> 1.85 us
  transfers between devices with their start and end apart: 25 -> 27, of which waited for: 15 -> 18; matrix products, arithmetic and copies ran while one was open for 0% -> 0% of each run, Pallas kernels for 2% -> 13%
where the time goes in v2:
time: 75 us; the launch traced here: 74.8 us
  starting transfers between devices  32.3 us (43%)
  waiting for transfers between devices  28.5 us (38%)
  Pallas kernels  11.7 us (16%)
  local copies, waits for them, and re-layouts  1.85 us (2%)
    ppermute x27, starting transfers between devices, send(): return lax.ppermute(x, axis, [(i, i ^ offset) for i in range(size)])  32.3 us
    ppermute x27, waiting for transfers between devices, send(): return lax.ppermute(x, axis, [(i, i ^ offset) for i in range(size)])  28.5 us
    pallas_call x2, Pallas kernels, embed_half(): pl.pallas_call(functools.partial(embed_kernel, count, far), out_shape=[sh...  7.16 us
    unnamed x26, local copies, waits for them, and re-layouts  1.85 us
    pallas_call x1, Pallas kernels, on_device(): call(attend_kernel, shape(rows, heads_width), limit=16)(queries, *pieces)  1.56 us
  transfers between devices with their start and end apart: 27, of which 18 were waited for; matrix products, arithmetic and copies ran while one was open for 0% of the time, Pallas kernels for 13%

profile of v2, /device:TPU:0, one launch (start us, length us, event | category | flops | bytes accessed | tf_op | source)
XLA Modules:
  0.0 74.8 jit_solution(3894062629856546349)
XLA Ops:
  0.0 0.9 %copy-done.2 = f32[128,512]{1,0:T(8,128)S(1)} copy-done((f32[128,512]{1,0:T(8,128)S(1)}, f32[128,512]{1,0:T(8,128)}, u32[]{:S(2)}) %copy-start.2) | copy-done | bytes 262168
  1.0 5.1 %collective-permute-start.18 = (f32[32,512]{1,0:T(8,128)S(1)}, f32[32,512]{1,0:T(8,128)S(1)}, u32[]{:S(2)}, u32[]{:S(2)}) collective-permute-start(f32[32,512]{1,0:T(8,128)S(1)} %shard_map.131), channel_id=1, source_target_pairs={{0,3},{1,2},{2,1},{3,0},{4,7},{5,6},{6,5},{7,4},{8,11},{9,10},{10,... | collective-permute-start | bytes 196616 | tf_op jit(solution)/shard_map/ppermute | solution.py:239
  6.0 0.6 collective-permute-start.16
  6.7 1.8 %collective-permute-done.18 = f32[32,512]{1,0:T(8,128)S(1)} collective-permute-done((f32[32,512]{1,0:T(8,128)S(1)}, f32[32,512]{1,0:T(8,128)S(1)}, u32[]{:S(2)}, u32[]{:S(2)}) %collective-permute-start.18) | collective-permute-done | bytes 65568 | tf_op jit(solution)/shard_map/ppermute | solution.py:239
  8.5 3.1 %collective-permute-done.17 = f32[32,512]{1,0:T(8,128)S(1)} collective-permute-done((f32[32,512]{1,0:T(8,128)S(1)}, f32[32,512]{1,0:T(8,128)S(1)}, u32[]{:S(2)}, u32[]{:S(2)}) %collective-permute-start.17) | collective-permute-done | bytes 65568 | tf_op jit(solution)/shard_map/ppermute | solution.py:239
  11.7 1.6 %collective-permute-start.19 = (f32[1,3,32,512]{3,2,1,0:T(8,128)S(1)}, f32[1,3,32,512]{3,2,1,0:T(8,128)S(1)}, u32[]{:S(2)}, u32[]{:S(2)}) collective-permute-start(f32[1,3,32,512]{3,2,1,0:T(8,128)S(1)} %maximum_bitcast_fusion), channel_id=1, source_target_pairs={{0,16},{4,20},{8,24},{12,28},{16,0},{20,4},{24,8},{28,12},{1,17},{... | collective-permute-start | bytes 589832 | tf_op jit(solution)/shard_map/ppermute | solution.py:239
  13.2 3.6 %embed_far.1 = (f32[128,128]{1,0:T(8,128)}, f32[128,128]{1,0:T(8,128)}) custom-call(f32[128,2048]{1,0:T(8,128)} %x_hbm.3, f32[2048,512]{1,0:T(8,128)} %w_hbm.3), custom_call_target="tpu_custom_call" | custom-call | flops 402653184 | bytes 2097152 | tf_op jit(solution)/shard_map/embed_far/pallas_call | solution.py:105
  16.9 1.7 %collective-permute-start.1 = (f32[128,128]{1,0:T(8,128)}, f32[128,128]{1,0:T(8,128)S(1)}, u32[]{:S(2)}, u32[]{:S(2)}) collective-permute-start(f32[128,128]{1,0:T(8,128)} %get-tuple-element.17), channel_id=1, source_target_pairs={{0,2},{1,3},{2,0},{3,1},{4,6},{5,7},{6,4},{7,5},{8,10},{9,11},{10,... | collective-permute-start | bytes 196616 | tf_op jit(solution)/shard_map/ppermute | solution.py:239
  18.5 1.9 %collective-permute-start.2 = (f32[128,128]{1,0:T(8,128)}, f32[128,128]{1,0:T(8,128)S(1)}, u32[]{:S(2)}, u32[]{:S(2)}) collective-permute-start(f32[128,128]{1,0:T(8,128)} %get-tuple-element.18), channel_id=1, source_target_pairs={{0,3},{1,2},{2,1},{3,0},{4,7},{5,6},{6,5},{7,4},{8,11},{9,10},{10,... | collective-permute-start | bytes 196616 | tf_op jit(solution)/shard_map/ppermute | solution.py:239
  20.4 3.6 %embed_near.1 = (f32[128,128]{1,0:T(8,128)}, f32[128,128]{1,0:T(8,128)}) custom-call(f32[128,2048]{1,0:T(8,128)} %x_hbm.3, f32[2048,512]{1,0:T(8,128)} %w_hbm.3), custom_call_target="tpu_custom_call" | custom-call | flops 402653184 | bytes 2097152 | tf_op jit(solution)/shard_map/embed_near/pallas_call | solution.py:105
  24.0 0.1 collective-permute-start
  24.2 0.7 collective-permute-done.2.refs_3_
  24.9 3.6 %collective-permute-done.refs_1_ = f32[128,128]{1,0:T(8,128)S(1)} collective-permute-done((f32[128,128]{1,0:T(8,128)}, f32[128,128]{1,0:T(8,128)S(1)}, u32[]{:S(2)}, u32[]{:S(2)}) %collective-permute-start) | collective-permute-done | bytes 65568 | tf_op jit(solution)/shard_map/ppermute | solution.py:239
  28.6 0.8 %copy-done.7 = f32[128,128]{1,0:T(8,128)S(1)} copy-done((f32[128,128]{1,0:T(8,128)S(1)}, f32[128,128]{1,0:T(8,128)}, u32[]{:S(2)}) %copy-start.7) | copy-done | bytes 65560
  29.4 2.0 %collective-permute-start.5 = (f32[128,128]{1,0:T(8,128)S(1)}, f32[128,128]{1,0:T(8,128)S(1)}, u32[]{:S(2)}, u32[]{:S(2)}) collective-permute-start(f32[128,128]{1,0:T(8,128)S(1)} %shard_map.127.refs_0_.refs_4_), channel_id=1, source_target_pairs={{0,3},{1,2},{2,1},{3,0},{4,7},{5,6},{6,5},{7,4},{8,11},{9,10},{10,... | collective-permute-start | bytes 196616 | tf_op jit(solution)/shard_map/ppermute | solution.py:239
  31.5 2.4 %collective-permute-start.3 = (f32[128,128]{1,0:T(8,128)S(1)}, f32[128,128]{1,0:T(8,128)S(1)}, u32[]{:S(2)}, u32[]{:S(2)}) collective-permute-start(f32[128,128]{1,0:T(8,128)S(1)} %shard_map.127.refs_0_.refs_4_), channel_id=1, source_target_pairs={{0,1},{1,0},{2,3},{3,2},{4,5},{5,4},{6,7},{7,6},{8,9},{9,8},{10,11... | collective-permute-start | bytes 196616 | tf_op jit(solution)/shard_map/ppermute | solution.py:239
  33.9 1.7 %collective-permute-done.5.refs_3_.refs_7_ = f32[128,128]{1,0:T(8,128)S(1)} collective-permute-done((f32[128,128]{1,0:T(8,128)S(1)}, f32[128,128]{1,0:T(8,128)S(1)}, u32[]{:S(2)}, u32[]{:S(2)}) %collective-permute-start.5) | collective-permute-done | bytes 65568 | tf_op jit(solution)/shard_map/ppermute | solution.py:239
  35.6 1.4 %collective-permute-done.4.refs_2_.refs_6_ = f32[128,128]{1,0:T(8,128)S(1)} collective-permute-done((f32[128,128]{1,0:T(8,128)S(1)}, f32[128,128]{1,0:T(8,128)S(1)}, u32[]{:S(2)}, u32[]{:S(2)}) %collective-permute-start.4) | collective-permute-done | bytes 65568 | tf_op jit(solution)/shard_map/ppermute | solution.py:239
  37.0 0.4 shard_map.129.refs_0_
  37.3 1.5 %collective-permute-start.8 = (f32[128,256]{1,0:T(8,128)S(1)}, f32[128,256]{1,0:T(8,128)S(1)}, u32[]{:S(2)}, u32[]{:S(2)}) collective-permute-start(f32[128,256]{1,0:T(8,128)S(1)} %shard_map.129.refs_0_), channel_id=1, source_target_pairs={{0,24},{4,28},{8,16},{12,20},{16,8},{20,12},{24,0},{28,4},{1,25},{... | collective-permute-start | bytes 393224 | tf_op jit(solution)/shard_map/ppermute | solution.py:239
  38.8 1.5 %collective-permute-start.7 = (f32[128,256]{1,0:T(8,128)S(1)}, f32[128,256]{1,0:T(8,128)S(1)}, u32[]{:S(2)}, u32[]{:S(2)}) collective-permute-start(f32[128,256]{1,0:T(8,128)S(1)} %shard_map.129.refs_0_), channel_id=1, source_target_pairs={{0,16},{4,20},{8,24},{12,28},{16,0},{20,4},{24,8},{28,12},{1,17},{... | collective-permute-start | bytes 393224 | tf_op jit(solution)/shard_map/ppermute | solution.py:239
  40.4 0.5 collective-permute-start.6
  40.9 2.5 %collective-permute-done.8.refs_3_ = f32[128,256]{1,0:T(8,128)S(1)} collective-permute-done((f32[128,256]{1,0:T(8,128)S(1)}, f32[128,256]{1,0:T(8,128)S(1)}, u32[]{:S(2)}, u32[]{:S(2)}) %collective-permute-start.8) | collective-permute-done | bytes 131104 | tf_op jit(solution)/shard_map/ppermute | solution.py:239
  43.4 1.3 %collective-permute-done.7.refs_2_ = f32[128,256]{1,0:T(8,128)S(1)} collective-permute-done((f32[128,256]{1,0:T(8,128)S(1)}, f32[128,256]{1,0:T(8,128)S(1)}, u32[]{:S(2)}, u32[]{:S(2)}) %collective-permute-start.7) | collective-permute-done | bytes 131104 | tf_op jit(solution)/shard_map/ppermute | solution.py:239
  44.7 0.6 collective-permute-done.6.refs_1_
  45.3 0.3 shard_map.128.q_ref
  45.7 0.4 collective-permute-done.11.refs_6_
  46.0 0.6 collective-permute-done.10.refs_5_
  46.7 1.6 %shard_map.130.refs_0_ = f32[128,128]{1,0:T(8,128)S(1)} custom-call(f32[128,128]{1,0:T(8,128)S(1)} %shard_map.128.q_ref, f32[128,256]{1,0:T(8,128)S(1)} %shard_map.129.refs_0_, f32[128,256]{1,0:T(8,128)S(1)} %collective-permute-done.6.refs_1_, f32[128,256]{1,0:T(8,128)S(1)} %collective-permute-done.7.refs_2_, f32[128,256]{1,0:T(8,128)S(1)} %collective-permute-done.8.refs_3_, ...), custom_call_target="tpu_custom_call" | custom-call | tf_op jit(solution)/shard_map/pallas_call | solution.py:288
  48.2 2.0 %collective-permute-start.15 = (f32[128,128]{1,0:T(8,128)S(1)}, f32[128,128]{1,0:T(8,128)S(1)}, u32[]{:S(2)}, u32[]{:S(2)}) collective-permute-start(f32[128,128]{1,0:T(8,128)S(1)} %shard_map.130.refs_0_), channel_id=1, source_target_pairs={{0,3},{1,2},{2,1},{3,0},{4,7},{5,6},{6,5},{7,4},{8,11},{9,10},{10,... | collective-permute-start | bytes 196616 | tf_op jit(solution)/shard_map/ppermute | solution.py:239
  50.3 0.7 collective-permute-start.14
  50.9 1.8 %collective-permute-start.13 = (f32[128,128]{1,0:T(8,128)S(1)}, f32[128,128]{1,0:T(8,128)S(1)}, u32[]{:S(2)}, u32[]{:S(2)}) collective-permute-start(f32[128,128]{1,0:T(8,128)S(1)} %shard_map.130.refs_0_), channel_id=1, source_target_pairs={{0,1},{1,0},{2,3},{3,2},{4,5},{5,4},{6,7},{7,6},{8,9},{9,8},{10,11... | collective-permute-start | bytes 196616 | tf_op jit(solution)/shard_map/ppermute | solution.py:239
  52.8 0.1 shard_map.132.refs_8_
  52.8 2.3 %collective-permute-done.15.refs_3_ = f32[128,128]{1,0:T(8,128)S(1)} collective-permute-done((f32[128,128]{1,0:T(8,128)S(1)}, f32[128,128]{1,0:T(8,128)S(1)}, u32[]{:S(2)}, u32[]{:S(2)}) %collective-permute-start.15) | collective-permute-done | bytes 65568 | tf_op jit(solution)/shard_map/ppermute | solution.py:239
  55.1 2.3 %collective-permute-done.14.refs_2_ = f32[128,128]{1,0:T(8,128)S(1)} collective-permute-done((f32[128,128]{1,0:T(8,128)S(1)}, f32[128,128]{1,0:T(8,128)S(1)}, u32[]{:S(2)}, u32[]{:S(2)}) %collective-permute-start.14) | collective-permute-done | bytes 65568 | tf_op jit(solution)/shard_map/ppermute | solution.py:239
  57.4 1.3 %shard_map.133 = (f32[128,128]{1,0:T(8,128)S(1)}, f32[128,128]{1,0:T(8,128)S(1)}, f32[128,128]{1,0:T(8,128)S(1)}, f32[128,128]{1,0:T(8,128)S(1)}) custom-call(f32[128,128]{1,0:T(8,128)S(1)} %shard_map.130.refs_0_, f32[128,128]{1,0:T(8,128)S(1)} %collective-permute-done.13.refs_1_, f32[128,128]{1,0:T(8,128)S(1)} %collective-permute-done.14.refs_2_, ...), custom_call_target="tpu_custom_call" | custom-call | tf_op jit(solution)/shard_map/pallas_call | solution.py:290
  58.8 2.5 %collective-permute-start.22 = (f32[128,128]{1,0:T(8,128)S(1)}, f32[128,128]{1,0:T(8,128)S(1)}, u32[]{:S(2)}, u32[]{:S(2)}) collective-permute-start(f32[128,128]{1,0:T(8,128)S(1)} %get-tuple-element.21), channel_id=1, source_target_pairs={{0,2},{1,3},{2,0},{3,1},{4,6},{5,7},{6,4},{7,5},{8,10},{9,11},{10,... | collective-permute-start | bytes 196616 | tf_op jit(solution)/shard_map/ppermute | solution.py:239
  61.3 1.9 %collective-permute-start.23 = (f32[128,128]{1,0:T(8,128)S(1)}, f32[128,128]{1,0:T(8,128)S(1)}, u32[]{:S(2)}, u32[]{:S(2)}) collective-permute-start(f32[128,128]{1,0:T(8,128)S(1)} %get-tuple-element.22), channel_id=1, source_target_pairs={{0,3},{1,2},{2,1},{3,0},{4,7},{5,6},{6,5},{7,4},{8,11},{9,10},{10,... | collective-permute-start | bytes 196616 | tf_op jit(solution)/shard_map/ppermute | solution.py:239
  63.2 0.5 collective-permute-done.21.refs_1_
  63.7 2.8 %collective-permute-done.22.refs_2_ = f32[128,128]{1,0:T(8,128)S(1)} collective-permute-done((f32[128,128]{1,0:T(8,128)S(1)}, f32[128,128]{1,0:T(8,128)S(1)}, u32[]{:S(2)}, u32[]{:S(2)}) %collective-permute-start.22) | collective-permute-done | bytes 65568 | tf_op jit(solution)/shard_map/ppermute | solution.py:239
  66.5 0.9 %collective-permute-done.23.refs_3_ = f32[128,128]{1,0:T(8,128)S(1)} collective-permute-done((f32[128,128]{1,0:T(8,128)S(1)}, f32[128,128]{1,0:T(8,128)S(1)}, u32[]{:S(2)}, u32[]{:S(2)}) %collective-permute-start.23) | collective-permute-done | bytes 65568 | tf_op jit(solution)/shard_map/ppermute | solution.py:239
  67.5 0.1 shard_map.134
  67.6 1.8 %collective-permute-start.26 = (f32[2,128]{1,0:T(2,128)S(1)}, f32[2,128]{1,0:T(2,128)S(1)}, u32[]{:S(2)}, u32[]{:S(2)}) collective-permute-start(f32[2,128]{1,0:T(2,128)S(1)} %get-tuple-element.24.refs_0_), channel_id=1, source_target_pairs={{0,3},{1,2},{2,1},{3,0},{4,7},{5,6},{6,5},{7,4},{8,11},{9,10},{10,... | collective-permute-start | bytes 3080 | tf_op jit(solution)/shard_map/ppermute | solution.py:239
  69.4 0.7 collective-permute-start.25
  70.2 1.9 %collective-permute-start.24 = (f32[2,128]{1,0:T(2,128)S(1)}, f32[2,128]{1,0:T(2,128)S(1)}, u32[]{:S(2)}, u32[]{:S(2)}) collective-permute-start(f32[2,128]{1,0:T(2,128)S(1)} %get-tuple-element.24.refs_0_), channel_id=1, source_target_pairs={{0,1},{1,0},{2,3},{3,2},{4,5},{5,4},{6,7},{7,6},{8,9},{9,8},{10,11... | collective-permute-start | bytes 3080 | tf_op jit(solution)/shard_map/ppermute | solution.py:239
  72.1 1.0 %collective-permute-done.26.refs_3_ = f32[2,128]{1,0:T(2,128)S(1)} collective-permute-done((f32[2,128]{1,0:T(2,128)S(1)}, f32[2,128]{1,0:T(2,128)S(1)}, u32[]{:S(2)}, u32[]{:S(2)}) %collective-permute-start.26) | collective-permute-done | bytes 1056 | tf_op jit(solution)/shard_map/ppermute | solution.py:239
  73.0 0.8 %collective-permute-done.25.refs_2_ = f32[2,128]{1,0:T(2,128)S(1)} collective-permute-done((f32[2,128]{1,0:T(2,128)S(1)}, f32[2,128]{1,0:T(2,128)S(1)}, u32[]{:S(2)}, u32[]{:S(2)}) %collective-permute-start.25) | collective-permute-done | bytes 1056 | tf_op jit(solution)/shard_map/ppermute | solution.py:239
  73.9 0.8 %shard_map.135 = f32[128,128]{1,0:T(8,128)} custom-call(f32[128,128]{1,0:T(8,128)S(1)} %get-tuple-element.23.x_ref, f32[2,128]{1,0:T(2,128)S(1)} %get-tuple-element.24.refs_0_, f32[2,128]{1,0:T(2,128)S(1)} %collective-permute-done.24.refs_1_, f32[2,128]{1,0:T(2,128)S(1)} %collective-permute-done.25.refs_2_, f32[2,128]{1,0:T(2,128)S(1)} %collective-permute-done.26.refs_3_, ...), custom_call_target="tpu_custom_call" | custom-call | tf_op jit(solution)/shard_map/pallas_call | solution.py:295
  (46 shorter events, 0.4 us)
Async XLA Ops:
  0.0 0.9 %copy-start.2 = (f32[128,512]{1,0:T(8,128)S(1)}, f32[128,512]{1,0:T(8,128)}, u32[]{:S(2)}) copy-start(f32[128,512]{1,0:T(8,128)} %own_ref.1) | copy-start | bytes 786436
  1.0 7.6 %collective-permute-start.18 = (f32[32,512]{1,0:T(8,128)S(1)}, f32[32,512]{1,0:T(8,128)S(1)}, u32[]{:S(2)}, u32[]{:S(2)}) collective-permute-start(f32[32,512]{1,0:T(8,128)S(1)} %shard_map.131), channel_id=1, source_target_pairs={{0,3},{1,2},{2,1},{3,0},{4,7},{5,6},{6,5},{7,4},{8,11},{9,10},{10,... | collective-permute-start | bytes 196616 | tf_op jit(solution)/shard_map/ppermute | solution.py:239
  6.0 5.6 %collective-permute-start.17 = (f32[32,512]{1,0:T(8,128)S(1)}, f32[32,512]{1,0:T(8,128)S(1)}, u32[]{:S(2)}, u32[]{:S(2)}) collective-permute-start(f32[32,512]{1,0:T(8,128)S(1)} %shard_map.131), channel_id=1, source_target_pairs={{0,2},{1,3},{2,0},{3,1},{4,6},{5,7},{6,4},{7,5},{8,10},{9,11},{10,... | collective-permute-start | bytes 196616 | tf_op jit(solution)/shard_map/ppermute | solution.py:239
  6.0 5.6 %collective-permute-start.16 = (f32[32,512]{1,0:T(8,128)S(1)}, f32[32,512]{1,0:T(8,128)S(1)}, u32[]{:S(2)}, u32[]{:S(2)}) collective-permute-start(f32[32,512]{1,0:T(8,128)S(1)} %shard_map.131), channel_id=1, source_target_pairs={{0,1},{1,0},{2,3},{3,2},{4,5},{5,4},{6,7},{7,6},{8,9},{9,8},{10,11... | collective-permute-start | bytes 196616 | tf_op jit(solution)/shard_map/ppermute | solution.py:239
  11.7 12.5 %collective-permute-start.19 = (f32[1,3,32,512]{3,2,1,0:T(8,128)S(1)}, f32[1,3,32,512]{3,2,1,0:T(8,128)S(1)}, u32[]{:S(2)}, u32[]{:S(2)}) collective-permute-start(f32[1,3,32,512]{3,2,1,0:T(8,128)S(1)} %maximum_bitcast_fusion), channel_id=1, source_target_pairs={{0,16},{4,20},{8,24},{12,28},{16,0},{20,4},{24,8},{28,12},{1,17},{... | collective-permute-start | bytes 589832 | tf_op jit(solution)/shard_map/ppermute | solution.py:239
  16.8 11.7 %copy-start.8 = (f32[512]{0:T(512)S(1)}, f32[512]{0:T(512)}, u32[]{:S(2)}) copy-start(f32[512]{0:T(512)} %param.15) | copy-start | bytes 6148
  16.8 20.1 %copy-start.4 = (f32[512,128]{1,0:T(8,128)S(1)}, f32[512,128]{1,0:T(8,128)}, u32[]{:S(2)}) copy-start(f32[512,128]{1,0:T(8,128)} %refs_4_.3) | copy-start | bytes 786436
  16.9 20.1 %copy-start.5 = (f32[512,128]{1,0:T(8,128)S(1)}, f32[512,128]{1,0:T(8,128)}, u32[]{:S(2)}) copy-start(f32[512,128]{1,0:T(8,128)} %refs_5_.1) | copy-start | bytes 786436
  16.9 28.5 %copy-start.6 = (f32[512,128]{1,0:T(8,128)S(1)}, f32[512,128]{1,0:T(8,128)}, u32[]{:S(2)}) copy-start(f32[512,128]{1,0:T(8,128)} %refs_4_.2) | copy-start | bytes 786436
  16.9 7.4 %collective-permute-start.1 = (f32[128,128]{1,0:T(8,128)}, f32[128,128]{1,0:T(8,128)S(1)}, u32[]{:S(2)}, u32[]{:S(2)}) collective-permute-start(f32[128,128]{1,0:T(8,128)} %get-tuple-element.17), channel_id=1, source_target_pairs={{0,2},{1,3},{2,0},{3,1},{4,6},{5,7},{6,4},{7,5},{8,10},{9,11},{10,... | collective-permute-start | bytes 196616 | tf_op jit(solution)/shard_map/ppermute | solution.py:239
  18.5 34.2 %copy-start.3 = (f32[128,512]{1,0:T(8,128)S(1)}, f32[128,512]{1,0:T(8,128)}, u32[]{:S(2)}) copy-start(f32[128,512]{1,0:T(8,128)} %own_ref.1) | copy-start | bytes 786436
  18.5 6.4 %collective-permute-start.2 = (f32[128,128]{1,0:T(8,128)}, f32[128,128]{1,0:T(8,128)S(1)}, u32[]{:S(2)}, u32[]{:S(2)}) collective-permute-start(f32[128,128]{1,0:T(8,128)} %get-tuple-element.18), channel_id=1, source_target_pairs={{0,3},{1,2},{2,1},{3,0},{4,7},{5,6},{6,5},{7,4},{8,11},{9,10},{10,... | collective-permute-start | bytes 196616 | tf_op jit(solution)/shard_map/ppermute | solution.py:239
  20.4 37.0 %copy-start.9 = (f32[512]{0:T(512)S(1)}, f32[512]{0:T(512)}, u32[]{:S(2)}) copy-start(f32[512]{0:T(512)} %param.20) | copy-start | bytes 6148
  20.4 37.0 %copy-start.10 = (f32[512]{0:T(512)S(1)}, f32[512]{0:T(512)}, u32[]{:S(2)}) copy-start(f32[512]{0:T(512)} %param.21) | copy-start | bytes 6148
  24.0 33.4 %copy-start = (f32[512,512]{1,0:T(8,128)S(1)}, f32[512,512]{1,0:T(8,128)}, u32[]{:S(2)}) copy-start(f32[512,512]{1,0:T(8,128)} %refs_11_.1) | copy-start | bytes 3145732
  24.0 33.4 %copy-start.1 = (f32[512,512]{1,0:T(8,128)S(1)}, f32[512,512]{1,0:T(8,128)}, u32[]{:S(2)}) copy-start(f32[512,512]{1,0:T(8,128)} %refs_12_.1) | copy-start | bytes 3145732
  24.0 4.5 %collective-permute-start = (f32[128,128]{1,0:T(8,128)}, f32[128,128]{1,0:T(8,128)S(1)}, u32[]{:S(2)}, u32[]{:S(2)}) collective-permute-start(f32[128,128]{1,0:T(8,128)} %get-tuple-element.16), channel_id=1, source_target_pairs={{0,1},{1,0},{2,3},{3,2},{4,5},{5,4},{6,7},{7,6},{8,9},{9,8},{10,11... | collective-permute-start | bytes 196616 | tf_op jit(solution)/shard_map/ppermute | solution.py:239
  24.2 28.5 %collective-permute-start.20 = (f32[2,3,32,512]{3,2,1,0:T(8,128)S(1)}, f32[2,3,32,512]{3,2,1,0:T(8,128)S(1)}, u32[]{:S(2)}, u32[]{:S(2)}) collective-permute-start(f32[2,3,32,512]{3,2,1,0:T(8,128)S(1)} %pad_maximum_fusion.1), channel_id=1, source_target_pairs={{0,4},{4,0},{8,12},{12,8},{16,20},{20,16},{24,28},{28,24},{1,5},{5... | collective-permute-start | bytes 1179656 | tf_op jit(solution)/shard_map/ppermute | solution.py:239
  28.6 0.8 %copy-start.7 = (f32[128,128]{1,0:T(8,128)S(1)}, f32[128,128]{1,0:T(8,128)}, u32[]{:S(2)}) copy-start(f32[128,128]{1,0:T(8,128)} %get-tuple-element.15.refs_0_) | copy-start | bytes 196612
  29.4 6.1 %collective-permute-start.5 = (f32[128,128]{1,0:T(8,128)S(1)}, f32[128,128]{1,0:T(8,128)S(1)}, u32[]{:S(2)}, u32[]{:S(2)}) collective-permute-start(f32[128,128]{1,0:T(8,128)S(1)} %shard_map.127.refs_0_.refs_4_), channel_id=1, source_target_pairs={{0,3},{1,2},{2,1},{3,0},{4,7},{5,6},{6,5},{7,4},{8,11},{9,10},{10,... | collective-permute-start | bytes 196616 | tf_op jit(solution)/shard_map/ppermute | solution.py:239
  31.4 5.5 %collective-permute-start.4 = (f32[128,128]{1,0:T(8,128)S(1)}, f32[128,128]{1,0:T(8,128)S(1)}, u32[]{:S(2)}, u32[]{:S(2)}) collective-permute-start(f32[128,128]{1,0:T(8,128)S(1)} %shard_map.127.refs_0_.refs_4_), channel_id=1, source_target_pairs={{0,2},{1,3},{2,0},{3,1},{4,6},{5,7},{6,4},{7,5},{8,10},{9,11},{10,... | collective-permute-start | bytes 196616 | tf_op jit(solution)/shard_map/ppermute | solution.py:239
  31.5 5.5 %collective-permute-start.3 = (f32[128,128]{1,0:T(8,128)S(1)}, f32[128,128]{1,0:T(8,128)S(1)}, u32[]{:S(2)}, u32[]{:S(2)}) collective-permute-start(f32[128,128]{1,0:T(8,128)S(1)} %shard_map.127.refs_0_.refs_4_), channel_id=1, source_target_pairs={{0,1},{1,0},{2,3},{3,2},{4,5},{5,4},{6,7},{7,6},{8,9},{9,8},{10,11... | collective-permute-start | bytes 196616 | tf_op jit(solution)/shard_map/ppermute | solution.py:239
  37.3 6.0 %collective-permute-start.8 = (f32[128,256]{1,0:T(8,128)S(1)}, f32[128,256]{1,0:T(8,128)S(1)}, u32[]{:S(2)}, u32[]{:S(2)}) collective-permute-start(f32[128,256]{1,0:T(8,128)S(1)} %shard_map.129.refs_0_), channel_id=1, source_target_pairs={{0,24},{4,28},{8,16},{12,20},{16,8},{20,12},{24,0},{28,4},{1,25},{... | collective-permute-start | bytes 393224 | tf_op jit(solution)/shard_map/ppermute | solution.py:239
  38.8 5.8 %collective-permute-start.7 = (f32[128,256]{1,0:T(8,128)S(1)}, f32[128,256]{1,0:T(8,128)S(1)}, u32[]{:S(2)}, u32[]{:S(2)}) collective-permute-start(f32[128,256]{1,0:T(8,128)S(1)} %shard_map.129.refs_0_), channel_id=1, source_target_pairs={{0,16},{4,20},{8,24},{12,28},{16,0},{20,4},{24,8},{28,12},{1,17},{... | collective-permute-start | bytes 393224 | tf_op jit(solution)/shard_map/ppermute | solution.py:239
  40.4 5.0 %collective-permute-start.6 = (f32[128,256]{1,0:T(8,128)S(1)}, f32[128,256]{1,0:T(8,128)S(1)}, u32[]{:S(2)}, u32[]{:S(2)}) collective-permute-start(f32[128,256]{1,0:T(8,128)S(1)} %shard_map.129.refs_0_), channel_id=1, source_target_pairs={{0,8},{4,12},{8,0},{12,4},{16,24},{20,28},{24,16},{28,20},{1,9},{5... | collective-permute-start | bytes 393224 | tf_op jit(solution)/shard_map/ppermute | solution.py:239
  40.9 4.7 %collective-permute-start.9 = (f32[128,256]{1,0:T(8,128)S(1)}, f32[128,256]{1,0:T(8,128)S(1)}, u32[]{:S(2)}, u32[]{:S(2)}) collective-permute-start(f32[128,256]{1,0:T(8,128)S(1)} %shard_map.129.refs_0_), channel_id=1, source_target_pairs={{0,4},{4,0},{8,12},{12,8},{16,20},{20,16},{24,28},{28,24},{1,5},{5... | collective-permute-start | bytes 393224 | tf_op jit(solution)/shard_map/ppermute | solution.py:239
  43.4 2.3 %collective-permute-start.12 = (f32[128,256]{1,0:T(8,128)S(1)}, f32[128,256]{1,0:T(8,128)S(1)}, u32[]{:S(2)}, u32[]{:S(2)}) collective-permute-start(f32[128,256]{1,0:T(8,128)S(1)} %collective-permute-done.8.refs_3_), channel_id=1, source_target_pairs={{0,4},{4,0},{8,12},{12,8},{16,20},{20,16},{24,28},{28,24},{1,5},{5... | collective-permute-start | bytes 393224 | tf_op jit(solution)/shard_map/ppermute | solution.py:239
  44.7 1.3 %collective-permute-start.11 = (f32[128,256]{1,0:T(8,128)S(1)}, f32[128,256]{1,0:T(8,128)S(1)}, u32[]{:S(2)}, u32[]{:S(2)}) collective-permute-start(f32[128,256]{1,0:T(8,128)S(1)} %collective-permute-done.7.refs_2_), channel_id=1, source_target_pairs={{0,4},{4,0},{8,12},{12,8},{16,20},{20,16},{24,28},{28,24},{1,5},{5... | collective-permute-start | bytes 393224 | tf_op jit(solution)/shard_map/ppermute | solution.py:239
  45.3 1.3 %collective-permute-start.10 = (f32[128,256]{1,0:T(8,128)S(1)}, f32[128,256]{1,0:T(8,128)S(1)}, u32[]{:S(2)}, u32[]{:S(2)}) collective-permute-start(f32[128,256]{1,0:T(8,128)S(1)} %collective-permute-done.6.refs_1_), channel_id=1, source_target_pairs={{0,4},{4,0},{8,12},{12,8},{16,20},{20,16},{24,28},{28,24},{1,5},{5... | collective-permute-start | bytes 393224 | tf_op jit(solution)/shard_map/ppermute | solution.py:239
  45.6 28.3 %copy-start.11 = (f32[512]{0:T(512)S(1)}, f32[512]{0:T(512)}, u32[]{:S(2)}) copy-start(f32[512]{0:T(512)} %param.24) | copy-start | bytes 6148
  45.6 28.3 %copy-start.12 = (f32[512]{0:T(512)S(1)}, f32[512]{0:T(512)}, u32[]{:S(2)}) copy-start(f32[512]{0:T(512)} %param.25) | copy-start | bytes 6148
  48.2 6.9 %collective-permute-start.15 = (f32[128,128]{1,0:T(8,128)S(1)}, f32[128,128]{1,0:T(8,128)S(1)}, u32[]{:S(2)}, u32[]{:S(2)}) collective-permute-start(f32[128,128]{1,0:T(8,128)S(1)} %shard_map.130.refs_0_), channel_id=1, source_target_pairs={{0,3},{1,2},{2,1},{3,0},{4,7},{5,6},{6,5},{7,4},{8,11},{9,10},{10,... | collective-permute-start | bytes 196616 | tf_op jit(solution)/shard_map/ppermute | solution.py:239
  50.3 7.1 %collective-permute-start.14 = (f32[128,128]{1,0:T(8,128)S(1)}, f32[128,128]{1,0:T(8,128)S(1)}, u32[]{:S(2)}, u32[]{:S(2)}) collective-permute-start(f32[128,128]{1,0:T(8,128)S(1)} %shard_map.130.refs_0_), channel_id=1, source_target_pairs={{0,2},{1,3},{2,0},{3,1},{4,6},{5,7},{6,4},{7,5},{8,10},{9,11},{10,... | collective-permute-start | bytes 196616 | tf_op jit(solution)/shard_map/ppermute | solution.py:239
  50.9 6.5 %collective-permute-start.13 = (f32[128,128]{1,0:T(8,128)S(1)}, f32[128,128]{1,0:T(8,128)S(1)}, u32[]{:S(2)}, u32[]{:S(2)}) collective-permute-start(f32[128,128]{1,0:T(8,128)S(1)} %shard_map.130.refs_0_), channel_id=1, source_target_pairs={{0,1},{1,0},{2,3},{3,2},{4,5},{5,4},{6,7},{7,6},{8,9},{9,8},{10,11... | collective-permute-start | bytes 196616 | tf_op jit(solution)/shard_map/ppermute | solution.py:239
  58.7 5.0 %collective-permute-start.21 = (f32[128,128]{1,0:T(8,128)S(1)}, f32[128,128]{1,0:T(8,128)S(1)}, u32[]{:S(2)}, u32[]{:S(2)}) collective-permute-start(f32[128,128]{1,0:T(8,128)S(1)} %get-tuple-element.20), channel_id=1, source_target_pairs={{0,1},{1,0},{2,3},{3,2},{4,5},{5,4},{6,7},{7,6},{8,9},{9,8},{10,11... | collective-permute-start | bytes 196616 | tf_op jit(solution)/shard_map/ppermute | solution.py:239
  58.8 7.7 %collective-permute-start.22 = (f32[128,128]{1,0:T(8,128)S(1)}, f32[128,128]{1,0:T(8,128)S(1)}, u32[]{:S(2)}, u32[]{:S(2)}) collective-permute-start(f32[128,128]{1,0:T(8,128)S(1)} %get-tuple-element.21), channel_id=1, source_target_pairs={{0,2},{1,3},{2,0},{3,1},{4,6},{5,7},{6,4},{7,5},{8,10},{9,11},{10,... | collective-permute-start | bytes 196616 | tf_op jit(solution)/shard_map/ppermute | solution.py:239
  61.3 6.2 %collective-permute-start.23 = (f32[128,128]{1,0:T(8,128)S(1)}, f32[128,128]{1,0:T(8,128)S(1)}, u32[]{:S(2)}, u32[]{:S(2)}) collective-permute-start(f32[128,128]{1,0:T(8,128)S(1)} %get-tuple-element.22), channel_id=1, source_target_pairs={{0,3},{1,2},{2,1},{3,0},{4,7},{5,6},{6,5},{7,4},{8,11},{9,10},{10,... | collective-permute-start | bytes 196616 | tf_op jit(solution)/shard_map/ppermute | solution.py:239
  67.6 5.4 %collective-permute-start.26 = (f32[2,128]{1,0:T(2,128)S(1)}, f32[2,128]{1,0:T(2,128)S(1)}, u32[]{:S(2)}, u32[]{:S(2)}) collective-permute-start(f32[2,128]{1,0:T(2,128)S(1)} %get-tuple-element.24.refs_0_), channel_id=1, source_target_pairs={{0,3},{1,2},{2,1},{3,0},{4,7},{5,6},{6,5},{7,4},{8,11},{9,10},{10,... | collective-permute-start | bytes 3080 | tf_op jit(solution)/shard_map/ppermute | solution.py:239
  69.4 4.5 %collective-permute-start.25 = (f32[2,128]{1,0:T(2,128)S(1)}, f32[2,128]{1,0:T(2,128)S(1)}, u32[]{:S(2)}, u32[]{:S(2)}) collective-permute-start(f32[2,128]{1,0:T(2,128)S(1)} %get-tuple-element.24.refs_0_), channel_id=1, source_target_pairs={{0,2},{1,3},{2,0},{3,1},{4,6},{5,7},{6,4},{7,5},{8,10},{9,11},{10,... | collective-permute-start | bytes 3080 | tf_op jit(solution)/shard_map/ppermute | solution.py:239
  70.2 3.7 %collective-permute-start.24 = (f32[2,128]{1,0:T(2,128)S(1)}, f32[2,128]{1,0:T(2,128)S(1)}, u32[]{:S(2)}, u32[]{:S(2)}) collective-permute-start(f32[2,128]{1,0:T(2,128)S(1)} %get-tuple-element.24.refs_0_), channel_id=1, source_target_pairs={{0,1},{1,0},{2,3},{3,2},{4,5},{5,4},{6,7},{7,6},{8,9},{9,8},{10,11... | collective-permute-start | bytes 3080 | tf_op jit(solution)/shard_map/ppermute | solution.py:239

commit v3 on v2

--- a/solution.py
+++ b/solution.py
@@ -67,53 +67,55 @@
     return jax.ShapeDtypeStruct(dims, F32)
 
 
-def embed_kernel(count, far, x_hbm, w_hbm, *rest):
-    outs, (x_buf, w_buf, sems) = rest[: count // 2], rest[count // 2 :]
+def embed_kernel(count, x_hbm, w_hbm, *rest):
+    outs, (x_buf, w_buf, x_sems, w_sems) = rest[:count], rest[count:]
     pos = lax.axis_index("head")
-    half = w_hbm.shape[1] // 2
-    side = pos // (count // 2)
-    side = 1 - side if far else side
-    cols = pl.ds(pl.multiple_of(side * half, half), half)
     steps, step = w_buf.shape[0], w_buf.shape[1]
-    copies = []
+    halves, wide = x_buf.shape[0], x_buf.shape[2]
+    x_copies = [
+        pltpu.make_async_copy(x_hbm.at[:, pl.ds(at * wide, wide)], x_buf.at[at], x_sems.at[at]) for at in range(halves)
+    ]
+    w_copies = [
+        pltpu.make_async_copy(w_hbm.at[pl.ds(at * step, step), :], w_buf.at[at], w_sems.at[at]) for at in range(steps)
+    ]
     for at in range(steps):
-        span = pl.ds(at * step, step)
-        copies.append(
-            (
-                pltpu.make_async_copy(x_hbm.at[:, span], x_buf.at[at], sems.at[0, at]),
-                pltpu.make_async_copy(w_hbm.at[span, cols], w_buf.at[at], sems.at[1, at]),
-            )
-        )
-        for copy in copies[-1]:
-            copy.start()
+        if (at * step) % wide == 0:
+            x_copies[at * step // wide].start()
+        w_copies[at].start()
     total = None
     for at in range(steps):
-        for copy in copies[at]:
-            copy.wait()
-        part = dot3(x_buf[at], w_buf[at])
+        half, start = divmod(at * step, wide)
+        if start == 0:
+            x_copies[half].wait()
+        w_copies[at].wait()
+        part = dot3(x_buf[half, :, start : start + step], w_buf[at])
         total = part if total is None else total + part
-    for ref, block in zip(outs, butterfly(columns(total, count // 2), pos)):
+    for ref, block in zip(outs, butterfly(columns(total, count), pos)):
         ref[...] = block
 
 
-def embed_half(count, far, series, emb_weight):
+def embed(count, series, emb_weight):
     rows, depth = series.shape
-    half = emb_weight.shape[1] // 2
+    model = emb_weight.shape[1]
     step = math.gcd(depth, 256)
     steps = depth // step
+    halves = 2 if steps % 2 == 0 else 1
     hbm = pl.BlockSpec(memory_space=pltpu.HBM)
     return pl.pallas_call(
-        functools.partial(embed_kernel, count, far),
-        out_shape=[shape(rows, 2 * half // count)] * (count // 2),
+        functools.partial(embed_kernel, count),
+        out_shape=[shape(rows, model // count)] * count,
         in_specs=[hbm, hbm],
         scratch_shapes=[
-            pltpu.VMEM((steps, rows, step), F32),
-            pltpu.VMEM((steps, step, half), F32),
-            pltpu.SemaphoreType.DMA((2, steps)),
+            pltpu.VMEM((halves, rows, depth // halves), F32),
+            pltpu.VMEM((steps, step, model), F32),
+            pltpu.SemaphoreType.DMA((halves,)),
+            pltpu.SemaphoreType.DMA((steps,)),
         ],
-        name="embed_far" if far else "embed_near",
-        compiler_params=pltpu.CompilerParams(vmem_limit_bytes=(127 if far else 121) * MIB // 2),
-        cost_estimate=pl.CostEstimate(flops=6 * rows * depth * half, bytes_accessed=4 * depth * half, transcendentals=0),
+        name="embed",
+        compiler_params=pltpu.CompilerParams(vmem_limit_bytes=122 * MIB // 2),
+        cost_estimate=pl.CostEstimate(
+            flops=6 * rows * depth * model, bytes_accessed=4 * depth * (model + rows), transcendentals=0
+        ),
     )(series, emb_weight)
 
 
@@ -138,13 +140,15 @@
             out[pl.ds(start, size), :] = rest_ref[apart, k]
 
 
-def embed_reduce_kernel(count, *refs):
-    pos = lax.axis_index("head")
-    parts, bias, out = refs[:count], refs[count], refs[count + 1]
-    total = parts[0][...]
-    for part in parts[1:]:
+def bias_kernel(x_ref, bias, out):
+    out[...] = x_ref[...] + bias[lax.axis_index("head")]
+
+
+def add_kernel(*refs):
+    total = refs[0][...]
+    for part in refs[1:-1]:
         total = total + part[...]
-    out[...] = total + bias[pos]
+    refs[-1][...] = total
 
 
 def rows_of(weight, block, width):
@@ -268,15 +272,12 @@
 
     var_bits = lax.axis_size("var").bit_length() - 1
     bits = [var_bits - 1, 0]
-    far = embed_half(n, True, series, emb_weight)
-    near = embed_half(n, False, series, emb_weight)
-    parts = [*near, *far]
+    parts = embed(n, series, emb_weight)
     got = hand_out(parts, "head")
+    got[0] = call(bias_kernel, block)(parts[0], emb_bias.reshape(n, 1, width))
     cut = call(functools.partial(cut_kernel, bits), shape(heads_width >> len(bits), model))(out_weight)
     rest = jnp.stack(spread_out(cut, "head")[1:])[None]
-    mine = call(functools.partial(embed_reduce_kernel, n), block)(
-        *got, emb_bias.reshape(n, 1, width)
-    )
+    mine = call(add_kernel, block)(*got)
     emb = spread_out(mine, "head")
     for bit in bits:
         rest = jnp.concatenate([rest, send(rest, "var", 1 << bit)], 0)

time: 75 us -> 73 us (0.973)
  Pallas kernels: 11.7 us -> 8.78 us
  starting transfers between devices: 32.3 us -> 33.3 us
    pallas_call x3, Pallas kernels: 7.18 us -> 4.2 us  [the longest x1 4.18 us: embed(): pl.pallas_call(functools.partial(embed_kernel, count), out_shape=[shape(r...]
    ppermute x27, starting transfers between devices: 32.3 us -> 33.3 us  [send(): return lax.ppermute(x, axis, [(i, i ^ offset) for i in range(size)])]
  transfers between devices with their start and end apart: 27 -> 27, of which waited for: 18 -> 17; matrix products, arithmetic and copies ran while one was open for 0% -> 0% of each run, Pallas kernels for 13% -> 9%
where the time goes in v3:
time: 73 us; the launch traced here: 72.8 us
  starting transfers between devices  33.3 us (46%)
  waiting for transfers between devices  28.6 us (39%)
  Pallas kernels  8.78 us (12%)
  local copies, waits for them, and re-layouts  1.84 us (3%)
    ppermute x27, starting transfers between devices, send(): return lax.ppermute(x, axis, [(i, i ^ offset) for i in range(size)])  33.3 us
    ppermute x27, waiting for transfers between devices, send(): return lax.ppermute(x, axis, [(i, i ^ offset) for i in range(size)])  28.6 us
    pallas_call x1, Pallas kernels, embed(): pl.pallas_call(functools.partial(embed_kernel, count), out_shape=[shape(r...  4.18 us
    unnamed x26, local copies, waits for them, and re-layouts  1.84 us
    pallas_call x1, Pallas kernels, on_device(): call(attend_kernel, shape(rows, heads_width), limit=16)(queries, *pieces)  1.55 us
  transfers between devices with their start and end apart: 27, of which 17 were waited for; matrix products, arithmetic and copies ran while one was open for 0% of the time, Pallas kernels for 9%

profile of v3, /device:TPU:0, one launch (start us, length us, event | category | flops | bytes accessed | tf_op | source)
XLA Modules:
  0.0 72.8 jit_solution(2551906006882196735)
XLA Ops:
  0.0 0.9 %copy-done.2 = f32[128,512]{1,0:T(8,128)S(1)} copy-done((f32[128,512]{1,0:T(8,128)S(1)}, f32[128,512]{1,0:T(8,128)}, u32[]{:S(2)}) %copy-start.2) | copy-done | bytes 262168
  1.0 5.1 %collective-permute-start.18 = (f32[32,512]{1,0:T(8,128)S(1)}, f32[32,512]{1,0:T(8,128)S(1)}, u32[]{:S(2)}, u32[]{:S(2)}) collective-permute-start(f32[32,512]{1,0:T(8,128)S(1)} %shard_map.132), channel_id=1, source_target_pairs={{0,3},{1,2},{2,1},{3,0},{4,7},{5,6},{6,5},{7,4},{8,11},{9,10},{10,... | collective-permute-start | bytes 196616 | tf_op jit(solution)/shard_map/ppermute | solution.py:243
  6.1 0.6 collective-permute-start.16
  6.8 1.8 %collective-permute-done.18 = f32[32,512]{1,0:T(8,128)S(1)} collective-permute-done((f32[32,512]{1,0:T(8,128)S(1)}, f32[32,512]{1,0:T(8,128)S(1)}, u32[]{:S(2)}, u32[]{:S(2)}) %collective-permute-start.18) | collective-permute-done | bytes 65568 | tf_op jit(solution)/shard_map/ppermute | solution.py:243
  8.6 3.1 %collective-permute-done.17 = f32[32,512]{1,0:T(8,128)S(1)} collective-permute-done((f32[32,512]{1,0:T(8,128)S(1)}, f32[32,512]{1,0:T(8,128)S(1)}, u32[]{:S(2)}, u32[]{:S(2)}) %collective-permute-start.17) | collective-permute-done | bytes 65568 | tf_op jit(solution)/shard_map/ppermute | solution.py:243
  11.8 1.6 %collective-permute-start.19 = (f32[1,3,32,512]{3,2,1,0:T(8,128)S(1)}, f32[1,3,32,512]{3,2,1,0:T(8,128)S(1)}, u32[]{:S(2)}, u32[]{:S(2)}) collective-permute-start(f32[1,3,32,512]{3,2,1,0:T(8,128)S(1)} %maximum_bitcast_fusion), channel_id=1, source_target_pairs={{0,16},{4,20},{8,24},{12,28},{16,0},{20,4},{24,8},{28,12},{1,17},{... | collective-permute-start | bytes 589832 | tf_op jit(solution)/shard_map/ppermute | solution.py:243
  13.4 4.2 %embed.1 = (f32[128,128]{1,0:T(8,128)}, f32[128,128]{1,0:T(8,128)}, f32[128,128]{1,0:T(8,128)}, f32[128,128]{1,0:T(8,128)}) custom-call(f32[128,2048]{1,0:T(8,128)} %x_hbm.1, f32[2048,512]{1,0:T(8,128)} %w_hbm.1), custom_call_target="tpu_custom_call" | custom-call | flops 805306368 | bytes 5242880 | tf_op jit(solution)/shard_map/embed/pallas_call | solution.py:104
  17.6 1.1 %collective-permute-start = (f32[128,128]{1,0:T(8,128)}, f32[128,128]{1,0:T(8,128)S(1)}, u32[]{:S(2)}, u32[]{:S(2)}) collective-permute-start(f32[128,128]{1,0:T(8,128)} %get-tuple-element.16), channel_id=1, source_target_pairs={{0,1},{1,0},{2,3},{3,2},{4,5},{5,4},{6,7},{7,6},{8,9},{9,8},{10,11... | collective-permute-start | bytes 196616 | tf_op jit(solution)/shard_map/ppermute | solution.py:243
  18.7 2.2 %collective-permute-start.1 = (f32[128,128]{1,0:T(8,128)}, f32[128,128]{1,0:T(8,128)S(1)}, u32[]{:S(2)}, u32[]{:S(2)}) collective-permute-start(f32[128,128]{1,0:T(8,128)} %get-tuple-element.17), channel_id=1, source_target_pairs={{0,2},{1,3},{2,0},{3,1},{4,6},{5,7},{6,4},{7,5},{8,10},{9,11},{10,... | collective-permute-start | bytes 196616 | tf_op jit(solution)/shard_map/ppermute | solution.py:243
  20.9 1.1 %collective-permute-start.2 = (f32[128,128]{1,0:T(8,128)}, f32[128,128]{1,0:T(8,128)S(1)}, u32[]{:S(2)}, u32[]{:S(2)}) collective-permute-start(f32[128,128]{1,0:T(8,128)} %get-tuple-element.18), channel_id=1, source_target_pairs={{0,3},{1,2},{2,1},{3,0},{4,7},{5,6},{6,5},{7,4},{8,11},{9,10},{10,... | collective-permute-start | bytes 196616 | tf_op jit(solution)/shard_map/ppermute | solution.py:243
  22.1 0.1 collective-permute-start.20
  22.2 0.8 %copy-done.7 = f32[128,128]{1,0:T(8,128)S(1)} copy-done((f32[128,128]{1,0:T(8,128)S(1)}, f32[128,128]{1,0:T(8,128)}, u32[]{:S(2)}) %copy-start.7) | copy-done | bytes 65560
  23.0 2.4 %collective-permute-done.1.refs_2_ = f32[128,128]{1,0:T(8,128)S(1)} collective-permute-done((f32[128,128]{1,0:T(8,128)}, f32[128,128]{1,0:T(8,128)S(1)}, u32[]{:S(2)}, u32[]{:S(2)}) %collective-permute-start.1) | collective-permute-done | bytes 65568 | tf_op jit(solution)/shard_map/ppermute | solution.py:243
  25.4 1.9 %collective-permute-done.2.refs_3_ = f32[128,128]{1,0:T(8,128)S(1)} collective-permute-done((f32[128,128]{1,0:T(8,128)}, f32[128,128]{1,0:T(8,128)S(1)}, u32[]{:S(2)}, u32[]{:S(2)}) %collective-permute-start.2) | collective-permute-done | bytes 65568 | tf_op jit(solution)/shard_map/ppermute | solution.py:243
  27.3 1.1 %collective-permute-start.5 = (f32[128,128]{1,0:T(8,128)S(1)}, f32[128,128]{1,0:T(8,128)S(1)}, u32[]{:S(2)}, u32[]{:S(2)}) collective-permute-start(f32[128,128]{1,0:T(8,128)S(1)} %shard_map.128.refs_0_.refs_4_), channel_id=1, source_target_pairs={{0,3},{1,2},{2,1},{3,0},{4,7},{5,6},{6,5},{7,4},{8,11},{9,10},{10,... | collective-permute-start | bytes 196616 | tf_op jit(solution)/shard_map/ppermute | solution.py:243
  28.4 0.3 collective-permute-start.4
  28.7 3.1 %collective-permute-start.3 = (f32[128,128]{1,0:T(8,128)S(1)}, f32[128,128]{1,0:T(8,128)S(1)}, u32[]{:S(2)}, u32[]{:S(2)}) collective-permute-start(f32[128,128]{1,0:T(8,128)S(1)} %shard_map.128.refs_0_.refs_4_), channel_id=1, source_target_pairs={{0,1},{1,0},{2,3},{3,2},{4,5},{5,4},{6,7},{7,6},{8,9},{9,8},{10,11... | collective-permute-start | bytes 196616 | tf_op jit(solution)/shard_map/ppermute | solution.py:243
  31.8 1.8 %collective-permute-done.5.refs_3_.refs_7_ = f32[128,128]{1,0:T(8,128)S(1)} collective-permute-done((f32[128,128]{1,0:T(8,128)S(1)}, f32[128,128]{1,0:T(8,128)S(1)}, u32[]{:S(2)}, u32[]{:S(2)}) %collective-permute-start.5) | collective-permute-done | bytes 65568 | tf_op jit(solution)/shard_map/ppermute | solution.py:243
  33.5 1.3 %collective-permute-done.4.refs_2_.refs_6_ = f32[128,128]{1,0:T(8,128)S(1)} collective-permute-done((f32[128,128]{1,0:T(8,128)S(1)}, f32[128,128]{1,0:T(8,128)S(1)}, u32[]{:S(2)}, u32[]{:S(2)}) %collective-permute-start.4) | collective-permute-done | bytes 65568 | tf_op jit(solution)/shard_map/ppermute | solution.py:243
  34.9 0.4 shard_map.130.refs_0_
  35.2 1.5 %collective-permute-start.8 = (f32[128,256]{1,0:T(8,128)S(1)}, f32[128,256]{1,0:T(8,128)S(1)}, u32[]{:S(2)}, u32[]{:S(2)}) collective-permute-start(f32[128,256]{1,0:T(8,128)S(1)} %shard_map.130.refs_0_), channel_id=1, source_target_pairs={{0,24},{4,28},{8,16},{12,20},{16,8},{20,12},{24,0},{28,4},{1,25},{... | collective-permute-start | bytes 393224 | tf_op jit(solution)/shard_map/ppermute | solution.py:243
  36.7 1.5 %collective-permute-start.7 = (f32[128,256]{1,0:T(8,128)S(1)}, f32[128,256]{1,0:T(8,128)S(1)}, u32[]{:S(2)}, u32[]{:S(2)}) collective-permute-start(f32[128,256]{1,0:T(8,128)S(1)} %shard_map.130.refs_0_), channel_id=1, source_target_pairs={{0,16},{4,20},{8,24},{12,28},{16,0},{20,4},{24,8},{28,12},{1,17},{... | collective-permute-start | bytes 393224 | tf_op jit(solution)/shard_map/ppermute | solution.py:243
  38.3 0.5 collective-permute-start.6
  38.8 2.5 %collective-permute-done.8.refs_3_ = f32[128,256]{1,0:T(8,128)S(1)} collective-permute-done((f32[128,256]{1,0:T(8,128)S(1)}, f32[128,256]{1,0:T(8,128)S(1)}, u32[]{:S(2)}, u32[]{:S(2)}) %collective-permute-start.8) | collective-permute-done | bytes 131104 | tf_op jit(solution)/shard_map/ppermute | solution.py:243
  41.3 1.3 %collective-permute-done.7.refs_2_ = f32[128,256]{1,0:T(8,128)S(1)} collective-permute-done((f32[128,256]{1,0:T(8,128)S(1)}, f32[128,256]{1,0:T(8,128)S(1)}, u32[]{:S(2)}, u32[]{:S(2)}) %collective-permute-start.7) | collective-permute-done | bytes 131104 | tf_op jit(solution)/shard_map/ppermute | solution.py:243
  42.6 0.6 collective-permute-done.6.refs_1_
  43.2 0.3 shard_map.129.q_ref
  43.6 0.4 collective-permute-done.11.refs_6_
  43.9 0.7 collective-permute-done.10.refs_5_
  44.6 1.6 %shard_map.131.refs_0_ = f32[128,128]{1,0:T(8,128)S(1)} custom-call(f32[128,128]{1,0:T(8,128)S(1)} %shard_map.129.q_ref, f32[128,256]{1,0:T(8,128)S(1)} %shard_map.130.refs_0_, f32[128,256]{1,0:T(8,128)S(1)} %collective-permute-done.6.refs_1_, f32[128,256]{1,0:T(8,128)S(1)} %collective-permute-done.7.refs_2_, f32[128,256]{1,0:T(8,128)S(1)} %collective-permute-done.8.refs_3_, ...), custom_call_target="tpu_custom_call" | custom-call | tf_op jit(solution)/shard_map/pallas_call | solution.py:289
  46.1 1.7 %collective-permute-start.15 = (f32[128,128]{1,0:T(8,128)S(1)}, f32[128,128]{1,0:T(8,128)S(1)}, u32[]{:S(2)}, u32[]{:S(2)}) collective-permute-start(f32[128,128]{1,0:T(8,128)S(1)} %shard_map.131.refs_0_), channel_id=1, source_target_pairs={{0,3},{1,2},{2,1},{3,0},{4,7},{5,6},{6,5},{7,4},{8,11},{9,10},{10,... | collective-permute-start | bytes 196616 | tf_op jit(solution)/shard_map/ppermute | solution.py:243
  47.9 1.0 %collective-permute-start.14 = (f32[128,128]{1,0:T(8,128)S(1)}, f32[128,128]{1,0:T(8,128)S(1)}, u32[]{:S(2)}, u32[]{:S(2)}) collective-permute-start(f32[128,128]{1,0:T(8,128)S(1)} %shard_map.131.refs_0_), channel_id=1, source_target_pairs={{0,2},{1,3},{2,0},{3,1},{4,6},{5,7},{6,4},{7,5},{8,10},{9,11},{10,... | collective-permute-start | bytes 196616 | tf_op jit(solution)/shard_map/ppermute | solution.py:243
  48.8 1.7 %collective-permute-start.13 = (f32[128,128]{1,0:T(8,128)S(1)}, f32[128,128]{1,0:T(8,128)S(1)}, u32[]{:S(2)}, u32[]{:S(2)}) collective-permute-start(f32[128,128]{1,0:T(8,128)S(1)} %shard_map.131.refs_0_), channel_id=1, source_target_pairs={{0,1},{1,0},{2,3},{3,2},{4,5},{5,4},{6,7},{7,6},{8,9},{9,8},{10,11... | collective-permute-start | bytes 196616 | tf_op jit(solution)/shard_map/ppermute | solution.py:243
  50.7 0.1 shard_map.133.refs_8_
  50.7 2.3 %collective-permute-done.15.refs_3_ = f32[128,128]{1,0:T(8,128)S(1)} collective-permute-done((f32[128,128]{1,0:T(8,128)S(1)}, f32[128,128]{1,0:T(8,128)S(1)}, u32[]{:S(2)}, u32[]{:S(2)}) %collective-permute-start.15) | collective-permute-done | bytes 65568 | tf_op jit(solution)/shard_map/ppermute | solution.py:243
  53.0 2.3 %collective-permute-done.14.refs_2_ = f32[128,128]{1,0:T(8,128)S(1)} collective-permute-done((f32[128,128]{1,0:T(8,128)S(1)}, f32[128,128]{1,0:T(8,128)S(1)}, u32[]{:S(2)}, u32[]{:S(2)}) %collective-permute-start.14) | collective-permute-done | bytes 65568 | tf_op jit(solution)/shard_map/ppermute | solution.py:243
  55.3 1.3 %shard_map.134 = (f32[128,128]{1,0:T(8,128)S(1)}, f32[128,128]{1,0:T(8,128)S(1)}, f32[128,128]{1,0:T(8,128)S(1)}, f32[128,128]{1,0:T(8,128)S(1)}) custom-call(f32[128,128]{1,0:T(8,128)S(1)} %shard_map.131.refs_0_, f32[128,128]{1,0:T(8,128)S(1)} %collective-permute-done.13.refs_1_, f32[128,128]{1,0:T(8,128)S(1)} %collective-permute-done.14.refs_2_, ...), custom_call_target="tpu_custom_call" | custom-call | tf_op jit(solution)/shard_map/pallas_call | solution.py:291
  56.7 1.9 %collective-permute-start.22 = (f32[128,128]{1,0:T(8,128)S(1)}, f32[128,128]{1,0:T(8,128)S(1)}, u32[]{:S(2)}, u32[]{:S(2)}) collective-permute-start(f32[128,128]{1,0:T(8,128)S(1)} %get-tuple-element.21), channel_id=1, source_target_pairs={{0,2},{1,3},{2,0},{3,1},{4,6},{5,7},{6,4},{7,5},{8,10},{9,11},{10,... | collective-permute-start | bytes 196616 | tf_op jit(solution)/shard_map/ppermute | solution.py:243
  58.6 2.5 %collective-permute-start.23 = (f32[128,128]{1,0:T(8,128)S(1)}, f32[128,128]{1,0:T(8,128)S(1)}, u32[]{:S(2)}, u32[]{:S(2)}) collective-permute-start(f32[128,128]{1,0:T(8,128)S(1)} %get-tuple-element.22), channel_id=1, source_target_pairs={{0,3},{1,2},{2,1},{3,0},{4,7},{5,6},{6,5},{7,4},{8,11},{9,10},{10,... | collective-permute-start | bytes 196616 | tf_op jit(solution)/shard_map/ppermute | solution.py:243
  61.1 0.5 collective-permute-done.21.refs_1_
  61.6 3.5 %collective-permute-done.22.refs_2_ = f32[128,128]{1,0:T(8,128)S(1)} collective-permute-done((f32[128,128]{1,0:T(8,128)S(1)}, f32[128,128]{1,0:T(8,128)S(1)}, u32[]{:S(2)}, u32[]{:S(2)}) %collective-permute-start.22) | collective-permute-done | bytes 65568 | tf_op jit(solution)/shard_map/ppermute | solution.py:243
  65.0 0.1 shard_map.135
  65.2 2.3 %collective-permute-start.26 = (f32[2,128]{1,0:T(2,128)S(1)}, f32[2,128]{1,0:T(2,128)S(1)}, u32[]{:S(2)}, u32[]{:S(2)}) collective-permute-start(f32[2,128]{1,0:T(2,128)S(1)} %get-tuple-element.24.refs_0_), channel_id=1, source_target_pairs={{0,3},{1,2},{2,1},{3,0},{4,7},{5,6},{6,5},{7,4},{8,11},{9,10},{10,... | collective-permute-start | bytes 3080 | tf_op jit(solution)/shard_map/ppermute | solution.py:243
  67.4 0.5 collective-permute-start.25
  68.0 1.7 %collective-permute-start.24 = (f32[2,128]{1,0:T(2,128)S(1)}, f32[2,128]{1,0:T(2,128)S(1)}, u32[]{:S(2)}, u32[]{:S(2)}) collective-permute-start(f32[2,128]{1,0:T(2,128)S(1)} %get-tuple-element.24.refs_0_), channel_id=1, source_target_pairs={{0,1},{1,0},{2,3},{3,2},{4,5},{5,4},{6,7},{7,6},{8,9},{9,8},{10,11... | collective-permute-start | bytes 3080 | tf_op jit(solution)/shard_map/ppermute | solution.py:243
  69.6 1.0 %collective-permute-done.26.refs_3_ = f32[2,128]{1,0:T(2,128)S(1)} collective-permute-done((f32[2,128]{1,0:T(2,128)S(1)}, f32[2,128]{1,0:T(2,128)S(1)}, u32[]{:S(2)}, u32[]{:S(2)}) %collective-permute-start.26) | collective-permute-done | bytes 1056 | tf_op jit(solution)/shard_map/ppermute | solution.py:243
  70.6 1.3 %collective-permute-done.25.refs_2_ = f32[2,128]{1,0:T(2,128)S(1)} collective-permute-done((f32[2,128]{1,0:T(2,128)S(1)}, f32[2,128]{1,0:T(2,128)S(1)}, u32[]{:S(2)}, u32[]{:S(2)}) %collective-permute-start.25) | collective-permute-done | bytes 1056 | tf_op jit(solution)/shard_map/ppermute | solution.py:243
  71.9 0.8 %shard_map.136 = f32[128,128]{1,0:T(8,128)} custom-call(f32[128,128]{1,0:T(8,128)S(1)} %get-tuple-element.23.x_ref, f32[2,128]{1,0:T(2,128)S(1)} %get-tuple-element.24.refs_0_, f32[2,128]{1,0:T(2,128)S(1)} %collective-permute-done.24.refs_1_, f32[2,128]{1,0:T(2,128)S(1)} %collective-permute-done.25.refs_2_, f32[2,128]{1,0:T(2,128)S(1)} %collective-permute-done.26.refs_3_, ...), custom_call_target="tpu_custom_call" | custom-call | tf_op jit(solution)/shard_map/pallas_call | solution.py:296
  (46 shorter events, 0.3 us)
Async XLA Ops:
  0.0 0.9 %copy-start.2 = (f32[128,512]{1,0:T(8,128)S(1)}, f32[128,512]{1,0:T(8,128)}, u32[]{:S(2)}) copy-start(f32[128,512]{1,0:T(8,128)} %own_ref.1) | copy-start | bytes 786436
  1.0 21.2 %copy-start.8 = (f32[512]{0:T(512)S(1)}, f32[512]{0:T(512)}, u32[]{:S(2)}) copy-start(f32[512]{0:T(512)} %param.15) | copy-start | bytes 6148
  1.0 33.9 %copy-start.4 = (f32[512,128]{1,0:T(8,128)S(1)}, f32[512,128]{1,0:T(8,128)}, u32[]{:S(2)}) copy-start(f32[512,128]{1,0:T(8,128)} %refs_4_.3) | copy-start | bytes 786436
  1.0 33.9 %copy-start.5 = (f32[512,128]{1,0:T(8,128)S(1)}, f32[512,128]{1,0:T(8,128)}, u32[]{:S(2)}) copy-start(f32[512,128]{1,0:T(8,128)} %refs_5_.1) | copy-start | bytes 786436
  1.0 42.3 %copy-start.6 = (f32[512,128]{1,0:T(8,128)S(1)}, f32[512,128]{1,0:T(8,128)}, u32[]{:S(2)}) copy-start(f32[512,128]{1,0:T(8,128)} %refs_4_.2) | copy-start | bytes 786436
  1.0 7.6 %collective-permute-start.18 = (f32[32,512]{1,0:T(8,128)S(1)}, f32[32,512]{1,0:T(8,128)S(1)}, u32[]{:S(2)}, u32[]{:S(2)}) collective-permute-start(f32[32,512]{1,0:T(8,128)S(1)} %shard_map.132), channel_id=1, source_target_pairs={{0,3},{1,2},{2,1},{3,0},{4,7},{5,6},{6,5},{7,4},{8,11},{9,10},{10,... | collective-permute-start | bytes 196616 | tf_op jit(solution)/shard_map/ppermute | solution.py:243
  6.1 5.6 %collective-permute-start.17 = (f32[32,512]{1,0:T(8,128)S(1)}, f32[32,512]{1,0:T(8,128)S(1)}, u32[]{:S(2)}, u32[]{:S(2)}) collective-permute-start(f32[32,512]{1,0:T(8,128)S(1)} %shard_map.132), channel_id=1, source_target_pairs={{0,2},{1,3},{2,0},{3,1},{4,6},{5,7},{6,4},{7,5},{8,10},{9,11},{10,... | collective-permute-start | bytes 196616 | tf_op jit(solution)/shard_map/ppermute | solution.py:243
  6.1 5.6 %collective-permute-start.16 = (f32[32,512]{1,0:T(8,128)S(1)}, f32[32,512]{1,0:T(8,128)S(1)}, u32[]{:S(2)}, u32[]{:S(2)}) collective-permute-start(f32[32,512]{1,0:T(8,128)S(1)} %shard_map.132), channel_id=1, source_target_pairs={{0,1},{1,0},{2,3},{3,2},{4,5},{5,4},{6,7},{7,6},{8,9},{9,8},{10,11... | collective-permute-start | bytes 196616 | tf_op jit(solution)/shard_map/ppermute | solution.py:243
  11.8 38.9 %copy-start.3 = (f32[128,512]{1,0:T(8,128)S(1)}, f32[128,512]{1,0:T(8,128)}, u32[]{:S(2)}) copy-start(f32[128,512]{1,0:T(8,128)} %own_ref.1) | copy-start | bytes 786436
  11.8 10.3 %collective-permute-start.19 = (f32[1,3,32,512]{3,2,1,0:T(8,128)S(1)}, f32[1,3,32,512]{3,2,1,0:T(8,128)S(1)}, u32[]{:S(2)}, u32[]{:S(2)}) collective-permute-start(f32[1,3,32,512]{3,2,1,0:T(8,128)S(1)} %maximum_bitcast_fusion), channel_id=1, source_target_pairs={{0,16},{4,20},{8,24},{12,28},{16,0},{20,4},{24,8},{28,12},{1,17},{... | collective-permute-start | bytes 589832 | tf_op jit(solution)/shard_map/ppermute | solution.py:243
  13.4 41.9 %copy-start.9 = (f32[512]{0:T(512)S(1)}, f32[512]{0:T(512)}, u32[]{:S(2)}) copy-start(f32[512]{0:T(512)} %param.20) | copy-start | bytes 6148
  13.4 41.9 %copy-start.10 = (f32[512]{0:T(512)S(1)}, f32[512]{0:T(512)}, u32[]{:S(2)}) copy-start(f32[512]{0:T(512)} %param.21) | copy-start | bytes 6148
  17.5 37.8 %copy-start = (f32[512,512]{1,0:T(8,128)S(1)}, f32[512,512]{1,0:T(8,128)}, u32[]{:S(2)}) copy-start(f32[512,512]{1,0:T(8,128)} %refs_11_.1) | copy-start | bytes 3145732
  17.6 37.8 %copy-start.1 = (f32[512,512]{1,0:T(8,128)S(1)}, f32[512,512]{1,0:T(8,128)}, u32[]{:S(2)}) copy-start(f32[512,512]{1,0:T(8,128)} %refs_12_.1) | copy-start | bytes 3145732
  17.6 5.4 %collective-permute-start = (f32[128,128]{1,0:T(8,128)}, f32[128,128]{1,0:T(8,128)S(1)}, u32[]{:S(2)}, u32[]{:S(2)}) collective-permute-start(f32[128,128]{1,0:T(8,128)} %get-tuple-element.16), channel_id=1, source_target_pairs={{0,1},{1,0},{2,3},{3,2},{4,5},{5,4},{6,7},{7,6},{8,9},{9,8},{10,11... | collective-permute-start | bytes 196616 | tf_op jit(solution)/shard_map/ppermute | solution.py:243
  18.7 6.7 %collective-permute-start.1 = (f32[128,128]{1,0:T(8,128)}, f32[128,128]{1,0:T(8,128)S(1)}, u32[]{:S(2)}, u32[]{:S(2)}) collective-permute-start(f32[128,128]{1,0:T(8,128)} %get-tuple-element.17), channel_id=1, source_target_pairs={{0,2},{1,3},{2,0},{3,1},{4,6},{5,7},{6,4},{7,5},{8,10},{9,11},{10,... | collective-permute-start | bytes 196616 | tf_op jit(solution)/shard_map/ppermute | solution.py:243
  20.9 6.4 %collective-permute-start.2 = (f32[128,128]{1,0:T(8,128)}, f32[128,128]{1,0:T(8,128)S(1)}, u32[]{:S(2)}, u32[]{:S(2)}) collective-permute-start(f32[128,128]{1,0:T(8,128)} %get-tuple-element.18), channel_id=1, source_target_pairs={{0,3},{1,2},{2,1},{3,0},{4,7},{5,6},{6,5},{7,4},{8,11},{9,10},{10,... | collective-permute-start | bytes 196616 | tf_op jit(solution)/shard_map/ppermute | solution.py:243
  22.1 28.5 %collective-permute-start.20 = (f32[2,3,32,512]{3,2,1,0:T(8,128)S(1)}, f32[2,3,32,512]{3,2,1,0:T(8,128)S(1)}, u32[]{:S(2)}, u32[]{:S(2)}) collective-permute-start(f32[2,3,32,512]{3,2,1,0:T(8,128)S(1)} %pad_maximum_fusion.1), channel_id=1, source_target_pairs={{0,4},{4,0},{8,12},{12,8},{16,20},{20,16},{24,28},{28,24},{1,5},{5... | collective-permute-start | bytes 1179656 | tf_op jit(solution)/shard_map/ppermute | solution.py:243
  22.1 0.8 %copy-start.7 = (f32[128,128]{1,0:T(8,128)S(1)}, f32[128,128]{1,0:T(8,128)}, u32[]{:S(2)}) copy-start(f32[128,128]{1,0:T(8,128)} %get-tuple-element.15.x_ref) | copy-start | bytes 196612
  27.3 6.2 %collective-permute-start.5 = (f32[128,128]{1,0:T(8,128)S(1)}, f32[128,128]{1,0:T(8,128)S(1)}, u32[]{:S(2)}, u32[]{:S(2)}) collective-permute-start(f32[128,128]{1,0:T(8,128)S(1)} %shard_map.128.refs_0_.refs_4_), channel_id=1, source_target_pairs={{0,3},{1,2},{2,1},{3,0},{4,7},{5,6},{6,5},{7,4},{8,11},{9,10},{10,... | collective-permute-start | bytes 196616 | tf_op jit(solution)/shard_map/ppermute | solution.py:243
  28.4 6.5 %collective-permute-start.4 = (f32[128,128]{1,0:T(8,128)S(1)}, f32[128,128]{1,0:T(8,128)S(1)}, u32[]{:S(2)}, u32[]{:S(2)}) collective-permute-start(f32[128,128]{1,0:T(8,128)S(1)} %shard_map.128.refs_0_.refs_4_), channel_id=1, source_target_pairs={{0,2},{1,3},{2,0},{3,1},{4,6},{5,7},{6,4},{7,5},{8,10},{9,11},{10,... | collective-permute-start | bytes 196616 | tf_op jit(solution)/shard_map/ppermute | solution.py:243
  28.7 6.1 %collective-permute-start.3 = (f32[128,128]{1,0:T(8,128)S(1)}, f32[128,128]{1,0:T(8,128)S(1)}, u32[]{:S(2)}, u32[]{:S(2)}) collective-permute-start(f32[128,128]{1,0:T(8,128)S(1)} %shard_map.128.refs_0_.refs_4_), channel_id=1, source_target_pairs={{0,1},{1,0},{2,3},{3,2},{4,5},{5,4},{6,7},{7,6},{8,9},{9,8},{10,11... | collective-permute-start | bytes 196616 | tf_op jit(solution)/shard_map/ppermute | solution.py:243
  35.2 6.0 %collective-permute-start.8 = (f32[128,256]{1,0:T(8,128)S(1)}, f32[128,256]{1,0:T(8,128)S(1)}, u32[]{:S(2)}, u32[]{:S(2)}) collective-permute-start(f32[128,256]{1,0:T(8,128)S(1)} %shard_map.130.refs_0_), channel_id=1, source_target_pairs={{0,24},{4,28},{8,16},{12,20},{16,8},{20,12},{24,0},{28,4},{1,25},{... | collective-permute-start | bytes 393224 | tf_op jit(solution)/shard_map/ppermute | solution.py:243
  36.7 5.8 %collective-permute-start.7 = (f32[128,256]{1,0:T(8,128)S(1)}, f32[128,256]{1,0:T(8,128)S(1)}, u32[]{:S(2)}, u32[]{:S(2)}) collective-permute-start(f32[128,256]{1,0:T(8,128)S(1)} %shard_map.130.refs_0_), channel_id=1, source_target_pairs={{0,16},{4,20},{8,24},{12,28},{16,0},{20,4},{24,8},{28,12},{1,17},{... | collective-permute-start | bytes 393224 | tf_op jit(solution)/shard_map/ppermute | solution.py:243
  38.3 5.0 %collective-permute-start.6 = (f32[128,256]{1,0:T(8,128)S(1)}, f32[128,256]{1,0:T(8,128)S(1)}, u32[]{:S(2)}, u32[]{:S(2)}) collective-permute-start(f32[128,256]{1,0:T(8,128)S(1)} %shard_map.130.refs_0_), channel_id=1, source_target_pairs={{0,8},{4,12},{8,0},{12,4},{16,24},{20,28},{24,16},{28,20},{1,9},{5... | collective-permute-start | bytes 393224 | tf_op jit(solution)/shard_map/ppermute | solution.py:243
  38.8 4.7 %collective-permute-start.9 = (f32[128,256]{1,0:T(8,128)S(1)}, f32[128,256]{1,0:T(8,128)S(1)}, u32[]{:S(2)}, u32[]{:S(2)}) collective-permute-start(f32[128,256]{1,0:T(8,128)S(1)} %shard_map.130.refs_0_), channel_id=1, source_target_pairs={{0,4},{4,0},{8,12},{12,8},{16,20},{20,16},{24,28},{28,24},{1,5},{5... | collective-permute-start | bytes 393224 | tf_op jit(solution)/shard_map/ppermute | solution.py:243
  41.3 2.3 %collective-permute-start.12 = (f32[128,256]{1,0:T(8,128)S(1)}, f32[128,256]{1,0:T(8,128)S(1)}, u32[]{:S(2)}, u32[]{:S(2)}) collective-permute-start(f32[128,256]{1,0:T(8,128)S(1)} %collective-permute-done.8.refs_3_), channel_id=1, source_target_pairs={{0,4},{4,0},{8,12},{12,8},{16,20},{20,16},{24,28},{28,24},{1,5},{5... | collective-permute-start | bytes 393224 | tf_op jit(solution)/shard_map/ppermute | solution.py:243
  42.6 1.3 %collective-permute-start.11 = (f32[128,256]{1,0:T(8,128)S(1)}, f32[128,256]{1,0:T(8,128)S(1)}, u32[]{:S(2)}, u32[]{:S(2)}) collective-permute-start(f32[128,256]{1,0:T(8,128)S(1)} %collective-permute-done.7.refs_2_), channel_id=1, source_target_pairs={{0,4},{4,0},{8,12},{12,8},{16,20},{20,16},{24,28},{28,24},{1,5},{5... | collective-permute-start | bytes 393224 | tf_op jit(solution)/shard_map/ppermute | solution.py:243
  43.2 1.3 %collective-permute-start.10 = (f32[128,256]{1,0:T(8,128)S(1)}, f32[128,256]{1,0:T(8,128)S(1)}, u32[]{:S(2)}, u32[]{:S(2)}) collective-permute-start(f32[128,256]{1,0:T(8,128)S(1)} %collective-permute-done.6.refs_1_), channel_id=1, source_target_pairs={{0,4},{4,0},{8,12},{12,8},{16,20},{20,16},{24,28},{28,24},{1,5},{5... | collective-permute-start | bytes 393224 | tf_op jit(solution)/shard_map/ppermute | solution.py:243
  43.5 28.4 %copy-start.11 = (f32[512]{0:T(512)S(1)}, f32[512]{0:T(512)}, u32[]{:S(2)}) copy-start(f32[512]{0:T(512)} %param.24) | copy-start | bytes 6148
  43.5 28.4 %copy-start.12 = (f32[512]{0:T(512)S(1)}, f32[512]{0:T(512)}, u32[]{:S(2)}) copy-start(f32[512]{0:T(512)} %param.25) | copy-start | bytes 6148
  46.1 6.9 %collective-permute-start.15 = (f32[128,128]{1,0:T(8,128)S(1)}, f32[128,128]{1,0:T(8,128)S(1)}, u32[]{:S(2)}, u32[]{:S(2)}) collective-permute-start(f32[128,128]{1,0:T(8,128)S(1)} %shard_map.131.refs_0_), channel_id=1, source_target_pairs={{0,3},{1,2},{2,1},{3,0},{4,7},{5,6},{6,5},{7,4},{8,11},{9,10},{10,... | collective-permute-start | bytes 196616 | tf_op jit(solution)/shard_map/ppermute | solution.py:243
  47.9 7.4 %collective-permute-start.14 = (f32[128,128]{1,0:T(8,128)S(1)}, f32[128,128]{1,0:T(8,128)S(1)}, u32[]{:S(2)}, u32[]{:S(2)}) collective-permute-start(f32[128,128]{1,0:T(8,128)S(1)} %shard_map.131.refs_0_), channel_id=1, source_target_pairs={{0,2},{1,3},{2,0},{3,1},{4,6},{5,7},{6,4},{7,5},{8,10},{9,11},{10,... | collective-permute-start | bytes 196616 | tf_op jit(solution)/shard_map/ppermute | solution.py:243
  48.8 6.5 %collective-permute-start.13 = (f32[128,128]{1,0:T(8,128)S(1)}, f32[128,128]{1,0:T(8,128)S(1)}, u32[]{:S(2)}, u32[]{:S(2)}) collective-permute-start(f32[128,128]{1,0:T(8,128)S(1)} %shard_map.131.refs_0_), channel_id=1, source_target_pairs={{0,1},{1,0},{2,3},{3,2},{4,5},{5,4},{6,7},{7,6},{8,9},{9,8},{10,11... | collective-permute-start | bytes 196616 | tf_op jit(solution)/shard_map/ppermute | solution.py:243
  56.6 5.0 %collective-permute-start.21 = (f32[128,128]{1,0:T(8,128)S(1)}, f32[128,128]{1,0:T(8,128)S(1)}, u32[]{:S(2)}, u32[]{:S(2)}) collective-permute-start(f32[128,128]{1,0:T(8,128)S(1)} %get-tuple-element.20), channel_id=1, source_target_pairs={{0,1},{1,0},{2,3},{3,2},{4,5},{5,4},{6,7},{7,6},{8,9},{9,8},{10,11... | collective-permute-start | bytes 196616 | tf_op jit(solution)/shard_map/ppermute | solution.py:243
  56.7 8.3 %collective-permute-start.22 = (f32[128,128]{1,0:T(8,128)S(1)}, f32[128,128]{1,0:T(8,128)S(1)}, u32[]{:S(2)}, u32[]{:S(2)}) collective-permute-start(f32[128,128]{1,0:T(8,128)S(1)} %get-tuple-element.21), channel_id=1, source_target_pairs={{0,2},{1,3},{2,0},{3,1},{4,6},{5,7},{6,4},{7,5},{8,10},{9,11},{10,... | collective-permute-start | bytes 196616 | tf_op jit(solution)/shard_map/ppermute | solution.py:243
  58.6 6.5 %collective-permute-start.23 = (f32[128,128]{1,0:T(8,128)S(1)}, f32[128,128]{1,0:T(8,128)S(1)}, u32[]{:S(2)}, u32[]{:S(2)}) collective-permute-start(f32[128,128]{1,0:T(8,128)S(1)} %get-tuple-element.22), channel_id=1, source_target_pairs={{0,3},{1,2},{2,1},{3,0},{4,7},{5,6},{6,5},{7,4},{8,11},{9,10},{10,... | collective-permute-start | bytes 196616 | tf_op jit(solution)/shard_map/ppermute | solution.py:243
  65.2 5.4 %collective-permute-start.26 = (f32[2,128]{1,0:T(2,128)S(1)}, f32[2,128]{1,0:T(2,128)S(1)}, u32[]{:S(2)}, u32[]{:S(2)}) collective-permute-start(f32[2,128]{1,0:T(2,128)S(1)} %get-tuple-element.24.refs_0_), channel_id=1, source_target_pairs={{0,3},{1,2},{2,1},{3,0},{4,7},{5,6},{6,5},{7,4},{8,11},{9,10},{10,... | collective-permute-start | bytes 3080 | tf_op jit(solution)/shard_map/ppermute | solution.py:243
  67.4 4.5 %collective-permute-start.25 = (f32[2,128]{1,0:T(2,128)S(1)}, f32[2,128]{1,0:T(2,128)S(1)}, u32[]{:S(2)}, u32[]{:S(2)}) collective-permute-start(f32[2,128]{1,0:T(2,128)S(1)} %get-tuple-element.24.refs_0_), channel_id=1, source_target_pairs={{0,2},{1,3},{2,0},{3,1},{4,6},{5,7},{6,4},{7,5},{8,10},{9,11},{10,... | collective-permute-start | bytes 3080 | tf_op jit(solution)/shard_map/ppermute | solution.py:243
  68.0 4.0 %collective-permute-start.24 = (f32[2,128]{1,0:T(2,128)S(1)}, f32[2,128]{1,0:T(2,128)S(1)}, u32[]{:S(2)}, u32[]{:S(2)}) collective-permute-start(f32[2,128]{1,0:T(2,128)S(1)} %get-tuple-element.24.refs_0_), channel_id=1, source_target_pairs={{0,1},{1,0},{2,3},{3,2},{4,5},{5,4},{6,7},{7,6},{8,9},{9,8},{10,11... | collective-permute-start | bytes 3080 | tf_op jit(solution)/shard_map/ppermute | solution.py:243

commit v4 on v3

--- a/solution.py
+++ b/solution.py
@@ -97,7 +97,7 @@
 def embed(count, series, emb_weight):
     rows, depth = series.shape
     model = emb_weight.shape[1]
-    step = math.gcd(depth, 256)
+    step = math.gcd(depth, 512)
     steps = depth // step
     halves = 2 if steps % 2 == 0 else 1
     hbm = pl.BlockSpec(memory_space=pltpu.HBM)
@@ -206,34 +206,43 @@
     normed = normalise(embedded + attention, gain[...], bias[...])
     hidden = gelu(dot3(normed, w_in[...]))
     partial = butterfly(columns(dot3(hidden, w_out[...]), count), pos)
-    mine = butterfly(columns(normed, count), pos)[0]
-    outs[0][...] = mine + partial[0]
-    for ref, block in zip(outs[1:], partial[1:]):
-        ref[...] = block
-
-
-def stats_kernel(count, *refs):
-    parts, out, stats = refs[:count], refs[count], refs[count + 1]
-    total = parts[0][...]
-    for part in parts[1:]:
-        total = total + part[...]
-    flipped = total.T
+    partial[0] = partial[0] + butterfly(columns(normed, count), pos)[0]
+    store_halves(partial, outs)
+
+
+def store_halves(blocks, outs):
+    outs[0][...] = jnp.concatenate(blocks[::2], 1)
+    outs[1][...] = jnp.concatenate(blocks[1::2], 1)
+
+
+def halve_kernel(count, kept, got, *outs):
+    total = kept[...] + got[...]
+    if len(outs) == 1:
+        outs[0][...] = total
+    else:
+        store_halves(columns(total, count), outs)
+
+
+def stats_kernel(kept, got, out, stats):
+    width = out.shape[0]
+    other = jnp.concatenate([got[:, width:], got[:, :width]], 1)
+    flipped = (kept[...] + other).T
     centre = jnp.mean(flipped, axis=0, keepdims=True)
     spread = flipped - centre
-    out[...] = flipped
+    out[...] = flipped[:width]
     stats[...] = jnp.concatenate([centre, jnp.sum(spread * spread, axis=0, keepdims=True)], 0)
 
 
-def final_kernel(count, x_ref, *refs):
+def final_kernel(share, x_ref, *refs):
     pos = lax.axis_index("head")
-    stats, gain, bias, out = refs[:count], refs[count], refs[count + 1], refs[count + 2]
+    stats, (gain, bias, out) = refs[:-3], refs[-3:]
     width = x_ref.shape[0]
     centres = [s[0:1, :] for s in stats]
-    centre = sum(centres[1:], centres[0]) * (1.0 / count)
+    centre = sum(centres[1:], centres[0]) * (1.0 / len(stats))
     square = sum((s[1:2, :] for s in stats[1:]), stats[0][1:2, :])
     for each in centres:
-        square = square + width * (each - centre) * (each - centre)
-    scale = lax.rsqrt(square * (1.0 / (count * width)) + EPS)
+        square = square + share * (each - centre) * (each - centre)
+    scale = lax.rsqrt(square * (1.0 / (len(stats) * share)) + EPS)
     pair = jnp.concatenate([gain[pos], bias[pos], jnp.zeros((6, width), F32)], 0).T
     out[...] = (x_ref[...] - centre) * scale * pair[:, 0:1] + pair[:, 1:2]
 
@@ -249,6 +258,23 @@
 
 def hand_out(parts, axis):
     return [parts[0]] + [send(parts[k], axis, k) for k in range(1, lax.axis_size(axis))]
+
+
+def bits_below(count):
+    return [1 << at for at in range(count.bit_length() - 1)]
+
+
+def halving(kept, give, count):
+    left = count // 2
+    for bit in bits_below(count // 2):
+        got = send(give, "head", bit)
+        rows, wide = kept.shape
+        last = left == 2
+        outs = shape(rows, wide) if last else [shape(rows, wide // 2)] * 2
+        result = call(functools.partial(halve_kernel, left), outs)(kept, got)
+        kept, give = (result, None) if last else result
+        left //= 2
+    return kept
 
 
 def gather_pieces(piece):
@@ -288,13 +314,17 @@
     whole_out = call(order, shape(n * heads_width, model))(out_weight, rest)
     mixed = call(attend_kernel, shape(rows, heads_width), limit=16)(queries, *pieces)
     mixes = spread_out(mixed, "head")
-    partial = call(functools.partial(post_kernel, n), [block] * n, limit=16)(
+    kept, give = call(functools.partial(post_kernel, n), [shape(rows, model // 2)] * 2, limit=16)(
         *mixes, *emb, whole_out, norm1_gain[None, :], norm1_bias[None, :], ffn_in, ffn_out
     )
-    got = hand_out(partial, "head")
-    flipped, stats = call(functools.partial(stats_kernel, n), [shape(width, rows), shape(2, rows)])(*got)
-    return call(functools.partial(final_kernel, n), shape(width, rows))(
-        flipped, *spread_out(stats, "head"), norm2_gain.reshape(n, 1, width), norm2_bias.reshape(n, 1, width)
+    kept = halving(kept, give, n)
+    got = send(kept, "head", n // 2)
+    flipped, stats = call(stats_kernel, [shape(width, rows), shape(2, rows)])(kept, got)
+    every = [stats]
+    for bit in bits_below(n // 2):
+        every += [send(each, "head", bit) for each in every]
+    return call(functools.partial(final_kernel, 2 * width), shape(width, rows))(
+        flipped, *every, norm2_gain.reshape(n, 1, width), norm2_bias.reshape(n, 1, width)
     )
 
 

time: 73 us -> 74.5 us (1.021)
  waiting for transfers between devices: 28.6 us -> 39 us
  starting transfers between devices: 33.3 us -> 24.9 us
    ppermute x27 -> x24, waiting for transfers between devices: 28.6 us -> 39 us  [send(): return lax.ppermute(x, axis, [(i, i ^ offset) for i in range(size)])]
    ppermute x27 -> x24, starting transfers between devices: 33.3 us -> 24.9 us  [send(): return lax.ppermute(x, axis, [(i, i ^ offset) for i in range(size)])]
    pallas_call x3 -> x4, Pallas kernels: 2.27 us -> 2.32 us  [the longest x1 1.29 us: on_device(): call(functools.partial(post_kernel, n), [shape(rows, model // 2)] * 2, li...]
  transfers between devices with their start and end apart: 27 -> 24, of which waited for: 17 -> 16; matrix products, arithmetic and copies ran while one was open for 0% -> 0% of each run, Pallas kernels for 9% -> 8%
where the time goes in v4:
time: 74.5 us; the launch traced here: 74.3 us
  waiting for transfers between devices  39 us (52%)
  starting transfers between devices  24.9 us (33%)
  Pallas kernels  8.27 us (11%)
  local copies, waits for them, and re-layouts  1.84 us (2%)
    ppermute x24, waiting for transfers between devices, send(): return lax.ppermute(x, axis, [(i, i ^ offset) for i in range(size)])  39 us
    ppermute x24, starting transfers between devices, send(): return lax.ppermute(x, axis, [(i, i ^ offset) for i in range(size)])  24.9 us
    pallas_call x1, Pallas kernels, embed(): pl.pallas_call(functools.partial(embed_kernel, count), out_shape=[shape(r...  3.62 us
    unnamed x26, local copies, waits for them, and re-layouts  1.84 us
    pallas_call x1, Pallas kernels, on_device(): call(attend_kernel, shape(rows, heads_width), limit=16)(queries, *pieces)  1.56 us
  transfers between devices with their start and end apart: 24, of which 16 were waited for; matrix products, arithmetic and copies ran while one was open for 0% of the time, Pallas kernels for 8%

profile of v4, /device:TPU:0, one launch (start us, length us, event | category | flops | bytes accessed | tf_op | source)
XLA Modules:
  0.0 74.3 jit_solution(11725495177532153665)
XLA Ops:
  0.0 0.9 %copy-done.2 = f32[128,512]{1,0:T(8,128)S(1)} copy-done((f32[128,512]{1,0:T(8,128)S(1)}, f32[128,512]{1,0:T(8,128)}, u32[]{:S(2)}) %copy-start.2) | copy-done | bytes 262168
  1.0 5.1 %collective-permute-start.18 = (f32[32,512]{1,0:T(8,128)S(1)}, f32[32,512]{1,0:T(8,128)S(1)}, u32[]{:S(2)}, u32[]{:S(2)}) collective-permute-start(f32[32,512]{1,0:T(8,128)S(1)} %shard_map.132), channel_id=1, source_target_pairs={{0,3},{1,2},{2,1},{3,0},{4,7},{5,6},{6,5},{7,4},{8,11},{9,10},{10,... | collective-permute-start | bytes 196616 | tf_op jit(solution)/shard_map/ppermute | solution.py:252
  6.1 0.6 collective-permute-start.16
  6.8 1.8 %collective-permute-done.18 = f32[32,512]{1,0:T(8,128)S(1)} collective-permute-done((f32[32,512]{1,0:T(8,128)S(1)}, f32[32,512]{1,0:T(8,128)S(1)}, u32[]{:S(2)}, u32[]{:S(2)}) %collective-permute-start.18) | collective-permute-done | bytes 65568 | tf_op jit(solution)/shard_map/ppermute | solution.py:252
  8.6 3.1 %collective-permute-done.17 = f32[32,512]{1,0:T(8,128)S(1)} collective-permute-done((f32[32,512]{1,0:T(8,128)S(1)}, f32[32,512]{1,0:T(8,128)S(1)}, u32[]{:S(2)}, u32[]{:S(2)}) %collective-permute-start.17) | collective-permute-done | bytes 65568 | tf_op jit(solution)/shard_map/ppermute | solution.py:252
  11.8 1.6 %collective-permute-start.19 = (f32[1,3,32,512]{3,2,1,0:T(8,128)S(1)}, f32[1,3,32,512]{3,2,1,0:T(8,128)S(1)}, u32[]{:S(2)}, u32[]{:S(2)}) collective-permute-start(f32[1,3,32,512]{3,2,1,0:T(8,128)S(1)} %maximum_bitcast_fusion), channel_id=1, source_target_pairs={{0,16},{4,20},{8,24},{12,28},{16,0},{20,4},{24,8},{28,12},{1,17},{... | collective-permute-start | bytes 589832 | tf_op jit(solution)/shard_map/ppermute | solution.py:252
  13.4 3.6 %embed.1 = (f32[128,128]{1,0:T(8,128)}, f32[128,128]{1,0:T(8,128)}, f32[128,128]{1,0:T(8,128)}, f32[128,128]{1,0:T(8,128)}) custom-call(f32[128,2048]{1,0:T(8,128)} %x_hbm.1, f32[2048,512]{1,0:T(8,128)} %w_hbm.1), custom_call_target="tpu_custom_call" | custom-call | flops 805306368 | bytes 5242880 | tf_op jit(solution)/shard_map/embed/pallas_call | solution.py:104
  17.0 0.0 copy-start.1
  17.0 1.1 %collective-permute-start = (f32[128,128]{1,0:T(8,128)}, f32[128,128]{1,0:T(8,128)S(1)}, u32[]{:S(2)}, u32[]{:S(2)}) collective-permute-start(f32[128,128]{1,0:T(8,128)} %get-tuple-element.14), channel_id=1, source_target_pairs={{0,1},{1,0},{2,3},{3,2},{4,5},{5,4},{6,7},{7,6},{8,9},{9,8},{10,11... | collective-permute-start | bytes 196616 | tf_op jit(solution)/shard_map/ppermute | solution.py:252
  18.2 2.2 %collective-permute-start.1 = (f32[128,128]{1,0:T(8,128)}, f32[128,128]{1,0:T(8,128)S(1)}, u32[]{:S(2)}, u32[]{:S(2)}) collective-permute-start(f32[128,128]{1,0:T(8,128)} %get-tuple-element.15), channel_id=1, source_target_pairs={{0,2},{1,3},{2,0},{3,1},{4,6},{5,7},{6,4},{7,5},{8,10},{9,11},{10,... | collective-permute-start | bytes 196616 | tf_op jit(solution)/shard_map/ppermute | solution.py:252
  20.4 1.1 %collective-permute-start.2 = (f32[128,128]{1,0:T(8,128)}, f32[128,128]{1,0:T(8,128)S(1)}, u32[]{:S(2)}, u32[]{:S(2)}) collective-permute-start(f32[128,128]{1,0:T(8,128)} %get-tuple-element.16), channel_id=1, source_target_pairs={{0,3},{1,2},{2,1},{3,0},{4,7},{5,6},{6,5},{7,4},{8,11},{9,10},{10,... | collective-permute-start | bytes 196616 | tf_op jit(solution)/shard_map/ppermute | solution.py:252
  21.5 0.1 collective-permute-start.20
  21.6 0.0 copy-start.7
  21.6 0.8 %copy-done.7 = f32[128,128]{1,0:T(8,128)S(1)} copy-done((f32[128,128]{1,0:T(8,128)S(1)}, f32[128,128]{1,0:T(8,128)}, u32[]{:S(2)}) %copy-start.7) | copy-done | bytes 65560
  22.5 2.4 %collective-permute-done.1.refs_2_ = f32[128,128]{1,0:T(8,128)S(1)} collective-permute-done((f32[128,128]{1,0:T(8,128)}, f32[128,128]{1,0:T(8,128)S(1)}, u32[]{:S(2)}, u32[]{:S(2)}) %collective-permute-start.1) | collective-permute-done | bytes 65568 | tf_op jit(solution)/shard_map/ppermute | solution.py:252
  24.9 1.9 %collective-permute-done.2.refs_3_ = f32[128,128]{1,0:T(8,128)S(1)} collective-permute-done((f32[128,128]{1,0:T(8,128)}, f32[128,128]{1,0:T(8,128)S(1)}, u32[]{:S(2)}, u32[]{:S(2)}) %collective-permute-start.2) | collective-permute-done | bytes 65568 | tf_op jit(solution)/shard_map/ppermute | solution.py:252
  26.8 1.1 %collective-permute-start.5 = (f32[128,128]{1,0:T(8,128)S(1)}, f32[128,128]{1,0:T(8,128)S(1)}, u32[]{:S(2)}, u32[]{:S(2)}) collective-permute-start(f32[128,128]{1,0:T(8,128)S(1)} %shard_map.128.refs_0_.refs_4_), channel_id=1, source_target_pairs={{0,3},{1,2},{2,1},{3,0},{4,7},{5,6},{6,5},{7,4},{8,11},{9,10},{10,... | collective-permute-start | bytes 196616 | tf_op jit(solution)/shard_map/ppermute | solution.py:252
  27.8 0.3 collective-permute-start.4
  28.1 3.1 %collective-permute-start.3 = (f32[128,128]{1,0:T(8,128)S(1)}, f32[128,128]{1,0:T(8,128)S(1)}, u32[]{:S(2)}, u32[]{:S(2)}) collective-permute-start(f32[128,128]{1,0:T(8,128)S(1)} %shard_map.128.refs_0_.refs_4_), channel_id=1, source_target_pairs={{0,1},{1,0},{2,3},{3,2},{4,5},{5,4},{6,7},{7,6},{8,9},{9,8},{10,11... | collective-permute-start | bytes 196616 | tf_op jit(solution)/shard_map/ppermute | solution.py:252
  31.2 1.8 %collective-permute-done.5.refs_3_.refs_7_ = f32[128,128]{1,0:T(8,128)S(1)} collective-permute-done((f32[128,128]{1,0:T(8,128)S(1)}, f32[128,128]{1,0:T(8,128)S(1)}, u32[]{:S(2)}, u32[]{:S(2)}) %collective-permute-start.5) | collective-permute-done | bytes 65568 | tf_op jit(solution)/shard_map/ppermute | solution.py:252
  33.0 1.3 %collective-permute-done.4.refs_2_.refs_6_ = f32[128,128]{1,0:T(8,128)S(1)} collective-permute-done((f32[128,128]{1,0:T(8,128)S(1)}, f32[128,128]{1,0:T(8,128)S(1)}, u32[]{:S(2)}, u32[]{:S(2)}) %collective-permute-start.4) | collective-permute-done | bytes 65568 | tf_op jit(solution)/shard_map/ppermute | solution.py:252
  34.3 0.4 shard_map.130.refs_0_
  34.7 1.5 %collective-permute-start.8 = (f32[128,256]{1,0:T(8,128)S(1)}, f32[128,256]{1,0:T(8,128)S(1)}, u32[]{:S(2)}, u32[]{:S(2)}) collective-permute-start(f32[128,256]{1,0:T(8,128)S(1)} %shard_map.130.refs_0_), channel_id=1, source_target_pairs={{0,24},{4,28},{8,16},{12,20},{16,8},{20,12},{24,0},{28,4},{1,25},{... | collective-permute-start | bytes 393224 | tf_op jit(solution)/shard_map/ppermute | solution.py:252
  36.2 1.5 %collective-permute-start.7 = (f32[128,256]{1,0:T(8,128)S(1)}, f32[128,256]{1,0:T(8,128)S(1)}, u32[]{:S(2)}, u32[]{:S(2)}) collective-permute-start(f32[128,256]{1,0:T(8,128)S(1)} %shard_map.130.refs_0_), channel_id=1, source_target_pairs={{0,16},{4,20},{8,24},{12,28},{16,0},{20,4},{24,8},{28,12},{1,17},{... | collective-permute-start | bytes 393224 | tf_op jit(solution)/shard_map/ppermute | solution.py:252
  37.7 0.5 collective-permute-start.6
  38.2 2.5 %collective-permute-done.8.refs_3_ = f32[128,256]{1,0:T(8,128)S(1)} collective-permute-done((f32[128,256]{1,0:T(8,128)S(1)}, f32[128,256]{1,0:T(8,128)S(1)}, u32[]{:S(2)}, u32[]{:S(2)}) %collective-permute-start.8) | collective-permute-done | bytes 131104 | tf_op jit(solution)/shard_map/ppermute | solution.py:252
  40.7 1.3 %collective-permute-done.7.refs_2_ = f32[128,256]{1,0:T(8,128)S(1)} collective-permute-done((f32[128,256]{1,0:T(8,128)S(1)}, f32[128,256]{1,0:T(8,128)S(1)}, u32[]{:S(2)}, u32[]{:S(2)}) %collective-permute-start.7) | collective-permute-done | bytes 131104 | tf_op jit(solution)/shard_map/ppermute | solution.py:252
  42.0 0.6 collective-permute-done.6.refs_1_
  42.7 0.3 shard_map.129.q_ref
  43.0 0.4 collective-permute-done.11.refs_6_
  43.4 0.7 collective-permute-done.10.refs_5_
  44.0 1.6 %shard_map.131.refs_0_ = f32[128,128]{1,0:T(8,128)S(1)} custom-call(f32[128,128]{1,0:T(8,128)S(1)} %shard_map.129.q_ref, f32[128,256]{1,0:T(8,128)S(1)} %shard_map.130.refs_0_, f32[128,256]{1,0:T(8,128)S(1)} %collective-permute-done.6.refs_1_, f32[128,256]{1,0:T(8,128)S(1)} %collective-permute-done.7.refs_2_, f32[128,256]{1,0:T(8,128)S(1)} %collective-permute-done.8.refs_3_, ...), custom_call_target="tpu_custom_call" | custom-call | tf_op jit(solution)/shard_map/pallas_call | solution.py:315
  45.6 1.7 %collective-permute-start.15 = (f32[128,128]{1,0:T(8,128)S(1)}, f32[128,128]{1,0:T(8,128)S(1)}, u32[]{:S(2)}, u32[]{:S(2)}) collective-permute-start(f32[128,128]{1,0:T(8,128)S(1)} %shard_map.131.refs_0_), channel_id=1, source_target_pairs={{0,3},{1,2},{2,1},{3,0},{4,7},{5,6},{6,5},{7,4},{8,11},{9,10},{10,... | collective-permute-start | bytes 196616 | tf_op jit(solution)/shard_map/ppermute | solution.py:252
  47.3 1.0 %collective-permute-start.14 = (f32[128,128]{1,0:T(8,128)S(1)}, f32[128,128]{1,0:T(8,128)S(1)}, u32[]{:S(2)}, u32[]{:S(2)}) collective-permute-start(f32[128,128]{1,0:T(8,128)S(1)} %shard_map.131.refs_0_), channel_id=1, source_target_pairs={{0,2},{1,3},{2,0},{3,1},{4,6},{5,7},{6,4},{7,5},{8,10},{9,11},{10,... | collective-permute-start | bytes 196616 | tf_op jit(solution)/shard_map/ppermute | solution.py:252
  48.3 1.7 %collective-permute-start.13 = (f32[128,128]{1,0:T(8,128)S(1)}, f32[128,128]{1,0:T(8,128)S(1)}, u32[]{:S(2)}, u32[]{:S(2)}) collective-permute-start(f32[128,128]{1,0:T(8,128)S(1)} %shard_map.131.refs_0_), channel_id=1, source_target_pairs={{0,1},{1,0},{2,3},{3,2},{4,5},{5,4},{6,7},{7,6},{8,9},{9,8},{10,11... | collective-permute-start | bytes 196616 | tf_op jit(solution)/shard_map/ppermute | solution.py:252
  50.1 0.1 pad_maximum_fusion.rest_ref
  50.1 0.1 shard_map.133.refs_8_
  50.2 2.3 %collective-permute-done.15.refs_3_ = f32[128,128]{1,0:T(8,128)S(1)} collective-permute-done((f32[128,128]{1,0:T(8,128)S(1)}, f32[128,128]{1,0:T(8,128)S(1)}, u32[]{:S(2)}, u32[]{:S(2)}) %collective-permute-start.15) | collective-permute-done | bytes 65568 | tf_op jit(solution)/shard_map/ppermute | solution.py:252
  52.5 2.3 %collective-permute-done.14.refs_2_ = f32[128,128]{1,0:T(8,128)S(1)} collective-permute-done((f32[128,128]{1,0:T(8,128)S(1)}, f32[128,128]{1,0:T(8,128)S(1)}, u32[]{:S(2)}, u32[]{:S(2)}) %collective-permute-start.14) | collective-permute-done | bytes 65568 | tf_op jit(solution)/shard_map/ppermute | solution.py:252
  54.8 1.3 %shard_map.134 = (f32[128,256]{1,0:T(8,128)S(1)}, f32[128,256]{1,0:T(8,128)S(1)}) custom-call(f32[128,128]{1,0:T(8,128)S(1)} %shard_map.131.refs_0_, f32[128,128]{1,0:T(8,128)S(1)} %collective-permute-done.13.refs_1_, f32[128,128]{1,0:T(8,128)S(1)} %collective-permute-done.14.refs_2_, f32[128,128]{1,0:T(8,128)S(1)} %collective-permute-done.15.refs_3_, ...), custom_call_target="tpu_custom_call" | custom-call | tf_op jit(solution)/shard_map/pallas_call | solution.py:317
  56.1 0.1 collective-permute-start.21
  56.2 5.2 %collective-permute-done.21.got = f32[128,256]{1,0:T(8,128)S(1)} collective-permute-done((f32[128,256]{1,0:T(8,128)S(1)}, f32[128,256]{1,0:T(8,128)S(1)}, u32[]{:S(2)}, u32[]{:S(2)}) %collective-permute-start.21) | collective-permute-done | bytes 131104 | tf_op jit(solution)/shard_map/ppermute | solution.py:252
  61.4 0.4 collective-permute-start.22
  61.8 7.8 %collective-permute-done.22.got = f32[128,256]{1,0:T(8,128)S(1)} collective-permute-done((f32[128,256]{1,0:T(8,128)S(1)}, f32[128,256]{1,0:T(8,128)S(1)}, u32[]{:S(2)}, u32[]{:S(2)}) %collective-permute-start.22) | collective-permute-done | bytes 131104 | tf_op jit(solution)/shard_map/ppermute | solution.py:252
  69.6 0.2 shard_map.136
  69.8 0.1 collective-permute-start.23
  69.9 3.6 %collective-permute-done.23.refs_1_ = f32[2,128]{1,0:T(2,128)S(1)} collective-permute-done((f32[2,128]{1,0:T(2,128)S(1)}, f32[2,128]{1,0:T(2,128)S(1)}, u32[]{:S(2)}, u32[]{:S(2)}) %collective-permute-start.23) | collective-permute-done | bytes 1056 | tf_op jit(solution)/shard_map/ppermute | solution.py:252
  73.4 0.8 %shard_map.137 = f32[128,128]{1,0:T(8,128)} custom-call(f32[128,128]{1,0:T(8,128)S(1)} %get-tuple-element.19.x_ref, f32[2,128]{1,0:T(2,128)S(1)} %get-tuple-element.20.refs_0_, f32[2,128]{1,0:T(2,128)S(1)} %collective-permute-done.23.refs_1_, f32[4,1,128]{2,1,0:T(1,128)S(1)} %bitcast.13, f32[4,1,128]{2,1,0:T(1,128)S(1)} %bitcast.14), custom_call_target="tpu_custom_call" | custom-call | tf_op jit(solution)/shard_map/pallas_call | solution.py:326
  (41 shorter events, 0.2 us)
Async XLA Ops:
  0.0 0.9 %copy-start.2 = (f32[128,512]{1,0:T(8,128)S(1)}, f32[128,512]{1,0:T(8,128)}, u32[]{:S(2)}) copy-start(f32[128,512]{1,0:T(8,128)} %own_ref.1) | copy-start | bytes 786436
  1.0 20.6 %copy-start.8 = (f32[512]{0:T(512)S(1)}, f32[512]{0:T(512)}, u32[]{:S(2)}) copy-start(f32[512]{0:T(512)} %param.15) | copy-start | bytes 6148
  1.0 33.3 %copy-start.4 = (f32[512,128]{1,0:T(8,128)S(1)}, f32[512,128]{1,0:T(8,128)}, u32[]{:S(2)}) copy-start(f32[512,128]{1,0:T(8,128)} %refs_4_.3) | copy-start | bytes 786436
  1.0 33.3 %copy-start.5 = (f32[512,128]{1,0:T(8,128)S(1)}, f32[512,128]{1,0:T(8,128)}, u32[]{:S(2)}) copy-start(f32[512,128]{1,0:T(8,128)} %refs_5_.1) | copy-start | bytes 786436
  1.0 41.7 %copy-start.6 = (f32[512,128]{1,0:T(8,128)S(1)}, f32[512,128]{1,0:T(8,128)}, u32[]{:S(2)}) copy-start(f32[512,128]{1,0:T(8,128)} %refs_4_.2) | copy-start | bytes 786436
  1.0 7.6 %collective-permute-start.18 = (f32[32,512]{1,0:T(8,128)S(1)}, f32[32,512]{1,0:T(8,128)S(1)}, u32[]{:S(2)}, u32[]{:S(2)}) collective-permute-start(f32[32,512]{1,0:T(8,128)S(1)} %shard_map.132), channel_id=1, source_target_pairs={{0,3},{1,2},{2,1},{3,0},{4,7},{5,6},{6,5},{7,4},{8,11},{9,10},{10,... | collective-permute-start | bytes 196616 | tf_op jit(solution)/shard_map/ppermute | solution.py:252
  6.1 5.6 %collective-permute-start.17 = (f32[32,512]{1,0:T(8,128)S(1)}, f32[32,512]{1,0:T(8,128)S(1)}, u32[]{:S(2)}, u32[]{:S(2)}) collective-permute-start(f32[32,512]{1,0:T(8,128)S(1)} %shard_map.132), channel_id=1, source_target_pairs={{0,2},{1,3},{2,0},{3,1},{4,6},{5,7},{6,4},{7,5},{8,10},{9,11},{10,... | collective-permute-start | bytes 196616 | tf_op jit(solution)/shard_map/ppermute | solution.py:252
  6.1 5.6 %collective-permute-start.16 = (f32[32,512]{1,0:T(8,128)S(1)}, f32[32,512]{1,0:T(8,128)S(1)}, u32[]{:S(2)}, u32[]{:S(2)}) collective-permute-start(f32[32,512]{1,0:T(8,128)S(1)} %shard_map.132), channel_id=1, source_target_pairs={{0,1},{1,0},{2,3},{3,2},{4,5},{5,4},{6,7},{7,6},{8,9},{9,8},{10,11... | collective-permute-start | bytes 196616 | tf_op jit(solution)/shard_map/ppermute | solution.py:252
  11.8 38.4 %copy-start.3 = (f32[128,512]{1,0:T(8,128)S(1)}, f32[128,512]{1,0:T(8,128)}, u32[]{:S(2)}) copy-start(f32[128,512]{1,0:T(8,128)} %own_ref.1) | copy-start | bytes 786436
  11.8 9.7 %collective-permute-start.19 = (f32[1,3,32,512]{3,2,1,0:T(8,128)S(1)}, f32[1,3,32,512]{3,2,1,0:T(8,128)S(1)}, u32[]{:S(2)}, u32[]{:S(2)}) collective-permute-start(f32[1,3,32,512]{3,2,1,0:T(8,128)S(1)} %maximum_bitcast_fusion), channel_id=1, source_target_pairs={{0,16},{4,20},{8,24},{12,28},{16,0},{20,4},{24,8},{28,12},{1,17},{... | collective-permute-start | bytes 589832 | tf_op jit(solution)/shard_map/ppermute | solution.py:252
  13.4 41.4 %copy-start.9 = (f32[512]{0:T(512)S(1)}, f32[512]{0:T(512)}, u32[]{:S(2)}) copy-start(f32[512]{0:T(512)} %param.20) | copy-start | bytes 6148
  13.4 41.4 %copy-start.10 = (f32[512]{0:T(512)S(1)}, f32[512]{0:T(512)}, u32[]{:S(2)}) copy-start(f32[512]{0:T(512)} %param.21) | copy-start | bytes 6148
  17.0 37.8 %copy-start = (f32[512,512]{1,0:T(8,128)S(1)}, f32[512,512]{1,0:T(8,128)}, u32[]{:S(2)}) copy-start(f32[512,512]{1,0:T(8,128)} %refs_11_.1) | copy-start | bytes 3145732
  17.0 37.8 %copy-start.1 = (f32[512,512]{1,0:T(8,128)S(1)}, f32[512,512]{1,0:T(8,128)}, u32[]{:S(2)}) copy-start(f32[512,512]{1,0:T(8,128)} %refs_12_.1) | copy-start | bytes 3145732
  17.0 5.4 %collective-permute-start = (f32[128,128]{1,0:T(8,128)}, f32[128,128]{1,0:T(8,128)S(1)}, u32[]{:S(2)}, u32[]{:S(2)}) collective-permute-start(f32[128,128]{1,0:T(8,128)} %get-tuple-element.14), channel_id=1, source_target_pairs={{0,1},{1,0},{2,3},{3,2},{4,5},{5,4},{6,7},{7,6},{8,9},{9,8},{10,11... | collective-permute-start | bytes 196616 | tf_op jit(solution)/shard_map/ppermute | solution.py:252
  18.2 6.7 %collective-permute-start.1 = (f32[128,128]{1,0:T(8,128)}, f32[128,128]{1,0:T(8,128)S(1)}, u32[]{:S(2)}, u32[]{:S(2)}) collective-permute-start(f32[128,128]{1,0:T(8,128)} %get-tuple-element.15), channel_id=1, source_target_pairs={{0,2},{1,3},{2,0},{3,1},{4,6},{5,7},{6,4},{7,5},{8,10},{9,11},{10,... | collective-permute-start | bytes 196616 | tf_op jit(solution)/shard_map/ppermute | solution.py:252
  20.4 6.4 %collective-permute-start.2 = (f32[128,128]{1,0:T(8,128)}, f32[128,128]{1,0:T(8,128)S(1)}, u32[]{:S(2)}, u32[]{:S(2)}) collective-permute-start(f32[128,128]{1,0:T(8,128)} %get-tuple-element.16), channel_id=1, source_target_pairs={{0,3},{1,2},{2,1},{3,0},{4,7},{5,6},{6,5},{7,4},{8,11},{9,10},{10,... | collective-permute-start | bytes 196616 | tf_op jit(solution)/shard_map/ppermute | solution.py:252
  21.5 28.6 %collective-permute-start.20 = (f32[2,3,32,512]{3,2,1,0:T(8,128)S(1)}, f32[2,3,32,512]{3,2,1,0:T(8,128)S(1)}, u32[]{:S(2)}, u32[]{:S(2)}) collective-permute-start(f32[2,3,32,512]{3,2,1,0:T(8,128)S(1)} %pad_maximum_fusion.1), channel_id=1, source_target_pairs={{0,4},{4,0},{8,12},{12,8},{16,20},{20,16},{24,28},{28,24},{1,5},{5... | collective-permute-start | bytes 1179656 | tf_op jit(solution)/shard_map/ppermute | solution.py:252
  21.6 0.8 %copy-start.7 = (f32[128,128]{1,0:T(8,128)S(1)}, f32[128,128]{1,0:T(8,128)}, u32[]{:S(2)}) copy-start(f32[128,128]{1,0:T(8,128)} %get-tuple-element.13.x_ref) | copy-start | bytes 196612
  26.8 6.2 %collective-permute-start.5 = (f32[128,128]{1,0:T(8,128)S(1)}, f32[128,128]{1,0:T(8,128)S(1)}, u32[]{:S(2)}, u32[]{:S(2)}) collective-permute-start(f32[128,128]{1,0:T(8,128)S(1)} %shard_map.128.refs_0_.refs_4_), channel_id=1, source_target_pairs={{0,3},{1,2},{2,1},{3,0},{4,7},{5,6},{6,5},{7,4},{8,11},{9,10},{10,... | collective-permute-start | bytes 196616 | tf_op jit(solution)/shard_map/ppermute | solution.py:252
  27.8 6.5 %collective-permute-start.4 = (f32[128,128]{1,0:T(8,128)S(1)}, f32[128,128]{1,0:T(8,128)S(1)}, u32[]{:S(2)}, u32[]{:S(2)}) collective-permute-start(f32[128,128]{1,0:T(8,128)S(1)} %shard_map.128.refs_0_.refs_4_), channel_id=1, source_target_pairs={{0,2},{1,3},{2,0},{3,1},{4,6},{5,7},{6,4},{7,5},{8,10},{9,11},{10,... | collective-permute-start | bytes 196616 | tf_op jit(solution)/shard_map/ppermute | solution.py:252
  28.1 6.1 %collective-permute-start.3 = (f32[128,128]{1,0:T(8,128)S(1)}, f32[128,128]{1,0:T(8,128)S(1)}, u32[]{:S(2)}, u32[]{:S(2)}) collective-permute-start(f32[128,128]{1,0:T(8,128)S(1)} %shard_map.128.refs_0_.refs_4_), channel_id=1, source_target_pairs={{0,1},{1,0},{2,3},{3,2},{4,5},{5,4},{6,7},{7,6},{8,9},{9,8},{10,11... | collective-permute-start | bytes 196616 | tf_op jit(solution)/shard_map/ppermute | solution.py:252
  34.7 6.0 %collective-permute-start.8 = (f32[128,256]{1,0:T(8,128)S(1)}, f32[128,256]{1,0:T(8,128)S(1)}, u32[]{:S(2)}, u32[]{:S(2)}) collective-permute-start(f32[128,256]{1,0:T(8,128)S(1)} %shard_map.130.refs_0_), channel_id=1, source_target_pairs={{0,24},{4,28},{8,16},{12,20},{16,8},{20,12},{24,0},{28,4},{1,25},{... | collective-permute-start | bytes 393224 | tf_op jit(solution)/shard_map/ppermute | solution.py:252
  36.2 5.8 %collective-permute-start.7 = (f32[128,256]{1,0:T(8,128)S(1)}, f32[128,256]{1,0:T(8,128)S(1)}, u32[]{:S(2)}, u32[]{:S(2)}) collective-permute-start(f32[128,256]{1,0:T(8,128)S(1)} %shard_map.130.refs_0_), channel_id=1, source_target_pairs={{0,16},{4,20},{8,24},{12,28},{16,0},{20,4},{24,8},{28,12},{1,17},{... | collective-permute-start | bytes 393224 | tf_op jit(solution)/shard_map/ppermute | solution.py:252
  37.7 5.0 %collective-permute-start.6 = (f32[128,256]{1,0:T(8,128)S(1)}, f32[128,256]{1,0:T(8,128)S(1)}, u32[]{:S(2)}, u32[]{:S(2)}) collective-permute-start(f32[128,256]{1,0:T(8,128)S(1)} %shard_map.130.refs_0_), channel_id=1, source_target_pairs={{0,8},{4,12},{8,0},{12,4},{16,24},{20,28},{24,16},{28,20},{1,9},{5... | collective-permute-start | bytes 393224 | tf_op jit(solution)/shard_map/ppermute | solution.py:252
  38.2 4.7 %collective-permute-start.9 = (f32[128,256]{1,0:T(8,128)S(1)}, f32[128,256]{1,0:T(8,128)S(1)}, u32[]{:S(2)}, u32[]{:S(2)}) collective-permute-start(f32[128,256]{1,0:T(8,128)S(1)} %shard_map.130.refs_0_), channel_id=1, source_target_pairs={{0,4},{4,0},{8,12},{12,8},{16,20},{20,16},{24,28},{28,24},{1,5},{5... | collective-permute-start | bytes 393224 | tf_op jit(solution)/shard_map/ppermute | solution.py:252
  40.7 2.3 %collective-permute-start.12 = (f32[128,256]{1,0:T(8,128)S(1)}, f32[128,256]{1,0:T(8,128)S(1)}, u32[]{:S(2)}, u32[]{:S(2)}) collective-permute-start(f32[128,256]{1,0:T(8,128)S(1)} %collective-permute-done.8.refs_3_), channel_id=1, source_target_pairs={{0,4},{4,0},{8,12},{12,8},{16,20},{20,16},{24,28},{28,24},{1,5},{5... | collective-permute-start | bytes 393224 | tf_op jit(solution)/shard_map/ppermute | solution.py:252
  42.0 1.3 %collective-permute-start.11 = (f32[128,256]{1,0:T(8,128)S(1)}, f32[128,256]{1,0:T(8,128)S(1)}, u32[]{:S(2)}, u32[]{:S(2)}) collective-permute-start(f32[128,256]{1,0:T(8,128)S(1)} %collective-permute-done.7.refs_2_), channel_id=1, source_target_pairs={{0,4},{4,0},{8,12},{12,8},{16,20},{20,16},{24,28},{28,24},{1,5},{5... | collective-permute-start | bytes 393224 | tf_op jit(solution)/shard_map/ppermute | solution.py:252
  42.7 1.3 %collective-permute-start.10 = (f32[128,256]{1,0:T(8,128)S(1)}, f32[128,256]{1,0:T(8,128)S(1)}, u32[]{:S(2)}, u32[]{:S(2)}) collective-permute-start(f32[128,256]{1,0:T(8,128)S(1)} %collective-permute-done.6.refs_1_), channel_id=1, source_target_pairs={{0,4},{4,0},{8,12},{12,8},{16,20},{20,16},{24,28},{28,24},{1,5},{5... | collective-permute-start | bytes 393224 | tf_op jit(solution)/shard_map/ppermute | solution.py:252
  45.6 27.8 %copy-start.11 = (f32[512]{0:T(512)S(1)}, f32[512]{0:T(512)}, u32[]{:S(2)}) copy-start(f32[512]{0:T(512)} %param.24) | copy-start | bytes 6148
  45.6 27.8 %copy-start.12 = (f32[512]{0:T(512)S(1)}, f32[512]{0:T(512)}, u32[]{:S(2)}) copy-start(f32[512]{0:T(512)} %param.25) | copy-start | bytes 6148
  45.6 6.9 %collective-permute-start.15 = (f32[128,128]{1,0:T(8,128)S(1)}, f32[128,128]{1,0:T(8,128)S(1)}, u32[]{:S(2)}, u32[]{:S(2)}) collective-permute-start(f32[128,128]{1,0:T(8,128)S(1)} %shard_map.131.refs_0_), channel_id=1, source_target_pairs={{0,3},{1,2},{2,1},{3,0},{4,7},{5,6},{6,5},{7,4},{8,11},{9,10},{10,... | collective-permute-start | bytes 196616 | tf_op jit(solution)/shard_map/ppermute | solution.py:252
  47.3 7.4 %collective-permute-start.14 = (f32[128,128]{1,0:T(8,128)S(1)}, f32[128,128]{1,0:T(8,128)S(1)}, u32[]{:S(2)}, u32[]{:S(2)}) collective-permute-start(f32[128,128]{1,0:T(8,128)S(1)} %shard_map.131.refs_0_), channel_id=1, source_target_pairs={{0,2},{1,3},{2,0},{3,1},{4,6},{5,7},{6,4},{7,5},{8,10},{9,11},{10,... | collective-permute-start | bytes 196616 | tf_op jit(solution)/shard_map/ppermute | solution.py:252
  48.3 6.5 %collective-permute-start.13 = (f32[128,128]{1,0:T(8,128)S(1)}, f32[128,128]{1,0:T(8,128)S(1)}, u32[]{:S(2)}, u32[]{:S(2)}) collective-permute-start(f32[128,128]{1,0:T(8,128)S(1)} %shard_map.131.refs_0_), channel_id=1, source_target_pairs={{0,1},{1,0},{2,3},{3,2},{4,5},{5,4},{6,7},{7,6},{8,9},{9,8},{10,11... | collective-permute-start | bytes 196616 | tf_op jit(solution)/shard_map/ppermute | solution.py:252
  56.1 5.3 %collective-permute-start.21 = (f32[128,256]{1,0:T(8,128)S(1)}, f32[128,256]{1,0:T(8,128)S(1)}, u32[]{:S(2)}, u32[]{:S(2)}) collective-permute-start(f32[128,256]{1,0:T(8,128)S(1)} %get-tuple-element.18), channel_id=1, source_target_pairs={{0,1},{1,0},{2,3},{3,2},{4,5},{5,4},{6,7},{7,6},{8,9},{9,8},{10,11... | collective-permute-start | bytes 393224 | tf_op jit(solution)/shard_map/ppermute | solution.py:252
  61.4 8.2 %collective-permute-start.22 = (f32[128,256]{1,0:T(8,128)S(1)}, f32[128,256]{1,0:T(8,128)S(1)}, u32[]{:S(2)}, u32[]{:S(2)}) collective-permute-start(f32[128,256]{1,0:T(8,128)S(1)} %shard_map.135.kept), channel_id=1, source_target_pairs={{0,2},{1,3},{2,0},{3,1},{4,6},{5,7},{6,4},{7,5},{8,10},{9,11},{10,... | collective-permute-start | bytes 393224 | tf_op jit(solution)/shard_map/ppermute | solution.py:252
  69.8 3.6 %collective-permute-start.23 = (f32[2,128]{1,0:T(2,128)S(1)}, f32[2,128]{1,0:T(2,128)S(1)}, u32[]{:S(2)}, u32[]{:S(2)}) collective-permute-start(f32[2,128]{1,0:T(2,128)S(1)} %get-tuple-element.20.refs_0_), channel_id=1, source_target_pairs={{0,1},{1,0},{2,3},{3,2},{4,5},{5,4},{6,7},{7,6},{8,9},{9,8},{10,11... | collective-permute-start | bytes 3080 | tf_op jit(solution)/shard_map/ppermute | solution.py:252

commit v5 on v3

--- a/solution.py
+++ b/solution.py
@@ -97,7 +97,7 @@
 def embed(count, series, emb_weight):
     rows, depth = series.shape
     model = emb_weight.shape[1]
-    step = math.gcd(depth, 256)
+    step = math.gcd(depth, 512)
     steps = depth // step
     halves = 2 if steps % 2 == 0 else 1
     hbm = pl.BlockSpec(memory_space=pltpu.HBM)
@@ -251,6 +251,10 @@
     return [parts[0]] + [send(parts[k], axis, k) for k in range(1, lax.axis_size(axis))]
 
 
+def bits_below(count):
+    return [1 << at for at in range(count.bit_length() - 1)]
+
+
 def gather_pieces(piece):
     size = lax.axis_size("var")
     if size > 8:
@@ -276,7 +280,10 @@
     got = hand_out(parts, "head")
     got[0] = call(bias_kernel, block)(parts[0], emb_bias.reshape(n, 1, width))
     cut = call(functools.partial(cut_kernel, bits), shape(heads_width >> len(bits), model))(out_weight)
-    rest = jnp.stack(spread_out(cut, "head")[1:])[None]
+    have = cut[None]
+    for bit in bits_below(n):
+        have = jnp.concatenate([have, send(have, "head", bit)], 0)
+    rest = have[None, 1:]
     mine = call(add_kernel, block)(*got)
     emb = spread_out(mine, "head")
     for bit in bits:

time: 73 us -> 76.1 us (1.042)
  waiting for transfers between devices: 28.6 us -> 31.7 us
    ppermute x27 -> x26, waiting for transfers between devices: 28.6 us -> 31.7 us  [send(): return lax.ppermute(x, axis, [(i, i ^ offset) for i in range(size)])]
    ppermute x27 -> x26, starting transfers between devices: 33.3 us -> 33.7 us  [send(): return lax.ppermute(x, axis, [(i, i ^ offset) for i in range(size)])]
  transfers between devices with their start and end apart: 27 -> 26, of which waited for: 17 -> 17; matrix products, arithmetic and copies ran while one was open for 0% -> 0% of each run, Pallas kernels for 9% -> 8%
where the time goes in v5:
time: 76.1 us; the launch traced here: 75.9 us
  starting transfers between devices  33.7 us (44%)
  waiting for transfers between devices  31.7 us (42%)
  Pallas kernels  8.22 us (11%)
  local copies, waits for them, and re-layouts  1.84 us (2%)
    ppermute x26, starting transfers between devices, send(): return lax.ppermute(x, axis, [(i, i ^ offset) for i in range(size)])  33.7 us
    ppermute x26, waiting for transfers between devices, send(): return lax.ppermute(x, axis, [(i, i ^ offset) for i in range(size)])  31.7 us
    pallas_call x1, Pallas kernels, embed(): pl.pallas_call(functools.partial(embed_kernel, count), out_shape=[shape(r...  3.63 us
    unnamed x26, local copies, waits for them, and re-layouts  1.84 us
    pallas_call x1, Pallas kernels, on_device(): call(attend_kernel, shape(rows, heads_width), limit=16)(queries, *pieces)  1.56 us
  transfers between devices with their start and end apart: 26, of which 17 were waited for; matrix products, arithmetic and copies ran while one was open for 0% of the time, Pallas kernels for 8%

profile of v5, /device:TPU:0, one launch (start us, length us, event | category | flops | bytes accessed | tf_op | source)
XLA Modules:
  0.0 75.9 jit_solution(6749164872785647309)
XLA Ops:
  0.0 0.9 %copy-done.2 = f32[128,512]{1,0:T(8,128)S(1)} copy-done((f32[128,512]{1,0:T(8,128)S(1)}, f32[128,512]{1,0:T(8,128)}, u32[]{:S(2)}) %copy-start.2) | copy-done | bytes 262168
  1.0 3.1 %collective-permute-start.16 = (f32[1,32,512]{2,1,0:T(8,128)S(1)}, f32[1,32,512]{2,1,0:T(8,128)S(1)}, u32[]{:S(2)}, u32[]{:S(2)}) collective-permute-start(f32[1,32,512]{2,1,0:T(8,128)S(1)} %bitcast.8), channel_id=1, source_target_pairs={{0,1},{1,0},{2,3},{3,2},{4,5},{5,4},{6,7},{7,6},{8,9},{9,8},{10,11... | collective-permute-start | bytes 196616 | tf_op jit(solution)/shard_map/ppermute | solution.py:243
  4.1 2.2 %collective-permute-done.16 = f32[1,32,512]{2,1,0:T(8,128)S(1)} collective-permute-done((f32[1,32,512]{2,1,0:T(8,128)S(1)}, f32[1,32,512]{2,1,0:T(8,128)S(1)}, u32[]{:S(2)}, u32[]{:S(2)}) %collective-permute-start.16) | collective-permute-done | bytes 65568 | tf_op jit(solution)/shard_map/ppermute | solution.py:243
  6.4 3.1 %collective-permute-start.17 = (f32[2,32,512]{2,1,0:T(8,128)S(1)}, f32[2,32,512]{2,1,0:T(8,128)S(1)}, u32[]{:S(2)}, u32[]{:S(2)}) collective-permute-start(f32[2,32,512]{2,1,0:T(8,128)S(1)} %pad_maximum_fusion.2), channel_id=1, source_target_pairs={{0,2},{1,3},{2,0},{3,1},{4,6},{5,7},{6,4},{7,5},{8,10},{9,11},{10,... | collective-permute-start | bytes 393224 | tf_op jit(solution)/shard_map/ppermute | solution.py:243
  9.5 5.2 %collective-permute-done.17 = f32[2,32,512]{2,1,0:T(8,128)S(1)} collective-permute-done((f32[2,32,512]{2,1,0:T(8,128)S(1)}, f32[2,32,512]{2,1,0:T(8,128)S(1)}, u32[]{:S(2)}, u32[]{:S(2)}) %collective-permute-start.17) | collective-permute-done | bytes 131104 | tf_op jit(solution)/shard_map/ppermute | solution.py:243
  14.7 1.6 %collective-permute-start.18 = (f32[1,3,32,512]{3,2,1,0:T(8,128)S(1)}, f32[1,3,32,512]{3,2,1,0:T(8,128)S(1)}, u32[]{:S(2)}, u32[]{:S(2)}) collective-permute-start(f32[1,3,32,512]{3,2,1,0:T(8,128)S(1)} %maximum_bitcast_fusion), channel_id=1, source_target_pairs={{0,16},{4,20},{8,24},{12,28},{16,0},{20,4},{24,8},{28,12},{1,17},{... | collective-permute-start | bytes 589832 | tf_op jit(solution)/shard_map/ppermute | solution.py:243
  16.3 3.6 %embed.1 = (f32[128,128]{1,0:T(8,128)}, f32[128,128]{1,0:T(8,128)}, f32[128,128]{1,0:T(8,128)}, f32[128,128]{1,0:T(8,128)}) custom-call(f32[128,2048]{1,0:T(8,128)} %x_hbm.1, f32[2048,512]{1,0:T(8,128)} %w_hbm.1), custom_call_target="tpu_custom_call" | custom-call | flops 805306368 | bytes 5242880 | tf_op jit(solution)/shard_map/embed/pallas_call | solution.py:104
  19.9 0.7 collective-permute-start
  20.7 3.4 %collective-permute-start.1 = (f32[128,128]{1,0:T(8,128)}, f32[128,128]{1,0:T(8,128)S(1)}, u32[]{:S(2)}, u32[]{:S(2)}) collective-permute-start(f32[128,128]{1,0:T(8,128)} %get-tuple-element.17), channel_id=1, source_target_pairs={{0,2},{1,3},{2,0},{3,1},{4,6},{5,7},{6,4},{7,5},{8,10},{9,11},{10,... | collective-permute-start | bytes 196616 | tf_op jit(solution)/shard_map/ppermute | solution.py:243
  24.1 0.3 collective-permute-start.2
  24.4 0.1 collective-permute-start.19
  24.5 0.8 %copy-done.7 = f32[128,128]{1,0:T(8,128)S(1)} copy-done((f32[128,128]{1,0:T(8,128)S(1)}, f32[128,128]{1,0:T(8,128)}, u32[]{:S(2)}) %copy-start.7) | copy-done | bytes 65560
  25.4 2.5 %collective-permute-done.1.refs_2_ = f32[128,128]{1,0:T(8,128)S(1)} collective-permute-done((f32[128,128]{1,0:T(8,128)}, f32[128,128]{1,0:T(8,128)S(1)}, u32[]{:S(2)}, u32[]{:S(2)}) %collective-permute-start.1) | collective-permute-done | bytes 65568 | tf_op jit(solution)/shard_map/ppermute | solution.py:243
  27.9 2.5 %collective-permute-done.2.refs_3_ = f32[128,128]{1,0:T(8,128)S(1)} collective-permute-done((f32[128,128]{1,0:T(8,128)}, f32[128,128]{1,0:T(8,128)S(1)}, u32[]{:S(2)}, u32[]{:S(2)}) %collective-permute-start.2) | collective-permute-done | bytes 65568 | tf_op jit(solution)/shard_map/ppermute | solution.py:243
  30.4 0.8 %collective-permute-start.5 = (f32[128,128]{1,0:T(8,128)S(1)}, f32[128,128]{1,0:T(8,128)S(1)}, u32[]{:S(2)}, u32[]{:S(2)}) collective-permute-start(f32[128,128]{1,0:T(8,128)S(1)} %shard_map.128.refs_0_.refs_4_), channel_id=1, source_target_pairs={{0,3},{1,2},{2,1},{3,0},{4,7},{5,6},{6,5},{7,4},{8,11},{9,10},{10,... | collective-permute-start | bytes 196616 | tf_op jit(solution)/shard_map/ppermute | solution.py:243
  31.2 3.6 %collective-permute-start.3 = (f32[128,128]{1,0:T(8,128)S(1)}, f32[128,128]{1,0:T(8,128)S(1)}, u32[]{:S(2)}, u32[]{:S(2)}) collective-permute-start(f32[128,128]{1,0:T(8,128)S(1)} %shard_map.128.refs_0_.refs_4_), channel_id=1, source_target_pairs={{0,1},{1,0},{2,3},{3,2},{4,5},{5,4},{6,7},{7,6},{8,9},{9,8},{10,11... | collective-permute-start | bytes 196616 | tf_op jit(solution)/shard_map/ppermute | solution.py:243
  34.9 1.8 %collective-permute-done.5.refs_3_.refs_7_ = f32[128,128]{1,0:T(8,128)S(1)} collective-permute-done((f32[128,128]{1,0:T(8,128)S(1)}, f32[128,128]{1,0:T(8,128)S(1)}, u32[]{:S(2)}, u32[]{:S(2)}) %collective-permute-start.5) | collective-permute-done | bytes 65568 | tf_op jit(solution)/shard_map/ppermute | solution.py:243
  36.7 1.1 %collective-permute-done.4.refs_2_.refs_6_ = f32[128,128]{1,0:T(8,128)S(1)} collective-permute-done((f32[128,128]{1,0:T(8,128)S(1)}, f32[128,128]{1,0:T(8,128)S(1)}, u32[]{:S(2)}, u32[]{:S(2)}) %collective-permute-start.4) | collective-permute-done | bytes 65568 | tf_op jit(solution)/shard_map/ppermute | solution.py:243
  37.8 0.4 shard_map.130.refs_0_
  38.2 1.5 %collective-permute-start.8 = (f32[128,256]{1,0:T(8,128)S(1)}, f32[128,256]{1,0:T(8,128)S(1)}, u32[]{:S(2)}, u32[]{:S(2)}) collective-permute-start(f32[128,256]{1,0:T(8,128)S(1)} %shard_map.130.refs_0_), channel_id=1, source_target_pairs={{0,24},{4,28},{8,16},{12,20},{16,8},{20,12},{24,0},{28,4},{1,25},{... | collective-permute-start | bytes 393224 | tf_op jit(solution)/shard_map/ppermute | solution.py:243
  39.7 1.5 %collective-permute-start.7 = (f32[128,256]{1,0:T(8,128)S(1)}, f32[128,256]{1,0:T(8,128)S(1)}, u32[]{:S(2)}, u32[]{:S(2)}) collective-permute-start(f32[128,256]{1,0:T(8,128)S(1)} %shard_map.130.refs_0_), channel_id=1, source_target_pairs={{0,16},{4,20},{8,24},{12,28},{16,0},{20,4},{24,8},{28,12},{1,17},{... | collective-permute-start | bytes 393224 | tf_op jit(solution)/shard_map/ppermute | solution.py:243
  41.2 0.5 collective-permute-start.6
  41.8 2.5 %collective-permute-done.8.refs_3_ = f32[128,256]{1,0:T(8,128)S(1)} collective-permute-done((f32[128,256]{1,0:T(8,128)S(1)}, f32[128,256]{1,0:T(8,128)S(1)}, u32[]{:S(2)}, u32[]{:S(2)}) %collective-permute-start.8) | collective-permute-done | bytes 131104 | tf_op jit(solution)/shard_map/ppermute | solution.py:243
  44.2 1.3 %collective-permute-done.7.refs_2_ = f32[128,256]{1,0:T(8,128)S(1)} collective-permute-done((f32[128,256]{1,0:T(8,128)S(1)}, f32[128,256]{1,0:T(8,128)S(1)}, u32[]{:S(2)}, u32[]{:S(2)}) %collective-permute-start.7) | collective-permute-done | bytes 131104 | tf_op jit(solution)/shard_map/ppermute | solution.py:243
  45.5 0.6 collective-permute-done.6.refs_1_
  46.2 0.3 shard_map.129.q_ref
  46.5 0.4 collective-permute-done.11.refs_6_
  46.9 0.6 collective-permute-done.10.refs_5_
  47.5 1.6 %shard_map.131.refs_0_ = f32[128,128]{1,0:T(8,128)S(1)} custom-call(f32[128,128]{1,0:T(8,128)S(1)} %shard_map.129.q_ref, f32[128,256]{1,0:T(8,128)S(1)} %shard_map.130.refs_0_, f32[128,256]{1,0:T(8,128)S(1)} %collective-permute-done.6.refs_1_, f32[128,256]{1,0:T(8,128)S(1)} %collective-permute-done.7.refs_2_, f32[128,256]{1,0:T(8,128)S(1)} %collective-permute-done.8.refs_3_, ...), custom_call_target="tpu_custom_call" | custom-call | tf_op jit(solution)/shard_map/pallas_call | solution.py:296
  49.1 1.7 %collective-permute-start.15 = (f32[128,128]{1,0:T(8,128)S(1)}, f32[128,128]{1,0:T(8,128)S(1)}, u32[]{:S(2)}, u32[]{:S(2)}) collective-permute-start(f32[128,128]{1,0:T(8,128)S(1)} %shard_map.131.refs_0_), channel_id=1, source_target_pairs={{0,3},{1,2},{2,1},{3,0},{4,7},{5,6},{6,5},{7,4},{8,11},{9,10},{10,... | collective-permute-start | bytes 196616 | tf_op jit(solution)/shard_map/ppermute | solution.py:243
  50.8 1.1 %collective-permute-start.14 = (f32[128,128]{1,0:T(8,128)S(1)}, f32[128,128]{1,0:T(8,128)S(1)}, u32[]{:S(2)}, u32[]{:S(2)}) collective-permute-start(f32[128,128]{1,0:T(8,128)S(1)} %shard_map.131.refs_0_), channel_id=1, source_target_pairs={{0,2},{1,3},{2,0},{3,1},{4,6},{5,7},{6,4},{7,5},{8,10},{9,11},{10,... | collective-permute-start | bytes 196616 | tf_op jit(solution)/shard_map/ppermute | solution.py:243
  51.9 1.6 %collective-permute-start.13 = (f32[128,128]{1,0:T(8,128)S(1)}, f32[128,128]{1,0:T(8,128)S(1)}, u32[]{:S(2)}, u32[]{:S(2)}) collective-permute-start(f32[128,128]{1,0:T(8,128)S(1)} %shard_map.131.refs_0_), channel_id=1, source_target_pairs={{0,1},{1,0},{2,3},{3,2},{4,5},{5,4},{6,7},{7,6},{8,9},{9,8},{10,11... | collective-permute-start | bytes 196616 | tf_op jit(solution)/shard_map/ppermute | solution.py:243
  53.6 0.1 shard_map.133.refs_8_
  53.7 2.3 %collective-permute-done.15.refs_3_ = f32[128,128]{1,0:T(8,128)S(1)} collective-permute-done((f32[128,128]{1,0:T(8,128)S(1)}, f32[128,128]{1,0:T(8,128)S(1)}, u32[]{:S(2)}, u32[]{:S(2)}) %collective-permute-start.15) | collective-permute-done | bytes 65568 | tf_op jit(solution)/shard_map/ppermute | solution.py:243
  56.0 2.4 %collective-permute-done.14.refs_2_ = f32[128,128]{1,0:T(8,128)S(1)} collective-permute-done((f32[128,128]{1,0:T(8,128)S(1)}, f32[128,128]{1,0:T(8,128)S(1)}, u32[]{:S(2)}, u32[]{:S(2)}) %collective-permute-start.14) | collective-permute-done | bytes 65568 | tf_op jit(solution)/shard_map/ppermute | solution.py:243
  58.4 1.3 %shard_map.134 = (f32[128,128]{1,0:T(8,128)S(1)}, f32[128,128]{1,0:T(8,128)S(1)}, f32[128,128]{1,0:T(8,128)S(1)}, f32[128,128]{1,0:T(8,128)S(1)}) custom-call(f32[128,128]{1,0:T(8,128)S(1)} %shard_map.131.refs_0_, f32[128,128]{1,0:T(8,128)S(1)} %collective-permute-done.13.refs_1_, f32[128,128]{1,0:T(8,128)S(1)} %collective-permute-done.14.refs_2_, ...), custom_call_target="tpu_custom_call" | custom-call | tf_op jit(solution)/shard_map/pallas_call | solution.py:298
  59.7 0.1 collective-permute-start.20
  59.8 1.9 %collective-permute-start.21 = (f32[128,128]{1,0:T(8,128)S(1)}, f32[128,128]{1,0:T(8,128)S(1)}, u32[]{:S(2)}, u32[]{:S(2)}) collective-permute-start(f32[128,128]{1,0:T(8,128)S(1)} %get-tuple-element.21), channel_id=1, source_target_pairs={{0,2},{1,3},{2,0},{3,1},{4,6},{5,7},{6,4},{7,5},{8,10},{9,11},{10,... | collective-permute-start | bytes 196616 | tf_op jit(solution)/shard_map/ppermute | solution.py:243
  61.7 2.5 %collective-permute-start.22 = (f32[128,128]{1,0:T(8,128)S(1)}, f32[128,128]{1,0:T(8,128)S(1)}, u32[]{:S(2)}, u32[]{:S(2)}) collective-permute-start(f32[128,128]{1,0:T(8,128)S(1)} %get-tuple-element.22), channel_id=1, source_target_pairs={{0,3},{1,2},{2,1},{3,0},{4,7},{5,6},{6,5},{7,4},{8,11},{9,10},{10,... | collective-permute-start | bytes 196616 | tf_op jit(solution)/shard_map/ppermute | solution.py:243
  64.2 0.3 collective-permute-done.20.refs_1_
  64.5 3.5 %collective-permute-done.21.refs_2_ = f32[128,128]{1,0:T(8,128)S(1)} collective-permute-done((f32[128,128]{1,0:T(8,128)S(1)}, f32[128,128]{1,0:T(8,128)S(1)}, u32[]{:S(2)}, u32[]{:S(2)}) %collective-permute-start.21) | collective-permute-done | bytes 65568 | tf_op jit(solution)/shard_map/ppermute | solution.py:243
  68.0 0.1 shard_map.135
  68.1 2.4 %collective-permute-start.25 = (f32[2,128]{1,0:T(2,128)S(1)}, f32[2,128]{1,0:T(2,128)S(1)}, u32[]{:S(2)}, u32[]{:S(2)}) collective-permute-start(f32[2,128]{1,0:T(2,128)S(1)} %get-tuple-element.24.refs_0_), channel_id=1, source_target_pairs={{0,3},{1,2},{2,1},{3,0},{4,7},{5,6},{6,5},{7,4},{8,11},{9,10},{10,... | collective-permute-start | bytes 3080 | tf_op jit(solution)/shard_map/ppermute | solution.py:243
  70.5 0.4 collective-permute-start.24
  70.9 1.7 %collective-permute-start.23 = (f32[2,128]{1,0:T(2,128)S(1)}, f32[2,128]{1,0:T(2,128)S(1)}, u32[]{:S(2)}, u32[]{:S(2)}) collective-permute-start(f32[2,128]{1,0:T(2,128)S(1)} %get-tuple-element.24.refs_0_), channel_id=1, source_target_pairs={{0,1},{1,0},{2,3},{3,2},{4,5},{5,4},{6,7},{7,6},{8,9},{9,8},{10,11... | collective-permute-start | bytes 3080 | tf_op jit(solution)/shard_map/ppermute | solution.py:243
  72.6 1.0 %collective-permute-done.25.refs_3_ = f32[2,128]{1,0:T(2,128)S(1)} collective-permute-done((f32[2,128]{1,0:T(2,128)S(1)}, f32[2,128]{1,0:T(2,128)S(1)}, u32[]{:S(2)}, u32[]{:S(2)}) %collective-permute-start.25) | collective-permute-done | bytes 1056 | tf_op jit(solution)/shard_map/ppermute | solution.py:243
  73.6 1.5 %collective-permute-done.24.refs_2_ = f32[2,128]{1,0:T(2,128)S(1)} collective-permute-done((f32[2,128]{1,0:T(2,128)S(1)}, f32[2,128]{1,0:T(2,128)S(1)}, u32[]{:S(2)}, u32[]{:S(2)}) %collective-permute-start.24) | collective-permute-done | bytes 1056 | tf_op jit(solution)/shard_map/ppermute | solution.py:243
  75.0 0.8 %shard_map.136 = f32[128,128]{1,0:T(8,128)} custom-call(f32[128,128]{1,0:T(8,128)S(1)} %get-tuple-element.23.x_ref, f32[2,128]{1,0:T(2,128)S(1)} %get-tuple-element.24.refs_0_, f32[2,128]{1,0:T(2,128)S(1)} %collective-permute-done.23.refs_1_, f32[2,128]{1,0:T(2,128)S(1)} %collective-permute-done.24.refs_2_, f32[2,128]{1,0:T(2,128)S(1)} %collective-permute-done.25.refs_3_, ...), custom_call_target="tpu_custom_call" | custom-call | tf_op jit(solution)/shard_map/pallas_call | solution.py:303
  (45 shorter events, 0.3 us)
Async XLA Ops:
  0.0 0.9 %copy-start.2 = (f32[128,512]{1,0:T(8,128)S(1)}, f32[128,512]{1,0:T(8,128)}, u32[]{:S(2)}) copy-start(f32[128,512]{1,0:T(8,128)} %own_ref.1) | copy-start | bytes 786436
  1.0 23.6 %copy-start.8 = (f32[512]{0:T(512)S(1)}, f32[512]{0:T(512)}, u32[]{:S(2)}) copy-start(f32[512]{0:T(512)} %param.15) | copy-start | bytes 6148
  1.0 36.9 %copy-start.4 = (f32[512,128]{1,0:T(8,128)S(1)}, f32[512,128]{1,0:T(8,128)}, u32[]{:S(2)}) copy-start(f32[512,128]{1,0:T(8,128)} %refs_4_.3) | copy-start | bytes 786436
  1.0 36.9 %copy-start.5 = (f32[512,128]{1,0:T(8,128)S(1)}, f32[512,128]{1,0:T(8,128)}, u32[]{:S(2)}) copy-start(f32[512,128]{1,0:T(8,128)} %refs_5_.1) | copy-start | bytes 786436
  1.0 45.2 %copy-start.6 = (f32[512,128]{1,0:T(8,128)S(1)}, f32[512,128]{1,0:T(8,128)}, u32[]{:S(2)}) copy-start(f32[512,128]{1,0:T(8,128)} %refs_4_.2) | copy-start | bytes 786436
  1.0 5.4 %collective-permute-start.16 = (f32[1,32,512]{2,1,0:T(8,128)S(1)}, f32[1,32,512]{2,1,0:T(8,128)S(1)}, u32[]{:S(2)}, u32[]{:S(2)}) collective-permute-start(f32[1,32,512]{2,1,0:T(8,128)S(1)} %bitcast.8), channel_id=1, source_target_pairs={{0,1},{1,0},{2,3},{3,2},{4,5},{5,4},{6,7},{7,6},{8,9},{9,8},{10,11... | collective-permute-start | bytes 196616 | tf_op jit(solution)/shard_map/ppermute | solution.py:243
  6.4 8.3 %collective-permute-start.17 = (f32[2,32,512]{2,1,0:T(8,128)S(1)}, f32[2,32,512]{2,1,0:T(8,128)S(1)}, u32[]{:S(2)}, u32[]{:S(2)}) collective-permute-start(f32[2,32,512]{2,1,0:T(8,128)S(1)} %pad_maximum_fusion.2), channel_id=1, source_target_pairs={{0,2},{1,3},{2,0},{3,1},{4,6},{5,7},{6,4},{7,5},{8,10},{9,11},{10,... | collective-permute-start | bytes 393224 | tf_op jit(solution)/shard_map/ppermute | solution.py:243
  14.6 39.0 %copy-start.3 = (f32[128,512]{1,0:T(8,128)S(1)}, f32[128,512]{1,0:T(8,128)}, u32[]{:S(2)}) copy-start(f32[128,512]{1,0:T(8,128)} %own_ref.1) | copy-start | bytes 786436
  14.7 9.8 %collective-permute-start.18 = (f32[1,3,32,512]{3,2,1,0:T(8,128)S(1)}, f32[1,3,32,512]{3,2,1,0:T(8,128)S(1)}, u32[]{:S(2)}, u32[]{:S(2)}) collective-permute-start(f32[1,3,32,512]{3,2,1,0:T(8,128)S(1)} %maximum_bitcast_fusion), channel_id=1, source_target_pairs={{0,16},{4,20},{8,24},{12,28},{16,0},{20,4},{24,8},{28,12},{1,17},{... | collective-permute-start | bytes 589832 | tf_op jit(solution)/shard_map/ppermute | solution.py:243
  16.3 42.1 %copy-start.9 = (f32[512]{0:T(512)S(1)}, f32[512]{0:T(512)}, u32[]{:S(2)}) copy-start(f32[512]{0:T(512)} %param.20) | copy-start | bytes 6148
  16.3 42.1 %copy-start.10 = (f32[512]{0:T(512)S(1)}, f32[512]{0:T(512)}, u32[]{:S(2)}) copy-start(f32[512]{0:T(512)} %param.21) | copy-start | bytes 6148
  19.9 38.5 %copy-start = (f32[512,512]{1,0:T(8,128)S(1)}, f32[512,512]{1,0:T(8,128)}, u32[]{:S(2)}) copy-start(f32[512,512]{1,0:T(8,128)} %refs_11_.1) | copy-start | bytes 3145732
  19.9 38.5 %copy-start.1 = (f32[512,512]{1,0:T(8,128)S(1)}, f32[512,512]{1,0:T(8,128)}, u32[]{:S(2)}) copy-start(f32[512,512]{1,0:T(8,128)} %refs_12_.1) | copy-start | bytes 3145732
  19.9 5.4 %collective-permute-start = (f32[128,128]{1,0:T(8,128)}, f32[128,128]{1,0:T(8,128)S(1)}, u32[]{:S(2)}, u32[]{:S(2)}) collective-permute-start(f32[128,128]{1,0:T(8,128)} %get-tuple-element.16), channel_id=1, source_target_pairs={{0,1},{1,0},{2,3},{3,2},{4,5},{5,4},{6,7},{7,6},{8,9},{9,8},{10,11... | collective-permute-start | bytes 196616 | tf_op jit(solution)/shard_map/ppermute | solution.py:243
  20.7 7.2 %collective-permute-start.1 = (f32[128,128]{1,0:T(8,128)}, f32[128,128]{1,0:T(8,128)S(1)}, u32[]{:S(2)}, u32[]{:S(2)}) collective-permute-start(f32[128,128]{1,0:T(8,128)} %get-tuple-element.17), channel_id=1, source_target_pairs={{0,2},{1,3},{2,0},{3,1},{4,6},{5,7},{6,4},{7,5},{8,10},{9,11},{10,... | collective-permute-start | bytes 196616 | tf_op jit(solution)/shard_map/ppermute | solution.py:243
  24.1 6.3 %collective-permute-start.2 = (f32[128,128]{1,0:T(8,128)}, f32[128,128]{1,0:T(8,128)S(1)}, u32[]{:S(2)}, u32[]{:S(2)}) collective-permute-start(f32[128,128]{1,0:T(8,128)} %get-tuple-element.18), channel_id=1, source_target_pairs={{0,3},{1,2},{2,1},{3,0},{4,7},{5,6},{6,5},{7,4},{8,11},{9,10},{10,... | collective-permute-start | bytes 196616 | tf_op jit(solution)/shard_map/ppermute | solution.py:243
  24.4 29.1 %collective-permute-start.19 = (f32[2,3,32,512]{3,2,1,0:T(8,128)S(1)}, f32[2,3,32,512]{3,2,1,0:T(8,128)S(1)}, u32[]{:S(2)}, u32[]{:S(2)}) collective-permute-start(f32[2,3,32,512]{3,2,1,0:T(8,128)S(1)} %pad_maximum_fusion.1), channel_id=1, source_target_pairs={{0,4},{4,0},{8,12},{12,8},{16,20},{20,16},{24,28},{28,24},{1,5},{5... | collective-permute-start | bytes 1179656 | tf_op jit(solution)/shard_map/ppermute | solution.py:243
  24.5 0.8 %copy-start.7 = (f32[128,128]{1,0:T(8,128)S(1)}, f32[128,128]{1,0:T(8,128)}, u32[]{:S(2)}) copy-start(f32[128,128]{1,0:T(8,128)} %get-tuple-element.15.x_ref) | copy-start | bytes 196612
  30.4 6.3 %collective-permute-start.5 = (f32[128,128]{1,0:T(8,128)S(1)}, f32[128,128]{1,0:T(8,128)S(1)}, u32[]{:S(2)}, u32[]{:S(2)}) collective-permute-start(f32[128,128]{1,0:T(8,128)S(1)} %shard_map.128.refs_0_.refs_4_), channel_id=1, source_target_pairs={{0,3},{1,2},{2,1},{3,0},{4,7},{5,6},{6,5},{7,4},{8,11},{9,10},{10,... | collective-permute-start | bytes 196616 | tf_op jit(solution)/shard_map/ppermute | solution.py:243
  31.2 6.6 %collective-permute-start.4 = (f32[128,128]{1,0:T(8,128)S(1)}, f32[128,128]{1,0:T(8,128)S(1)}, u32[]{:S(2)}, u32[]{:S(2)}) collective-permute-start(f32[128,128]{1,0:T(8,128)S(1)} %shard_map.128.refs_0_.refs_4_), channel_id=1, source_target_pairs={{0,2},{1,3},{2,0},{3,1},{4,6},{5,7},{6,4},{7,5},{8,10},{9,11},{10,... | collective-permute-start | bytes 196616 | tf_op jit(solution)/shard_map/ppermute | solution.py:243
  31.2 6.6 %collective-permute-start.3 = (f32[128,128]{1,0:T(8,128)S(1)}, f32[128,128]{1,0:T(8,128)S(1)}, u32[]{:S(2)}, u32[]{:S(2)}) collective-permute-start(f32[128,128]{1,0:T(8,128)S(1)} %shard_map.128.refs_0_.refs_4_), channel_id=1, source_target_pairs={{0,1},{1,0},{2,3},{3,2},{4,5},{5,4},{6,7},{7,6},{8,9},{9,8},{10,11... | collective-permute-start | bytes 196616 | tf_op jit(solution)/shard_map/ppermute | solution.py:243
  38.2 6.0 %collective-permute-start.8 = (f32[128,256]{1,0:T(8,128)S(1)}, f32[128,256]{1,0:T(8,128)S(1)}, u32[]{:S(2)}, u32[]{:S(2)}) collective-permute-start(f32[128,256]{1,0:T(8,128)S(1)} %shard_map.130.refs_0_), channel_id=1, source_target_pairs={{0,24},{4,28},{8,16},{12,20},{16,8},{20,12},{24,0},{28,4},{1,25},{... | collective-permute-start | bytes 393224 | tf_op jit(solution)/shard_map/ppermute | solution.py:243
  39.7 5.8 %collective-permute-start.7 = (f32[128,256]{1,0:T(8,128)S(1)}, f32[128,256]{1,0:T(8,128)S(1)}, u32[]{:S(2)}, u32[]{:S(2)}) collective-permute-start(f32[128,256]{1,0:T(8,128)S(1)} %shard_map.130.refs_0_), channel_id=1, source_target_pairs={{0,16},{4,20},{8,24},{12,28},{16,0},{20,4},{24,8},{28,12},{1,17},{... | collective-permute-start | bytes 393224 | tf_op jit(solution)/shard_map/ppermute | solution.py:243
  41.2 5.0 %collective-permute-start.6 = (f32[128,256]{1,0:T(8,128)S(1)}, f32[128,256]{1,0:T(8,128)S(1)}, u32[]{:S(2)}, u32[]{:S(2)}) collective-permute-start(f32[128,256]{1,0:T(8,128)S(1)} %shard_map.130.refs_0_), channel_id=1, source_target_pairs={{0,8},{4,12},{8,0},{12,4},{16,24},{20,28},{24,16},{28,20},{1,9},{5... | collective-permute-start | bytes 393224 | tf_op jit(solution)/shard_map/ppermute | solution.py:243
  41.8 4.7 %collective-permute-start.9 = (f32[128,256]{1,0:T(8,128)S(1)}, f32[128,256]{1,0:T(8,128)S(1)}, u32[]{:S(2)}, u32[]{:S(2)}) collective-permute-start(f32[128,256]{1,0:T(8,128)S(1)} %shard_map.130.refs_0_), channel_id=1, source_target_pairs={{0,4},{4,0},{8,12},{12,8},{16,20},{20,16},{24,28},{28,24},{1,5},{5... | collective-permute-start | bytes 393224 | tf_op jit(solution)/shard_map/ppermute | solution.py:243
  44.2 2.3 %collective-permute-start.12 = (f32[128,256]{1,0:T(8,128)S(1)}, f32[128,256]{1,0:T(8,128)S(1)}, u32[]{:S(2)}, u32[]{:S(2)}) collective-permute-start(f32[128,256]{1,0:T(8,128)S(1)} %collective-permute-done.8.refs_3_), channel_id=1, source_target_pairs={{0,4},{4,0},{8,12},{12,8},{16,20},{20,16},{24,28},{28,24},{1,5},{5... | collective-permute-start | bytes 393224 | tf_op jit(solution)/shard_map/ppermute | solution.py:243
  45.5 1.3 %collective-permute-start.11 = (f32[128,256]{1,0:T(8,128)S(1)}, f32[128,256]{1,0:T(8,128)S(1)}, u32[]{:S(2)}, u32[]{:S(2)}) collective-permute-start(f32[128,256]{1,0:T(8,128)S(1)} %collective-permute-done.7.refs_2_), channel_id=1, source_target_pairs={{0,4},{4,0},{8,12},{12,8},{16,20},{20,16},{24,28},{28,24},{1,5},{5... | collective-permute-start | bytes 393224 | tf_op jit(solution)/shard_map/ppermute | solution.py:243
  46.2 1.3 %collective-permute-start.10 = (f32[128,256]{1,0:T(8,128)S(1)}, f32[128,256]{1,0:T(8,128)S(1)}, u32[]{:S(2)}, u32[]{:S(2)}) collective-permute-start(f32[128,256]{1,0:T(8,128)S(1)} %collective-permute-done.6.refs_1_), channel_id=1, source_target_pairs={{0,4},{4,0},{8,12},{12,8},{16,20},{20,16},{24,28},{28,24},{1,5},{5... | collective-permute-start | bytes 393224 | tf_op jit(solution)/shard_map/ppermute | solution.py:243
  46.5 28.6 %copy-start.11 = (f32[512]{0:T(512)S(1)}, f32[512]{0:T(512)}, u32[]{:S(2)}) copy-start(f32[512]{0:T(512)} %param.24) | copy-start | bytes 6148
  46.5 28.6 %copy-start.12 = (f32[512]{0:T(512)S(1)}, f32[512]{0:T(512)}, u32[]{:S(2)}) copy-start(f32[512]{0:T(512)} %param.25) | copy-start | bytes 6148
  49.1 6.9 %collective-permute-start.15 = (f32[128,128]{1,0:T(8,128)S(1)}, f32[128,128]{1,0:T(8,128)S(1)}, u32[]{:S(2)}, u32[]{:S(2)}) collective-permute-start(f32[128,128]{1,0:T(8,128)S(1)} %shard_map.131.refs_0_), channel_id=1, source_target_pairs={{0,3},{1,2},{2,1},{3,0},{4,7},{5,6},{6,5},{7,4},{8,11},{9,10},{10,... | collective-permute-start | bytes 196616 | tf_op jit(solution)/shard_map/ppermute | solution.py:243
  50.8 7.6 %collective-permute-start.14 = (f32[128,128]{1,0:T(8,128)S(1)}, f32[128,128]{1,0:T(8,128)S(1)}, u32[]{:S(2)}, u32[]{:S(2)}) collective-permute-start(f32[128,128]{1,0:T(8,128)S(1)} %shard_map.131.refs_0_), channel_id=1, source_target_pairs={{0,2},{1,3},{2,0},{3,1},{4,6},{5,7},{6,4},{7,5},{8,10},{9,11},{10,... | collective-permute-start | bytes 196616 | tf_op jit(solution)/shard_map/ppermute | solution.py:243
  51.9 6.5 %collective-permute-start.13 = (f32[128,128]{1,0:T(8,128)S(1)}, f32[128,128]{1,0:T(8,128)S(1)}, u32[]{:S(2)}, u32[]{:S(2)}) collective-permute-start(f32[128,128]{1,0:T(8,128)S(1)} %shard_map.131.refs_0_), channel_id=1, source_target_pairs={{0,1},{1,0},{2,3},{3,2},{4,5},{5,4},{6,7},{7,6},{8,9},{9,8},{10,11... | collective-permute-start | bytes 196616 | tf_op jit(solution)/shard_map/ppermute | solution.py:243
  59.7 4.8 %collective-permute-start.20 = (f32[128,128]{1,0:T(8,128)S(1)}, f32[128,128]{1,0:T(8,128)S(1)}, u32[]{:S(2)}, u32[]{:S(2)}) collective-permute-start(f32[128,128]{1,0:T(8,128)S(1)} %get-tuple-element.20), channel_id=1, source_target_pairs={{0,1},{1,0},{2,3},{3,2},{4,5},{5,4},{6,7},{7,6},{8,9},{9,8},{10,11... | collective-permute-start | bytes 196616 | tf_op jit(solution)/shard_map/ppermute | solution.py:243
  59.8 8.2 %collective-permute-start.21 = (f32[128,128]{1,0:T(8,128)S(1)}, f32[128,128]{1,0:T(8,128)S(1)}, u32[]{:S(2)}, u32[]{:S(2)}) collective-permute-start(f32[128,128]{1,0:T(8,128)S(1)} %get-tuple-element.21), channel_id=1, source_target_pairs={{0,2},{1,3},{2,0},{3,1},{4,6},{5,7},{6,4},{7,5},{8,10},{9,11},{10,... | collective-permute-start | bytes 196616 | tf_op jit(solution)/shard_map/ppermute | solution.py:243
  61.7 6.3 %collective-permute-start.22 = (f32[128,128]{1,0:T(8,128)S(1)}, f32[128,128]{1,0:T(8,128)S(1)}, u32[]{:S(2)}, u32[]{:S(2)}) collective-permute-start(f32[128,128]{1,0:T(8,128)S(1)} %get-tuple-element.22), channel_id=1, source_target_pairs={{0,3},{1,2},{2,1},{3,0},{4,7},{5,6},{6,5},{7,4},{8,11},{9,10},{10,... | collective-permute-start | bytes 196616 | tf_op jit(solution)/shard_map/ppermute | solution.py:243
  68.1 5.4 %collective-permute-start.25 = (f32[2,128]{1,0:T(2,128)S(1)}, f32[2,128]{1,0:T(2,128)S(1)}, u32[]{:S(2)}, u32[]{:S(2)}) collective-permute-start(f32[2,128]{1,0:T(2,128)S(1)} %get-tuple-element.24.refs_0_), channel_id=1, source_target_pairs={{0,3},{1,2},{2,1},{3,0},{4,7},{5,6},{6,5},{7,4},{8,11},{9,10},{10,... | collective-permute-start | bytes 3080 | tf_op jit(solution)/shard_map/ppermute | solution.py:243
  70.5 4.5 %collective-permute-start.24 = (f32[2,128]{1,0:T(2,128)S(1)}, f32[2,128]{1,0:T(2,128)S(1)}, u32[]{:S(2)}, u32[]{:S(2)}) collective-permute-start(f32[2,128]{1,0:T(2,128)S(1)} %get-tuple-element.24.refs_0_), channel_id=1, source_target_pairs={{0,2},{1,3},{2,0},{3,1},{4,6},{5,7},{6,4},{7,5},{8,10},{9,11},{10,... | collective-permute-start | bytes 3080 | tf_op jit(solution)/shard_map/ppermute | solution.py:243
  70.9 4.1 %collective-permute-start.23 = (f32[2,128]{1,0:T(2,128)S(1)}, f32[2,128]{1,0:T(2,128)S(1)}, u32[]{:S(2)}, u32[]{:S(2)}) collective-permute-start(f32[2,128]{1,0:T(2,128)S(1)} %get-tuple-element.24.refs_0_), channel_id=1, source_target_pairs={{0,1},{1,0},{2,3},{3,2},{4,5},{5,4},{6,7},{7,6},{8,9},{9,8},{10,11... | collective-permute-start | bytes 3080 | tf_op jit(solution)/shard_map/ppermute | solution.py:243

commit v6 on v5

--- a/solution.py
+++ b/solution.py
@@ -25,12 +25,15 @@
     return lax.dot_general(a, b, (dims, ((), ())), preferred_element_type=F32)
 
 
-def dot3(a, b, dims=((1,), (0,))):
+def dot3_split(a, b_hi, b_lo, dims=((1,), (0,))):
     a_hi, a_lo = split(a)
-    b_hi, b_lo = split(b)
     rows = a.shape[0]
     first = mm(jnp.concatenate([a_hi, a_lo], 0), b_hi, dims)
     return first[:rows] + (first[rows:] + mm(a_hi, b_lo, dims))
+
+
+def dot3(a, b, dims=((1,), (0,))):
+    return dot3_split(a, *split(b), dims)
 
 
 def butterfly(blocks, pos):
@@ -63,8 +66,12 @@
     )
 
 
-def shape(*dims):
-    return jax.ShapeDtypeStruct(dims, F32)
+def shape(*dims, dtype=F32):
+    return jax.ShapeDtypeStruct(dims, dtype)
+
+
+def halves_of(*dims):
+    return [shape(*dims, dtype=BF16)] * 2
 
 
 def embed_kernel(count, x_hbm, w_hbm, *rest):
@@ -112,7 +119,7 @@
             pltpu.SemaphoreType.DMA((steps,)),
         ],
         name="embed",
-        compiler_params=pltpu.CompilerParams(vmem_limit_bytes=122 * MIB // 2),
+        compiler_params=pltpu.CompilerParams(vmem_limit_bytes=126 * MIB // 2),
         cost_estimate=pl.CostEstimate(
             flops=6 * rows * depth * model, bytes_accessed=4 * depth * (model + rows), transcendentals=0
         ),
@@ -129,15 +136,15 @@
     out[...] = w_ref[pl.ds(pl.multiple_of(part * size, size), size), :]
 
 
-def order_kernel(bits, own_ref, rest_ref, out):
+def order_kernel(bits, own_ref, rest_ref, hi, lo):
     me = piece_of(lax.axis_index("var"), bits)
     rows = own_ref.shape[0]
     size = rows >> len(bits)
-    out[0:rows, :] = own_ref[...]
+    hi[0:rows, :], lo[0:rows, :] = split(own_ref[...])
     for apart in range(1 << len(bits)):
         for k in range(rest_ref.shape[1]):
-            start = pl.multiple_of((k + 1) * rows + (me ^ apart) * size, size)
-            out[pl.ds(start, size), :] = rest_ref[apart, k]
+            at = pl.ds(pl.multiple_of((k + 1) * rows + (me ^ apart) * size, size), size)
+            hi[at, :], lo[at, :] = split(rest_ref[apart, k])
 
 
 def bias_kernel(x_ref, bias, out):
@@ -151,25 +158,33 @@
     refs[-1][...] = total
 
 
-def rows_of(weight, block, width):
-    return weight[pl.ds(pl.multiple_of(block * width, width), width), :]
-
-
-def project_kernel(count, scale, *refs):
+def split_kernel(*refs):
+    count = len(refs) // 3
+    for at in range(count):
+        refs[count + 2 * at][...], refs[count + 2 * at + 1][...] = split(refs[at][...])
+
+
+def ordered_kernel(count, k_ref, v_ref, q_ref, *outs):
     pos = lax.axis_index("head")
-    blocks, weights, out = refs[:count], refs[count:-1], refs[-1]
-    width = blocks[0].shape[1]
-    stream = jnp.concatenate([block[...] for block in blocks], 1)
-    at = 0
-    for weight in weights:
-        ordered = jnp.concatenate([rows_of(weight, pos ^ k, width) for k in range(count)], 0)
-        result = dot3(stream, ordered)
-        out[:, at : at + result.shape[1]] = result * scale if scale != 1.0 else result
-        at += result.shape[1]
-
-
-def attend_kernel(q_ref, *refs):
-    pieces, out = refs[:-1], refs[-1]
+    width, cols = k_ref.shape[0] // count, k_ref.shape[1]
+    for k in range(count):
+        rows = pl.ds(pl.multiple_of((pos ^ k) * width, width), width)
+        at = slice(k * width, (k + 1) * width)
+        outs[0][at, :cols], outs[1][at, :cols] = split(k_ref[rows, :])
+        outs[0][at, cols:], outs[1][at, cols:] = split(v_ref[rows, :])
+        outs[2][at, :], outs[3][at, :] = split(q_ref[rows, :] * (1.0 / math.sqrt(DH)))
+
+
+def project_kernel(*refs):
+    blocks, hi, lo, out = refs[:-3], *refs[-3:]
+    out[...] = dot3_split(jnp.concatenate([block[...] for block in blocks], 1), hi[...], lo[...])
+
+
+def attend_kernel(q_ref, *refs, merge):
+    if merge:
+        (acc_a, top_a, sum_a), pieces, out = refs[:3], refs[3:-1], refs[-1]
+    else:
+        pieces, (acc_out, top_out, sum_out) = refs[:-3], refs[-3:]
     heads_width = q_ref.shape[1]
     for head in range(heads_width // DH):
         cols = slice(head * DH, (head + 1) * DH)
@@ -179,9 +194,19 @@
         values = jnp.concatenate([piece[:, vcols] for piece in pieces], 0)
         scores = dot3(query, keys, ((1,), (1,)))
         top = jnp.max(scores, axis=1, keepdims=True)
+        if merge:
+            before = top_a[:, cols][:, :1]
+            top = jnp.maximum(top, before)
         weights = jnp.exp(scores - top)
         total = jnp.sum(weights, axis=1, keepdims=True)
-        out[:, cols] = dot3(weights, values) / total
+        acc = dot3(weights, values)
+        if merge:
+            fade = jnp.exp(before - top)
+            out[:, cols] = (acc + acc_a[:, cols] * fade) / (total + sum_a[:, cols][:, :1] * fade)
+        else:
+            acc_out[:, cols] = acc
+            top_out[:, cols] = jnp.broadcast_to(top, acc.shape)
+            sum_out[:, cols] = jnp.broadcast_to(total, acc.shape)
 
 
 def normalise(x, gain, bias):
@@ -198,14 +223,14 @@
 def post_kernel(count, *refs):
     pos = lax.axis_index("head")
     mixed, emb = refs[:count], refs[count : 2 * count]
-    weight, gain, bias, w_in, w_out = refs[2 * count : 2 * count + 5]
-    outs = refs[2 * count + 5 :]
+    o_hi, o_lo, gain, bias, in_hi, in_lo, out_hi, out_lo = refs[2 * count : 2 * count + 8]
+    outs = refs[2 * count + 8 :]
     stream = jnp.concatenate([m[...] for m in mixed], 1)
-    attention = dot3(stream, weight[...])
+    attention = dot3_split(stream, o_hi[...], o_lo[...])
     embedded = jnp.concatenate(butterfly([e[...] for e in emb], pos), 1)
     normed = normalise(embedded + attention, gain[...], bias[...])
-    hidden = gelu(dot3(normed, w_in[...]))
-    partial = butterfly(columns(dot3(hidden, w_out[...]), count), pos)
+    hidden = gelu(dot3_split(normed, in_hi[...], in_lo[...]))
+    partial = butterfly(columns(dot3_split(hidden, out_hi[...], out_lo[...]), count), pos)
     mine = butterfly(columns(normed, count), pos)[0]
     outs[0][...] = mine + partial[0]
     for ref, block in zip(outs[1:], partial[1:]):
@@ -258,9 +283,12 @@
 def gather_pieces(piece):
     size = lax.axis_size("var")
     if size > 8:
-        return [lax.all_gather(piece, "var", axis=0, tiled=True)]
+        whole = lax.all_gather(piece, "var", axis=0, tiled=True)
+        cut = whole.shape[0] // 2
+        return [whole[:cut]], [whole[cut:]]
     far = [piece] + [send(piece, "var", k) for k in range(2, size, 2)]
-    return far + [send(each, "var", 1) for each in far]
+    near = [send(each, "var", 1) for each in far]
+    return far + near[:1], near[1:]
 
 
 def on_device(
@@ -288,15 +316,23 @@
     emb = spread_out(mine, "head")
     for bit in bits:
         rest = jnp.concatenate([rest, send(rest, "var", 1 << bit)], 0)
-    pair = call(functools.partial(project_kernel, n, 1.0), shape(rows, 2 * heads_width))(*emb, k_weight, v_weight)
-    queries = call(functools.partial(project_kernel, n, 1.0 / math.sqrt(DH)), shape(rows, heads_width))(*emb, q_weight)
-    pieces = gather_pieces(pair)
+    wide = halves_of(model, 2 * heads_width) + halves_of(model, heads_width)
+    kv_hi, kv_lo, q_hi, q_lo = call(functools.partial(ordered_kernel, n), wide)(k_weight, v_weight, q_weight)
+    pair = call(project_kernel, shape(rows, 2 * heads_width))(*emb, kv_hi, kv_lo)
+    queries = call(project_kernel, shape(rows, heads_width))(*emb, q_hi, q_lo)
+    first, later = gather_pieces(pair)
+    ffn = call(split_kernel, halves_of(*ffn_in.shape) + halves_of(*ffn_out.shape))(ffn_in, ffn_out)
     order = functools.partial(order_kernel, bits)
-    whole_out = call(order, shape(n * heads_width, model))(out_weight, rest)
-    mixed = call(attend_kernel, shape(rows, heads_width), limit=16)(queries, *pieces)
+    whole_out = call(order, halves_of(n * heads_width, model))(out_weight, rest)
+    state = call(
+        functools.partial(attend_kernel, merge=False), [shape(rows, heads_width)] * 3, limit=16
+    )(queries, *first)
+    mixed = call(
+        functools.partial(attend_kernel, merge=True), shape(rows, heads_width), limit=16
+    )(queries, *state, *later)
     mixes = spread_out(mixed, "head")
     partial = call(functools.partial(post_kernel, n), [block] * n, limit=16)(
-        *mixes, *emb, whole_out, norm1_gain[None, :], norm1_bias[None, :], ffn_in, ffn_out
+        *mixes, *emb, *whole_out, norm1_gain[None, :], norm1_bias[None, :], *ffn
     )
     got = hand_out(partial, "head")
     flipped, stats = call(functools.partial(stats_kernel, n), [shape(width, rows), shape(2, rows)])(*got)

time: 76.1 us -> 79.6 us (1.046)
  waiting for transfers between devices: 31.7 us -> 28.8 us
  other arithmetic: 0.11 us -> 2.83 us
  local copies, waits for them, and re-layouts: 1.84 us -> 4.28 us
  Pallas kernels: 8.22 us -> 9.5 us
    ppermute x26, waiting for transfers between devices: 31.7 us -> 28.8 us  [send(): return lax.ppermute(x, axis, [(i, i ^ offset) for i in range(size)])]
    unnamed x26, local copies, waits for them, and re-layouts: 1.84 us -> 4.28 us
    concatenate x2, other arithmetic: 0.08 us -> 2.12 us  [on_device(): rest = jnp.concatenate([rest, send(rest, 'var', 1 << bit)], 0)]
    pallas_call x4 -> x7, Pallas kernels: 2.28 us -> 3.66 us  [the longest x1 1.34 us: on_device(): call(functools.partial(attend_kernel, merge=True), shape(rows, heads_widt...]
  transfers between devices with their start and end apart: 26 -> 26, of which waited for: 17 -> 15; matrix products, arithmetic and copies ran while one was open for 0% -> 3% of each run, Pallas kernels for 8% -> 9%
where the time goes in v6:
time: 79.6 us; the launch traced here: 79.3 us
  starting transfers between devices  33.7 us (42%)
  waiting for transfers between devices  28.8 us (36%)
  Pallas kernels  9.5 us (12%)
  local copies, waits for them, and re-layouts  4.28 us (5%)
  other arithmetic  2.83 us (4%)
    ppermute x26, starting transfers between devices, send(): return lax.ppermute(x, axis, [(i, i ^ offset) for i in range(size)])  33.7 us
    ppermute x26, waiting for transfers between devices, send(): return lax.ppermute(x, axis, [(i, i ^ offset) for i in range(size)])  28.8 us
    unnamed x26, local copies, waits for them, and re-layouts  4.28 us
    pallas_call x1, Pallas kernels, embed(): pl.pallas_call(functools.partial(embed_kernel, count), out_shape=[shape(r...  3.61 us
    concatenate x2, other arithmetic, on_device(): rest = jnp.concatenate([rest, send(rest, 'var', 1 << bit)], 0)  2.12 us
  transfers between devices with their start and end apart: 26, of which 15 were waited for; matrix products, arithmetic and copies ran while one was open for 3% of the time, Pallas kernels for 9%

profile of v6, /device:TPU:0, one launch (start us, length us, event | category | flops | bytes accessed | tf_op | source)
XLA Modules:
  0.0 79.3 jit_solution(13525568556714004735)
XLA Ops:
  0.0 0.9 %copy-done.2 = f32[128,512]{1,0:T(8,128)S(1)} copy-done((f32[128,512]{1,0:T(8,128)S(1)}, f32[128,512]{1,0:T(8,128)}, u32[]{:S(2)}) %copy-start.2) | copy-done | bytes 262168
  1.0 3.1 %collective-permute-start.16 = (f32[1,32,512]{2,1,0:T(8,128)S(1)}, f32[1,32,512]{2,1,0:T(8,128)S(1)}, u32[]{:S(2)}, u32[]{:S(2)}) collective-permute-start(f32[1,32,512]{2,1,0:T(8,128)S(1)} %bitcast.8), channel_id=1, source_target_pairs={{0,1},{1,0},{2,3},{3,2},{4,5},{5,4},{6,7},{7,6},{8,9},{9,8},{10,11... | collective-permute-start | bytes 196616 | tf_op jit(solution)/shard_map/ppermute | solution.py:268
  4.1 2.2 %collective-permute-done.16 = f32[1,32,512]{2,1,0:T(8,128)S(1)} collective-permute-done((f32[1,32,512]{2,1,0:T(8,128)S(1)}, f32[1,32,512]{2,1,0:T(8,128)S(1)}, u32[]{:S(2)}, u32[]{:S(2)}) %collective-permute-start.16) | collective-permute-done | bytes 65568 | tf_op jit(solution)/shard_map/ppermute | solution.py:268
  6.4 3.1 %collective-permute-start.17 = (f32[2,32,512]{2,1,0:T(8,128)S(1)}, f32[2,32,512]{2,1,0:T(8,128)S(1)}, u32[]{:S(2)}, u32[]{:S(2)}) collective-permute-start(f32[2,32,512]{2,1,0:T(8,128)S(1)} %pad_maximum_fusion.2), channel_id=1, source_target_pairs={{0,2},{1,3},{2,0},{3,1},{4,6},{5,7},{6,4},{7,5},{8,10},{9,11},{10,... | collective-permute-start | bytes 393224 | tf_op jit(solution)/shard_map/ppermute | solution.py:268
  9.5 5.2 %collective-permute-done.17 = f32[2,32,512]{2,1,0:T(8,128)S(1)} collective-permute-done((f32[2,32,512]{2,1,0:T(8,128)S(1)}, f32[2,32,512]{2,1,0:T(8,128)S(1)}, u32[]{:S(2)}, u32[]{:S(2)}) %collective-permute-start.17) | collective-permute-done | bytes 131104 | tf_op jit(solution)/shard_map/ppermute | solution.py:268
  14.6 0.7 maximum_bitcast_fusion
  15.3 1.6 %collective-permute-start.18 = (f32[1,3,32,512]{3,2,1,0:T(8,128)}, f32[1,3,32,512]{3,2,1,0:T(8,128)}, u32[]{:S(2)}, u32[]{:S(2)}) collective-permute-start(f32[1,3,32,512]{3,2,1,0:T(8,128)} %maximum_bitcast_fusion), channel_id=1, source_target_pairs={{0,16},{4,20},{8,24},{12,28},{16,0},{20,4},{24,8},{28,12},{1,17},{... | collective-permute-start | bytes 589832 | tf_op jit(solution)/shard_map/ppermute | solution.py:268
  16.9 3.6 %embed.1 = (f32[128,128]{1,0:T(8,128)}, f32[128,128]{1,0:T(8,128)}, f32[128,128]{1,0:T(8,128)}, f32[128,128]{1,0:T(8,128)}) custom-call(f32[128,2048]{1,0:T(8,128)} %x_hbm.1, f32[2048,512]{1,0:T(8,128)} %w_hbm.1), custom_call_target="tpu_custom_call" | custom-call | flops 805306368 | bytes 5242880 | tf_op jit(solution)/shard_map/embed/pallas_call | solution.py:111
  20.5 0.7 collective-permute-start
  21.2 3.4 %collective-permute-start.1 = (f32[128,128]{1,0:T(8,128)}, f32[128,128]{1,0:T(8,128)S(1)}, u32[]{:S(2)}, u32[]{:S(2)}) collective-permute-start(f32[128,128]{1,0:T(8,128)} %get-tuple-element.30), channel_id=1, source_target_pairs={{0,2},{1,3},{2,0},{3,1},{4,6},{5,7},{6,4},{7,5},{8,10},{9,11},{10,... | collective-permute-start | bytes 196616 | tf_op jit(solution)/shard_map/ppermute | solution.py:268
  24.6 0.3 collective-permute-start.2
  25.0 1.0 %pad_maximum_fusion.1 = f32[2,3,32,512]{3,2,1,0:T(8,128)S(1)} fusion(f32[1,3,32,512]{3,2,1,0:T(8,128)} %collective-permute-done.18, f32[1,3,32,512]{3,2,1,0:T(8,128)} %maximum_bitcast_fusion), kind=kLoop, calls=%fused_computation.1 | loop fusion | flops 98304 | bytes 786432 | tf_op jit(solution)/shard_map/concatenate | solution.py:318
  26.1 0.8 %copy-done.7 = f32[128,128]{1,0:T(8,128)S(1)} copy-done((f32[128,128]{1,0:T(8,128)S(1)}, f32[128,128]{1,0:T(8,128)}, u32[]{:S(2)}) %copy-start.7) | copy-done | bytes 65560
  27.0 1.5 %collective-permute-done.1.refs_2_ = f32[128,128]{1,0:T(8,128)S(1)} collective-permute-done((f32[128,128]{1,0:T(8,128)}, f32[128,128]{1,0:T(8,128)S(1)}, u32[]{:S(2)}, u32[]{:S(2)}) %collective-permute-start.1) | collective-permute-done | bytes 65568 | tf_op jit(solution)/shard_map/ppermute | solution.py:268
  28.5 2.5 %collective-permute-done.2.refs_3_ = f32[128,128]{1,0:T(8,128)S(1)} collective-permute-done((f32[128,128]{1,0:T(8,128)}, f32[128,128]{1,0:T(8,128)S(1)}, u32[]{:S(2)}, u32[]{:S(2)}) %collective-permute-start.2) | collective-permute-done | bytes 65568 | tf_op jit(solution)/shard_map/ppermute | solution.py:268
  31.0 0.8 collective-permute-start.5
  31.8 3.7 %collective-permute-start.3 = (f32[128,128]{1,0:T(8,128)S(1)}, f32[128,128]{1,0:T(8,128)S(1)}, u32[]{:S(2)}, u32[]{:S(2)}) collective-permute-start(f32[128,128]{1,0:T(8,128)S(1)} %shard_map.128.refs_0_.refs_4_), channel_id=1, source_target_pairs={{0,1},{1,0},{2,3},{3,2},{4,5},{5,4},{6,7},{7,6},{8,9},{9,8},{10,11... | collective-permute-start | bytes 196616 | tf_op jit(solution)/shard_map/ppermute | solution.py:268
  35.6 1.7 %collective-permute-done.5.refs_3_.refs_7_ = f32[128,128]{1,0:T(8,128)S(1)} collective-permute-done((f32[128,128]{1,0:T(8,128)S(1)}, f32[128,128]{1,0:T(8,128)S(1)}, u32[]{:S(2)}, u32[]{:S(2)}) %collective-permute-start.5) | collective-permute-done | bytes 65568 | tf_op jit(solution)/shard_map/ppermute | solution.py:268
  37.3 1.1 %collective-permute-done.4.refs_2_.refs_6_ = f32[128,128]{1,0:T(8,128)S(1)} collective-permute-done((f32[128,128]{1,0:T(8,128)S(1)}, f32[128,128]{1,0:T(8,128)S(1)}, u32[]{:S(2)}, u32[]{:S(2)}) %collective-permute-start.4) | collective-permute-done | bytes 65568 | tf_op jit(solution)/shard_map/ppermute | solution.py:268
  38.4 0.3 shard_map.131.refs_0_
  38.7 1.5 %collective-permute-start.8 = (f32[128,256]{1,0:T(8,128)S(1)}, f32[128,256]{1,0:T(8,128)S(1)}, u32[]{:S(2)}, u32[]{:S(2)}) collective-permute-start(f32[128,256]{1,0:T(8,128)S(1)} %shard_map.131.refs_0_), channel_id=1, source_target_pairs={{0,24},{4,28},{8,16},{12,20},{16,8},{20,12},{24,0},{28,4},{1,25},{... | collective-permute-start | bytes 393224 | tf_op jit(solution)/shard_map/ppermute | solution.py:268
  40.2 1.5 %collective-permute-start.7 = (f32[128,256]{1,0:T(8,128)S(1)}, f32[128,256]{1,0:T(8,128)S(1)}, u32[]{:S(2)}, u32[]{:S(2)}) collective-permute-start(f32[128,256]{1,0:T(8,128)S(1)} %shard_map.131.refs_0_), channel_id=1, source_target_pairs={{0,16},{4,20},{8,24},{12,28},{16,0},{20,4},{24,8},{28,12},{1,17},{... | collective-permute-start | bytes 393224 | tf_op jit(solution)/shard_map/ppermute | solution.py:268
  41.7 0.5 collective-permute-start.6
  42.2 2.5 %collective-permute-done.8.refs_3_ = f32[128,256]{1,0:T(8,128)S(1)} collective-permute-done((f32[128,256]{1,0:T(8,128)S(1)}, f32[128,256]{1,0:T(8,128)S(1)}, u32[]{:S(2)}, u32[]{:S(2)}) %collective-permute-start.8) | collective-permute-done | bytes 131104 | tf_op jit(solution)/shard_map/ppermute | solution.py:268
  44.7 1.3 %collective-permute-done.7.refs_2_ = f32[128,256]{1,0:T(8,128)S(1)} collective-permute-done((f32[128,256]{1,0:T(8,128)S(1)}, f32[128,256]{1,0:T(8,128)S(1)}, u32[]{:S(2)}, u32[]{:S(2)}) %collective-permute-start.7) | collective-permute-done | bytes 131104 | tf_op jit(solution)/shard_map/ppermute | solution.py:268
  46.0 0.6 collective-permute-done.6.refs_1_
  46.7 1.2 %copy-done = f32[512,512]{1,0:T(8,128)S(1)} copy-done((f32[512,512]{1,0:T(8,128)S(1)}, f32[512,512]{1,0:T(8,128)}, u32[]{:S(2)}) %copy-start) | copy-done | bytes 1048600
  47.9 1.2 %copy-done.1 = f32[512,512]{1,0:T(8,128)S(1)} copy-done((f32[512,512]{1,0:T(8,128)S(1)}, f32[512,512]{1,0:T(8,128)}, u32[]{:S(2)}) %copy-start.1) | copy-done | bytes 1048600
  49.1 0.3 shard_map.136
  49.7 1.2 %shard_map.132 = (f32[128,128]{1,0:T(8,128)S(1)}, f32[128,128]{1,0:T(8,128)S(1)}, f32[128,128]{1,0:T(8,128)S(1)}) custom-call(f32[128,128]{1,0:T(8,128)S(1)} %shard_map.130.q_ref, f32[128,256]{1,0:T(8,128)S(1)} %shard_map.131.refs_0_, f32[128,256]{1,0:T(8,128)S(1)} %collective-permute-done.6.refs_1_, f32[128,256]{1,0:T(8,128)S(1)} %collective-permute-done.7.refs_2_, ...), custom_call_target="tpu_custom_call" | custom-call | tf_op jit(solution)/shard_map/pallas_call | solution.py:327
  51.0 1.3 %shard_map.133.refs_0_ = f32[128,128]{1,0:T(8,128)S(1)} custom-call(f32[128,128]{1,0:T(8,128)S(1)} %shard_map.130.q_ref, f32[128,128]{1,0:T(8,128)S(1)} %get-tuple-element.36.refs_0_, f32[128,128]{1,0:T(8,128)S(1)} %get-tuple-element.37.refs_1_, f32[128,128]{1,0:T(8,128)S(1)} %get-tuple-element.38.refs_2_, f32[128,256]{1,0:T(8,128)S(1)} %collective-permute-done.10.refs_3_, ...), custom_call_target="tpu_custom_call" | custom-call | tf_op jit(solution)/shard_map/pallas_call | solution.py:330
  52.3 1.8 %collective-permute-start.15 = (f32[128,128]{1,0:T(8,128)S(1)}, f32[128,128]{1,0:T(8,128)S(1)}, u32[]{:S(2)}, u32[]{:S(2)}) collective-permute-start(f32[128,128]{1,0:T(8,128)S(1)} %shard_map.133.refs_0_), channel_id=1, source_target_pairs={{0,3},{1,2},{2,1},{3,0},{4,7},{5,6},{6,5},{7,4},{8,11},{9,10},{10,... | collective-permute-start | bytes 196616 | tf_op jit(solution)/shard_map/ppermute | solution.py:268
  54.1 1.1 %collective-permute-start.14 = (f32[128,128]{1,0:T(8,128)S(1)}, f32[128,128]{1,0:T(8,128)S(1)}, u32[]{:S(2)}, u32[]{:S(2)}) collective-permute-start(f32[128,128]{1,0:T(8,128)S(1)} %shard_map.133.refs_0_), channel_id=1, source_target_pairs={{0,2},{1,3},{2,0},{3,1},{4,6},{5,7},{6,4},{7,5},{8,10},{9,11},{10,... | collective-permute-start | bytes 196616 | tf_op jit(solution)/shard_map/ppermute | solution.py:268
  55.2 1.5 %collective-permute-start.13 = (f32[128,128]{1,0:T(8,128)S(1)}, f32[128,128]{1,0:T(8,128)S(1)}, u32[]{:S(2)}, u32[]{:S(2)}) collective-permute-start(f32[128,128]{1,0:T(8,128)S(1)} %shard_map.133.refs_0_), channel_id=1, source_target_pairs={{0,1},{1,0},{2,3},{3,2},{4,5},{5,4},{6,7},{7,6},{8,9},{9,8},{10,11... | collective-permute-start | bytes 196616 | tf_op jit(solution)/shard_map/ppermute | solution.py:268
  56.8 1.1 %pad_maximum_fusion.rest_ref = f32[4,3,32,512]{3,2,1,0:T(8,128)S(1)} fusion(f32[2,3,32,512]{3,2,1,0:T(8,128)S(1)} %collective-permute-done.19, f32[1,3,32,512]{3,2,1,0:T(8,128)} %collective-permute-done.18, f32[1,3,32,512]{3,2,1,0:T(8,128)} %maximum_bitcast_fusion), kind=kLoop, calls=%fused_computation | loop fusion | flops 393216 | bytes 1572864 | tf_op jit(solution)/shard_map/concatenate | solution.py:318
  58.0 1.2 %collective-permute-done.15.refs_3_ = f32[128,128]{1,0:T(8,128)S(1)} collective-permute-done((f32[128,128]{1,0:T(8,128)S(1)}, f32[128,128]{1,0:T(8,128)S(1)}, u32[]{:S(2)}, u32[]{:S(2)}) %collective-permute-start.15) | collective-permute-done | bytes 65568 | tf_op jit(solution)/shard_map/ppermute | solution.py:268
  59.2 2.7 %collective-permute-done.14.refs_2_ = f32[128,128]{1,0:T(8,128)S(1)} collective-permute-done((f32[128,128]{1,0:T(8,128)S(1)}, f32[128,128]{1,0:T(8,128)S(1)}, u32[]{:S(2)}, u32[]{:S(2)}) %collective-permute-start.14) | collective-permute-done | bytes 65568 | tf_op jit(solution)/shard_map/ppermute | solution.py:268
  61.9 1.2 %shard_map.137 = (f32[128,128]{1,0:T(8,128)S(1)}, f32[128,128]{1,0:T(8,128)S(1)}, f32[128,128]{1,0:T(8,128)S(1)}, f32[128,128]{1,0:T(8,128)S(1)}) custom-call(f32[128,128]{1,0:T(8,128)S(1)} %shard_map.133.refs_0_, f32[128,128]{1,0:T(8,128)S(1)} %collective-permute-done.13.refs_1_, f32[128,128]{1,0:T(8,128)S(1)} %collective-permute-done.14.refs_2_, ...), custom_call_target="tpu_custom_call" | custom-call | tf_op jit(solution)/shard_map/pallas_call | solution.py:334
  63.2 1.9 %collective-permute-start.21 = (f32[128,128]{1,0:T(8,128)S(1)}, f32[128,128]{1,0:T(8,128)S(1)}, u32[]{:S(2)}, u32[]{:S(2)}) collective-permute-start(f32[128,128]{1,0:T(8,128)S(1)} %get-tuple-element.47), channel_id=1, source_target_pairs={{0,2},{1,3},{2,0},{3,1},{4,6},{5,7},{6,4},{7,5},{8,10},{9,11},{10,... | collective-permute-start | bytes 196616 | tf_op jit(solution)/shard_map/ppermute | solution.py:268
  65.1 2.5 %collective-permute-start.22 = (f32[128,128]{1,0:T(8,128)S(1)}, f32[128,128]{1,0:T(8,128)S(1)}, u32[]{:S(2)}, u32[]{:S(2)}) collective-permute-start(f32[128,128]{1,0:T(8,128)S(1)} %get-tuple-element.48), channel_id=1, source_target_pairs={{0,3},{1,2},{2,1},{3,0},{4,7},{5,6},{6,5},{7,4},{8,11},{9,10},{10,... | collective-permute-start | bytes 196616 | tf_op jit(solution)/shard_map/ppermute | solution.py:268
  67.6 0.4 collective-permute-done.20.refs_1_
  68.0 3.5 %collective-permute-done.21.refs_2_ = f32[128,128]{1,0:T(8,128)S(1)} collective-permute-done((f32[128,128]{1,0:T(8,128)S(1)}, f32[128,128]{1,0:T(8,128)S(1)}, u32[]{:S(2)}, u32[]{:S(2)}) %collective-permute-start.21) | collective-permute-done | bytes 65568 | tf_op jit(solution)/shard_map/ppermute | solution.py:268
  71.6 2.3 %collective-permute-start.25 = (f32[2,128]{1,0:T(2,128)S(1)}, f32[2,128]{1,0:T(2,128)S(1)}, u32[]{:S(2)}, u32[]{:S(2)}) collective-permute-start(f32[2,128]{1,0:T(2,128)S(1)} %get-tuple-element.50.refs_0_), channel_id=1, source_target_pairs={{0,3},{1,2},{2,1},{3,0},{4,7},{5,6},{6,5},{7,4},{8,11},{9,10},{10,... | collective-permute-start | bytes 3080 | tf_op jit(solution)/shard_map/ppermute | solution.py:268
  73.9 0.5 collective-permute-start.24
  74.4 1.7 %collective-permute-start.23 = (f32[2,128]{1,0:T(2,128)S(1)}, f32[2,128]{1,0:T(2,128)S(1)}, u32[]{:S(2)}, u32[]{:S(2)}) collective-permute-start(f32[2,128]{1,0:T(2,128)S(1)} %get-tuple-element.50.refs_0_), channel_id=1, source_target_pairs={{0,1},{1,0},{2,3},{3,2},{4,5},{5,4},{6,7},{7,6},{8,9},{9,8},{10,11... | collective-permute-start | bytes 3080 | tf_op jit(solution)/shard_map/ppermute | solution.py:268
  76.1 1.0 %collective-permute-done.25.refs_3_ = f32[2,128]{1,0:T(2,128)S(1)} collective-permute-done((f32[2,128]{1,0:T(2,128)S(1)}, f32[2,128]{1,0:T(2,128)S(1)}, u32[]{:S(2)}, u32[]{:S(2)}) %collective-permute-start.25) | collective-permute-done | bytes 1056 | tf_op jit(solution)/shard_map/ppermute | solution.py:268
  77.0 1.4 %collective-permute-done.24.refs_2_ = f32[2,128]{1,0:T(2,128)S(1)} collective-permute-done((f32[2,128]{1,0:T(2,128)S(1)}, f32[2,128]{1,0:T(2,128)S(1)}, u32[]{:S(2)}, u32[]{:S(2)}) %collective-permute-start.24) | collective-permute-done | bytes 1056 | tf_op jit(solution)/shard_map/ppermute | solution.py:268
  78.4 0.8 %shard_map.139 = f32[128,128]{1,0:T(8,128)} custom-call(f32[128,128]{1,0:T(8,128)S(1)} %get-tuple-element.49.x_ref, f32[2,128]{1,0:T(2,128)S(1)} %get-tuple-element.50.refs_0_, f32[2,128]{1,0:T(2,128)S(1)} %collective-permute-done.23.refs_1_, f32[2,128]{1,0:T(2,128)S(1)} %collective-permute-done.24.refs_2_, f32[2,128]{1,0:T(2,128)S(1)} %collective-permute-done.25.refs_3_, ...), custom_call_target="tpu_custom_call" | custom-call | tf_op jit(solution)/shard_map/pallas_call | solution.py:339
  (48 shorter events, 0.9 us)
Async XLA Ops:
  0.0 0.9 %copy-start.2 = (f32[128,512]{1,0:T(8,128)S(1)}, f32[128,512]{1,0:T(8,128)}, u32[]{:S(2)}) copy-start(f32[128,512]{1,0:T(8,128)} %own_ref.1) | copy-start | bytes 786436
  1.0 25.1 %copy-start.8 = (f32[512]{0:T(512)S(1)}, f32[512]{0:T(512)}, u32[]{:S(2)}) copy-start(f32[512]{0:T(512)} %param.15) | copy-start | bytes 6148
  1.0 34.6 %copy-start.4 = (f32[512,128]{1,0:T(8,128)S(1)}, f32[512,128]{1,0:T(8,128)}, u32[]{:S(2)}) copy-start(f32[512,128]{1,0:T(8,128)} %k_ref.1) | copy-start | bytes 786436
  1.0 34.6 %copy-start.5 = (f32[512,128]{1,0:T(8,128)S(1)}, f32[512,128]{1,0:T(8,128)}, u32[]{:S(2)}) copy-start(f32[512,128]{1,0:T(8,128)} %v_ref.1) | copy-start | bytes 786436
  1.0 34.6 %copy-start.6 = (f32[512,128]{1,0:T(8,128)S(1)}, f32[512,128]{1,0:T(8,128)}, u32[]{:S(2)}) copy-start(f32[512,128]{1,0:T(8,128)} %q_ref.1) | copy-start | bytes 786436
  1.0 5.4 %collective-permute-start.16 = (f32[1,32,512]{2,1,0:T(8,128)S(1)}, f32[1,32,512]{2,1,0:T(8,128)S(1)}, u32[]{:S(2)}, u32[]{:S(2)}) collective-permute-start(f32[1,32,512]{2,1,0:T(8,128)S(1)} %bitcast.8), channel_id=1, source_target_pairs={{0,1},{1,0},{2,3},{3,2},{4,5},{5,4},{6,7},{7,6},{8,9},{9,8},{10,11... | collective-permute-start | bytes 196616 | tf_op jit(solution)/shard_map/ppermute | solution.py:268
  6.4 8.3 %collective-permute-start.17 = (f32[2,32,512]{2,1,0:T(8,128)S(1)}, f32[2,32,512]{2,1,0:T(8,128)S(1)}, u32[]{:S(2)}, u32[]{:S(2)}) collective-permute-start(f32[2,32,512]{2,1,0:T(8,128)S(1)} %pad_maximum_fusion.2), channel_id=1, source_target_pairs={{0,2},{1,3},{2,0},{3,1},{4,6},{5,7},{6,4},{7,5},{8,10},{9,11},{10,... | collective-permute-start | bytes 393224 | tf_op jit(solution)/shard_map/ppermute | solution.py:268
  15.3 9.6 %collective-permute-start.18 = (f32[1,3,32,512]{3,2,1,0:T(8,128)}, f32[1,3,32,512]{3,2,1,0:T(8,128)}, u32[]{:S(2)}, u32[]{:S(2)}) collective-permute-start(f32[1,3,32,512]{3,2,1,0:T(8,128)} %maximum_bitcast_fusion), channel_id=1, source_target_pairs={{0,16},{4,20},{8,24},{12,28},{16,0},{20,4},{24,8},{28,12},{1,17},{... | collective-permute-start | bytes 589832 | tf_op jit(solution)/shard_map/ppermute | solution.py:268
  20.5 6.5 %collective-permute-start = (f32[128,128]{1,0:T(8,128)}, f32[128,128]{1,0:T(8,128)S(1)}, u32[]{:S(2)}, u32[]{:S(2)}) collective-permute-start(f32[128,128]{1,0:T(8,128)} %get-tuple-element.29), channel_id=1, source_target_pairs={{0,1},{1,0},{2,3},{3,2},{4,5},{5,4},{6,7},{7,6},{8,9},{9,8},{10,11... | collective-permute-start | bytes 196616 | tf_op jit(solution)/shard_map/ppermute | solution.py:268
  21.2 7.2 %collective-permute-start.1 = (f32[128,128]{1,0:T(8,128)}, f32[128,128]{1,0:T(8,128)S(1)}, u32[]{:S(2)}, u32[]{:S(2)}) collective-permute-start(f32[128,128]{1,0:T(8,128)} %get-tuple-element.30), channel_id=1, source_target_pairs={{0,2},{1,3},{2,0},{3,1},{4,6},{5,7},{6,4},{7,5},{8,10},{9,11},{10,... | collective-permute-start | bytes 196616 | tf_op jit(solution)/shard_map/ppermute | solution.py:268
  24.6 33.2 %copy-start.3 = (f32[128,512]{1,0:T(8,128)S(1)}, f32[128,512]{1,0:T(8,128)}, u32[]{:S(2)}) copy-start(f32[128,512]{1,0:T(8,128)} %own_ref.1) | copy-start | bytes 786436
  24.6 6.4 %collective-permute-start.2 = (f32[128,128]{1,0:T(8,128)}, f32[128,128]{1,0:T(8,128)S(1)}, u32[]{:S(2)}, u32[]{:S(2)}) collective-permute-start(f32[128,128]{1,0:T(8,128)} %get-tuple-element.31), channel_id=1, source_target_pairs={{0,3},{1,2},{2,1},{3,0},{4,7},{5,6},{6,5},{7,4},{8,11},{9,10},{10,... | collective-permute-start | bytes 196616 | tf_op jit(solution)/shard_map/ppermute | solution.py:268
  26.0 30.8 %collective-permute-start.19 = (f32[2,3,32,512]{3,2,1,0:T(8,128)S(1)}, f32[2,3,32,512]{3,2,1,0:T(8,128)S(1)}, u32[]{:S(2)}, u32[]{:S(2)}) collective-permute-start(f32[2,3,32,512]{3,2,1,0:T(8,128)S(1)} %pad_maximum_fusion.1), channel_id=1, source_target_pairs={{0,4},{4,0},{8,12},{12,8},{16,20},{20,16},{24,28},{28,24},{1,5},{5... | collective-permute-start | bytes 1179656 | tf_op jit(solution)/shard_map/ppermute | solution.py:268
  26.1 0.8 %copy-start.7 = (f32[128,128]{1,0:T(8,128)S(1)}, f32[128,128]{1,0:T(8,128)}, u32[]{:S(2)}) copy-start(f32[128,128]{1,0:T(8,128)} %get-tuple-element.28.x_ref) | copy-start | bytes 196612
  31.0 30.9 %copy-start.9 = (f32[512]{0:T(512)S(1)}, f32[512]{0:T(512)}, u32[]{:S(2)}) copy-start(f32[512]{0:T(512)} %param.20) | copy-start | bytes 6148
  31.0 30.9 %copy-start.10 = (f32[512]{0:T(512)S(1)}, f32[512]{0:T(512)}, u32[]{:S(2)}) copy-start(f32[512]{0:T(512)} %param.21) | copy-start | bytes 6148
  31.0 6.3 %collective-permute-start.5 = (f32[128,128]{1,0:T(8,128)S(1)}, f32[128,128]{1,0:T(8,128)S(1)}, u32[]{:S(2)}, u32[]{:S(2)}) collective-permute-start(f32[128,128]{1,0:T(8,128)S(1)} %shard_map.128.refs_0_.refs_4_), channel_id=1, source_target_pairs={{0,3},{1,2},{2,1},{3,0},{4,7},{5,6},{6,5},{7,4},{8,11},{9,10},{10,... | collective-permute-start | bytes 196616 | tf_op jit(solution)/shard_map/ppermute | solution.py:268
  31.8 6.6 %collective-permute-start.4 = (f32[128,128]{1,0:T(8,128)S(1)}, f32[128,128]{1,0:T(8,128)S(1)}, u32[]{:S(2)}, u32[]{:S(2)}) collective-permute-start(f32[128,128]{1,0:T(8,128)S(1)} %shard_map.128.refs_0_.refs_4_), channel_id=1, source_target_pairs={{0,2},{1,3},{2,0},{3,1},{4,6},{5,7},{6,4},{7,5},{8,10},{9,11},{10,... | collective-permute-start | bytes 196616 | tf_op jit(solution)/shard_map/ppermute | solution.py:268
  31.8 6.6 %collective-permute-start.3 = (f32[128,128]{1,0:T(8,128)S(1)}, f32[128,128]{1,0:T(8,128)S(1)}, u32[]{:S(2)}, u32[]{:S(2)}) collective-permute-start(f32[128,128]{1,0:T(8,128)S(1)} %shard_map.128.refs_0_.refs_4_), channel_id=1, source_target_pairs={{0,1},{1,0},{2,3},{3,2},{4,5},{5,4},{6,7},{7,6},{8,9},{9,8},{10,11... | collective-permute-start | bytes 196616 | tf_op jit(solution)/shard_map/ppermute | solution.py:268
  38.7 6.0 %collective-permute-start.8 = (f32[128,256]{1,0:T(8,128)S(1)}, f32[128,256]{1,0:T(8,128)S(1)}, u32[]{:S(2)}, u32[]{:S(2)}) collective-permute-start(f32[128,256]{1,0:T(8,128)S(1)} %shard_map.131.refs_0_), channel_id=1, source_target_pairs={{0,24},{4,28},{8,16},{12,20},{16,8},{20,12},{24,0},{28,4},{1,25},{... | collective-permute-start | bytes 393224 | tf_op jit(solution)/shard_map/ppermute | solution.py:268
  40.2 5.8 %collective-permute-start.7 = (f32[128,256]{1,0:T(8,128)S(1)}, f32[128,256]{1,0:T(8,128)S(1)}, u32[]{:S(2)}, u32[]{:S(2)}) collective-permute-start(f32[128,256]{1,0:T(8,128)S(1)} %shard_map.131.refs_0_), channel_id=1, source_target_pairs={{0,16},{4,20},{8,24},{12,28},{16,0},{20,4},{24,8},{28,12},{1,17},{... | collective-permute-start | bytes 393224 | tf_op jit(solution)/shard_map/ppermute | solution.py:268
  41.7 5.0 %collective-permute-start.6 = (f32[128,256]{1,0:T(8,128)S(1)}, f32[128,256]{1,0:T(8,128)S(1)}, u32[]{:S(2)}, u32[]{:S(2)}) collective-permute-start(f32[128,256]{1,0:T(8,128)S(1)} %shard_map.131.refs_0_), channel_id=1, source_target_pairs={{0,8},{4,12},{8,0},{12,4},{16,24},{20,28},{24,16},{28,20},{1,9},{5... | collective-permute-start | bytes 393224 | tf_op jit(solution)/shard_map/ppermute | solution.py:268
  42.2 7.5 %collective-permute-start.9 = (f32[128,256]{1,0:T(8,128)S(1)}, f32[128,256]{1,0:T(8,128)S(1)}, u32[]{:S(2)}, u32[]{:S(2)}) collective-permute-start(f32[128,256]{1,0:T(8,128)S(1)} %shard_map.131.refs_0_), channel_id=1, source_target_pairs={{0,4},{4,0},{8,12},{12,8},{16,20},{20,16},{24,28},{28,24},{1,5},{5... | collective-permute-start | bytes 393224 | tf_op jit(solution)/shard_map/ppermute | solution.py:268
  44.7 6.2 %collective-permute-start.12 = (f32[128,256]{1,0:T(8,128)S(1)}, f32[128,256]{1,0:T(8,128)S(1)}, u32[]{:S(2)}, u32[]{:S(2)}) collective-permute-start(f32[128,256]{1,0:T(8,128)S(1)} %collective-permute-done.8.refs_3_), channel_id=1, source_target_pairs={{0,4},{4,0},{8,12},{12,8},{16,20},{20,16},{24,28},{28,24},{1,5},{5... | collective-permute-start | bytes 393224 | tf_op jit(solution)/shard_map/ppermute | solution.py:268
  46.0 4.9 %collective-permute-start.11 = (f32[128,256]{1,0:T(8,128)S(1)}, f32[128,256]{1,0:T(8,128)S(1)}, u32[]{:S(2)}, u32[]{:S(2)}) collective-permute-start(f32[128,256]{1,0:T(8,128)S(1)} %collective-permute-done.7.refs_2_), channel_id=1, source_target_pairs={{0,4},{4,0},{8,12},{12,8},{16,20},{20,16},{24,28},{28,24},{1,5},{5... | collective-permute-start | bytes 393224 | tf_op jit(solution)/shard_map/ppermute | solution.py:268
  46.7 4.3 %collective-permute-start.10 = (f32[128,256]{1,0:T(8,128)S(1)}, f32[128,256]{1,0:T(8,128)S(1)}, u32[]{:S(2)}, u32[]{:S(2)}) collective-permute-start(f32[128,256]{1,0:T(8,128)S(1)} %collective-permute-done.6.refs_1_), channel_id=1, source_target_pairs={{0,4},{4,0},{8,12},{12,8},{16,20},{20,16},{24,28},{28,24},{1,5},{5... | collective-permute-start | bytes 393224 | tf_op jit(solution)/shard_map/ppermute | solution.py:268
  46.7 1.2 %copy-start = (f32[512,512]{1,0:T(8,128)S(1)}, f32[512,512]{1,0:T(8,128)}, u32[]{:S(2)}) copy-start(f32[512,512]{1,0:T(8,128)} %refs_0_.1) | copy-start | bytes 3145732
  47.9 1.2 %copy-start.1 = (f32[512,512]{1,0:T(8,128)S(1)}, f32[512,512]{1,0:T(8,128)}, u32[]{:S(2)}) copy-start(f32[512,512]{1,0:T(8,128)} %refs_1_.1) | copy-start | bytes 3145732
  49.4 29.0 %copy-start.11 = (f32[512]{0:T(512)S(1)}, f32[512]{0:T(512)}, u32[]{:S(2)}) copy-start(f32[512]{0:T(512)} %param.24) | copy-start | bytes 6148
  49.4 29.0 %copy-start.12 = (f32[512]{0:T(512)S(1)}, f32[512]{0:T(512)}, u32[]{:S(2)}) copy-start(f32[512]{0:T(512)} %param.25) | copy-start | bytes 6148
  52.3 6.9 %collective-permute-start.15 = (f32[128,128]{1,0:T(8,128)S(1)}, f32[128,128]{1,0:T(8,128)S(1)}, u32[]{:S(2)}, u32[]{:S(2)}) collective-permute-start(f32[128,128]{1,0:T(8,128)S(1)} %shard_map.133.refs_0_), channel_id=1, source_target_pairs={{0,3},{1,2},{2,1},{3,0},{4,7},{5,6},{6,5},{7,4},{8,11},{9,10},{10,... | collective-permute-start | bytes 196616 | tf_op jit(solution)/shard_map/ppermute | solution.py:268
  54.1 7.8 %collective-permute-start.14 = (f32[128,128]{1,0:T(8,128)S(1)}, f32[128,128]{1,0:T(8,128)S(1)}, u32[]{:S(2)}, u32[]{:S(2)}) collective-permute-start(f32[128,128]{1,0:T(8,128)S(1)} %shard_map.133.refs_0_), channel_id=1, source_target_pairs={{0,2},{1,3},{2,0},{3,1},{4,6},{5,7},{6,4},{7,5},{8,10},{9,11},{10,... | collective-permute-start | bytes 196616 | tf_op jit(solution)/shard_map/ppermute | solution.py:268
  55.2 6.7 %collective-permute-start.13 = (f32[128,128]{1,0:T(8,128)S(1)}, f32[128,128]{1,0:T(8,128)S(1)}, u32[]{:S(2)}, u32[]{:S(2)}) collective-permute-start(f32[128,128]{1,0:T(8,128)S(1)} %shard_map.133.refs_0_), channel_id=1, source_target_pairs={{0,1},{1,0},{2,3},{3,2},{4,5},{5,4},{6,7},{7,6},{8,9},{9,8},{10,11... | collective-permute-start | bytes 196616 | tf_op jit(solution)/shard_map/ppermute | solution.py:268
  63.1 4.8 %collective-permute-start.20 = (f32[128,128]{1,0:T(8,128)S(1)}, f32[128,128]{1,0:T(8,128)S(1)}, u32[]{:S(2)}, u32[]{:S(2)}) collective-permute-start(f32[128,128]{1,0:T(8,128)S(1)} %get-tuple-element.46), channel_id=1, source_target_pairs={{0,1},{1,0},{2,3},{3,2},{4,5},{5,4},{6,7},{7,6},{8,9},{9,8},{10,11... | collective-permute-start | bytes 196616 | tf_op jit(solution)/shard_map/ppermute | solution.py:268
  63.2 8.3 %collective-permute-start.21 = (f32[128,128]{1,0:T(8,128)S(1)}, f32[128,128]{1,0:T(8,128)S(1)}, u32[]{:S(2)}, u32[]{:S(2)}) collective-permute-start(f32[128,128]{1,0:T(8,128)S(1)} %get-tuple-element.47), channel_id=1, source_target_pairs={{0,2},{1,3},{2,0},{3,1},{4,6},{5,7},{6,4},{7,5},{8,10},{9,11},{10,... | collective-permute-start | bytes 196616 | tf_op jit(solution)/shard_map/ppermute | solution.py:268
  65.1 6.4 %collective-permute-start.22 = (f32[128,128]{1,0:T(8,128)S(1)}, f32[128,128]{1,0:T(8,128)S(1)}, u32[]{:S(2)}, u32[]{:S(2)}) collective-permute-start(f32[128,128]{1,0:T(8,128)S(1)} %get-tuple-element.48), channel_id=1, source_target_pairs={{0,3},{1,2},{2,1},{3,0},{4,7},{5,6},{6,5},{7,4},{8,11},{9,10},{10,... | collective-permute-start | bytes 196616 | tf_op jit(solution)/shard_map/ppermute | solution.py:268
  71.6 5.4 %collective-permute-start.25 = (f32[2,128]{1,0:T(2,128)S(1)}, f32[2,128]{1,0:T(2,128)S(1)}, u32[]{:S(2)}, u32[]{:S(2)}) collective-permute-start(f32[2,128]{1,0:T(2,128)S(1)} %get-tuple-element.50.refs_0_), channel_id=1, source_target_pairs={{0,3},{1,2},{2,1},{3,0},{4,7},{5,6},{6,5},{7,4},{8,11},{9,10},{10,... | collective-permute-start | bytes 3080 | tf_op jit(solution)/shard_map/ppermute | solution.py:268
  73.9 4.5 %collective-permute-start.24 = (f32[2,128]{1,0:T(2,128)S(1)}, f32[2,128]{1,0:T(2,128)S(1)}, u32[]{:S(2)}, u32[]{:S(2)}) collective-permute-start(f32[2,128]{1,0:T(2,128)S(1)} %get-tuple-element.50.refs_0_), channel_id=1, source_target_pairs={{0,2},{1,3},{2,0},{3,1},{4,6},{5,7},{6,4},{7,5},{8,10},{9,11},{10,... | collective-permute-start | bytes 3080 | tf_op jit(solution)/shard_map/ppermute | solution.py:268
  74.4 4.0 %collective-permute-start.23 = (f32[2,128]{1,0:T(2,128)S(1)}, f32[2,128]{1,0:T(2,128)S(1)}, u32[]{:S(2)}, u32[]{:S(2)}) collective-permute-start(f32[2,128]{1,0:T(2,128)S(1)} %get-tuple-element.50.refs_0_), channel_id=1, source_target_pairs={{0,1},{1,0},{2,3},{3,2},{4,5},{5,4},{6,7},{7,6},{8,9},{9,8},{10,11... | collective-permute-start | bytes 3080 | tf_op jit(solution)/shard_map/ppermute | solution.py:268

commit v7 on v6

--- a/solution.py
+++ b/solution.py
@@ -180,33 +180,44 @@
     out[...] = dot3_split(jnp.concatenate([block[...] for block in blocks], 1), hi[...], lo[...])
 
 
+def by_head(stacked, heads):
+    rows = stacked.shape[0] // heads
+    lane = lax.broadcasted_iota(jnp.int32, (rows, stacked.shape[1]), 1) // DH
+    out = stacked[:rows]
+    for head in range(1, heads):
+        out = jnp.where(lane == head, stacked[head * rows : (head + 1) * rows], out)
+    return out
+
+
 def attend_kernel(q_ref, *refs, merge):
     if merge:
         (acc_a, top_a, sum_a), pieces, out = refs[:3], refs[3:-1], refs[-1]
     else:
         pieces, (acc_out, top_out, sum_out) = refs[:-3], refs[-3:]
-    heads_width = q_ref.shape[1]
-    for head in range(heads_width // DH):
-        cols = slice(head * DH, (head + 1) * DH)
-        vcols = slice(heads_width + head * DH, heads_width + (head + 1) * DH)
-        query = q_ref[:, cols]
-        keys = jnp.concatenate([piece[:, cols] for piece in pieces], 0)
-        values = jnp.concatenate([piece[:, vcols] for piece in pieces], 0)
-        scores = dot3(query, keys, ((1,), (1,)))
-        top = jnp.max(scores, axis=1, keepdims=True)
-        if merge:
-            before = top_a[:, cols][:, :1]
-            top = jnp.maximum(top, before)
-        weights = jnp.exp(scores - top)
-        total = jnp.sum(weights, axis=1, keepdims=True)
-        acc = dot3(weights, values)
-        if merge:
-            fade = jnp.exp(before - top)
-            out[:, cols] = (acc + acc_a[:, cols] * fade) / (total + sum_a[:, cols][:, :1] * fade)
-        else:
-            acc_out[:, cols] = acc
-            top_out[:, cols] = jnp.broadcast_to(top, acc.shape)
-            sum_out[:, cols] = jnp.broadcast_to(total, acc.shape)
+    rows, wide = q_ref.shape
+    heads = wide // DH
+    query = q_ref[...]
+    lane = lax.broadcasted_iota(jnp.int32, query.shape, 1) // DH
+    stacked = jnp.concatenate([jnp.where(lane == head, query, 0.0) for head in range(heads)], 0)
+    keys = jnp.concatenate([piece[:, :wide] for piece in pieces], 0)
+    v_hi, v_lo = split(jnp.concatenate([piece[:, wide:] for piece in pieces], 0))
+    scores = dot3(stacked, keys, ((1,), (1,)))
+    top = jnp.max(scores, axis=1, keepdims=True)
+    w_hi, w_lo = split(jnp.exp(scores - top))
+    along = ((1,), (0,))
+    both = mm(jnp.concatenate([w_hi, w_lo], 0), jnp.concatenate([v_hi, jnp.ones_like(v_hi)], 1), along)
+    both = both[: heads * rows] + both[heads * rows :]
+    acc = by_head(both[:, :wide] + mm(w_hi, v_lo, along), heads)
+    total = by_head(both[:, wide:], heads)
+    top = by_head(jnp.broadcast_to(top, (heads * rows, wide)), heads)
+    if merge:
+        high = jnp.maximum(top, top_a[...])
+        fade_a, fade = jnp.exp(top_a[...] - high), jnp.exp(top - high)
+        out[...] = (acc * fade + acc_a[...] * fade_a) / (total * fade + sum_a[...] * fade_a)
+    else:
+        acc_out[...] = acc
+        top_out[...] = top
+        sum_out[...] = total
 
 
 def normalise(x, gain, bias):
@@ -282,13 +293,21 @@
 
 def gather_pieces(piece):
     size = lax.axis_size("var")
-    if size > 8:
+    if size != 8:
         whole = lax.all_gather(piece, "var", axis=0, tiled=True)
         cut = whole.shape[0] // 2
         return [whole[:cut]], [whole[cut:]]
-    far = [piece] + [send(piece, "var", k) for k in range(2, size, 2)]
-    near = [send(each, "var", 1) for each in far]
-    return far + near[:1], near[1:]
+
+    def hop(x, even, odd):
+        return lax.ppermute(x, "var", [(i, i ^ (odd if i & 1 else even)) for i in range(size)])
+
+    got_a = hop(piece, 4, 2)
+    got_b = hop(piece, 2, 4)
+    got_ab = hop(got_a, 2, 4)
+    swap, swap_a, swap_b, swap_ab = (
+        hop(each, 1, 1) for each in (piece, got_a, got_b, got_ab)
+    )
+    return [piece, got_a, got_b, swap], [swap_a, swap_b, got_ab, swap_ab]
 
 
 def on_device(

time: 79.6 us -> 81 us (1.018)
  waiting for transfers between devices: 28.8 us -> 30.4 us
  Pallas kernels: 9.5 us -> 8.69 us
    ppermute x0 -> x7, waiting for transfers between devices: none -> 4.99 us  [hop(): lax.ppermute(x, 'var', [(i, i ^ (odd if i & 1 else even)) for i in range(...]
    ppermute x0 -> x7, starting transfers between devices: none -> 4.12 us  [hop(): lax.ppermute(x, 'var', [(i, i ^ (odd if i & 1 else even)) for i in range(...]
    ppermute x26 -> x19, starting transfers between devices: 33.7 us -> 30.1 us  [send(): return lax.ppermute(x, axis, [(i, i ^ offset) for i in range(size)])]
    ppermute x26 -> x19, waiting for transfers between devices: 28.8 us -> 25.4 us  [send(): return lax.ppermute(x, axis, [(i, i ^ offset) for i in range(size)])]
  transfers between devices with their start and end apart: 26 -> 26, of which waited for: 15 -> 14; matrix products, arithmetic and copies ran while one was open for 3% -> 3% of each run, Pallas kernels for 9% -> 8%
where the time goes in v7:
time: 81 us; the launch traced here: 80.7 us
  starting transfers between devices  34.2 us (42%)
  waiting for transfers between devices  30.4 us (38%)
  Pallas kernels  8.69 us (11%)
  local copies, waits for them, and re-layouts  4.28 us (5%)
  other arithmetic  2.83 us (3%)
    ppermute x19, starting transfers between devices, send(): return lax.ppermute(x, axis, [(i, i ^ offset) for i in range(size)])  30.1 us
    ppermute x19, waiting for transfers between devices, send(): return lax.ppermute(x, axis, [(i, i ^ offset) for i in range(size)])  25.4 us
    ppermute x7, waiting for transfers between devices, hop(): lax.ppermute(x, 'var', [(i, i ^ (odd if i & 1 else even)) for i in range(...  4.99 us
    unnamed x26, local copies, waits for them, and re-layouts  4.28 us
    ppermute x7, starting transfers between devices, hop(): lax.ppermute(x, 'var', [(i, i ^ (odd if i & 1 else even)) for i in range(...  4.12 us
    pallas_call x1, Pallas kernels, embed(): pl.pallas_call(functools.partial(embed_kernel, count), out_shape=[shape(r...  3.61 us
    concatenate x2, other arithmetic, on_device(): rest = jnp.concatenate([rest, send(rest, 'var', 1 << bit)], 0)  2.12 us
  transfers between devices with their start and end apart: 26, of which 14 were waited for; matrix products, arithmetic and copies ran while one was open for 3% of the time, Pallas kernels for 8%

profile of v7, /device:TPU:0, one launch (start us, length us, event | category | flops | bytes accessed | tf_op | source)
XLA Modules:
  0.0 80.7 jit_solution(2722638626139735266)
XLA Ops:
  0.0 0.9 %copy-done.2 = f32[128,512]{1,0:T(8,128)S(1)} copy-done((f32[128,512]{1,0:T(8,128)S(1)}, f32[128,512]{1,0:T(8,128)}, u32[]{:S(2)}) %copy-start.2) | copy-done | bytes 262168
  1.0 3.1 %collective-permute-start.16 = (f32[1,32,512]{2,1,0:T(8,128)S(1)}, f32[1,32,512]{2,1,0:T(8,128)S(1)}, u32[]{:S(2)}, u32[]{:S(2)}) collective-permute-start(f32[1,32,512]{2,1,0:T(8,128)S(1)} %bitcast.8), channel_id=1, source_target_pairs={{0,1},{1,0},{2,3},{3,2},{4,5},{5,4},{6,7},{7,6},{8,9},{9,8},{10,11... | collective-permute-start | bytes 196616 | tf_op jit(solution)/shard_map/ppermute | solution.py:279
  4.1 2.2 %collective-permute-done.16 = f32[1,32,512]{2,1,0:T(8,128)S(1)} collective-permute-done((f32[1,32,512]{2,1,0:T(8,128)S(1)}, f32[1,32,512]{2,1,0:T(8,128)S(1)}, u32[]{:S(2)}, u32[]{:S(2)}) %collective-permute-start.16) | collective-permute-done | bytes 65568 | tf_op jit(solution)/shard_map/ppermute | solution.py:279
  6.4 3.1 %collective-permute-start.17 = (f32[2,32,512]{2,1,0:T(8,128)S(1)}, f32[2,32,512]{2,1,0:T(8,128)S(1)}, u32[]{:S(2)}, u32[]{:S(2)}) collective-permute-start(f32[2,32,512]{2,1,0:T(8,128)S(1)} %pad_maximum_fusion.2), channel_id=1, source_target_pairs={{0,2},{1,3},{2,0},{3,1},{4,6},{5,7},{6,4},{7,5},{8,10},{9,11},{10,... | collective-permute-start | bytes 393224 | tf_op jit(solution)/shard_map/ppermute | solution.py:279
  9.5 5.2 %collective-permute-done.17 = f32[2,32,512]{2,1,0:T(8,128)S(1)} collective-permute-done((f32[2,32,512]{2,1,0:T(8,128)S(1)}, f32[2,32,512]{2,1,0:T(8,128)S(1)}, u32[]{:S(2)}, u32[]{:S(2)}) %collective-permute-start.17) | collective-permute-done | bytes 131104 | tf_op jit(solution)/shard_map/ppermute | solution.py:279
  14.6 0.7 maximum_bitcast_fusion
  15.3 1.6 %collective-permute-start.18 = (f32[1,3,32,512]{3,2,1,0:T(8,128)}, f32[1,3,32,512]{3,2,1,0:T(8,128)}, u32[]{:S(2)}, u32[]{:S(2)}) collective-permute-start(f32[1,3,32,512]{3,2,1,0:T(8,128)} %maximum_bitcast_fusion), channel_id=1, source_target_pairs={{0,16},{4,20},{8,24},{12,28},{16,0},{20,4},{24,8},{28,12},{1,17},{... | collective-permute-start | bytes 589832 | tf_op jit(solution)/shard_map/ppermute | solution.py:279
  16.9 3.6 %embed.1 = (f32[128,128]{1,0:T(8,128)}, f32[128,128]{1,0:T(8,128)}, f32[128,128]{1,0:T(8,128)}, f32[128,128]{1,0:T(8,128)}) custom-call(f32[128,2048]{1,0:T(8,128)} %x_hbm.1, f32[2048,512]{1,0:T(8,128)} %w_hbm.1), custom_call_target="tpu_custom_call" | custom-call | flops 805306368 | bytes 5242880 | tf_op jit(solution)/shard_map/embed/pallas_call | solution.py:111
  20.5 0.7 collective-permute-start
  21.2 3.4 %collective-permute-start.1 = (f32[128,128]{1,0:T(8,128)}, f32[128,128]{1,0:T(8,128)S(1)}, u32[]{:S(2)}, u32[]{:S(2)}) collective-permute-start(f32[128,128]{1,0:T(8,128)} %get-tuple-element.30), channel_id=1, source_target_pairs={{0,2},{1,3},{2,0},{3,1},{4,6},{5,7},{6,4},{7,5},{8,10},{9,11},{10,... | collective-permute-start | bytes 196616 | tf_op jit(solution)/shard_map/ppermute | solution.py:279
  24.6 0.3 collective-permute-start.2
  25.0 0.8 %copy-done.7 = f32[128,128]{1,0:T(8,128)S(1)} copy-done((f32[128,128]{1,0:T(8,128)S(1)}, f32[128,128]{1,0:T(8,128)}, u32[]{:S(2)}) %copy-start.7) | copy-done | bytes 65560
  25.8 2.6 %collective-permute-done.1.refs_2_ = f32[128,128]{1,0:T(8,128)S(1)} collective-permute-done((f32[128,128]{1,0:T(8,128)}, f32[128,128]{1,0:T(8,128)S(1)}, u32[]{:S(2)}, u32[]{:S(2)}) %collective-permute-start.1) | collective-permute-done | bytes 65568 | tf_op jit(solution)/shard_map/ppermute | solution.py:279
  28.5 2.5 %collective-permute-done.2.refs_3_ = f32[128,128]{1,0:T(8,128)S(1)} collective-permute-done((f32[128,128]{1,0:T(8,128)}, f32[128,128]{1,0:T(8,128)S(1)}, u32[]{:S(2)}, u32[]{:S(2)}) %collective-permute-start.2) | collective-permute-done | bytes 65568 | tf_op jit(solution)/shard_map/ppermute | solution.py:279
  31.0 0.8 collective-permute-start.5
  31.8 3.6 %collective-permute-start.3 = (f32[128,128]{1,0:T(8,128)S(1)}, f32[128,128]{1,0:T(8,128)S(1)}, u32[]{:S(2)}, u32[]{:S(2)}) collective-permute-start(f32[128,128]{1,0:T(8,128)S(1)} %shard_map.128.refs_0_.refs_4_), channel_id=1, source_target_pairs={{0,1},{1,0},{2,3},{3,2},{4,5},{5,4},{6,7},{7,6},{8,9},{9,8},{10,11... | collective-permute-start | bytes 196616 | tf_op jit(solution)/shard_map/ppermute | solution.py:279
  35.6 1.7 %collective-permute-done.5.refs_3_.refs_7_ = f32[128,128]{1,0:T(8,128)S(1)} collective-permute-done((f32[128,128]{1,0:T(8,128)S(1)}, f32[128,128]{1,0:T(8,128)S(1)}, u32[]{:S(2)}, u32[]{:S(2)}) %collective-permute-start.5) | collective-permute-done | bytes 65568 | tf_op jit(solution)/shard_map/ppermute | solution.py:279
  37.2 1.1 %collective-permute-done.4.refs_2_.refs_6_ = f32[128,128]{1,0:T(8,128)S(1)} collective-permute-done((f32[128,128]{1,0:T(8,128)S(1)}, f32[128,128]{1,0:T(8,128)S(1)}, u32[]{:S(2)}, u32[]{:S(2)}) %collective-permute-start.4) | collective-permute-done | bytes 65568 | tf_op jit(solution)/shard_map/ppermute | solution.py:279
  38.4 0.3 shard_map.131.refs_0_
  38.7 0.6 collective-permute-start.6
  39.2 1.0 %pad_maximum_fusion.1 = f32[2,3,32,512]{3,2,1,0:T(8,128)S(1)} fusion(f32[1,3,32,512]{3,2,1,0:T(8,128)} %collective-permute-done.18, f32[1,3,32,512]{3,2,1,0:T(8,128)} %maximum_bitcast_fusion), kind=kLoop, calls=%fused_computation.1 | loop fusion | flops 98304 | bytes 786432 | tf_op jit(solution)/shard_map/concatenate | solution.py:337
  40.4 1.6 %collective-permute-start.7 = (f32[128,256]{1,0:T(8,128)S(1)}, f32[128,256]{1,0:T(8,128)S(1)}, u32[]{:S(2)}, u32[]{:S(2)}) collective-permute-start(f32[128,256]{1,0:T(8,128)S(1)} %shard_map.131.refs_0_), channel_id=1, source_target_pairs={{0,8},{4,20},{8,0},{12,28},{16,24},{20,4},{24,16},{28,12},{1,9},{5... | collective-permute-start | bytes 393224 | tf_op jit(solution)/shard_map/ppermute | solution.py:302
  41.9 2.0 %collective-permute-done.6.refs_1_ = f32[128,256]{1,0:T(8,128)S(1)} collective-permute-done((f32[128,256]{1,0:T(8,128)S(1)}, f32[128,256]{1,0:T(8,128)S(1)}, u32[]{:S(2)}, u32[]{:S(2)}) %collective-permute-start.6) | collective-permute-done | bytes 131104 | tf_op jit(solution)/shard_map/ppermute | solution.py:302
  43.9 1.5 %collective-permute-start.11 = (f32[128,256]{1,0:T(8,128)S(1)}, f32[128,256]{1,0:T(8,128)S(1)}, u32[]{:S(2)}, u32[]{:S(2)}) collective-permute-start(f32[128,256]{1,0:T(8,128)S(1)} %collective-permute-done.6.refs_1_), channel_id=1, source_target_pairs={{0,8},{4,20},{8,0},{12,28},{16,24},{20,4},{24,16},{28,12},{1,9},{5... | collective-permute-start | bytes 393224 | tf_op jit(solution)/shard_map/ppermute | solution.py:302
  45.4 0.5 collective-permute-start.9
  45.9 3.0 %collective-permute-done.11.refs_5_ = f32[128,256]{1,0:T(8,128)S(1)} collective-permute-done((f32[128,256]{1,0:T(8,128)S(1)}, f32[128,256]{1,0:T(8,128)S(1)}, u32[]{:S(2)}, u32[]{:S(2)}) %collective-permute-start.11) | collective-permute-done | bytes 131104 | tf_op jit(solution)/shard_map/ppermute | solution.py:302
  48.9 1.2 %copy-done = f32[512,512]{1,0:T(8,128)S(1)} copy-done((f32[512,512]{1,0:T(8,128)S(1)}, f32[512,512]{1,0:T(8,128)}, u32[]{:S(2)}) %copy-start) | copy-done | bytes 1048600
  50.1 1.2 %copy-done.1 = f32[512,512]{1,0:T(8,128)S(1)} copy-done((f32[512,512]{1,0:T(8,128)S(1)}, f32[512,512]{1,0:T(8,128)}, u32[]{:S(2)}) %copy-start.1) | copy-done | bytes 1048600
  51.3 0.3 shard_map.136
  51.9 0.9 %shard_map.132 = (f32[128,128]{1,0:T(8,128)S(1)}, f32[128,128]{1,0:T(8,128)S(1)}, f32[128,128]{1,0:T(8,128)S(1)}) custom-call(f32[128,128]{1,0:T(8,128)S(1)} %shard_map.130.q_ref, f32[128,256]{1,0:T(8,128)S(1)} %shard_map.131.refs_0_, f32[128,256]{1,0:T(8,128)S(1)} %collective-permute-done.6.refs_1_, f32[128,256]{1,0:T(8,128)S(1)} %collective-permute-done.7.refs_2_, ...), custom_call_target="tpu_custom_call" | custom-call | tf_op jit(solution)/shard_map/pallas_call | solution.py:346
  52.8 0.9 %shard_map.133.refs_0_ = f32[128,128]{1,0:T(8,128)S(1)} custom-call(f32[128,128]{1,0:T(8,128)S(1)} %shard_map.130.q_ref, f32[128,128]{1,0:T(8,128)S(1)} %get-tuple-element.36.refs_0_, f32[128,128]{1,0:T(8,128)S(1)} %get-tuple-element.37.refs_1_, f32[128,128]{1,0:T(8,128)S(1)} %get-tuple-element.38.refs_2_, f32[128,256]{1,0:T(8,128)S(1)} %collective-permute-done.9.refs_3_, ...), custom_call_target="tpu_custom_call" | custom-call | tf_op jit(solution)/shard_map/pallas_call | solution.py:349
  53.7 1.7 %collective-permute-start.15 = (f32[128,128]{1,0:T(8,128)S(1)}, f32[128,128]{1,0:T(8,128)S(1)}, u32[]{:S(2)}, u32[]{:S(2)}) collective-permute-start(f32[128,128]{1,0:T(8,128)S(1)} %shard_map.133.refs_0_), channel_id=1, source_target_pairs={{0,3},{1,2},{2,1},{3,0},{4,7},{5,6},{6,5},{7,4},{8,11},{9,10},{10,... | collective-permute-start | bytes 196616 | tf_op jit(solution)/shard_map/ppermute | solution.py:279
  55.5 1.1 %collective-permute-start.14 = (f32[128,128]{1,0:T(8,128)S(1)}, f32[128,128]{1,0:T(8,128)S(1)}, u32[]{:S(2)}, u32[]{:S(2)}) collective-permute-start(f32[128,128]{1,0:T(8,128)S(1)} %shard_map.133.refs_0_), channel_id=1, source_target_pairs={{0,2},{1,3},{2,0},{3,1},{4,6},{5,7},{6,4},{7,5},{8,10},{9,11},{10,... | collective-permute-start | bytes 196616 | tf_op jit(solution)/shard_map/ppermute | solution.py:279
  56.6 1.6 %collective-permute-start.13 = (f32[128,128]{1,0:T(8,128)S(1)}, f32[128,128]{1,0:T(8,128)S(1)}, u32[]{:S(2)}, u32[]{:S(2)}) collective-permute-start(f32[128,128]{1,0:T(8,128)S(1)} %shard_map.133.refs_0_), channel_id=1, source_target_pairs={{0,1},{1,0},{2,3},{3,2},{4,5},{5,4},{6,7},{7,6},{8,9},{9,8},{10,11... | collective-permute-start | bytes 196616 | tf_op jit(solution)/shard_map/ppermute | solution.py:279
  58.2 1.1 %pad_maximum_fusion.rest_ref = f32[4,3,32,512]{3,2,1,0:T(8,128)S(1)} fusion(f32[2,3,32,512]{3,2,1,0:T(8,128)S(1)} %collective-permute-done.19, f32[1,3,32,512]{3,2,1,0:T(8,128)} %collective-permute-done.18, f32[1,3,32,512]{3,2,1,0:T(8,128)} %maximum_bitcast_fusion), kind=kLoop, calls=%fused_computation | loop fusion | flops 393216 | bytes 1572864 | tf_op jit(solution)/shard_map/concatenate | solution.py:337
  59.4 1.2 %collective-permute-done.15.refs_3_ = f32[128,128]{1,0:T(8,128)S(1)} collective-permute-done((f32[128,128]{1,0:T(8,128)S(1)}, f32[128,128]{1,0:T(8,128)S(1)}, u32[]{:S(2)}, u32[]{:S(2)}) %collective-permute-start.15) | collective-permute-done | bytes 65568 | tf_op jit(solution)/shard_map/ppermute | solution.py:279
  60.7 2.6 %collective-permute-done.14.refs_2_ = f32[128,128]{1,0:T(8,128)S(1)} collective-permute-done((f32[128,128]{1,0:T(8,128)S(1)}, f32[128,128]{1,0:T(8,128)S(1)}, u32[]{:S(2)}, u32[]{:S(2)}) %collective-permute-start.14) | collective-permute-done | bytes 65568 | tf_op jit(solution)/shard_map/ppermute | solution.py:279
  63.3 1.2 %shard_map.137 = (f32[128,128]{1,0:T(8,128)S(1)}, f32[128,128]{1,0:T(8,128)S(1)}, f32[128,128]{1,0:T(8,128)S(1)}, f32[128,128]{1,0:T(8,128)S(1)}) custom-call(f32[128,128]{1,0:T(8,128)S(1)} %shard_map.133.refs_0_, f32[128,128]{1,0:T(8,128)S(1)} %collective-permute-done.13.refs_1_, f32[128,128]{1,0:T(8,128)S(1)} %collective-permute-done.14.refs_2_, ...), custom_call_target="tpu_custom_call" | custom-call | tf_op jit(solution)/shard_map/pallas_call | solution.py:353
  64.6 1.8 %collective-permute-start.21 = (f32[128,128]{1,0:T(8,128)S(1)}, f32[128,128]{1,0:T(8,128)S(1)}, u32[]{:S(2)}, u32[]{:S(2)}) collective-permute-start(f32[128,128]{1,0:T(8,128)S(1)} %get-tuple-element.47), channel_id=1, source_target_pairs={{0,2},{1,3},{2,0},{3,1},{4,6},{5,7},{6,4},{7,5},{8,10},{9,11},{10,... | collective-permute-start | bytes 196616 | tf_op jit(solution)/shard_map/ppermute | solution.py:279
  66.4 2.5 %collective-permute-start.22 = (f32[128,128]{1,0:T(8,128)S(1)}, f32[128,128]{1,0:T(8,128)S(1)}, u32[]{:S(2)}, u32[]{:S(2)}) collective-permute-start(f32[128,128]{1,0:T(8,128)S(1)} %get-tuple-element.48), channel_id=1, source_target_pairs={{0,3},{1,2},{2,1},{3,0},{4,7},{5,6},{6,5},{7,4},{8,11},{9,10},{10,... | collective-permute-start | bytes 196616 | tf_op jit(solution)/shard_map/ppermute | solution.py:279
  69.0 0.4 collective-permute-done.20.refs_1_
  69.4 3.5 %collective-permute-done.21.refs_2_ = f32[128,128]{1,0:T(8,128)S(1)} collective-permute-done((f32[128,128]{1,0:T(8,128)S(1)}, f32[128,128]{1,0:T(8,128)S(1)}, u32[]{:S(2)}, u32[]{:S(2)}) %collective-permute-start.21) | collective-permute-done | bytes 65568 | tf_op jit(solution)/shard_map/ppermute | solution.py:279
  73.0 2.3 %collective-permute-start.25 = (f32[2,128]{1,0:T(2,128)S(1)}, f32[2,128]{1,0:T(2,128)S(1)}, u32[]{:S(2)}, u32[]{:S(2)}) collective-permute-start(f32[2,128]{1,0:T(2,128)S(1)} %get-tuple-element.50.refs_0_), channel_id=1, source_target_pairs={{0,3},{1,2},{2,1},{3,0},{4,7},{5,6},{6,5},{7,4},{8,11},{9,10},{10,... | collective-permute-start | bytes 3080 | tf_op jit(solution)/shard_map/ppermute | solution.py:279
  75.3 0.5 collective-permute-start.24
  75.8 1.7 %collective-permute-start.23 = (f32[2,128]{1,0:T(2,128)S(1)}, f32[2,128]{1,0:T(2,128)S(1)}, u32[]{:S(2)}, u32[]{:S(2)}) collective-permute-start(f32[2,128]{1,0:T(2,128)S(1)} %get-tuple-element.50.refs_0_), channel_id=1, source_target_pairs={{0,1},{1,0},{2,3},{3,2},{4,5},{5,4},{6,7},{7,6},{8,9},{9,8},{10,11... | collective-permute-start | bytes 3080 | tf_op jit(solution)/shard_map/ppermute | solution.py:279
  77.5 1.0 %collective-permute-done.25.refs_3_ = f32[2,128]{1,0:T(2,128)S(1)} collective-permute-done((f32[2,128]{1,0:T(2,128)S(1)}, f32[2,128]{1,0:T(2,128)S(1)}, u32[]{:S(2)}, u32[]{:S(2)}) %collective-permute-start.25) | collective-permute-done | bytes 1056 | tf_op jit(solution)/shard_map/ppermute | solution.py:279
  78.5 1.3 %collective-permute-done.24.refs_2_ = f32[2,128]{1,0:T(2,128)S(1)} collective-permute-done((f32[2,128]{1,0:T(2,128)S(1)}, f32[2,128]{1,0:T(2,128)S(1)}, u32[]{:S(2)}, u32[]{:S(2)}) %collective-permute-start.24) | collective-permute-done | bytes 1056 | tf_op jit(solution)/shard_map/ppermute | solution.py:279
  79.8 0.8 %shard_map.139 = f32[128,128]{1,0:T(8,128)} custom-call(f32[128,128]{1,0:T(8,128)S(1)} %get-tuple-element.49.x_ref, f32[2,128]{1,0:T(2,128)S(1)} %get-tuple-element.50.refs_0_, f32[2,128]{1,0:T(2,128)S(1)} %collective-permute-done.23.refs_1_, f32[2,128]{1,0:T(2,128)S(1)} %collective-permute-done.24.refs_2_, f32[2,128]{1,0:T(2,128)S(1)} %collective-permute-done.25.refs_3_, ...), custom_call_target="tpu_custom_call" | custom-call | tf_op jit(solution)/shard_map/pallas_call | solution.py:358
  (48 shorter events, 0.9 us)
Async XLA Ops:
  0.0 0.9 %copy-start.2 = (f32[128,512]{1,0:T(8,128)S(1)}, f32[128,512]{1,0:T(8,128)}, u32[]{:S(2)}) copy-start(f32[128,512]{1,0:T(8,128)} %own_ref.1) | copy-start | bytes 786436
  1.0 24.0 %copy-start.8 = (f32[512]{0:T(512)S(1)}, f32[512]{0:T(512)}, u32[]{:S(2)}) copy-start(f32[512]{0:T(512)} %param.15) | copy-start | bytes 6148
  1.0 34.5 %copy-start.4 = (f32[512,128]{1,0:T(8,128)S(1)}, f32[512,128]{1,0:T(8,128)}, u32[]{:S(2)}) copy-start(f32[512,128]{1,0:T(8,128)} %k_ref.1) | copy-start | bytes 786436
  1.0 34.5 %copy-start.5 = (f32[512,128]{1,0:T(8,128)S(1)}, f32[512,128]{1,0:T(8,128)}, u32[]{:S(2)}) copy-start(f32[512,128]{1,0:T(8,128)} %v_ref.1) | copy-start | bytes 786436
  1.0 34.5 %copy-start.6 = (f32[512,128]{1,0:T(8,128)S(1)}, f32[512,128]{1,0:T(8,128)}, u32[]{:S(2)}) copy-start(f32[512,128]{1,0:T(8,128)} %q_ref.1) | copy-start | bytes 786436
  1.0 5.4 %collective-permute-start.16 = (f32[1,32,512]{2,1,0:T(8,128)S(1)}, f32[1,32,512]{2,1,0:T(8,128)S(1)}, u32[]{:S(2)}, u32[]{:S(2)}) collective-permute-start(f32[1,32,512]{2,1,0:T(8,128)S(1)} %bitcast.8), channel_id=1, source_target_pairs={{0,1},{1,0},{2,3},{3,2},{4,5},{5,4},{6,7},{7,6},{8,9},{9,8},{10,11... | collective-permute-start | bytes 196616 | tf_op jit(solution)/shard_map/ppermute | solution.py:279
  6.4 8.3 %collective-permute-start.17 = (f32[2,32,512]{2,1,0:T(8,128)S(1)}, f32[2,32,512]{2,1,0:T(8,128)S(1)}, u32[]{:S(2)}, u32[]{:S(2)}) collective-permute-start(f32[2,32,512]{2,1,0:T(8,128)S(1)} %pad_maximum_fusion.2), channel_id=1, source_target_pairs={{0,2},{1,3},{2,0},{3,1},{4,6},{5,7},{6,4},{7,5},{8,10},{9,11},{10,... | collective-permute-start | bytes 393224 | tf_op jit(solution)/shard_map/ppermute | solution.py:279
  15.3 23.9 %collective-permute-start.18 = (f32[1,3,32,512]{3,2,1,0:T(8,128)}, f32[1,3,32,512]{3,2,1,0:T(8,128)}, u32[]{:S(2)}, u32[]{:S(2)}) collective-permute-start(f32[1,3,32,512]{3,2,1,0:T(8,128)} %maximum_bitcast_fusion), channel_id=1, source_target_pairs={{0,16},{4,20},{8,24},{12,28},{16,0},{20,4},{24,8},{28,12},{1,17},{... | collective-permute-start | bytes 589832 | tf_op jit(solution)/shard_map/ppermute | solution.py:279
  20.5 5.3 %collective-permute-start = (f32[128,128]{1,0:T(8,128)}, f32[128,128]{1,0:T(8,128)S(1)}, u32[]{:S(2)}, u32[]{:S(2)}) collective-permute-start(f32[128,128]{1,0:T(8,128)} %get-tuple-element.29), channel_id=1, source_target_pairs={{0,1},{1,0},{2,3},{3,2},{4,5},{5,4},{6,7},{7,6},{8,9},{9,8},{10,11... | collective-permute-start | bytes 196616 | tf_op jit(solution)/shard_map/ppermute | solution.py:279
  21.2 7.2 %collective-permute-start.1 = (f32[128,128]{1,0:T(8,128)}, f32[128,128]{1,0:T(8,128)S(1)}, u32[]{:S(2)}, u32[]{:S(2)}) collective-permute-start(f32[128,128]{1,0:T(8,128)} %get-tuple-element.30), channel_id=1, source_target_pairs={{0,2},{1,3},{2,0},{3,1},{4,6},{5,7},{6,4},{7,5},{8,10},{9,11},{10,... | collective-permute-start | bytes 196616 | tf_op jit(solution)/shard_map/ppermute | solution.py:279
  24.6 6.3 %collective-permute-start.2 = (f32[128,128]{1,0:T(8,128)}, f32[128,128]{1,0:T(8,128)S(1)}, u32[]{:S(2)}, u32[]{:S(2)}) collective-permute-start(f32[128,128]{1,0:T(8,128)} %get-tuple-element.31), channel_id=1, source_target_pairs={{0,3},{1,2},{2,1},{3,0},{4,7},{5,6},{6,5},{7,4},{8,11},{9,10},{10,... | collective-permute-start | bytes 196616 | tf_op jit(solution)/shard_map/ppermute | solution.py:279
  25.0 0.8 %copy-start.7 = (f32[128,128]{1,0:T(8,128)S(1)}, f32[128,128]{1,0:T(8,128)}, u32[]{:S(2)}) copy-start(f32[128,128]{1,0:T(8,128)} %get-tuple-element.28.x_ref) | copy-start | bytes 196612
  25.8 33.5 %copy-start.3 = (f32[128,512]{1,0:T(8,128)S(1)}, f32[128,512]{1,0:T(8,128)}, u32[]{:S(2)}) copy-start(f32[128,512]{1,0:T(8,128)} %own_ref.1) | copy-start | bytes 786436
  31.0 6.3 %collective-permute-start.5 = (f32[128,128]{1,0:T(8,128)S(1)}, f32[128,128]{1,0:T(8,128)S(1)}, u32[]{:S(2)}, u32[]{:S(2)}) collective-permute-start(f32[128,128]{1,0:T(8,128)S(1)} %shard_map.128.refs_0_.refs_4_), channel_id=1, source_target_pairs={{0,3},{1,2},{2,1},{3,0},{4,7},{5,6},{6,5},{7,4},{8,11},{9,10},{10,... | collective-permute-start | bytes 196616 | tf_op jit(solution)/shard_map/ppermute | solution.py:279
  31.8 6.6 %collective-permute-start.4 = (f32[128,128]{1,0:T(8,128)S(1)}, f32[128,128]{1,0:T(8,128)S(1)}, u32[]{:S(2)}, u32[]{:S(2)}) collective-permute-start(f32[128,128]{1,0:T(8,128)S(1)} %shard_map.128.refs_0_.refs_4_), channel_id=1, source_target_pairs={{0,2},{1,3},{2,0},{3,1},{4,6},{5,7},{6,4},{7,5},{8,10},{9,11},{10,... | collective-permute-start | bytes 196616 | tf_op jit(solution)/shard_map/ppermute | solution.py:279
  31.8 6.6 %collective-permute-start.3 = (f32[128,128]{1,0:T(8,128)S(1)}, f32[128,128]{1,0:T(8,128)S(1)}, u32[]{:S(2)}, u32[]{:S(2)}) collective-permute-start(f32[128,128]{1,0:T(8,128)S(1)} %shard_map.128.refs_0_.refs_4_), channel_id=1, source_target_pairs={{0,1},{1,0},{2,3},{3,2},{4,5},{5,4},{6,7},{7,6},{8,9},{9,8},{10,11... | collective-permute-start | bytes 196616 | tf_op jit(solution)/shard_map/ppermute | solution.py:279
  38.4 24.9 %copy-start.9 = (f32[512]{0:T(512)S(1)}, f32[512]{0:T(512)}, u32[]{:S(2)}) copy-start(f32[512]{0:T(512)} %param.20) | copy-start | bytes 6148
  38.4 24.9 %copy-start.10 = (f32[512]{0:T(512)S(1)}, f32[512]{0:T(512)}, u32[]{:S(2)}) copy-start(f32[512]{0:T(512)} %param.21) | copy-start | bytes 6148
  38.7 5.3 %collective-permute-start.6 = (f32[128,256]{1,0:T(8,128)S(1)}, f32[128,256]{1,0:T(8,128)S(1)}, u32[]{:S(2)}, u32[]{:S(2)}) collective-permute-start(f32[128,256]{1,0:T(8,128)S(1)} %shard_map.131.refs_0_), channel_id=1, source_target_pairs={{0,16},{4,12},{8,24},{12,4},{16,0},{20,28},{24,8},{28,20},{1,17},{... | collective-permute-start | bytes 393224 | tf_op jit(solution)/shard_map/ppermute | solution.py:302
  40.3 17.9 %collective-permute-start.19 = (f32[2,3,32,512]{3,2,1,0:T(8,128)S(1)}, f32[2,3,32,512]{3,2,1,0:T(8,128)S(1)}, u32[]{:S(2)}, u32[]{:S(2)}) collective-permute-start(f32[2,3,32,512]{3,2,1,0:T(8,128)S(1)} %pad_maximum_fusion.1), channel_id=1, source_target_pairs={{0,4},{4,0},{8,12},{12,8},{16,20},{20,16},{24,28},{28,24},{1,5},{5... | collective-permute-start | bytes 1179656 | tf_op jit(solution)/shard_map/ppermute | solution.py:279
  40.4 5.6 %collective-permute-start.7 = (f32[128,256]{1,0:T(8,128)S(1)}, f32[128,256]{1,0:T(8,128)S(1)}, u32[]{:S(2)}, u32[]{:S(2)}) collective-permute-start(f32[128,256]{1,0:T(8,128)S(1)} %shard_map.131.refs_0_), channel_id=1, source_target_pairs={{0,8},{4,20},{8,0},{12,28},{16,24},{20,4},{24,16},{28,12},{1,9},{5... | collective-permute-start | bytes 393224 | tf_op jit(solution)/shard_map/ppermute | solution.py:302
  43.9 5.0 %collective-permute-start.11 = (f32[128,256]{1,0:T(8,128)S(1)}, f32[128,256]{1,0:T(8,128)S(1)}, u32[]{:S(2)}, u32[]{:S(2)}) collective-permute-start(f32[128,256]{1,0:T(8,128)S(1)} %collective-permute-done.6.refs_1_), channel_id=1, source_target_pairs={{0,8},{4,20},{8,0},{12,28},{16,24},{20,4},{24,16},{28,12},{1,9},{5... | collective-permute-start | bytes 393224 | tf_op jit(solution)/shard_map/ppermute | solution.py:302
  45.4 6.5 %collective-permute-start.8 = (f32[128,256]{1,0:T(8,128)S(1)}, f32[128,256]{1,0:T(8,128)S(1)}, u32[]{:S(2)}, u32[]{:S(2)}) collective-permute-start(f32[128,256]{1,0:T(8,128)S(1)} %shard_map.131.refs_0_), channel_id=1, source_target_pairs={{0,4},{4,0},{8,12},{12,8},{16,20},{20,16},{24,28},{28,24},{1,5},{5... | collective-permute-start | bytes 393224 | tf_op jit(solution)/shard_map/ppermute | solution.py:302
  45.4 7.4 %collective-permute-start.9 = (f32[128,256]{1,0:T(8,128)S(1)}, f32[128,256]{1,0:T(8,128)S(1)}, u32[]{:S(2)}, u32[]{:S(2)}) collective-permute-start(f32[128,256]{1,0:T(8,128)S(1)} %collective-permute-done.6.refs_1_), channel_id=1, source_target_pairs={{0,4},{4,0},{8,12},{12,8},{16,20},{20,16},{24,28},{28,24},{1,5},{5... | collective-permute-start | bytes 393224 | tf_op jit(solution)/shard_map/ppermute | solution.py:302
  45.9 6.9 %collective-permute-start.10 = (f32[128,256]{1,0:T(8,128)S(1)}, f32[128,256]{1,0:T(8,128)S(1)}, u32[]{:S(2)}, u32[]{:S(2)}) collective-permute-start(f32[128,256]{1,0:T(8,128)S(1)} %collective-permute-done.7.refs_2_), channel_id=1, source_target_pairs={{0,4},{4,0},{8,12},{12,8},{16,20},{20,16},{24,28},{28,24},{1,5},{5... | collective-permute-start | bytes 393224 | tf_op jit(solution)/shard_map/ppermute | solution.py:302
  48.9 3.9 %collective-permute-start.12 = (f32[128,256]{1,0:T(8,128)S(1)}, f32[128,256]{1,0:T(8,128)S(1)}, u32[]{:S(2)}, u32[]{:S(2)}) collective-permute-start(f32[128,256]{1,0:T(8,128)S(1)} %collective-permute-done.11.refs_5_), channel_id=1, source_target_pairs={{0,4},{4,0},{8,12},{12,8},{16,20},{20,16},{24,28},{28,24},{1,5},{5... | collective-permute-start | bytes 393224 | tf_op jit(solution)/shard_map/ppermute | solution.py:302
  48.9 1.2 %copy-start = (f32[512,512]{1,0:T(8,128)S(1)}, f32[512,512]{1,0:T(8,128)}, u32[]{:S(2)}) copy-start(f32[512,512]{1,0:T(8,128)} %refs_0_.1) | copy-start | bytes 3145732
  50.1 1.2 %copy-start.1 = (f32[512,512]{1,0:T(8,128)S(1)}, f32[512,512]{1,0:T(8,128)}, u32[]{:S(2)}) copy-start(f32[512,512]{1,0:T(8,128)} %refs_1_.1) | copy-start | bytes 3145732
  51.6 28.2 %copy-start.11 = (f32[512]{0:T(512)S(1)}, f32[512]{0:T(512)}, u32[]{:S(2)}) copy-start(f32[512]{0:T(512)} %param.24) | copy-start | bytes 6148
  51.6 28.2 %copy-start.12 = (f32[512]{0:T(512)S(1)}, f32[512]{0:T(512)}, u32[]{:S(2)}) copy-start(f32[512]{0:T(512)} %param.25) | copy-start | bytes 6148
  53.7 6.9 %collective-permute-start.15 = (f32[128,128]{1,0:T(8,128)S(1)}, f32[128,128]{1,0:T(8,128)S(1)}, u32[]{:S(2)}, u32[]{:S(2)}) collective-permute-start(f32[128,128]{1,0:T(8,128)S(1)} %shard_map.133.refs_0_), channel_id=1, source_target_pairs={{0,3},{1,2},{2,1},{3,0},{4,7},{5,6},{6,5},{7,4},{8,11},{9,10},{10,... | collective-permute-start | bytes 196616 | tf_op jit(solution)/shard_map/ppermute | solution.py:279
  55.5 7.8 %collective-permute-start.14 = (f32[128,128]{1,0:T(8,128)S(1)}, f32[128,128]{1,0:T(8,128)S(1)}, u32[]{:S(2)}, u32[]{:S(2)}) collective-permute-start(f32[128,128]{1,0:T(8,128)S(1)} %shard_map.133.refs_0_), channel_id=1, source_target_pairs={{0,2},{1,3},{2,0},{3,1},{4,6},{5,7},{6,4},{7,5},{8,10},{9,11},{10,... | collective-permute-start | bytes 196616 | tf_op jit(solution)/shard_map/ppermute | solution.py:279
  56.6 6.7 %collective-permute-start.13 = (f32[128,128]{1,0:T(8,128)S(1)}, f32[128,128]{1,0:T(8,128)S(1)}, u32[]{:S(2)}, u32[]{:S(2)}) collective-permute-start(f32[128,128]{1,0:T(8,128)S(1)} %shard_map.133.refs_0_), channel_id=1, source_target_pairs={{0,1},{1,0},{2,3},{3,2},{4,5},{5,4},{6,7},{7,6},{8,9},{9,8},{10,11... | collective-permute-start | bytes 196616 | tf_op jit(solution)/shard_map/ppermute | solution.py:279
  64.5 4.9 %collective-permute-start.20 = (f32[128,128]{1,0:T(8,128)S(1)}, f32[128,128]{1,0:T(8,128)S(1)}, u32[]{:S(2)}, u32[]{:S(2)}) collective-permute-start(f32[128,128]{1,0:T(8,128)S(1)} %get-tuple-element.46), channel_id=1, source_target_pairs={{0,1},{1,0},{2,3},{3,2},{4,5},{5,4},{6,7},{7,6},{8,9},{9,8},{10,11... | collective-permute-start | bytes 196616 | tf_op jit(solution)/shard_map/ppermute | solution.py:279
  64.6 8.3 %collective-permute-start.21 = (f32[128,128]{1,0:T(8,128)S(1)}, f32[128,128]{1,0:T(8,128)S(1)}, u32[]{:S(2)}, u32[]{:S(2)}) collective-permute-start(f32[128,128]{1,0:T(8,128)S(1)} %get-tuple-element.47), channel_id=1, source_target_pairs={{0,2},{1,3},{2,0},{3,1},{4,6},{5,7},{6,4},{7,5},{8,10},{9,11},{10,... | collective-permute-start | bytes 196616 | tf_op jit(solution)/shard_map/ppermute | solution.py:279
  66.4 6.5 %collective-permute-start.22 = (f32[128,128]{1,0:T(8,128)S(1)}, f32[128,128]{1,0:T(8,128)S(1)}, u32[]{:S(2)}, u32[]{:S(2)}) collective-permute-start(f32[128,128]{1,0:T(8,128)S(1)} %get-tuple-element.48), channel_id=1, source_target_pairs={{0,3},{1,2},{2,1},{3,0},{4,7},{5,6},{6,5},{7,4},{8,11},{9,10},{10,... | collective-permute-start | bytes 196616 | tf_op jit(solution)/shard_map/ppermute | solution.py:279
  73.0 5.4 %collective-permute-start.25 = (f32[2,128]{1,0:T(2,128)S(1)}, f32[2,128]{1,0:T(2,128)S(1)}, u32[]{:S(2)}, u32[]{:S(2)}) collective-permute-start(f32[2,128]{1,0:T(2,128)S(1)} %get-tuple-element.50.refs_0_), channel_id=1, source_target_pairs={{0,3},{1,2},{2,1},{3,0},{4,7},{5,6},{6,5},{7,4},{8,11},{9,10},{10,... | collective-permute-start | bytes 3080 | tf_op jit(solution)/shard_map/ppermute | solution.py:279
  75.3 4.5 %collective-permute-start.24 = (f32[2,128]{1,0:T(2,128)S(1)}, f32[2,128]{1,0:T(2,128)S(1)}, u32[]{:S(2)}, u32[]{:S(2)}) collective-permute-start(f32[2,128]{1,0:T(2,128)S(1)} %get-tuple-element.50.refs_0_), channel_id=1, source_target_pairs={{0,2},{1,3},{2,0},{3,1},{4,6},{5,7},{6,4},{7,5},{8,10},{9,11},{10,... | collective-permute-start | bytes 3080 | tf_op jit(solution)/shard_map/ppermute | solution.py:279
  75.8 4.0 %collective-permute-start.23 = (f32[2,128]{1,0:T(2,128)S(1)}, f32[2,128]{1,0:T(2,128)S(1)}, u32[]{:S(2)}, u32[]{:S(2)}) collective-permute-start(f32[2,128]{1,0:T(2,128)S(1)} %get-tuple-element.50.refs_0_), channel_id=1, source_target_pairs={{0,1},{1,0},{2,3},{3,2},{4,5},{5,4},{6,7},{7,6},{8,9},{9,8},{10,11... | collective-permute-start | bytes 3080 | tf_op jit(solution)/shard_map/ppermute | solution.py:279

commit v8 on v7

--- a/solution.py
+++ b/solution.py
@@ -293,21 +293,13 @@
 
 def gather_pieces(piece):
     size = lax.axis_size("var")
-    if size != 8:
+    if size > 8:
         whole = lax.all_gather(piece, "var", axis=0, tiled=True)
         cut = whole.shape[0] // 2
         return [whole[:cut]], [whole[cut:]]
-
-    def hop(x, even, odd):
-        return lax.ppermute(x, "var", [(i, i ^ (odd if i & 1 else even)) for i in range(size)])
-
-    got_a = hop(piece, 4, 2)
-    got_b = hop(piece, 2, 4)
-    got_ab = hop(got_a, 2, 4)
-    swap, swap_a, swap_b, swap_ab = (
-        hop(each, 1, 1) for each in (piece, got_a, got_b, got_ab)
-    )
-    return [piece, got_a, got_b, swap], [swap_a, swap_b, got_ab, swap_ab]
+    far = [piece] + [send(piece, "var", k) for k in range(2, size, 2)]
+    near = [send(each, "var", 1) for each in far]
+    return far + near[:1], near[1:]
 
 
 def on_device(

time: 81 us -> 79 us (0.975)
  waiting for transfers between devices: 30.4 us -> 28.8 us
    ppermute x7 -> x0, waiting for transfers between devices: 4.99 us -> none  [hop(): lax.ppermute(x, 'var', [(i, i ^ (odd if i & 1 else even)) for i in range(...]
    ppermute x7 -> x0, starting transfers between devices: 4.12 us -> none  [hop(): lax.ppermute(x, 'var', [(i, i ^ (odd if i & 1 else even)) for i in range(...]
    ppermute x19 -> x26, starting transfers between devices: 30.1 us -> 33.7 us  [send(): return lax.ppermute(x, axis, [(i, i ^ offset) for i in range(size)])]
    ppermute x19 -> x26, waiting for transfers between devices: 25.4 us -> 28.8 us  [send(): return lax.ppermute(x, axis, [(i, i ^ offset) for i in range(size)])]
  transfers between devices with their start and end apart: 26 -> 26, of which waited for: 14 -> 15; matrix products, arithmetic and copies ran while one was open for 3% -> 3% of each run, Pallas kernels for 8% -> 9%
where the time goes in v8:
time: 79 us; the launch traced here: 78.7 us
  starting transfers between devices  33.7 us (43%)
  waiting for transfers between devices  28.8 us (36%)
  Pallas kernels  8.94 us (11%)
  local copies, waits for them, and re-layouts  4.28 us (5%)
  other arithmetic  2.83 us (4%)
    ppermute x26, starting transfers between devices, send(): return lax.ppermute(x, axis, [(i, i ^ offset) for i in range(size)])  33.7 us
    ppermute x26, waiting for transfers between devices, send(): return lax.ppermute(x, axis, [(i, i ^ offset) for i in range(size)])  28.8 us
    unnamed x26, local copies, waits for them, and re-layouts  4.28 us
    pallas_call x1, Pallas kernels, embed(): pl.pallas_call(functools.partial(embed_kernel, count), out_shape=[shape(r...  3.61 us
    concatenate x2, other arithmetic, on_device(): rest = jnp.concatenate([rest, send(rest, 'var', 1 << bit)], 0)  2.12 us
  transfers between devices with their start and end apart: 26, of which 15 were waited for; matrix products, arithmetic and copies ran while one was open for 3% of the time, Pallas kernels for 9%

profile of v8, /device:TPU:0, one launch (start us, length us, event | category | flops | bytes accessed | tf_op | source)
XLA Modules:
  0.0 78.7 jit_solution(14530301836413132377)
XLA Ops:
  0.0 0.9 %copy-done.2 = f32[128,512]{1,0:T(8,128)S(1)} copy-done((f32[128,512]{1,0:T(8,128)S(1)}, f32[128,512]{1,0:T(8,128)}, u32[]{:S(2)}) %copy-start.2) | copy-done | bytes 262168
  1.0 3.1 %collective-permute-start.16 = (f32[1,32,512]{2,1,0:T(8,128)S(1)}, f32[1,32,512]{2,1,0:T(8,128)S(1)}, u32[]{:S(2)}, u32[]{:S(2)}) collective-permute-start(f32[1,32,512]{2,1,0:T(8,128)S(1)} %bitcast.8), channel_id=1, source_target_pairs={{0,1},{1,0},{2,3},{3,2},{4,5},{5,4},{6,7},{7,6},{8,9},{9,8},{10,11... | collective-permute-start | bytes 196616 | tf_op jit(solution)/shard_map/ppermute | solution.py:279
  4.1 2.2 %collective-permute-done.16 = f32[1,32,512]{2,1,0:T(8,128)S(1)} collective-permute-done((f32[1,32,512]{2,1,0:T(8,128)S(1)}, f32[1,32,512]{2,1,0:T(8,128)S(1)}, u32[]{:S(2)}, u32[]{:S(2)}) %collective-permute-start.16) | collective-permute-done | bytes 65568 | tf_op jit(solution)/shard_map/ppermute | solution.py:279
  6.4 3.1 %collective-permute-start.17 = (f32[2,32,512]{2,1,0:T(8,128)S(1)}, f32[2,32,512]{2,1,0:T(8,128)S(1)}, u32[]{:S(2)}, u32[]{:S(2)}) collective-permute-start(f32[2,32,512]{2,1,0:T(8,128)S(1)} %pad_maximum_fusion.2), channel_id=1, source_target_pairs={{0,2},{1,3},{2,0},{3,1},{4,6},{5,7},{6,4},{7,5},{8,10},{9,11},{10,... | collective-permute-start | bytes 393224 | tf_op jit(solution)/shard_map/ppermute | solution.py:279
  9.5 5.2 %collective-permute-done.17 = f32[2,32,512]{2,1,0:T(8,128)S(1)} collective-permute-done((f32[2,32,512]{2,1,0:T(8,128)S(1)}, f32[2,32,512]{2,1,0:T(8,128)S(1)}, u32[]{:S(2)}, u32[]{:S(2)}) %collective-permute-start.17) | collective-permute-done | bytes 131104 | tf_op jit(solution)/shard_map/ppermute | solution.py:279
  14.6 0.7 maximum_bitcast_fusion
  15.3 1.6 %collective-permute-start.18 = (f32[1,3,32,512]{3,2,1,0:T(8,128)}, f32[1,3,32,512]{3,2,1,0:T(8,128)}, u32[]{:S(2)}, u32[]{:S(2)}) collective-permute-start(f32[1,3,32,512]{3,2,1,0:T(8,128)} %maximum_bitcast_fusion), channel_id=1, source_target_pairs={{0,16},{4,20},{8,24},{12,28},{16,0},{20,4},{24,8},{28,12},{1,17},{... | collective-permute-start | bytes 589832 | tf_op jit(solution)/shard_map/ppermute | solution.py:279
  16.9 3.6 %embed.1 = (f32[128,128]{1,0:T(8,128)}, f32[128,128]{1,0:T(8,128)}, f32[128,128]{1,0:T(8,128)}, f32[128,128]{1,0:T(8,128)}) custom-call(f32[128,2048]{1,0:T(8,128)} %x_hbm.1, f32[2048,512]{1,0:T(8,128)} %w_hbm.1), custom_call_target="tpu_custom_call" | custom-call | flops 805306368 | bytes 5242880 | tf_op jit(solution)/shard_map/embed/pallas_call | solution.py:111
  20.5 0.7 collective-permute-start
  21.2 3.4 %collective-permute-start.1 = (f32[128,128]{1,0:T(8,128)}, f32[128,128]{1,0:T(8,128)S(1)}, u32[]{:S(2)}, u32[]{:S(2)}) collective-permute-start(f32[128,128]{1,0:T(8,128)} %get-tuple-element.30), channel_id=1, source_target_pairs={{0,2},{1,3},{2,0},{3,1},{4,6},{5,7},{6,4},{7,5},{8,10},{9,11},{10,... | collective-permute-start | bytes 196616 | tf_op jit(solution)/shard_map/ppermute | solution.py:279
  24.6 0.3 collective-permute-start.2
  25.0 1.0 %pad_maximum_fusion.1 = f32[2,3,32,512]{3,2,1,0:T(8,128)S(1)} fusion(f32[1,3,32,512]{3,2,1,0:T(8,128)} %collective-permute-done.18, f32[1,3,32,512]{3,2,1,0:T(8,128)} %maximum_bitcast_fusion), kind=kLoop, calls=%fused_computation.1 | loop fusion | flops 98304 | bytes 786432 | tf_op jit(solution)/shard_map/concatenate | solution.py:329
  26.1 0.8 %copy-done.7 = f32[128,128]{1,0:T(8,128)S(1)} copy-done((f32[128,128]{1,0:T(8,128)S(1)}, f32[128,128]{1,0:T(8,128)}, u32[]{:S(2)}) %copy-start.7) | copy-done | bytes 65560
  27.0 1.5 %collective-permute-done.1.refs_2_ = f32[128,128]{1,0:T(8,128)S(1)} collective-permute-done((f32[128,128]{1,0:T(8,128)}, f32[128,128]{1,0:T(8,128)S(1)}, u32[]{:S(2)}, u32[]{:S(2)}) %collective-permute-start.1) | collective-permute-done | bytes 65568 | tf_op jit(solution)/shard_map/ppermute | solution.py:279
  28.5 2.5 %collective-permute-done.2.refs_3_ = f32[128,128]{1,0:T(8,128)S(1)} collective-permute-done((f32[128,128]{1,0:T(8,128)}, f32[128,128]{1,0:T(8,128)S(1)}, u32[]{:S(2)}, u32[]{:S(2)}) %collective-permute-start.2) | collective-permute-done | bytes 65568 | tf_op jit(solution)/shard_map/ppermute | solution.py:279
  31.0 0.8 collective-permute-start.5
  31.8 3.7 %collective-permute-start.3 = (f32[128,128]{1,0:T(8,128)S(1)}, f32[128,128]{1,0:T(8,128)S(1)}, u32[]{:S(2)}, u32[]{:S(2)}) collective-permute-start(f32[128,128]{1,0:T(8,128)S(1)} %shard_map.128.refs_0_.refs_4_), channel_id=1, source_target_pairs={{0,1},{1,0},{2,3},{3,2},{4,5},{5,4},{6,7},{7,6},{8,9},{9,8},{10,11... | collective-permute-start | bytes 196616 | tf_op jit(solution)/shard_map/ppermute | solution.py:279
  35.6 1.7 %collective-permute-done.5.refs_3_.refs_7_ = f32[128,128]{1,0:T(8,128)S(1)} collective-permute-done((f32[128,128]{1,0:T(8,128)S(1)}, f32[128,128]{1,0:T(8,128)S(1)}, u32[]{:S(2)}, u32[]{:S(2)}) %collective-permute-start.5) | collective-permute-done | bytes 65568 | tf_op jit(solution)/shard_map/ppermute | solution.py:279
  37.3 1.1 %collective-permute-done.4.refs_2_.refs_6_ = f32[128,128]{1,0:T(8,128)S(1)} collective-permute-done((f32[128,128]{1,0:T(8,128)S(1)}, f32[128,128]{1,0:T(8,128)S(1)}, u32[]{:S(2)}, u32[]{:S(2)}) %collective-permute-start.4) | collective-permute-done | bytes 65568 | tf_op jit(solution)/shard_map/ppermute | solution.py:279
  38.4 0.3 shard_map.131.refs_0_
  38.7 1.5 %collective-permute-start.8 = (f32[128,256]{1,0:T(8,128)S(1)}, f32[128,256]{1,0:T(8,128)S(1)}, u32[]{:S(2)}, u32[]{:S(2)}) collective-permute-start(f32[128,256]{1,0:T(8,128)S(1)} %shard_map.131.refs_0_), channel_id=1, source_target_pairs={{0,24},{4,28},{8,16},{12,20},{16,8},{20,12},{24,0},{28,4},{1,25},{... | collective-permute-start | bytes 393224 | tf_op jit(solution)/shard_map/ppermute | solution.py:279
  40.2 1.5 %collective-permute-start.7 = (f32[128,256]{1,0:T(8,128)S(1)}, f32[128,256]{1,0:T(8,128)S(1)}, u32[]{:S(2)}, u32[]{:S(2)}) collective-permute-start(f32[128,256]{1,0:T(8,128)S(1)} %shard_map.131.refs_0_), channel_id=1, source_target_pairs={{0,16},{4,20},{8,24},{12,28},{16,0},{20,4},{24,8},{28,12},{1,17},{... | collective-permute-start | bytes 393224 | tf_op jit(solution)/shard_map/ppermute | solution.py:279
  41.7 0.5 collective-permute-start.6
  42.2 2.5 %collective-permute-done.8.refs_3_ = f32[128,256]{1,0:T(8,128)S(1)} collective-permute-done((f32[128,256]{1,0:T(8,128)S(1)}, f32[128,256]{1,0:T(8,128)S(1)}, u32[]{:S(2)}, u32[]{:S(2)}) %collective-permute-start.8) | collective-permute-done | bytes 131104 | tf_op jit(solution)/shard_map/ppermute | solution.py:279
  44.7 1.3 %collective-permute-done.7.refs_2_ = f32[128,256]{1,0:T(8,128)S(1)} collective-permute-done((f32[128,256]{1,0:T(8,128)S(1)}, f32[128,256]{1,0:T(8,128)S(1)}, u32[]{:S(2)}, u32[]{:S(2)}) %collective-permute-start.7) | collective-permute-done | bytes 131104 | tf_op jit(solution)/shard_map/ppermute | solution.py:279
  46.0 0.6 collective-permute-done.6.refs_1_
  46.7 1.2 %copy-done = f32[512,512]{1,0:T(8,128)S(1)} copy-done((f32[512,512]{1,0:T(8,128)S(1)}, f32[512,512]{1,0:T(8,128)}, u32[]{:S(2)}) %copy-start) | copy-done | bytes 1048600
  47.9 1.2 %copy-done.1 = f32[512,512]{1,0:T(8,128)S(1)} copy-done((f32[512,512]{1,0:T(8,128)S(1)}, f32[512,512]{1,0:T(8,128)}, u32[]{:S(2)}) %copy-start.1) | copy-done | bytes 1048600
  49.1 0.3 shard_map.136
  49.7 1.2 %shard_map.132 = (f32[128,128]{1,0:T(8,128)S(1)}, f32[128,128]{1,0:T(8,128)S(1)}, f32[128,128]{1,0:T(8,128)S(1)}) custom-call(f32[128,128]{1,0:T(8,128)S(1)} %shard_map.130.q_ref, f32[128,256]{1,0:T(8,128)S(1)} %shard_map.131.refs_0_, f32[128,256]{1,0:T(8,128)S(1)} %collective-permute-done.6.refs_1_, f32[128,256]{1,0:T(8,128)S(1)} %collective-permute-done.7.refs_2_, ...), custom_call_target="tpu_custom_call" | custom-call | tf_op jit(solution)/shard_map/pallas_call | solution.py:338
  50.9 0.8 %shard_map.133.refs_0_ = f32[128,128]{1,0:T(8,128)S(1)} custom-call(f32[128,128]{1,0:T(8,128)S(1)} %shard_map.130.q_ref, f32[128,128]{1,0:T(8,128)S(1)} %get-tuple-element.36.refs_0_, f32[128,128]{1,0:T(8,128)S(1)} %get-tuple-element.37.refs_1_, f32[128,128]{1,0:T(8,128)S(1)} %get-tuple-element.38.refs_2_, f32[128,256]{1,0:T(8,128)S(1)} %collective-permute-done.10.refs_3_, ...), custom_call_target="tpu_custom_call" | custom-call | tf_op jit(solution)/shard_map/pallas_call | solution.py:341
  51.8 1.8 %collective-permute-start.15 = (f32[128,128]{1,0:T(8,128)S(1)}, f32[128,128]{1,0:T(8,128)S(1)}, u32[]{:S(2)}, u32[]{:S(2)}) collective-permute-start(f32[128,128]{1,0:T(8,128)S(1)} %shard_map.133.refs_0_), channel_id=1, source_target_pairs={{0,3},{1,2},{2,1},{3,0},{4,7},{5,6},{6,5},{7,4},{8,11},{9,10},{10,... | collective-permute-start | bytes 196616 | tf_op jit(solution)/shard_map/ppermute | solution.py:279
  53.6 1.1 %collective-permute-start.14 = (f32[128,128]{1,0:T(8,128)S(1)}, f32[128,128]{1,0:T(8,128)S(1)}, u32[]{:S(2)}, u32[]{:S(2)}) collective-permute-start(f32[128,128]{1,0:T(8,128)S(1)} %shard_map.133.refs_0_), channel_id=1, source_target_pairs={{0,2},{1,3},{2,0},{3,1},{4,6},{5,7},{6,4},{7,5},{8,10},{9,11},{10,... | collective-permute-start | bytes 196616 | tf_op jit(solution)/shard_map/ppermute | solution.py:279
  54.7 1.5 %collective-permute-start.13 = (f32[128,128]{1,0:T(8,128)S(1)}, f32[128,128]{1,0:T(8,128)S(1)}, u32[]{:S(2)}, u32[]{:S(2)}) collective-permute-start(f32[128,128]{1,0:T(8,128)S(1)} %shard_map.133.refs_0_), channel_id=1, source_target_pairs={{0,1},{1,0},{2,3},{3,2},{4,5},{5,4},{6,7},{7,6},{8,9},{9,8},{10,11... | collective-permute-start | bytes 196616 | tf_op jit(solution)/shard_map/ppermute | solution.py:279
  56.2 1.1 %pad_maximum_fusion.rest_ref = f32[4,3,32,512]{3,2,1,0:T(8,128)S(1)} fusion(f32[2,3,32,512]{3,2,1,0:T(8,128)S(1)} %collective-permute-done.19, f32[1,3,32,512]{3,2,1,0:T(8,128)} %collective-permute-done.18, f32[1,3,32,512]{3,2,1,0:T(8,128)} %maximum_bitcast_fusion), kind=kLoop, calls=%fused_computation | loop fusion | flops 393216 | bytes 1572864 | tf_op jit(solution)/shard_map/concatenate | solution.py:329
  57.4 1.2 %collective-permute-done.15.refs_3_ = f32[128,128]{1,0:T(8,128)S(1)} collective-permute-done((f32[128,128]{1,0:T(8,128)S(1)}, f32[128,128]{1,0:T(8,128)S(1)}, u32[]{:S(2)}, u32[]{:S(2)}) %collective-permute-start.15) | collective-permute-done | bytes 65568 | tf_op jit(solution)/shard_map/ppermute | solution.py:279
  58.7 2.7 %collective-permute-done.14.refs_2_ = f32[128,128]{1,0:T(8,128)S(1)} collective-permute-done((f32[128,128]{1,0:T(8,128)S(1)}, f32[128,128]{1,0:T(8,128)S(1)}, u32[]{:S(2)}, u32[]{:S(2)}) %collective-permute-start.14) | collective-permute-done | bytes 65568 | tf_op jit(solution)/shard_map/ppermute | solution.py:279
  61.4 1.2 %shard_map.137 = (f32[128,128]{1,0:T(8,128)S(1)}, f32[128,128]{1,0:T(8,128)S(1)}, f32[128,128]{1,0:T(8,128)S(1)}, f32[128,128]{1,0:T(8,128)S(1)}) custom-call(f32[128,128]{1,0:T(8,128)S(1)} %shard_map.133.refs_0_, f32[128,128]{1,0:T(8,128)S(1)} %collective-permute-done.13.refs_1_, f32[128,128]{1,0:T(8,128)S(1)} %collective-permute-done.14.refs_2_, ...), custom_call_target="tpu_custom_call" | custom-call | tf_op jit(solution)/shard_map/pallas_call | solution.py:345
  62.7 1.8 %collective-permute-start.21 = (f32[128,128]{1,0:T(8,128)S(1)}, f32[128,128]{1,0:T(8,128)S(1)}, u32[]{:S(2)}, u32[]{:S(2)}) collective-permute-start(f32[128,128]{1,0:T(8,128)S(1)} %get-tuple-element.47), channel_id=1, source_target_pairs={{0,2},{1,3},{2,0},{3,1},{4,6},{5,7},{6,4},{7,5},{8,10},{9,11},{10,... | collective-permute-start | bytes 196616 | tf_op jit(solution)/shard_map/ppermute | solution.py:279
  64.5 2.5 %collective-permute-start.22 = (f32[128,128]{1,0:T(8,128)S(1)}, f32[128,128]{1,0:T(8,128)S(1)}, u32[]{:S(2)}, u32[]{:S(2)}) collective-permute-start(f32[128,128]{1,0:T(8,128)S(1)} %get-tuple-element.48), channel_id=1, source_target_pairs={{0,3},{1,2},{2,1},{3,0},{4,7},{5,6},{6,5},{7,4},{8,11},{9,10},{10,... | collective-permute-start | bytes 196616 | tf_op jit(solution)/shard_map/ppermute | solution.py:279
  67.0 0.4 collective-permute-done.20.refs_1_
  67.4 3.5 %collective-permute-done.21.refs_2_ = f32[128,128]{1,0:T(8,128)S(1)} collective-permute-done((f32[128,128]{1,0:T(8,128)S(1)}, f32[128,128]{1,0:T(8,128)S(1)}, u32[]{:S(2)}, u32[]{:S(2)}) %collective-permute-start.21) | collective-permute-done | bytes 65568 | tf_op jit(solution)/shard_map/ppermute | solution.py:279
  71.0 2.3 %collective-permute-start.25 = (f32[2,128]{1,0:T(2,128)S(1)}, f32[2,128]{1,0:T(2,128)S(1)}, u32[]{:S(2)}, u32[]{:S(2)}) collective-permute-start(f32[2,128]{1,0:T(2,128)S(1)} %get-tuple-element.50.refs_0_), channel_id=1, source_target_pairs={{0,3},{1,2},{2,1},{3,0},{4,7},{5,6},{6,5},{7,4},{8,11},{9,10},{10,... | collective-permute-start | bytes 3080 | tf_op jit(solution)/shard_map/ppermute | solution.py:279
  73.4 0.4 collective-permute-start.24
  73.8 1.7 %collective-permute-start.23 = (f32[2,128]{1,0:T(2,128)S(1)}, f32[2,128]{1,0:T(2,128)S(1)}, u32[]{:S(2)}, u32[]{:S(2)}) collective-permute-start(f32[2,128]{1,0:T(2,128)S(1)} %get-tuple-element.50.refs_0_), channel_id=1, source_target_pairs={{0,1},{1,0},{2,3},{3,2},{4,5},{5,4},{6,7},{7,6},{8,9},{9,8},{10,11... | collective-permute-start | bytes 3080 | tf_op jit(solution)/shard_map/ppermute | solution.py:279
  75.5 1.0 %collective-permute-done.25.refs_3_ = f32[2,128]{1,0:T(2,128)S(1)} collective-permute-done((f32[2,128]{1,0:T(2,128)S(1)}, f32[2,128]{1,0:T(2,128)S(1)}, u32[]{:S(2)}, u32[]{:S(2)}) %collective-permute-start.25) | collective-permute-done | bytes 1056 | tf_op jit(solution)/shard_map/ppermute | solution.py:279
  76.5 1.4 %collective-permute-done.24.refs_2_ = f32[2,128]{1,0:T(2,128)S(1)} collective-permute-done((f32[2,128]{1,0:T(2,128)S(1)}, f32[2,128]{1,0:T(2,128)S(1)}, u32[]{:S(2)}, u32[]{:S(2)}) %collective-permute-start.24) | collective-permute-done | bytes 1056 | tf_op jit(solution)/shard_map/ppermute | solution.py:279
  77.9 0.8 %shard_map.139 = f32[128,128]{1,0:T(8,128)} custom-call(f32[128,128]{1,0:T(8,128)S(1)} %get-tuple-element.49.x_ref, f32[2,128]{1,0:T(2,128)S(1)} %get-tuple-element.50.refs_0_, f32[2,128]{1,0:T(2,128)S(1)} %collective-permute-done.23.refs_1_, f32[2,128]{1,0:T(2,128)S(1)} %collective-permute-done.24.refs_2_, f32[2,128]{1,0:T(2,128)S(1)} %collective-permute-done.25.refs_3_, ...), custom_call_target="tpu_custom_call" | custom-call | tf_op jit(solution)/shard_map/pallas_call | solution.py:350
  (48 shorter events, 0.9 us)
Async XLA Ops:
  0.0 0.9 %copy-start.2 = (f32[128,512]{1,0:T(8,128)S(1)}, f32[128,512]{1,0:T(8,128)}, u32[]{:S(2)}) copy-start(f32[128,512]{1,0:T(8,128)} %own_ref.1) | copy-start | bytes 786436
  1.0 25.1 %copy-start.8 = (f32[512]{0:T(512)S(1)}, f32[512]{0:T(512)}, u32[]{:S(2)}) copy-start(f32[512]{0:T(512)} %param.15) | copy-start | bytes 6148
  1.0 34.6 %copy-start.4 = (f32[512,128]{1,0:T(8,128)S(1)}, f32[512,128]{1,0:T(8,128)}, u32[]{:S(2)}) copy-start(f32[512,128]{1,0:T(8,128)} %k_ref.1) | copy-start | bytes 786436
  1.0 34.6 %copy-start.5 = (f32[512,128]{1,0:T(8,128)S(1)}, f32[512,128]{1,0:T(8,128)}, u32[]{:S(2)}) copy-start(f32[512,128]{1,0:T(8,128)} %v_ref.1) | copy-start | bytes 786436
  1.0 34.6 %copy-start.6 = (f32[512,128]{1,0:T(8,128)S(1)}, f32[512,128]{1,0:T(8,128)}, u32[]{:S(2)}) copy-start(f32[512,128]{1,0:T(8,128)} %q_ref.1) | copy-start | bytes 786436
  1.0 5.4 %collective-permute-start.16 = (f32[1,32,512]{2,1,0:T(8,128)S(1)}, f32[1,32,512]{2,1,0:T(8,128)S(1)}, u32[]{:S(2)}, u32[]{:S(2)}) collective-permute-start(f32[1,32,512]{2,1,0:T(8,128)S(1)} %bitcast.8), channel_id=1, source_target_pairs={{0,1},{1,0},{2,3},{3,2},{4,5},{5,4},{6,7},{7,6},{8,9},{9,8},{10,11... | collective-permute-start | bytes 196616 | tf_op jit(solution)/shard_map/ppermute | solution.py:279
  6.4 8.3 %collective-permute-start.17 = (f32[2,32,512]{2,1,0:T(8,128)S(1)}, f32[2,32,512]{2,1,0:T(8,128)S(1)}, u32[]{:S(2)}, u32[]{:S(2)}) collective-permute-start(f32[2,32,512]{2,1,0:T(8,128)S(1)} %pad_maximum_fusion.2), channel_id=1, source_target_pairs={{0,2},{1,3},{2,0},{3,1},{4,6},{5,7},{6,4},{7,5},{8,10},{9,11},{10,... | collective-permute-start | bytes 393224 | tf_op jit(solution)/shard_map/ppermute | solution.py:279
  15.3 9.6 %collective-permute-start.18 = (f32[1,3,32,512]{3,2,1,0:T(8,128)}, f32[1,3,32,512]{3,2,1,0:T(8,128)}, u32[]{:S(2)}, u32[]{:S(2)}) collective-permute-start(f32[1,3,32,512]{3,2,1,0:T(8,128)} %maximum_bitcast_fusion), channel_id=1, source_target_pairs={{0,16},{4,20},{8,24},{12,28},{16,0},{20,4},{24,8},{28,12},{1,17},{... | collective-permute-start | bytes 589832 | tf_op jit(solution)/shard_map/ppermute | solution.py:279
  20.5 6.5 %collective-permute-start = (f32[128,128]{1,0:T(8,128)}, f32[128,128]{1,0:T(8,128)S(1)}, u32[]{:S(2)}, u32[]{:S(2)}) collective-permute-start(f32[128,128]{1,0:T(8,128)} %get-tuple-element.29), channel_id=1, source_target_pairs={{0,1},{1,0},{2,3},{3,2},{4,5},{5,4},{6,7},{7,6},{8,9},{9,8},{10,11... | collective-permute-start | bytes 196616 | tf_op jit(solution)/shard_map/ppermute | solution.py:279
  21.2 7.2 %collective-permute-start.1 = (f32[128,128]{1,0:T(8,128)}, f32[128,128]{1,0:T(8,128)S(1)}, u32[]{:S(2)}, u32[]{:S(2)}) collective-permute-start(f32[128,128]{1,0:T(8,128)} %get-tuple-element.30), channel_id=1, source_target_pairs={{0,2},{1,3},{2,0},{3,1},{4,6},{5,7},{6,4},{7,5},{8,10},{9,11},{10,... | collective-permute-start | bytes 196616 | tf_op jit(solution)/shard_map/ppermute | solution.py:279
  24.6 32.7 %copy-start.3 = (f32[128,512]{1,0:T(8,128)S(1)}, f32[128,512]{1,0:T(8,128)}, u32[]{:S(2)}) copy-start(f32[128,512]{1,0:T(8,128)} %own_ref.1) | copy-start | bytes 786436
  24.6 6.4 %collective-permute-start.2 = (f32[128,128]{1,0:T(8,128)}, f32[128,128]{1,0:T(8,128)S(1)}, u32[]{:S(2)}, u32[]{:S(2)}) collective-permute-start(f32[128,128]{1,0:T(8,128)} %get-tuple-element.31), channel_id=1, source_target_pairs={{0,3},{1,2},{2,1},{3,0},{4,7},{5,6},{6,5},{7,4},{8,11},{9,10},{10,... | collective-permute-start | bytes 196616 | tf_op jit(solution)/shard_map/ppermute | solution.py:279
  26.0 30.2 %collective-permute-start.19 = (f32[2,3,32,512]{3,2,1,0:T(8,128)S(1)}, f32[2,3,32,512]{3,2,1,0:T(8,128)S(1)}, u32[]{:S(2)}, u32[]{:S(2)}) collective-permute-start(f32[2,3,32,512]{3,2,1,0:T(8,128)S(1)} %pad_maximum_fusion.1), channel_id=1, source_target_pairs={{0,4},{4,0},{8,12},{12,8},{16,20},{20,16},{24,28},{28,24},{1,5},{5... | collective-permute-start | bytes 1179656 | tf_op jit(solution)/shard_map/ppermute | solution.py:279
  26.1 0.8 %copy-start.7 = (f32[128,128]{1,0:T(8,128)S(1)}, f32[128,128]{1,0:T(8,128)}, u32[]{:S(2)}) copy-start(f32[128,128]{1,0:T(8,128)} %get-tuple-element.28.x_ref) | copy-start | bytes 196612
  31.0 30.3 %copy-start.9 = (f32[512]{0:T(512)S(1)}, f32[512]{0:T(512)}, u32[]{:S(2)}) copy-start(f32[512]{0:T(512)} %param.20) | copy-start | bytes 6148
  31.0 30.3 %copy-start.10 = (f32[512]{0:T(512)S(1)}, f32[512]{0:T(512)}, u32[]{:S(2)}) copy-start(f32[512]{0:T(512)} %param.21) | copy-start | bytes 6148
  31.0 6.3 %collective-permute-start.5 = (f32[128,128]{1,0:T(8,128)S(1)}, f32[128,128]{1,0:T(8,128)S(1)}, u32[]{:S(2)}, u32[]{:S(2)}) collective-permute-start(f32[128,128]{1,0:T(8,128)S(1)} %shard_map.128.refs_0_.refs_4_), channel_id=1, source_target_pairs={{0,3},{1,2},{2,1},{3,0},{4,7},{5,6},{6,5},{7,4},{8,11},{9,10},{10,... | collective-permute-start | bytes 196616 | tf_op jit(solution)/shard_map/ppermute | solution.py:279
  31.8 6.6 %collective-permute-start.4 = (f32[128,128]{1,0:T(8,128)S(1)}, f32[128,128]{1,0:T(8,128)S(1)}, u32[]{:S(2)}, u32[]{:S(2)}) collective-permute-start(f32[128,128]{1,0:T(8,128)S(1)} %shard_map.128.refs_0_.refs_4_), channel_id=1, source_target_pairs={{0,2},{1,3},{2,0},{3,1},{4,6},{5,7},{6,4},{7,5},{8,10},{9,11},{10,... | collective-permute-start | bytes 196616 | tf_op jit(solution)/shard_map/ppermute | solution.py:279
  31.8 6.6 %collective-permute-start.3 = (f32[128,128]{1,0:T(8,128)S(1)}, f32[128,128]{1,0:T(8,128)S(1)}, u32[]{:S(2)}, u32[]{:S(2)}) collective-permute-start(f32[128,128]{1,0:T(8,128)S(1)} %shard_map.128.refs_0_.refs_4_), channel_id=1, source_target_pairs={{0,1},{1,0},{2,3},{3,2},{4,5},{5,4},{6,7},{7,6},{8,9},{9,8},{10,11... | collective-permute-start | bytes 196616 | tf_op jit(solution)/shard_map/ppermute | solution.py:279
  38.7 6.0 %collective-permute-start.8 = (f32[128,256]{1,0:T(8,128)S(1)}, f32[128,256]{1,0:T(8,128)S(1)}, u32[]{:S(2)}, u32[]{:S(2)}) collective-permute-start(f32[128,256]{1,0:T(8,128)S(1)} %shard_map.131.refs_0_), channel_id=1, source_target_pairs={{0,24},{4,28},{8,16},{12,20},{16,8},{20,12},{24,0},{28,4},{1,25},{... | collective-permute-start | bytes 393224 | tf_op jit(solution)/shard_map/ppermute | solution.py:279
  40.2 5.8 %collective-permute-start.7 = (f32[128,256]{1,0:T(8,128)S(1)}, f32[128,256]{1,0:T(8,128)S(1)}, u32[]{:S(2)}, u32[]{:S(2)}) collective-permute-start(f32[128,256]{1,0:T(8,128)S(1)} %shard_map.131.refs_0_), channel_id=1, source_target_pairs={{0,16},{4,20},{8,24},{12,28},{16,0},{20,4},{24,8},{28,12},{1,17},{... | collective-permute-start | bytes 393224 | tf_op jit(solution)/shard_map/ppermute | solution.py:279
  41.7 5.0 %collective-permute-start.6 = (f32[128,256]{1,0:T(8,128)S(1)}, f32[128,256]{1,0:T(8,128)S(1)}, u32[]{:S(2)}, u32[]{:S(2)}) collective-permute-start(f32[128,256]{1,0:T(8,128)S(1)} %shard_map.131.refs_0_), channel_id=1, source_target_pairs={{0,8},{4,12},{8,0},{12,4},{16,24},{20,28},{24,16},{28,20},{1,9},{5... | collective-permute-start | bytes 393224 | tf_op jit(solution)/shard_map/ppermute | solution.py:279
  42.2 7.5 %collective-permute-start.9 = (f32[128,256]{1,0:T(8,128)S(1)}, f32[128,256]{1,0:T(8,128)S(1)}, u32[]{:S(2)}, u32[]{:S(2)}) collective-permute-start(f32[128,256]{1,0:T(8,128)S(1)} %shard_map.131.refs_0_), channel_id=1, source_target_pairs={{0,4},{4,0},{8,12},{12,8},{16,20},{20,16},{24,28},{28,24},{1,5},{5... | collective-permute-start | bytes 393224 | tf_op jit(solution)/shard_map/ppermute | solution.py:279
  44.7 6.2 %collective-permute-start.12 = (f32[128,256]{1,0:T(8,128)S(1)}, f32[128,256]{1,0:T(8,128)S(1)}, u32[]{:S(2)}, u32[]{:S(2)}) collective-permute-start(f32[128,256]{1,0:T(8,128)S(1)} %collective-permute-done.8.refs_3_), channel_id=1, source_target_pairs={{0,4},{4,0},{8,12},{12,8},{16,20},{20,16},{24,28},{28,24},{1,5},{5... | collective-permute-start | bytes 393224 | tf_op jit(solution)/shard_map/ppermute | solution.py:279
  46.0 4.9 %collective-permute-start.11 = (f32[128,256]{1,0:T(8,128)S(1)}, f32[128,256]{1,0:T(8,128)S(1)}, u32[]{:S(2)}, u32[]{:S(2)}) collective-permute-start(f32[128,256]{1,0:T(8,128)S(1)} %collective-permute-done.7.refs_2_), channel_id=1, source_target_pairs={{0,4},{4,0},{8,12},{12,8},{16,20},{20,16},{24,28},{28,24},{1,5},{5... | collective-permute-start | bytes 393224 | tf_op jit(solution)/shard_map/ppermute | solution.py:279
  46.7 4.2 %collective-permute-start.10 = (f32[128,256]{1,0:T(8,128)S(1)}, f32[128,256]{1,0:T(8,128)S(1)}, u32[]{:S(2)}, u32[]{:S(2)}) collective-permute-start(f32[128,256]{1,0:T(8,128)S(1)} %collective-permute-done.6.refs_1_), channel_id=1, source_target_pairs={{0,4},{4,0},{8,12},{12,8},{16,20},{20,16},{24,28},{28,24},{1,5},{5... | collective-permute-start | bytes 393224 | tf_op jit(solution)/shard_map/ppermute | solution.py:279
  46.7 1.2 %copy-start = (f32[512,512]{1,0:T(8,128)S(1)}, f32[512,512]{1,0:T(8,128)}, u32[]{:S(2)}) copy-start(f32[512,512]{1,0:T(8,128)} %refs_0_.1) | copy-start | bytes 3145732
  47.9 1.2 %copy-start.1 = (f32[512,512]{1,0:T(8,128)S(1)}, f32[512,512]{1,0:T(8,128)}, u32[]{:S(2)}) copy-start(f32[512,512]{1,0:T(8,128)} %refs_1_.1) | copy-start | bytes 3145732
  49.4 28.5 %copy-start.11 = (f32[512]{0:T(512)S(1)}, f32[512]{0:T(512)}, u32[]{:S(2)}) copy-start(f32[512]{0:T(512)} %param.24) | copy-start | bytes 6148
  49.4 28.5 %copy-start.12 = (f32[512]{0:T(512)S(1)}, f32[512]{0:T(512)}, u32[]{:S(2)}) copy-start(f32[512]{0:T(512)} %param.25) | copy-start | bytes 6148
  51.8 6.9 %collective-permute-start.15 = (f32[128,128]{1,0:T(8,128)S(1)}, f32[128,128]{1,0:T(8,128)S(1)}, u32[]{:S(2)}, u32[]{:S(2)}) collective-permute-start(f32[128,128]{1,0:T(8,128)S(1)} %shard_map.133.refs_0_), channel_id=1, source_target_pairs={{0,3},{1,2},{2,1},{3,0},{4,7},{5,6},{6,5},{7,4},{8,11},{9,10},{10,... | collective-permute-start | bytes 196616 | tf_op jit(solution)/shard_map/ppermute | solution.py:279
  53.6 7.8 %collective-permute-start.14 = (f32[128,128]{1,0:T(8,128)S(1)}, f32[128,128]{1,0:T(8,128)S(1)}, u32[]{:S(2)}, u32[]{:S(2)}) collective-permute-start(f32[128,128]{1,0:T(8,128)S(1)} %shard_map.133.refs_0_), channel_id=1, source_target_pairs={{0,2},{1,3},{2,0},{3,1},{4,6},{5,7},{6,4},{7,5},{8,10},{9,11},{10,... | collective-permute-start | bytes 196616 | tf_op jit(solution)/shard_map/ppermute | solution.py:279
  54.7 6.7 %collective-permute-start.13 = (f32[128,128]{1,0:T(8,128)S(1)}, f32[128,128]{1,0:T(8,128)S(1)}, u32[]{:S(2)}, u32[]{:S(2)}) collective-permute-start(f32[128,128]{1,0:T(8,128)S(1)} %shard_map.133.refs_0_), channel_id=1, source_target_pairs={{0,1},{1,0},{2,3},{3,2},{4,5},{5,4},{6,7},{7,6},{8,9},{9,8},{10,11... | collective-permute-start | bytes 196616 | tf_op jit(solution)/shard_map/ppermute | solution.py:279
  62.6 4.8 %collective-permute-start.20 = (f32[128,128]{1,0:T(8,128)S(1)}, f32[128,128]{1,0:T(8,128)S(1)}, u32[]{:S(2)}, u32[]{:S(2)}) collective-permute-start(f32[128,128]{1,0:T(8,128)S(1)} %get-tuple-element.46), channel_id=1, source_target_pairs={{0,1},{1,0},{2,3},{3,2},{4,5},{5,4},{6,7},{7,6},{8,9},{9,8},{10,11... | collective-permute-start | bytes 196616 | tf_op jit(solution)/shard_map/ppermute | solution.py:279
  62.7 8.2 %collective-permute-start.21 = (f32[128,128]{1,0:T(8,128)S(1)}, f32[128,128]{1,0:T(8,128)S(1)}, u32[]{:S(2)}, u32[]{:S(2)}) collective-permute-start(f32[128,128]{1,0:T(8,128)S(1)} %get-tuple-element.47), channel_id=1, source_target_pairs={{0,2},{1,3},{2,0},{3,1},{4,6},{5,7},{6,4},{7,5},{8,10},{9,11},{10,... | collective-permute-start | bytes 196616 | tf_op jit(solution)/shard_map/ppermute | solution.py:279
  64.5 6.4 %collective-permute-start.22 = (f32[128,128]{1,0:T(8,128)S(1)}, f32[128,128]{1,0:T(8,128)S(1)}, u32[]{:S(2)}, u32[]{:S(2)}) collective-permute-start(f32[128,128]{1,0:T(8,128)S(1)} %get-tuple-element.48), channel_id=1, source_target_pairs={{0,3},{1,2},{2,1},{3,0},{4,7},{5,6},{6,5},{7,4},{8,11},{9,10},{10,... | collective-permute-start | bytes 196616 | tf_op jit(solution)/shard_map/ppermute | solution.py:279
  71.0 5.4 %collective-permute-start.25 = (f32[2,128]{1,0:T(2,128)S(1)}, f32[2,128]{1,0:T(2,128)S(1)}, u32[]{:S(2)}, u32[]{:S(2)}) collective-permute-start(f32[2,128]{1,0:T(2,128)S(1)} %get-tuple-element.50.refs_0_), channel_id=1, source_target_pairs={{0,3},{1,2},{2,1},{3,0},{4,7},{5,6},{6,5},{7,4},{8,11},{9,10},{10,... | collective-permute-start | bytes 3080 | tf_op jit(solution)/shard_map/ppermute | solution.py:279
  73.4 4.5 %collective-permute-start.24 = (f32[2,128]{1,0:T(2,128)S(1)}, f32[2,128]{1,0:T(2,128)S(1)}, u32[]{:S(2)}, u32[]{:S(2)}) collective-permute-start(f32[2,128]{1,0:T(2,128)S(1)} %get-tuple-element.50.refs_0_), channel_id=1, source_target_pairs={{0,2},{1,3},{2,0},{3,1},{4,6},{5,7},{6,4},{7,5},{8,10},{9,11},{10,... | collective-permute-start | bytes 3080 | tf_op jit(solution)/shard_map/ppermute | solution.py:279
  73.8 4.0 %collective-permute-start.23 = (f32[2,128]{1,0:T(2,128)S(1)}, f32[2,128]{1,0:T(2,128)S(1)}, u32[]{:S(2)}, u32[]{:S(2)}) collective-permute-start(f32[2,128]{1,0:T(2,128)S(1)} %get-tuple-element.50.refs_0_), channel_id=1, source_target_pairs={{0,1},{1,0},{2,3},{3,2},{4,5},{5,4},{6,7},{7,6},{8,9},{9,8},{10,11... | collective-permute-start | bytes 3080 | tf_op jit(solution)/shard_map/ppermute | solution.py:279

commit v9 on v8

--- a/solution.py
+++ b/solution.py
@@ -199,16 +199,21 @@
     query = q_ref[...]
     lane = lax.broadcasted_iota(jnp.int32, query.shape, 1) // DH
     stacked = jnp.concatenate([jnp.where(lane == head, query, 0.0) for head in range(heads)], 0)
-    keys = jnp.concatenate([piece[:, :wide] for piece in pieces], 0)
+    k_hi, k_lo = split(jnp.concatenate([piece[:, :wide] for piece in pieces], 0))
     v_hi, v_lo = split(jnp.concatenate([piece[:, wide:] for piece in pieces], 0))
-    scores = dot3(stacked, keys, ((1,), (1,)))
+    s_hi, s_lo = split(stacked)
+    queries = jnp.concatenate(
+        [jnp.concatenate([s_hi, s_hi], 1), jnp.concatenate([s_lo, jnp.zeros_like(s_lo)], 1)], 0
+    )
+    scores = mm(queries, jnp.concatenate([k_hi, k_lo], 1), ((1,), (1,)))
+    scores = scores[: heads * rows] + scores[heads * rows :]
     top = jnp.max(scores, axis=1, keepdims=True)
-    w_hi, w_lo = split(jnp.exp(scores - top))
-    along = ((1,), (0,))
-    both = mm(jnp.concatenate([w_hi, w_lo], 0), jnp.concatenate([v_hi, jnp.ones_like(v_hi)], 1), along)
-    both = both[: heads * rows] + both[heads * rows :]
-    acc = by_head(both[:, :wide] + mm(w_hi, v_lo, along), heads)
-    total = by_head(both[:, wide:], heads)
+    weights = jnp.exp(scores - top)
+    total = jnp.sum(weights, axis=1, keepdims=True)
+    both = mm(jnp.concatenate(split(weights), 0), jnp.concatenate([v_hi, v_lo], 1), ((1,), (0,)))
+    above, below = both[: heads * rows], both[heads * rows :]
+    acc = by_head(above[:, :wide] + (above[:, wide:] + below[:, :wide]), heads)
+    total = by_head(jnp.broadcast_to(total, (heads * rows, wide)), heads)
     top = by_head(jnp.broadcast_to(top, (heads * rows, wide)), heads)
     if merge:
         high = jnp.maximum(top, top_a[...])
@@ -299,7 +304,7 @@
         return [whole[:cut]], [whole[cut:]]
     far = [piece] + [send(piece, "var", k) for k in range(2, size, 2)]
     near = [send(each, "var", 1) for each in far]
-    return far + near[:1], near[1:]
+    return far[:-1] + near[:-1], [far[-1], near[-1]]
 
 
 def on_device(

time: 79 us -> 78.7 us (level)
  transfers between devices with their start and end apart: 26 -> 26, of which waited for: 15 -> 15; matrix products, arithmetic and copies ran while one was open for 3% -> 3% of each run, Pallas kernels for 9% -> 8%
where the time goes in v9:
time: 78.7 us; the launch traced here: 78.4 us
  starting transfers between devices  33.7 us (43%)
  waiting for transfers between devices  28.7 us (36%)
  Pallas kernels  8.69 us (11%)
  local copies, waits for them, and re-layouts  4.28 us (5%)
  other arithmetic  2.83 us (4%)
    ppermute x26, starting transfers between devices, send(): return lax.ppermute(x, axis, [(i, i ^ offset) for i in range(size)])  33.7 us
    ppermute x26, waiting for transfers between devices, send(): return lax.ppermute(x, axis, [(i, i ^ offset) for i in range(size)])  28.7 us
    unnamed x26, local copies, waits for them, and re-layouts  4.28 us
    pallas_call x1, Pallas kernels, embed(): pl.pallas_call(functools.partial(embed_kernel, count), out_shape=[shape(r...  3.61 us
    concatenate x2, other arithmetic, on_device(): rest = jnp.concatenate([rest, send(rest, 'var', 1 << bit)], 0)  2.12 us
  transfers between devices with their start and end apart: 26, of which 15 were waited for; matrix products, arithmetic and copies ran while one was open for 3% of the time, Pallas kernels for 8%

profile of v9, /device:TPU:0, one launch (start us, length us, event | category | flops | bytes accessed | tf_op | source)
XLA Modules:
  0.0 78.4 jit_solution(9204098798633817359)
XLA Ops:
  0.0 0.9 %copy-done.2 = f32[128,512]{1,0:T(8,128)S(1)} copy-done((f32[128,512]{1,0:T(8,128)S(1)}, f32[128,512]{1,0:T(8,128)}, u32[]{:S(2)}) %copy-start.2) | copy-done | bytes 262168
  1.0 3.1 %collective-permute-start.16 = (f32[1,32,512]{2,1,0:T(8,128)S(1)}, f32[1,32,512]{2,1,0:T(8,128)S(1)}, u32[]{:S(2)}, u32[]{:S(2)}) collective-permute-start(f32[1,32,512]{2,1,0:T(8,128)S(1)} %bitcast.8), channel_id=1, source_target_pairs={{0,1},{1,0},{2,3},{3,2},{4,5},{5,4},{6,7},{7,6},{8,9},{9,8},{10,11... | collective-permute-start | bytes 196616 | tf_op jit(solution)/shard_map/ppermute | solution.py:284
  4.1 2.2 %collective-permute-done.16 = f32[1,32,512]{2,1,0:T(8,128)S(1)} collective-permute-done((f32[1,32,512]{2,1,0:T(8,128)S(1)}, f32[1,32,512]{2,1,0:T(8,128)S(1)}, u32[]{:S(2)}, u32[]{:S(2)}) %collective-permute-start.16) | collective-permute-done | bytes 65568 | tf_op jit(solution)/shard_map/ppermute | solution.py:284
  6.4 3.1 %collective-permute-start.17 = (f32[2,32,512]{2,1,0:T(8,128)S(1)}, f32[2,32,512]{2,1,0:T(8,128)S(1)}, u32[]{:S(2)}, u32[]{:S(2)}) collective-permute-start(f32[2,32,512]{2,1,0:T(8,128)S(1)} %pad_maximum_fusion.2), channel_id=1, source_target_pairs={{0,2},{1,3},{2,0},{3,1},{4,6},{5,7},{6,4},{7,5},{8,10},{9,11},{10,... | collective-permute-start | bytes 393224 | tf_op jit(solution)/shard_map/ppermute | solution.py:284
  9.5 5.2 %collective-permute-done.17 = f32[2,32,512]{2,1,0:T(8,128)S(1)} collective-permute-done((f32[2,32,512]{2,1,0:T(8,128)S(1)}, f32[2,32,512]{2,1,0:T(8,128)S(1)}, u32[]{:S(2)}, u32[]{:S(2)}) %collective-permute-start.17) | collective-permute-done | bytes 131104 | tf_op jit(solution)/shard_map/ppermute | solution.py:284
  14.6 0.7 maximum_bitcast_fusion
  15.3 1.6 %collective-permute-start.18 = (f32[1,3,32,512]{3,2,1,0:T(8,128)}, f32[1,3,32,512]{3,2,1,0:T(8,128)}, u32[]{:S(2)}, u32[]{:S(2)}) collective-permute-start(f32[1,3,32,512]{3,2,1,0:T(8,128)} %maximum_bitcast_fusion), channel_id=1, source_target_pairs={{0,16},{4,20},{8,24},{12,28},{16,0},{20,4},{24,8},{28,12},{1,17},{... | collective-permute-start | bytes 589832 | tf_op jit(solution)/shard_map/ppermute | solution.py:284
  16.9 3.6 %embed.1 = (f32[128,128]{1,0:T(8,128)}, f32[128,128]{1,0:T(8,128)}, f32[128,128]{1,0:T(8,128)}, f32[128,128]{1,0:T(8,128)}) custom-call(f32[128,2048]{1,0:T(8,128)} %x_hbm.1, f32[2048,512]{1,0:T(8,128)} %w_hbm.1), custom_call_target="tpu_custom_call" | custom-call | flops 805306368 | bytes 5242880 | tf_op jit(solution)/shard_map/embed/pallas_call | solution.py:111
  20.5 0.7 collective-permute-start
  21.2 3.4 %collective-permute-start.1 = (f32[128,128]{1,0:T(8,128)}, f32[128,128]{1,0:T(8,128)S(1)}, u32[]{:S(2)}, u32[]{:S(2)}) collective-permute-start(f32[128,128]{1,0:T(8,128)} %get-tuple-element.30), channel_id=1, source_target_pairs={{0,2},{1,3},{2,0},{3,1},{4,6},{5,7},{6,4},{7,5},{8,10},{9,11},{10,... | collective-permute-start | bytes 196616 | tf_op jit(solution)/shard_map/ppermute | solution.py:284
  24.6 0.3 collective-permute-start.2
  25.0 1.0 %pad_maximum_fusion.1 = f32[2,3,32,512]{3,2,1,0:T(8,128)S(1)} fusion(f32[1,3,32,512]{3,2,1,0:T(8,128)} %collective-permute-done.18, f32[1,3,32,512]{3,2,1,0:T(8,128)} %maximum_bitcast_fusion), kind=kLoop, calls=%fused_computation.1 | loop fusion | flops 98304 | bytes 786432 | tf_op jit(solution)/shard_map/concatenate | solution.py:334
  26.1 0.8 %copy-done.7 = f32[128,128]{1,0:T(8,128)S(1)} copy-done((f32[128,128]{1,0:T(8,128)S(1)}, f32[128,128]{1,0:T(8,128)}, u32[]{:S(2)}) %copy-start.7) | copy-done | bytes 65560
  27.0 1.5 %collective-permute-done.1.refs_2_ = f32[128,128]{1,0:T(8,128)S(1)} collective-permute-done((f32[128,128]{1,0:T(8,128)}, f32[128,128]{1,0:T(8,128)S(1)}, u32[]{:S(2)}, u32[]{:S(2)}) %collective-permute-start.1) | collective-permute-done | bytes 65568 | tf_op jit(solution)/shard_map/ppermute | solution.py:284
  28.5 2.5 %collective-permute-done.2.refs_3_ = f32[128,128]{1,0:T(8,128)S(1)} collective-permute-done((f32[128,128]{1,0:T(8,128)}, f32[128,128]{1,0:T(8,128)S(1)}, u32[]{:S(2)}, u32[]{:S(2)}) %collective-permute-start.2) | collective-permute-done | bytes 65568 | tf_op jit(solution)/shard_map/ppermute | solution.py:284
  31.0 0.8 collective-permute-start.5
  31.8 3.7 %collective-permute-start.3 = (f32[128,128]{1,0:T(8,128)S(1)}, f32[128,128]{1,0:T(8,128)S(1)}, u32[]{:S(2)}, u32[]{:S(2)}) collective-permute-start(f32[128,128]{1,0:T(8,128)S(1)} %shard_map.128.refs_0_.refs_4_), channel_id=1, source_target_pairs={{0,1},{1,0},{2,3},{3,2},{4,5},{5,4},{6,7},{7,6},{8,9},{9,8},{10,11... | collective-permute-start | bytes 196616 | tf_op jit(solution)/shard_map/ppermute | solution.py:284
  35.6 1.7 %collective-permute-done.5.refs_3_.refs_7_ = f32[128,128]{1,0:T(8,128)S(1)} collective-permute-done((f32[128,128]{1,0:T(8,128)S(1)}, f32[128,128]{1,0:T(8,128)S(1)}, u32[]{:S(2)}, u32[]{:S(2)}) %collective-permute-start.5) | collective-permute-done | bytes 65568 | tf_op jit(solution)/shard_map/ppermute | solution.py:284
  37.3 1.1 %collective-permute-done.4.refs_2_.refs_6_ = f32[128,128]{1,0:T(8,128)S(1)} collective-permute-done((f32[128,128]{1,0:T(8,128)S(1)}, f32[128,128]{1,0:T(8,128)S(1)}, u32[]{:S(2)}, u32[]{:S(2)}) %collective-permute-start.4) | collective-permute-done | bytes 65568 | tf_op jit(solution)/shard_map/ppermute | solution.py:284
  38.4 0.3 shard_map.131.refs_0_
  38.7 0.6 collective-permute-start.7
  39.2 1.5 %collective-permute-start.6 = (f32[128,256]{1,0:T(8,128)S(1)}, f32[128,256]{1,0:T(8,128)S(1)}, u32[]{:S(2)}, u32[]{:S(2)}) collective-permute-start(f32[128,256]{1,0:T(8,128)S(1)} %shard_map.131.refs_0_), channel_id=1, source_target_pairs={{0,8},{4,12},{8,0},{12,4},{16,24},{20,28},{24,16},{28,20},{1,9},{5... | collective-permute-start | bytes 393224 | tf_op jit(solution)/shard_map/ppermute | solution.py:284
  40.7 1.5 %collective-permute-start.11 = (f32[128,256]{1,0:T(8,128)S(1)}, f32[128,256]{1,0:T(8,128)S(1)}, u32[]{:S(2)}, u32[]{:S(2)}) collective-permute-start(f32[128,256]{1,0:T(8,128)S(1)} %shard_map.131.refs_0_), channel_id=1, source_target_pairs={{0,24},{4,28},{8,16},{12,20},{16,8},{20,12},{24,0},{28,4},{1,25},{... | collective-permute-start | bytes 393224 | tf_op jit(solution)/shard_map/ppermute | solution.py:284
  42.2 1.5 %collective-permute-done.7.refs_2_ = f32[128,256]{1,0:T(8,128)S(1)} collective-permute-done((f32[128,256]{1,0:T(8,128)S(1)}, f32[128,256]{1,0:T(8,128)S(1)}, u32[]{:S(2)}, u32[]{:S(2)}) %collective-permute-start.7) | collective-permute-done | bytes 131104 | tf_op jit(solution)/shard_map/ppermute | solution.py:284
  43.7 0.5 collective-permute-done.6.refs_1_
  44.2 2.4 %collective-permute-done.11.refs_3_ = f32[128,256]{1,0:T(8,128)S(1)} collective-permute-done((f32[128,256]{1,0:T(8,128)S(1)}, f32[128,256]{1,0:T(8,128)S(1)}, u32[]{:S(2)}, u32[]{:S(2)}) %collective-permute-start.11) | collective-permute-done | bytes 131104 | tf_op jit(solution)/shard_map/ppermute | solution.py:284
  46.6 1.2 %copy-done = f32[512,512]{1,0:T(8,128)S(1)} copy-done((f32[512,512]{1,0:T(8,128)S(1)}, f32[512,512]{1,0:T(8,128)}, u32[]{:S(2)}) %copy-start) | copy-done | bytes 1048600
  47.8 1.2 %copy-done.1 = f32[512,512]{1,0:T(8,128)S(1)} copy-done((f32[512,512]{1,0:T(8,128)S(1)}, f32[512,512]{1,0:T(8,128)}, u32[]{:S(2)}) %copy-start.1) | copy-done | bytes 1048600
  49.1 0.3 shard_map.136
  49.7 1.2 %shard_map.132 = (f32[128,128]{1,0:T(8,128)S(1)}, f32[128,128]{1,0:T(8,128)S(1)}, f32[128,128]{1,0:T(8,128)S(1)}) custom-call(f32[128,128]{1,0:T(8,128)S(1)} %shard_map.130.q_ref, f32[128,256]{1,0:T(8,128)S(1)} %shard_map.131.refs_0_, f32[128,256]{1,0:T(8,128)S(1)} %collective-permute-done.6.refs_1_, f32[128,256]{1,0:T(8,128)S(1)} %collective-permute-done.7.refs_2_, ...), custom_call_target="tpu_custom_call" | custom-call | tf_op jit(solution)/shard_map/pallas_call | solution.py:343
  50.8 0.6 shard_map.133.refs_0_
  51.5 1.8 %collective-permute-start.15 = (f32[128,128]{1,0:T(8,128)S(1)}, f32[128,128]{1,0:T(8,128)S(1)}, u32[]{:S(2)}, u32[]{:S(2)}) collective-permute-start(f32[128,128]{1,0:T(8,128)S(1)} %shard_map.133.refs_0_), channel_id=1, source_target_pairs={{0,3},{1,2},{2,1},{3,0},{4,7},{5,6},{6,5},{7,4},{8,11},{9,10},{10,... | collective-permute-start | bytes 196616 | tf_op jit(solution)/shard_map/ppermute | solution.py:284
  53.2 1.1 %collective-permute-start.14 = (f32[128,128]{1,0:T(8,128)S(1)}, f32[128,128]{1,0:T(8,128)S(1)}, u32[]{:S(2)}, u32[]{:S(2)}) collective-permute-start(f32[128,128]{1,0:T(8,128)S(1)} %shard_map.133.refs_0_), channel_id=1, source_target_pairs={{0,2},{1,3},{2,0},{3,1},{4,6},{5,7},{6,4},{7,5},{8,10},{9,11},{10,... | collective-permute-start | bytes 196616 | tf_op jit(solution)/shard_map/ppermute | solution.py:284
  54.4 1.5 %collective-permute-start.13 = (f32[128,128]{1,0:T(8,128)S(1)}, f32[128,128]{1,0:T(8,128)S(1)}, u32[]{:S(2)}, u32[]{:S(2)}) collective-permute-start(f32[128,128]{1,0:T(8,128)S(1)} %shard_map.133.refs_0_), channel_id=1, source_target_pairs={{0,1},{1,0},{2,3},{3,2},{4,5},{5,4},{6,7},{7,6},{8,9},{9,8},{10,11... | collective-permute-start | bytes 196616 | tf_op jit(solution)/shard_map/ppermute | solution.py:284
  55.9 1.1 %pad_maximum_fusion.rest_ref = f32[4,3,32,512]{3,2,1,0:T(8,128)S(1)} fusion(f32[2,3,32,512]{3,2,1,0:T(8,128)S(1)} %collective-permute-done.19, f32[1,3,32,512]{3,2,1,0:T(8,128)} %collective-permute-done.18, f32[1,3,32,512]{3,2,1,0:T(8,128)} %maximum_bitcast_fusion), kind=kLoop, calls=%fused_computation | loop fusion | flops 393216 | bytes 1572864 | tf_op jit(solution)/shard_map/concatenate | solution.py:334
  57.1 1.2 %collective-permute-done.15.refs_3_ = f32[128,128]{1,0:T(8,128)S(1)} collective-permute-done((f32[128,128]{1,0:T(8,128)S(1)}, f32[128,128]{1,0:T(8,128)S(1)}, u32[]{:S(2)}, u32[]{:S(2)}) %collective-permute-start.15) | collective-permute-done | bytes 65568 | tf_op jit(solution)/shard_map/ppermute | solution.py:284
  58.4 2.7 %collective-permute-done.14.refs_2_ = f32[128,128]{1,0:T(8,128)S(1)} collective-permute-done((f32[128,128]{1,0:T(8,128)S(1)}, f32[128,128]{1,0:T(8,128)S(1)}, u32[]{:S(2)}, u32[]{:S(2)}) %collective-permute-start.14) | collective-permute-done | bytes 65568 | tf_op jit(solution)/shard_map/ppermute | solution.py:284
  61.1 1.2 %shard_map.137 = (f32[128,128]{1,0:T(8,128)S(1)}, f32[128,128]{1,0:T(8,128)S(1)}, f32[128,128]{1,0:T(8,128)S(1)}, f32[128,128]{1,0:T(8,128)S(1)}) custom-call(f32[128,128]{1,0:T(8,128)S(1)} %shard_map.133.refs_0_, f32[128,128]{1,0:T(8,128)S(1)} %collective-permute-done.13.refs_1_, f32[128,128]{1,0:T(8,128)S(1)} %collective-permute-done.14.refs_2_, ...), custom_call_target="tpu_custom_call" | custom-call | tf_op jit(solution)/shard_map/pallas_call | solution.py:350
  62.3 1.9 %collective-permute-start.21 = (f32[128,128]{1,0:T(8,128)S(1)}, f32[128,128]{1,0:T(8,128)S(1)}, u32[]{:S(2)}, u32[]{:S(2)}) collective-permute-start(f32[128,128]{1,0:T(8,128)S(1)} %get-tuple-element.47), channel_id=1, source_target_pairs={{0,2},{1,3},{2,0},{3,1},{4,6},{5,7},{6,4},{7,5},{8,10},{9,11},{10,... | collective-permute-start | bytes 196616 | tf_op jit(solution)/shard_map/ppermute | solution.py:284
  64.2 2.5 %collective-permute-start.22 = (f32[128,128]{1,0:T(8,128)S(1)}, f32[128,128]{1,0:T(8,128)S(1)}, u32[]{:S(2)}, u32[]{:S(2)}) collective-permute-start(f32[128,128]{1,0:T(8,128)S(1)} %get-tuple-element.48), channel_id=1, source_target_pairs={{0,3},{1,2},{2,1},{3,0},{4,7},{5,6},{6,5},{7,4},{8,11},{9,10},{10,... | collective-permute-start | bytes 196616 | tf_op jit(solution)/shard_map/ppermute | solution.py:284
  66.7 0.4 collective-permute-done.20.refs_1_
  67.1 3.5 %collective-permute-done.21.refs_2_ = f32[128,128]{1,0:T(8,128)S(1)} collective-permute-done((f32[128,128]{1,0:T(8,128)S(1)}, f32[128,128]{1,0:T(8,128)S(1)}, u32[]{:S(2)}, u32[]{:S(2)}) %collective-permute-start.21) | collective-permute-done | bytes 65568 | tf_op jit(solution)/shard_map/ppermute | solution.py:284
  70.8 2.3 %collective-permute-start.25 = (f32[2,128]{1,0:T(2,128)S(1)}, f32[2,128]{1,0:T(2,128)S(1)}, u32[]{:S(2)}, u32[]{:S(2)}) collective-permute-start(f32[2,128]{1,0:T(2,128)S(1)} %get-tuple-element.50.refs_0_), channel_id=1, source_target_pairs={{0,3},{1,2},{2,1},{3,0},{4,7},{5,6},{6,5},{7,4},{8,11},{9,10},{10,... | collective-permute-start | bytes 3080 | tf_op jit(solution)/shard_map/ppermute | solution.py:284
  73.1 0.5 collective-permute-start.24
  73.5 1.7 %collective-permute-start.23 = (f32[2,128]{1,0:T(2,128)S(1)}, f32[2,128]{1,0:T(2,128)S(1)}, u32[]{:S(2)}, u32[]{:S(2)}) collective-permute-start(f32[2,128]{1,0:T(2,128)S(1)} %get-tuple-element.50.refs_0_), channel_id=1, source_target_pairs={{0,1},{1,0},{2,3},{3,2},{4,5},{5,4},{6,7},{7,6},{8,9},{9,8},{10,11... | collective-permute-start | bytes 3080 | tf_op jit(solution)/shard_map/ppermute | solution.py:284
  75.2 1.0 %collective-permute-done.25.refs_3_ = f32[2,128]{1,0:T(2,128)S(1)} collective-permute-done((f32[2,128]{1,0:T(2,128)S(1)}, f32[2,128]{1,0:T(2,128)S(1)}, u32[]{:S(2)}, u32[]{:S(2)}) %collective-permute-start.25) | collective-permute-done | bytes 1056 | tf_op jit(solution)/shard_map/ppermute | solution.py:284
  76.2 1.4 %collective-permute-done.24.refs_2_ = f32[2,128]{1,0:T(2,128)S(1)} collective-permute-done((f32[2,128]{1,0:T(2,128)S(1)}, f32[2,128]{1,0:T(2,128)S(1)}, u32[]{:S(2)}, u32[]{:S(2)}) %collective-permute-start.24) | collective-permute-done | bytes 1056 | tf_op jit(solution)/shard_map/ppermute | solution.py:284
  77.6 0.8 %shard_map.139 = f32[128,128]{1,0:T(8,128)} custom-call(f32[128,128]{1,0:T(8,128)S(1)} %get-tuple-element.49.x_ref, f32[2,128]{1,0:T(2,128)S(1)} %get-tuple-element.50.refs_0_, f32[2,128]{1,0:T(2,128)S(1)} %collective-permute-done.23.refs_1_, f32[2,128]{1,0:T(2,128)S(1)} %collective-permute-done.24.refs_2_, f32[2,128]{1,0:T(2,128)S(1)} %collective-permute-done.25.refs_3_, ...), custom_call_target="tpu_custom_call" | custom-call | tf_op jit(solution)/shard_map/pallas_call | solution.py:355
  (48 shorter events, 1.0 us)
Async XLA Ops:
  0.0 0.9 %copy-start.2 = (f32[128,512]{1,0:T(8,128)S(1)}, f32[128,512]{1,0:T(8,128)}, u32[]{:S(2)}) copy-start(f32[128,512]{1,0:T(8,128)} %own_ref.1) | copy-start | bytes 786436
  1.0 25.1 %copy-start.8 = (f32[512]{0:T(512)S(1)}, f32[512]{0:T(512)}, u32[]{:S(2)}) copy-start(f32[512]{0:T(512)} %param.15) | copy-start | bytes 6148
  1.0 34.6 %copy-start.4 = (f32[512,128]{1,0:T(8,128)S(1)}, f32[512,128]{1,0:T(8,128)}, u32[]{:S(2)}) copy-start(f32[512,128]{1,0:T(8,128)} %k_ref.1) | copy-start | bytes 786436
  1.0 34.6 %copy-start.5 = (f32[512,128]{1,0:T(8,128)S(1)}, f32[512,128]{1,0:T(8,128)}, u32[]{:S(2)}) copy-start(f32[512,128]{1,0:T(8,128)} %v_ref.1) | copy-start | bytes 786436
  1.0 34.6 %copy-start.6 = (f32[512,128]{1,0:T(8,128)S(1)}, f32[512,128]{1,0:T(8,128)}, u32[]{:S(2)}) copy-start(f32[512,128]{1,0:T(8,128)} %q_ref.1) | copy-start | bytes 786436
  1.0 5.4 %collective-permute-start.16 = (f32[1,32,512]{2,1,0:T(8,128)S(1)}, f32[1,32,512]{2,1,0:T(8,128)S(1)}, u32[]{:S(2)}, u32[]{:S(2)}) collective-permute-start(f32[1,32,512]{2,1,0:T(8,128)S(1)} %bitcast.8), channel_id=1, source_target_pairs={{0,1},{1,0},{2,3},{3,2},{4,5},{5,4},{6,7},{7,6},{8,9},{9,8},{10,11... | collective-permute-start | bytes 196616 | tf_op jit(solution)/shard_map/ppermute | solution.py:284
  6.4 8.3 %collective-permute-start.17 = (f32[2,32,512]{2,1,0:T(8,128)S(1)}, f32[2,32,512]{2,1,0:T(8,128)S(1)}, u32[]{:S(2)}, u32[]{:S(2)}) collective-permute-start(f32[2,32,512]{2,1,0:T(8,128)S(1)} %pad_maximum_fusion.2), channel_id=1, source_target_pairs={{0,2},{1,3},{2,0},{3,1},{4,6},{5,7},{6,4},{7,5},{8,10},{9,11},{10,... | collective-permute-start | bytes 393224 | tf_op jit(solution)/shard_map/ppermute | solution.py:284
  15.3 9.6 %collective-permute-start.18 = (f32[1,3,32,512]{3,2,1,0:T(8,128)}, f32[1,3,32,512]{3,2,1,0:T(8,128)}, u32[]{:S(2)}, u32[]{:S(2)}) collective-permute-start(f32[1,3,32,512]{3,2,1,0:T(8,128)} %maximum_bitcast_fusion), channel_id=1, source_target_pairs={{0,16},{4,20},{8,24},{12,28},{16,0},{20,4},{24,8},{28,12},{1,17},{... | collective-permute-start | bytes 589832 | tf_op jit(solution)/shard_map/ppermute | solution.py:284
  20.5 6.5 %collective-permute-start = (f32[128,128]{1,0:T(8,128)}, f32[128,128]{1,0:T(8,128)S(1)}, u32[]{:S(2)}, u32[]{:S(2)}) collective-permute-start(f32[128,128]{1,0:T(8,128)} %get-tuple-element.29), channel_id=1, source_target_pairs={{0,1},{1,0},{2,3},{3,2},{4,5},{5,4},{6,7},{7,6},{8,9},{9,8},{10,11... | collective-permute-start | bytes 196616 | tf_op jit(solution)/shard_map/ppermute | solution.py:284
  21.2 7.2 %collective-permute-start.1 = (f32[128,128]{1,0:T(8,128)}, f32[128,128]{1,0:T(8,128)S(1)}, u32[]{:S(2)}, u32[]{:S(2)}) collective-permute-start(f32[128,128]{1,0:T(8,128)} %get-tuple-element.30), channel_id=1, source_target_pairs={{0,2},{1,3},{2,0},{3,1},{4,6},{5,7},{6,4},{7,5},{8,10},{9,11},{10,... | collective-permute-start | bytes 196616 | tf_op jit(solution)/shard_map/ppermute | solution.py:284
  24.6 32.4 %copy-start.3 = (f32[128,512]{1,0:T(8,128)S(1)}, f32[128,512]{1,0:T(8,128)}, u32[]{:S(2)}) copy-start(f32[128,512]{1,0:T(8,128)} %own_ref.1) | copy-start | bytes 786436
  24.6 6.4 %collective-permute-start.2 = (f32[128,128]{1,0:T(8,128)}, f32[128,128]{1,0:T(8,128)S(1)}, u32[]{:S(2)}, u32[]{:S(2)}) collective-permute-start(f32[128,128]{1,0:T(8,128)} %get-tuple-element.31), channel_id=1, source_target_pairs={{0,3},{1,2},{2,1},{3,0},{4,7},{5,6},{6,5},{7,4},{8,11},{9,10},{10,... | collective-permute-start | bytes 196616 | tf_op jit(solution)/shard_map/ppermute | solution.py:284
  26.0 29.9 %collective-permute-start.19 = (f32[2,3,32,512]{3,2,1,0:T(8,128)S(1)}, f32[2,3,32,512]{3,2,1,0:T(8,128)S(1)}, u32[]{:S(2)}, u32[]{:S(2)}) collective-permute-start(f32[2,3,32,512]{3,2,1,0:T(8,128)S(1)} %pad_maximum_fusion.1), channel_id=1, source_target_pairs={{0,4},{4,0},{8,12},{12,8},{16,20},{20,16},{24,28},{28,24},{1,5},{5... | collective-permute-start | bytes 1179656 | tf_op jit(solution)/shard_map/ppermute | solution.py:284
  26.1 0.8 %copy-start.7 = (f32[128,128]{1,0:T(8,128)S(1)}, f32[128,128]{1,0:T(8,128)}, u32[]{:S(2)}) copy-start(f32[128,128]{1,0:T(8,128)} %get-tuple-element.28.x_ref) | copy-start | bytes 196612
  31.0 30.0 %copy-start.9 = (f32[512]{0:T(512)S(1)}, f32[512]{0:T(512)}, u32[]{:S(2)}) copy-start(f32[512]{0:T(512)} %param.20) | copy-start | bytes 6148
  31.0 30.0 %copy-start.10 = (f32[512]{0:T(512)S(1)}, f32[512]{0:T(512)}, u32[]{:S(2)}) copy-start(f32[512]{0:T(512)} %param.21) | copy-start | bytes 6148
  31.0 6.3 %collective-permute-start.5 = (f32[128,128]{1,0:T(8,128)S(1)}, f32[128,128]{1,0:T(8,128)S(1)}, u32[]{:S(2)}, u32[]{:S(2)}) collective-permute-start(f32[128,128]{1,0:T(8,128)S(1)} %shard_map.128.refs_0_.refs_4_), channel_id=1, source_target_pairs={{0,3},{1,2},{2,1},{3,0},{4,7},{5,6},{6,5},{7,4},{8,11},{9,10},{10,... | collective-permute-start | bytes 196616 | tf_op jit(solution)/shard_map/ppermute | solution.py:284
  31.8 6.6 %collective-permute-start.4 = (f32[128,128]{1,0:T(8,128)S(1)}, f32[128,128]{1,0:T(8,128)S(1)}, u32[]{:S(2)}, u32[]{:S(2)}) collective-permute-start(f32[128,128]{1,0:T(8,128)S(1)} %shard_map.128.refs_0_.refs_4_), channel_id=1, source_target_pairs={{0,2},{1,3},{2,0},{3,1},{4,6},{5,7},{6,4},{7,5},{8,10},{9,11},{10,... | collective-permute-start | bytes 196616 | tf_op jit(solution)/shard_map/ppermute | solution.py:284
  31.8 6.6 %collective-permute-start.3 = (f32[128,128]{1,0:T(8,128)S(1)}, f32[128,128]{1,0:T(8,128)S(1)}, u32[]{:S(2)}, u32[]{:S(2)}) collective-permute-start(f32[128,128]{1,0:T(8,128)S(1)} %shard_map.128.refs_0_.refs_4_), channel_id=1, source_target_pairs={{0,1},{1,0},{2,3},{3,2},{4,5},{5,4},{6,7},{7,6},{8,9},{9,8},{10,11... | collective-permute-start | bytes 196616 | tf_op jit(solution)/shard_map/ppermute | solution.py:284
  38.7 5.0 %collective-permute-start.7 = (f32[128,256]{1,0:T(8,128)S(1)}, f32[128,256]{1,0:T(8,128)S(1)}, u32[]{:S(2)}, u32[]{:S(2)}) collective-permute-start(f32[128,256]{1,0:T(8,128)S(1)} %shard_map.131.refs_0_), channel_id=1, source_target_pairs={{0,16},{4,20},{8,24},{12,28},{16,0},{20,4},{24,8},{28,12},{1,17},{... | collective-permute-start | bytes 393224 | tf_op jit(solution)/shard_map/ppermute | solution.py:284
  39.2 5.0 %collective-permute-start.6 = (f32[128,256]{1,0:T(8,128)S(1)}, f32[128,256]{1,0:T(8,128)S(1)}, u32[]{:S(2)}, u32[]{:S(2)}) collective-permute-start(f32[128,256]{1,0:T(8,128)S(1)} %shard_map.131.refs_0_), channel_id=1, source_target_pairs={{0,8},{4,12},{8,0},{12,4},{16,24},{20,28},{24,16},{28,20},{1,9},{5... | collective-permute-start | bytes 393224 | tf_op jit(solution)/shard_map/ppermute | solution.py:284
  40.7 5.9 %collective-permute-start.11 = (f32[128,256]{1,0:T(8,128)S(1)}, f32[128,256]{1,0:T(8,128)S(1)}, u32[]{:S(2)}, u32[]{:S(2)}) collective-permute-start(f32[128,256]{1,0:T(8,128)S(1)} %shard_map.131.refs_0_), channel_id=1, source_target_pairs={{0,24},{4,28},{8,16},{12,20},{16,8},{20,12},{24,0},{28,4},{1,25},{... | collective-permute-start | bytes 393224 | tf_op jit(solution)/shard_map/ppermute | solution.py:284
  42.2 7.4 %collective-permute-start.8 = (f32[128,256]{1,0:T(8,128)S(1)}, f32[128,256]{1,0:T(8,128)S(1)}, u32[]{:S(2)}, u32[]{:S(2)}) collective-permute-start(f32[128,256]{1,0:T(8,128)S(1)} %shard_map.131.refs_0_), channel_id=1, source_target_pairs={{0,4},{4,0},{8,12},{12,8},{16,20},{20,16},{24,28},{28,24},{1,5},{5... | collective-permute-start | bytes 393224 | tf_op jit(solution)/shard_map/ppermute | solution.py:284
  43.7 5.9 %collective-permute-start.10 = (f32[128,256]{1,0:T(8,128)S(1)}, f32[128,256]{1,0:T(8,128)S(1)}, u32[]{:S(2)}, u32[]{:S(2)}) collective-permute-start(f32[128,256]{1,0:T(8,128)S(1)} %collective-permute-done.7.refs_2_), channel_id=1, source_target_pairs={{0,4},{4,0},{8,12},{12,8},{16,20},{20,16},{24,28},{28,24},{1,5},{5... | collective-permute-start | bytes 393224 | tf_op jit(solution)/shard_map/ppermute | solution.py:284
  44.2 5.4 %collective-permute-start.9 = (f32[128,256]{1,0:T(8,128)S(1)}, f32[128,256]{1,0:T(8,128)S(1)}, u32[]{:S(2)}, u32[]{:S(2)}) collective-permute-start(f32[128,256]{1,0:T(8,128)S(1)} %collective-permute-done.6.refs_1_), channel_id=1, source_target_pairs={{0,4},{4,0},{8,12},{12,8},{16,20},{20,16},{24,28},{28,24},{1,5},{5... | collective-permute-start | bytes 393224 | tf_op jit(solution)/shard_map/ppermute | solution.py:284
  46.6 4.2 %collective-permute-start.12 = (f32[128,256]{1,0:T(8,128)S(1)}, f32[128,256]{1,0:T(8,128)S(1)}, u32[]{:S(2)}, u32[]{:S(2)}) collective-permute-start(f32[128,256]{1,0:T(8,128)S(1)} %collective-permute-done.11.refs_3_), channel_id=1, source_target_pairs={{0,4},{4,0},{8,12},{12,8},{16,20},{20,16},{24,28},{28,24},{1,5},{5... | collective-permute-start | bytes 393224 | tf_op jit(solution)/shard_map/ppermute | solution.py:284
  46.6 1.2 %copy-start = (f32[512,512]{1,0:T(8,128)S(1)}, f32[512,512]{1,0:T(8,128)}, u32[]{:S(2)}) copy-start(f32[512,512]{1,0:T(8,128)} %refs_0_.1) | copy-start | bytes 3145732
  47.8 1.2 %copy-start.1 = (f32[512,512]{1,0:T(8,128)S(1)}, f32[512,512]{1,0:T(8,128)}, u32[]{:S(2)}) copy-start(f32[512,512]{1,0:T(8,128)} %refs_1_.1) | copy-start | bytes 3145732
  49.3 28.2 %copy-start.11 = (f32[512]{0:T(512)S(1)}, f32[512]{0:T(512)}, u32[]{:S(2)}) copy-start(f32[512]{0:T(512)} %param.24) | copy-start | bytes 6148
  49.4 28.2 %copy-start.12 = (f32[512]{0:T(512)S(1)}, f32[512]{0:T(512)}, u32[]{:S(2)}) copy-start(f32[512]{0:T(512)} %param.25) | copy-start | bytes 6148
  51.5 6.9 %collective-permute-start.15 = (f32[128,128]{1,0:T(8,128)S(1)}, f32[128,128]{1,0:T(8,128)S(1)}, u32[]{:S(2)}, u32[]{:S(2)}) collective-permute-start(f32[128,128]{1,0:T(8,128)S(1)} %shard_map.133.refs_0_), channel_id=1, source_target_pairs={{0,3},{1,2},{2,1},{3,0},{4,7},{5,6},{6,5},{7,4},{8,11},{9,10},{10,... | collective-permute-start | bytes 196616 | tf_op jit(solution)/shard_map/ppermute | solution.py:284
  53.2 7.8 %collective-permute-start.14 = (f32[128,128]{1,0:T(8,128)S(1)}, f32[128,128]{1,0:T(8,128)S(1)}, u32[]{:S(2)}, u32[]{:S(2)}) collective-permute-start(f32[128,128]{1,0:T(8,128)S(1)} %shard_map.133.refs_0_), channel_id=1, source_target_pairs={{0,2},{1,3},{2,0},{3,1},{4,6},{5,7},{6,4},{7,5},{8,10},{9,11},{10,... | collective-permute-start | bytes 196616 | tf_op jit(solution)/shard_map/ppermute | solution.py:284
  54.4 6.7 %collective-permute-start.13 = (f32[128,128]{1,0:T(8,128)S(1)}, f32[128,128]{1,0:T(8,128)S(1)}, u32[]{:S(2)}, u32[]{:S(2)}) collective-permute-start(f32[128,128]{1,0:T(8,128)S(1)} %shard_map.133.refs_0_), channel_id=1, source_target_pairs={{0,1},{1,0},{2,3},{3,2},{4,5},{5,4},{6,7},{7,6},{8,9},{9,8},{10,11... | collective-permute-start | bytes 196616 | tf_op jit(solution)/shard_map/ppermute | solution.py:284
  62.3 4.9 %collective-permute-start.20 = (f32[128,128]{1,0:T(8,128)S(1)}, f32[128,128]{1,0:T(8,128)S(1)}, u32[]{:S(2)}, u32[]{:S(2)}) collective-permute-start(f32[128,128]{1,0:T(8,128)S(1)} %get-tuple-element.46), channel_id=1, source_target_pairs={{0,1},{1,0},{2,3},{3,2},{4,5},{5,4},{6,7},{7,6},{8,9},{9,8},{10,11... | collective-permute-start | bytes 196616 | tf_op jit(solution)/shard_map/ppermute | solution.py:284
  62.3 8.3 %collective-permute-start.21 = (f32[128,128]{1,0:T(8,128)S(1)}, f32[128,128]{1,0:T(8,128)S(1)}, u32[]{:S(2)}, u32[]{:S(2)}) collective-permute-start(f32[128,128]{1,0:T(8,128)S(1)} %get-tuple-element.47), channel_id=1, source_target_pairs={{0,2},{1,3},{2,0},{3,1},{4,6},{5,7},{6,4},{7,5},{8,10},{9,11},{10,... | collective-permute-start | bytes 196616 | tf_op jit(solution)/shard_map/ppermute | solution.py:284
  64.2 6.4 %collective-permute-start.22 = (f32[128,128]{1,0:T(8,128)S(1)}, f32[128,128]{1,0:T(8,128)S(1)}, u32[]{:S(2)}, u32[]{:S(2)}) collective-permute-start(f32[128,128]{1,0:T(8,128)S(1)} %get-tuple-element.48), channel_id=1, source_target_pairs={{0,3},{1,2},{2,1},{3,0},{4,7},{5,6},{6,5},{7,4},{8,11},{9,10},{10,... | collective-permute-start | bytes 196616 | tf_op jit(solution)/shard_map/ppermute | solution.py:284
  70.8 5.4 %collective-permute-start.25 = (f32[2,128]{1,0:T(2,128)S(1)}, f32[2,128]{1,0:T(2,128)S(1)}, u32[]{:S(2)}, u32[]{:S(2)}) collective-permute-start(f32[2,128]{1,0:T(2,128)S(1)} %get-tuple-element.50.refs_0_), channel_id=1, source_target_pairs={{0,3},{1,2},{2,1},{3,0},{4,7},{5,6},{6,5},{7,4},{8,11},{9,10},{10,... | collective-permute-start | bytes 3080 | tf_op jit(solution)/shard_map/ppermute | solution.py:284
  73.1 4.5 %collective-permute-start.24 = (f32[2,128]{1,0:T(2,128)S(1)}, f32[2,128]{1,0:T(2,128)S(1)}, u32[]{:S(2)}, u32[]{:S(2)}) collective-permute-start(f32[2,128]{1,0:T(2,128)S(1)} %get-tuple-element.50.refs_0_), channel_id=1, source_target_pairs={{0,2},{1,3},{2,0},{3,1},{4,6},{5,7},{6,4},{7,5},{8,10},{9,11},{10,... | collective-permute-start | bytes 3080 | tf_op jit(solution)/shard_map/ppermute | solution.py:284
  73.5 4.0 %collective-permute-start.23 = (f32[2,128]{1,0:T(2,128)S(1)}, f32[2,128]{1,0:T(2,128)S(1)}, u32[]{:S(2)}, u32[]{:S(2)}) collective-permute-start(f32[2,128]{1,0:T(2,128)S(1)} %get-tuple-element.50.refs_0_), channel_id=1, source_target_pairs={{0,1},{1,0},{2,3},{3,2},{4,5},{5,4},{6,7},{7,6},{8,9},{9,8},{10,11... | collective-permute-start | bytes 3080 | tf_op jit(solution)/shard_map/ppermute | solution.py:284

commit v10 on v9

--- a/solution.py
+++ b/solution.py
@@ -136,14 +136,12 @@
     out[...] = w_ref[pl.ds(pl.multiple_of(part * size, size), size), :]
 
 
-def order_kernel(bits, own_ref, rest_ref, hi, lo):
+def order_kernel(bits, rest_ref, hi, lo):
     me = piece_of(lax.axis_index("var"), bits)
-    rows = own_ref.shape[0]
-    size = rows >> len(bits)
-    hi[0:rows, :], lo[0:rows, :] = split(own_ref[...])
-    for apart in range(1 << len(bits)):
-        for k in range(rest_ref.shape[1]):
-            at = pl.ds(pl.multiple_of((k + 1) * rows + (me ^ apart) * size, size), size)
+    pieces, others, size, _ = rest_ref.shape
+    for apart in range(pieces):
+        for k in range(others):
+            at = pl.ds(pl.multiple_of(k * pieces * size + (me ^ apart) * size, size), size)
             hi[at, :], lo[at, :] = split(rest_ref[apart, k])
 
 
@@ -236,15 +234,20 @@
     return 0.5 * v * (1.0 + lax.erf(v * (1.0 / math.sqrt(2.0))))
 
 
-def post_kernel(count, *refs):
+def own_kernel(mixed, weight, *refs):
+    emb, out = refs[:-1], refs[-1]
+    embedded = jnp.concatenate(butterfly([e[...] for e in emb], lax.axis_index("head")), 1)
+    out[...] = embedded + dot3(mixed[...], weight[...])
+
+
+def post_kernel(count, base, *refs):
     pos = lax.axis_index("head")
-    mixed, emb = refs[:count], refs[count : 2 * count]
-    o_hi, o_lo, gain, bias, in_hi, in_lo, out_hi, out_lo = refs[2 * count : 2 * count + 8]
-    outs = refs[2 * count + 8 :]
+    mixed = refs[: count - 1]
+    o_hi, o_lo, gain, bias, in_hi, in_lo, out_hi, out_lo = refs[count - 1 : count + 7]
+    outs = refs[count + 7 :]
     stream = jnp.concatenate([m[...] for m in mixed], 1)
-    attention = dot3_split(stream, o_hi[...], o_lo[...])
-    embedded = jnp.concatenate(butterfly([e[...] for e in emb], pos), 1)
-    normed = normalise(embedded + attention, gain[...], bias[...])
+    attended = base[...] + dot3_split(stream, o_hi[...], o_lo[...])
+    normed = normalise(attended, gain[...], bias[...])
     hidden = gelu(dot3_split(normed, in_hi[...], in_lo[...]))
     partial = butterfly(columns(dot3_split(hidden, out_hi[...], out_lo[...]), count), pos)
     mine = butterfly(columns(normed, count), pos)[0]
@@ -265,9 +268,16 @@
     stats[...] = jnp.concatenate([centre, jnp.sum(spread * spread, axis=0, keepdims=True)], 0)
 
 
+def columns_kernel(gain, bias, *outs):
+    pos = lax.axis_index("head")
+    width, rows = outs[0].shape
+    pair = jnp.concatenate([gain[pos], bias[pos], jnp.zeros((6, width), F32)], 0).T
+    for at, out in enumerate(outs):
+        out[...] = jnp.broadcast_to(pair[:, at : at + 1], (width, rows))
+
+
 def final_kernel(count, x_ref, *refs):
-    pos = lax.axis_index("head")
-    stats, gain, bias, out = refs[:count], refs[count], refs[count + 1], refs[count + 2]
+    stats, (gain, bias, out) = refs[:count], refs[count:]
     width = x_ref.shape[0]
     centres = [s[0:1, :] for s in stats]
     centre = sum(centres[1:], centres[0]) * (1.0 / count)
@@ -275,8 +285,7 @@
     for each in centres:
         square = square + width * (each - centre) * (each - centre)
     scale = lax.rsqrt(square * (1.0 / (count * width)) + EPS)
-    pair = jnp.concatenate([gain[pos], bias[pos], jnp.zeros((6, width), F32)], 0).T
-    out[...] = (x_ref[...] - centre) * scale * pair[:, 0:1] + pair[:, 1:2]
+    out[...] = (x_ref[...] - centre) * scale * gain[...] + bias[...]
 
 
 def send(x, axis, offset):
@@ -339,7 +348,7 @@
     first, later = gather_pieces(pair)
     ffn = call(split_kernel, halves_of(*ffn_in.shape) + halves_of(*ffn_out.shape))(ffn_in, ffn_out)
     order = functools.partial(order_kernel, bits)
-    whole_out = call(order, halves_of(n * heads_width, model))(out_weight, rest)
+    whole_out = call(order, halves_of((n - 1) * heads_width, model))(rest)
     state = call(
         functools.partial(attend_kernel, merge=False), [shape(rows, heads_width)] * 3, limit=16
     )(queries, *first)
@@ -347,14 +356,16 @@
         functools.partial(attend_kernel, merge=True), shape(rows, heads_width), limit=16
     )(queries, *state, *later)
     mixes = spread_out(mixed, "head")
+    base = call(own_kernel, shape(rows, model))(mixed, out_weight, *emb)
     partial = call(functools.partial(post_kernel, n), [block] * n, limit=16)(
-        *mixes, *emb, *whole_out, norm1_gain[None, :], norm1_bias[None, :], *ffn
+        base, *mixes[1:], *whole_out, norm1_gain[None, :], norm1_bias[None, :], *ffn
+    )
+    scales = call(columns_kernel, [shape(width, rows)] * 2)(
+        norm2_gain.reshape(n, 1, width), norm2_bias.reshape(n, 1, width)
     )
     got = hand_out(partial, "head")
     flipped, stats = call(functools.partial(stats_kernel, n), [shape(width, rows), shape(2, rows)])(*got)
-    return call(functools.partial(final_kernel, n), shape(width, rows))(
-        flipped, *spread_out(stats, "head"), norm2_gain.reshape(n, 1, width), norm2_bias.reshape(n, 1, width)
-    )
+    return call(functools.partial(final_kernel, n), shape(width, rows))(flipped, *spread_out(stats, "head"), *scales)
 
 
 def solution(mesh):

time: 78.7 us -> 80.8 us (1.027)
  waiting for transfers between devices: 28.7 us -> 30 us
    ppermute x26, waiting for transfers between devices: 28.7 us -> 30 us  [send(): return lax.ppermute(x, axis, [(i, i ^ offset) for i in range(size)])]
  transfers between devices with their start and end apart: 26 -> 26, of which waited for: 15 -> 13; matrix products, arithmetic and copies ran while one was open for 3% -> 3% of each run, Pallas kernels for 8% -> 9%
where the time goes in v10:
time: 80.8 us; the launch traced here: 80.5 us
  starting transfers between devices  34.2 us (42%)
  waiting for transfers between devices  30 us (37%)
  Pallas kernels  8.89 us (11%)
  local copies, waits for them, and re-layouts  4.28 us (5%)
  other arithmetic  2.82 us (3%)
    ppermute x26, starting transfers between devices, send(): return lax.ppermute(x, axis, [(i, i ^ offset) for i in range(size)])  34.2 us
    ppermute x26, waiting for transfers between devices, send(): return lax.ppermute(x, axis, [(i, i ^ offset) for i in range(size)])  30 us
    unnamed x26, local copies, waits for them, and re-layouts  4.28 us
    pallas_call x1, Pallas kernels, embed(): pl.pallas_call(functools.partial(embed_kernel, count), out_shape=[shape(r...  3.6 us
    concatenate x2, other arithmetic, on_device(): rest = jnp.concatenate([rest, send(rest, 'var', 1 << bit)], 0)  2.12 us
  transfers between devices with their start and end apart: 26, of which 13 were waited for; matrix products, arithmetic and copies ran while one was open for 3% of the time, Pallas kernels for 9%

profile of v10, /device:TPU:0, one launch (start us, length us, event | category | flops | bytes accessed | tf_op | source)
XLA Modules:
  0.0 80.5 jit_solution(10378846636931214296)
XLA Ops:
  0.0 0.9 %copy-done = f32[128,512]{1,0:T(8,128)S(1)} copy-done((f32[128,512]{1,0:T(8,128)S(1)}, f32[128,512]{1,0:T(8,128)}, u32[]{:S(2)}) %copy-start) | copy-done | bytes 262168
  1.0 3.1 %collective-permute-start.16 = (f32[1,32,512]{2,1,0:T(8,128)S(1)}, f32[1,32,512]{2,1,0:T(8,128)S(1)}, u32[]{:S(2)}, u32[]{:S(2)}) collective-permute-start(f32[1,32,512]{2,1,0:T(8,128)S(1)} %bitcast.8), channel_id=1, source_target_pairs={{0,1},{1,0},{2,3},{3,2},{4,5},{5,4},{6,7},{7,6},{8,9},{9,8},{10,11... | collective-permute-start | bytes 196616 | tf_op jit(solution)/shard_map/ppermute | solution.py:293
  4.1 2.2 %collective-permute-done.16 = f32[1,32,512]{2,1,0:T(8,128)S(1)} collective-permute-done((f32[1,32,512]{2,1,0:T(8,128)S(1)}, f32[1,32,512]{2,1,0:T(8,128)S(1)}, u32[]{:S(2)}, u32[]{:S(2)}) %collective-permute-start.16) | collective-permute-done | bytes 65568 | tf_op jit(solution)/shard_map/ppermute | solution.py:293
  6.4 3.1 %collective-permute-start.17 = (f32[2,32,512]{2,1,0:T(8,128)S(1)}, f32[2,32,512]{2,1,0:T(8,128)S(1)}, u32[]{:S(2)}, u32[]{:S(2)}) collective-permute-start(f32[2,32,512]{2,1,0:T(8,128)S(1)} %pad_maximum_fusion.2), channel_id=1, source_target_pairs={{0,2},{1,3},{2,0},{3,1},{4,6},{5,7},{6,4},{7,5},{8,10},{9,11},{10,... | collective-permute-start | bytes 393224 | tf_op jit(solution)/shard_map/ppermute | solution.py:293
  9.5 5.2 %collective-permute-done.17 = f32[2,32,512]{2,1,0:T(8,128)S(1)} collective-permute-done((f32[2,32,512]{2,1,0:T(8,128)S(1)}, f32[2,32,512]{2,1,0:T(8,128)S(1)}, u32[]{:S(2)}, u32[]{:S(2)}) %collective-permute-start.17) | collective-permute-done | bytes 131104 | tf_op jit(solution)/shard_map/ppermute | solution.py:293
  14.6 0.7 maximum_bitcast_fusion
  15.3 1.6 %collective-permute-start.18 = (f32[1,3,32,512]{3,2,1,0:T(8,128)}, f32[1,3,32,512]{3,2,1,0:T(8,128)}, u32[]{:S(2)}, u32[]{:S(2)}) collective-permute-start(f32[1,3,32,512]{3,2,1,0:T(8,128)} %maximum_bitcast_fusion), channel_id=1, source_target_pairs={{0,16},{4,20},{8,24},{12,28},{16,0},{20,4},{24,8},{28,12},{1,17},{... | collective-permute-start | bytes 589832 | tf_op jit(solution)/shard_map/ppermute | solution.py:293
  16.9 3.6 %embed.1 = (f32[128,128]{1,0:T(8,128)}, f32[128,128]{1,0:T(8,128)}, f32[128,128]{1,0:T(8,128)}, f32[128,128]{1,0:T(8,128)}) custom-call(f32[128,2048]{1,0:T(8,128)} %x_hbm.1, f32[2048,512]{1,0:T(8,128)} %w_hbm.1), custom_call_target="tpu_custom_call" | custom-call | flops 805306368 | bytes 5242880 | tf_op jit(solution)/shard_map/embed/pallas_call | solution.py:111
  20.5 0.7 collective-permute-start
  21.2 3.4 %collective-permute-start.1 = (f32[128,128]{1,0:T(8,128)}, f32[128,128]{1,0:T(8,128)S(1)}, u32[]{:S(2)}, u32[]{:S(2)}) collective-permute-start(f32[128,128]{1,0:T(8,128)} %get-tuple-element.32), channel_id=1, source_target_pairs={{0,2},{1,3},{2,0},{3,1},{4,6},{5,7},{6,4},{7,5},{8,10},{9,11},{10,... | collective-permute-start | bytes 196616 | tf_op jit(solution)/shard_map/ppermute | solution.py:293
  24.6 0.3 collective-permute-start.2
  25.0 1.0 %pad_maximum_fusion.1 = f32[2,3,32,512]{3,2,1,0:T(8,128)S(1)} fusion(f32[1,3,32,512]{3,2,1,0:T(8,128)} %collective-permute-done.18, f32[1,3,32,512]{3,2,1,0:T(8,128)} %maximum_bitcast_fusion), kind=kLoop, calls=%fused_computation.1 | loop fusion | flops 98304 | bytes 786432 | tf_op jit(solution)/shard_map/concatenate | solution.py:343
  26.1 0.8 %copy-done.7 = f32[128,128]{1,0:T(8,128)S(1)} copy-done((f32[128,128]{1,0:T(8,128)S(1)}, f32[128,128]{1,0:T(8,128)}, u32[]{:S(2)}) %copy-start.7) | copy-done | bytes 65560
  27.0 1.5 %collective-permute-done.1.refs_2_ = f32[128,128]{1,0:T(8,128)S(1)} collective-permute-done((f32[128,128]{1,0:T(8,128)}, f32[128,128]{1,0:T(8,128)S(1)}, u32[]{:S(2)}, u32[]{:S(2)}) %collective-permute-start.1) | collective-permute-done | bytes 65568 | tf_op jit(solution)/shard_map/ppermute | solution.py:293
  28.5 2.4 %collective-permute-done.2.refs_3_ = f32[128,128]{1,0:T(8,128)S(1)} collective-permute-done((f32[128,128]{1,0:T(8,128)}, f32[128,128]{1,0:T(8,128)S(1)}, u32[]{:S(2)}, u32[]{:S(2)}) %collective-permute-start.2) | collective-permute-done | bytes 65568 | tf_op jit(solution)/shard_map/ppermute | solution.py:293
  31.0 1.3 %collective-permute-start.4 = (f32[128,128]{1,0:T(8,128)S(1)}, f32[128,128]{1,0:T(8,128)S(1)}, u32[]{:S(2)}, u32[]{:S(2)}) collective-permute-start(f32[128,128]{1,0:T(8,128)S(1)} %shard_map.128.refs_0_), channel_id=1, source_target_pairs={{0,2},{1,3},{2,0},{3,1},{4,6},{5,7},{6,4},{7,5},{8,10},{9,11},{10,... | collective-permute-start | bytes 196616 | tf_op jit(solution)/shard_map/ppermute | solution.py:293
  32.3 3.0 %collective-permute-start.5 = (f32[128,128]{1,0:T(8,128)S(1)}, f32[128,128]{1,0:T(8,128)S(1)}, u32[]{:S(2)}, u32[]{:S(2)}) collective-permute-start(f32[128,128]{1,0:T(8,128)S(1)} %shard_map.128.refs_0_), channel_id=1, source_target_pairs={{0,3},{1,2},{2,1},{3,0},{4,7},{5,6},{6,5},{7,4},{8,11},{9,10},{10,... | collective-permute-start | bytes 196616 | tf_op jit(solution)/shard_map/ppermute | solution.py:293
  35.6 1.3 %collective-permute-done.4.refs_2_ = f32[128,128]{1,0:T(8,128)S(1)} collective-permute-done((f32[128,128]{1,0:T(8,128)S(1)}, f32[128,128]{1,0:T(8,128)S(1)}, u32[]{:S(2)}, u32[]{:S(2)}) %collective-permute-start.4) | collective-permute-done | bytes 65568 | tf_op jit(solution)/shard_map/ppermute | solution.py:293
  36.8 1.6 %collective-permute-done.5.refs_3_ = f32[128,128]{1,0:T(8,128)S(1)} collective-permute-done((f32[128,128]{1,0:T(8,128)S(1)}, f32[128,128]{1,0:T(8,128)S(1)}, u32[]{:S(2)}, u32[]{:S(2)}) %collective-permute-start.5) | collective-permute-done | bytes 65568 | tf_op jit(solution)/shard_map/ppermute | solution.py:293
  38.4 0.3 shard_map.131.refs_0_
  38.7 0.6 collective-permute-start.7
  39.3 1.5 %collective-permute-start.6 = (f32[128,256]{1,0:T(8,128)S(1)}, f32[128,256]{1,0:T(8,128)S(1)}, u32[]{:S(2)}, u32[]{:S(2)}) collective-permute-start(f32[128,256]{1,0:T(8,128)S(1)} %shard_map.131.refs_0_), channel_id=1, source_target_pairs={{0,8},{4,12},{8,0},{12,4},{16,24},{20,28},{24,16},{28,20},{1,9},{5... | collective-permute-start | bytes 393224 | tf_op jit(solution)/shard_map/ppermute | solution.py:293
  40.8 1.5 %collective-permute-start.11 = (f32[128,256]{1,0:T(8,128)S(1)}, f32[128,256]{1,0:T(8,128)S(1)}, u32[]{:S(2)}, u32[]{:S(2)}) collective-permute-start(f32[128,256]{1,0:T(8,128)S(1)} %shard_map.131.refs_0_), channel_id=1, source_target_pairs={{0,24},{4,28},{8,16},{12,20},{16,8},{20,12},{24,0},{28,4},{1,25},{... | collective-permute-start | bytes 393224 | tf_op jit(solution)/shard_map/ppermute | solution.py:293
  42.3 2.1 %collective-permute-done.7.refs_2_ = f32[128,256]{1,0:T(8,128)S(1)} collective-permute-done((f32[128,256]{1,0:T(8,128)S(1)}, f32[128,256]{1,0:T(8,128)S(1)}, u32[]{:S(2)}, u32[]{:S(2)}) %collective-permute-start.7) | collective-permute-done | bytes 131104 | tf_op jit(solution)/shard_map/ppermute | solution.py:293
  44.4 0.5 collective-permute-start.9
  44.9 1.8 %collective-permute-done.11.refs_3_ = f32[128,256]{1,0:T(8,128)S(1)} collective-permute-done((f32[128,256]{1,0:T(8,128)S(1)}, f32[128,256]{1,0:T(8,128)S(1)}, u32[]{:S(2)}, u32[]{:S(2)}) %collective-permute-start.11) | collective-permute-done | bytes 131104 | tf_op jit(solution)/shard_map/ppermute | solution.py:293
  46.6 1.2 %copy-done.2 = f32[512,512]{1,0:T(8,128)S(1)} copy-done((f32[512,512]{1,0:T(8,128)S(1)}, f32[512,512]{1,0:T(8,128)}, u32[]{:S(2)}) %copy-start.2) | copy-done | bytes 1048600
  47.9 1.2 %copy-done.3 = f32[512,512]{1,0:T(8,128)S(1)} copy-done((f32[512,512]{1,0:T(8,128)S(1)}, f32[512,512]{1,0:T(8,128)}, u32[]{:S(2)}) %copy-start.3) | copy-done | bytes 1048600
  49.1 0.3 shard_map.137
  49.7 1.2 %shard_map.132 = (f32[128,128]{1,0:T(8,128)S(1)}, f32[128,128]{1,0:T(8,128)S(1)}, f32[128,128]{1,0:T(8,128)S(1)}) custom-call(f32[128,128]{1,0:T(8,128)S(1)} %shard_map.130.q_ref, f32[128,256]{1,0:T(8,128)S(1)} %shard_map.131.refs_0_, f32[128,256]{1,0:T(8,128)S(1)} %collective-permute-done.6.refs_1_, f32[128,256]{1,0:T(8,128)S(1)} %collective-permute-done.7.refs_2_, ...), custom_call_target="tpu_custom_call" | custom-call | tf_op jit(solution)/shard_map/pallas_call | solution.py:352
  50.9 0.6 shard_map.133.mixed
  51.5 1.2 %collective-permute-start.13 = (f32[128,128]{1,0:T(8,128)S(1)}, f32[128,128]{1,0:T(8,128)S(1)}, u32[]{:S(2)}, u32[]{:S(2)}) collective-permute-start(f32[128,128]{1,0:T(8,128)S(1)} %shard_map.133.mixed), channel_id=1, source_target_pairs={{0,1},{1,0},{2,3},{3,2},{4,5},{5,4},{6,7},{7,6},{8,9},{9,8},{10,11... | collective-permute-start | bytes 196616 | tf_op jit(solution)/shard_map/ppermute | solution.py:293
  52.6 2.5 %collective-permute-start.14 = (f32[128,128]{1,0:T(8,128)S(1)}, f32[128,128]{1,0:T(8,128)S(1)}, u32[]{:S(2)}, u32[]{:S(2)}) collective-permute-start(f32[128,128]{1,0:T(8,128)S(1)} %shard_map.133.mixed), channel_id=1, source_target_pairs={{0,2},{1,3},{2,0},{3,1},{4,6},{5,7},{6,4},{7,5},{8,10},{9,11},{10,... | collective-permute-start | bytes 196616 | tf_op jit(solution)/shard_map/ppermute | solution.py:293
  55.1 0.8 collective-permute-start.15
  56.2 1.1 %pad_maximum_fusion.rest_ref = f32[4,3,32,512]{3,2,1,0:T(8,128)S(1)} fusion(f32[2,3,32,512]{3,2,1,0:T(8,128)S(1)} %collective-permute-done.19, f32[1,3,32,512]{3,2,1,0:T(8,128)} %collective-permute-done.18, f32[1,3,32,512]{3,2,1,0:T(8,128)} %maximum_bitcast_fusion), kind=kLoop, calls=%fused_computation | loop fusion | flops 393216 | bytes 1572864 | tf_op jit(solution)/shard_map/concatenate | solution.py:343
  57.4 3.0 %collective-permute-done.14.refs_1_ = f32[128,128]{1,0:T(8,128)S(1)} collective-permute-done((f32[128,128]{1,0:T(8,128)S(1)}, f32[128,128]{1,0:T(8,128)S(1)}, u32[]{:S(2)}, u32[]{:S(2)}) %collective-permute-start.14) | collective-permute-done | bytes 65568 | tf_op jit(solution)/shard_map/ppermute | solution.py:293
  60.4 0.8 collective-permute-done.15.refs_2_
  61.2 1.2 %shard_map.138 = (f32[128,128]{1,0:T(8,128)S(1)}, f32[128,128]{1,0:T(8,128)S(1)}, f32[128,128]{1,0:T(8,128)S(1)}, f32[128,128]{1,0:T(8,128)S(1)}) custom-call(f32[128,512]{1,0:T(8,128)S(1)} %shard_map.134.base, f32[128,128]{1,0:T(8,128)S(1)} %collective-permute-done.13.refs_0_, f32[128,128]{1,0:T(8,128)S(1)} %collective-permute-done.14.refs_1_, ...), custom_call_target="tpu_custom_call" | custom-call | tf_op jit(solution)/shard_map/pallas_call | solution.py:360
  62.4 1.4 %collective-permute-start.20 = (f32[128,128]{1,0:T(8,128)S(1)}, f32[128,128]{1,0:T(8,128)S(1)}, u32[]{:S(2)}, u32[]{:S(2)}) collective-permute-start(f32[128,128]{1,0:T(8,128)S(1)} %get-tuple-element.48), channel_id=1, source_target_pairs={{0,1},{1,0},{2,3},{3,2},{4,5},{5,4},{6,7},{7,6},{8,9},{9,8},{10,11... | collective-permute-start | bytes 196616 | tf_op jit(solution)/shard_map/ppermute | solution.py:293
  63.9 1.3 %collective-permute-start.21 = (f32[128,128]{1,0:T(8,128)S(1)}, f32[128,128]{1,0:T(8,128)S(1)}, u32[]{:S(2)}, u32[]{:S(2)}) collective-permute-start(f32[128,128]{1,0:T(8,128)S(1)} %get-tuple-element.49), channel_id=1, source_target_pairs={{0,2},{1,3},{2,0},{3,1},{4,6},{5,7},{6,4},{7,5},{8,10},{9,11},{10,... | collective-permute-start | bytes 196616 | tf_op jit(solution)/shard_map/ppermute | solution.py:293
  65.2 1.7 %collective-permute-start.22 = (f32[128,128]{1,0:T(8,128)S(1)}, f32[128,128]{1,0:T(8,128)S(1)}, u32[]{:S(2)}, u32[]{:S(2)}) collective-permute-start(f32[128,128]{1,0:T(8,128)S(1)} %get-tuple-element.50), channel_id=1, source_target_pairs={{0,3},{1,2},{2,1},{3,0},{4,7},{5,6},{6,5},{7,4},{8,11},{9,10},{10,... | collective-permute-start | bytes 196616 | tf_op jit(solution)/shard_map/ppermute | solution.py:293
  66.9 4.7 %collective-permute-done.21.refs_2_ = f32[128,128]{1,0:T(8,128)S(1)} collective-permute-done((f32[128,128]{1,0:T(8,128)S(1)}, f32[128,128]{1,0:T(8,128)S(1)}, u32[]{:S(2)}, u32[]{:S(2)}) %collective-permute-start.21) | collective-permute-done | bytes 65568 | tf_op jit(solution)/shard_map/ppermute | solution.py:293
  71.7 1.3 %collective-permute-start.23 = (f32[2,128]{1,0:T(2,128)S(1)}, f32[2,128]{1,0:T(2,128)S(1)}, u32[]{:S(2)}, u32[]{:S(2)}) collective-permute-start(f32[2,128]{1,0:T(2,128)S(1)} %get-tuple-element.52.refs_0_), channel_id=1, source_target_pairs={{0,1},{1,0},{2,3},{3,2},{4,5},{5,4},{6,7},{7,6},{8,9},{9,8},{10,11... | collective-permute-start | bytes 3080 | tf_op jit(solution)/shard_map/ppermute | solution.py:293
  73.1 1.4 %collective-permute-start.24 = (f32[2,128]{1,0:T(2,128)S(1)}, f32[2,128]{1,0:T(2,128)S(1)}, u32[]{:S(2)}, u32[]{:S(2)}) collective-permute-start(f32[2,128]{1,0:T(2,128)S(1)} %get-tuple-element.52.refs_0_), channel_id=1, source_target_pairs={{0,2},{1,3},{2,0},{3,1},{4,6},{5,7},{6,4},{7,5},{8,10},{9,11},{10,... | collective-permute-start | bytes 3080 | tf_op jit(solution)/shard_map/ppermute | solution.py:293
  74.4 1.7 %collective-permute-start.25 = (f32[2,128]{1,0:T(2,128)S(1)}, f32[2,128]{1,0:T(2,128)S(1)}, u32[]{:S(2)}, u32[]{:S(2)}) collective-permute-start(f32[2,128]{1,0:T(2,128)S(1)} %get-tuple-element.52.refs_0_), channel_id=1, source_target_pairs={{0,3},{1,2},{2,1},{3,0},{4,7},{5,6},{6,5},{7,4},{8,11},{9,10},{10,... | collective-permute-start | bytes 3080 | tf_op jit(solution)/shard_map/ppermute | solution.py:293
  76.4 1.1 %collective-permute-done.24.refs_2_ = f32[2,128]{1,0:T(2,128)S(1)} collective-permute-done((f32[2,128]{1,0:T(2,128)S(1)}, f32[2,128]{1,0:T(2,128)S(1)}, u32[]{:S(2)}, u32[]{:S(2)}) %collective-permute-start.24) | collective-permute-done | bytes 1056 | tf_op jit(solution)/shard_map/ppermute | solution.py:293
  77.5 2.3 %collective-permute-done.25.refs_3_ = f32[2,128]{1,0:T(2,128)S(1)} collective-permute-done((f32[2,128]{1,0:T(2,128)S(1)}, f32[2,128]{1,0:T(2,128)S(1)}, u32[]{:S(2)}, u32[]{:S(2)}) %collective-permute-start.25) | collective-permute-done | bytes 1056 | tf_op jit(solution)/shard_map/ppermute | solution.py:293
  79.8 0.7 shard_map.141
  (50 shorter events, 1.4 us)
Async XLA Ops:
  0.0 0.9 %copy-start = (f32[128,512]{1,0:T(8,128)S(1)}, f32[128,512]{1,0:T(8,128)}, u32[]{:S(2)}) copy-start(f32[128,512]{1,0:T(8,128)} %w_ref.1) | copy-start | bytes 786436
  1.0 25.1 %copy-start.8 = (f32[512]{0:T(512)S(1)}, f32[512]{0:T(512)}, u32[]{:S(2)}) copy-start(f32[512]{0:T(512)} %param.15) | copy-start | bytes 6148
  1.0 34.4 %copy-start.4 = (f32[512,128]{1,0:T(8,128)S(1)}, f32[512,128]{1,0:T(8,128)}, u32[]{:S(2)}) copy-start(f32[512,128]{1,0:T(8,128)} %k_ref.1) | copy-start | bytes 786436
  1.0 34.4 %copy-start.5 = (f32[512,128]{1,0:T(8,128)S(1)}, f32[512,128]{1,0:T(8,128)}, u32[]{:S(2)}) copy-start(f32[512,128]{1,0:T(8,128)} %v_ref.1) | copy-start | bytes 786436
  1.0 34.4 %copy-start.6 = (f32[512,128]{1,0:T(8,128)S(1)}, f32[512,128]{1,0:T(8,128)}, u32[]{:S(2)}) copy-start(f32[512,128]{1,0:T(8,128)} %q_ref.1) | copy-start | bytes 786436
  1.0 5.4 %collective-permute-start.16 = (f32[1,32,512]{2,1,0:T(8,128)S(1)}, f32[1,32,512]{2,1,0:T(8,128)S(1)}, u32[]{:S(2)}, u32[]{:S(2)}) collective-permute-start(f32[1,32,512]{2,1,0:T(8,128)S(1)} %bitcast.8), channel_id=1, source_target_pairs={{0,1},{1,0},{2,3},{3,2},{4,5},{5,4},{6,7},{7,6},{8,9},{9,8},{10,11... | collective-permute-start | bytes 196616 | tf_op jit(solution)/shard_map/ppermute | solution.py:293
  6.4 8.3 %collective-permute-start.17 = (f32[2,32,512]{2,1,0:T(8,128)S(1)}, f32[2,32,512]{2,1,0:T(8,128)S(1)}, u32[]{:S(2)}, u32[]{:S(2)}) collective-permute-start(f32[2,32,512]{2,1,0:T(8,128)S(1)} %pad_maximum_fusion.2), channel_id=1, source_target_pairs={{0,2},{1,3},{2,0},{3,1},{4,6},{5,7},{6,4},{7,5},{8,10},{9,11},{10,... | collective-permute-start | bytes 393224 | tf_op jit(solution)/shard_map/ppermute | solution.py:293
  15.3 9.6 %collective-permute-start.18 = (f32[1,3,32,512]{3,2,1,0:T(8,128)}, f32[1,3,32,512]{3,2,1,0:T(8,128)}, u32[]{:S(2)}, u32[]{:S(2)}) collective-permute-start(f32[1,3,32,512]{3,2,1,0:T(8,128)} %maximum_bitcast_fusion), channel_id=1, source_target_pairs={{0,16},{4,20},{8,24},{12,28},{16,0},{20,4},{24,8},{28,12},{1,17},{... | collective-permute-start | bytes 589832 | tf_op jit(solution)/shard_map/ppermute | solution.py:293
  20.5 35.4 %copy-start.1 = (f32[128,512]{1,0:T(8,128)S(1)}, f32[128,512]{1,0:T(8,128)}, u32[]{:S(2)}) copy-start(f32[128,512]{1,0:T(8,128)} %w_ref.1) | copy-start | bytes 786436
  20.5 6.5 %collective-permute-start = (f32[128,128]{1,0:T(8,128)}, f32[128,128]{1,0:T(8,128)S(1)}, u32[]{:S(2)}, u32[]{:S(2)}) collective-permute-start(f32[128,128]{1,0:T(8,128)} %get-tuple-element.31), channel_id=1, source_target_pairs={{0,1},{1,0},{2,3},{3,2},{4,5},{5,4},{6,7},{7,6},{8,9},{9,8},{10,11... | collective-permute-start | bytes 196616 | tf_op jit(solution)/shard_map/ppermute | solution.py:293
  21.2 7.2 %collective-permute-start.1 = (f32[128,128]{1,0:T(8,128)}, f32[128,128]{1,0:T(8,128)S(1)}, u32[]{:S(2)}, u32[]{:S(2)}) collective-permute-start(f32[128,128]{1,0:T(8,128)} %get-tuple-element.32), channel_id=1, source_target_pairs={{0,2},{1,3},{2,0},{3,1},{4,6},{5,7},{6,4},{7,5},{8,10},{9,11},{10,... | collective-permute-start | bytes 196616 | tf_op jit(solution)/shard_map/ppermute | solution.py:293
  24.6 6.3 %collective-permute-start.2 = (f32[128,128]{1,0:T(8,128)}, f32[128,128]{1,0:T(8,128)S(1)}, u32[]{:S(2)}, u32[]{:S(2)}) collective-permute-start(f32[128,128]{1,0:T(8,128)} %get-tuple-element.33), channel_id=1, source_target_pairs={{0,3},{1,2},{2,1},{3,0},{4,7},{5,6},{6,5},{7,4},{8,11},{9,10},{10,... | collective-permute-start | bytes 196616 | tf_op jit(solution)/shard_map/ppermute | solution.py:293
  26.0 30.2 %collective-permute-start.19 = (f32[2,3,32,512]{3,2,1,0:T(8,128)S(1)}, f32[2,3,32,512]{3,2,1,0:T(8,128)S(1)}, u32[]{:S(2)}, u32[]{:S(2)}) collective-permute-start(f32[2,3,32,512]{3,2,1,0:T(8,128)S(1)} %pad_maximum_fusion.1), channel_id=1, source_target_pairs={{0,4},{4,0},{8,12},{12,8},{16,20},{20,16},{24,28},{28,24},{1,5},{5... | collective-permute-start | bytes 1179656 | tf_op jit(solution)/shard_map/ppermute | solution.py:293
  26.1 0.8 %copy-start.7 = (f32[128,128]{1,0:T(8,128)S(1)}, f32[128,128]{1,0:T(8,128)}, u32[]{:S(2)}) copy-start(f32[128,128]{1,0:T(8,128)} %get-tuple-element.30.x_ref) | copy-start | bytes 196612
  30.9 4.6 %collective-permute-start.3 = (f32[128,128]{1,0:T(8,128)S(1)}, f32[128,128]{1,0:T(8,128)S(1)}, u32[]{:S(2)}, u32[]{:S(2)}) collective-permute-start(f32[128,128]{1,0:T(8,128)S(1)} %shard_map.128.refs_0_), channel_id=1, source_target_pairs={{0,1},{1,0},{2,3},{3,2},{4,5},{5,4},{6,7},{7,6},{8,9},{9,8},{10,11... | collective-permute-start | bytes 196616 | tf_op jit(solution)/shard_map/ppermute | solution.py:293
  31.0 5.8 %collective-permute-start.4 = (f32[128,128]{1,0:T(8,128)S(1)}, f32[128,128]{1,0:T(8,128)S(1)}, u32[]{:S(2)}, u32[]{:S(2)}) collective-permute-start(f32[128,128]{1,0:T(8,128)S(1)} %shard_map.128.refs_0_), channel_id=1, source_target_pairs={{0,2},{1,3},{2,0},{3,1},{4,6},{5,7},{6,4},{7,5},{8,10},{9,11},{10,... | collective-permute-start | bytes 196616 | tf_op jit(solution)/shard_map/ppermute | solution.py:293
  32.3 6.1 %collective-permute-start.5 = (f32[128,128]{1,0:T(8,128)S(1)}, f32[128,128]{1,0:T(8,128)S(1)}, u32[]{:S(2)}, u32[]{:S(2)}) collective-permute-start(f32[128,128]{1,0:T(8,128)S(1)} %shard_map.128.refs_0_), channel_id=1, source_target_pairs={{0,3},{1,2},{2,1},{3,0},{4,7},{5,6},{6,5},{7,4},{8,11},{9,10},{10,... | collective-permute-start | bytes 196616 | tf_op jit(solution)/shard_map/ppermute | solution.py:293
  35.5 25.7 %copy-start.9 = (f32[512]{0:T(512)S(1)}, f32[512]{0:T(512)}, u32[]{:S(2)}) copy-start(f32[512]{0:T(512)} %param.20) | copy-start | bytes 6148
  35.5 25.7 %copy-start.10 = (f32[512]{0:T(512)S(1)}, f32[512]{0:T(512)}, u32[]{:S(2)}) copy-start(f32[512]{0:T(512)} %param.21) | copy-start | bytes 6148
  38.7 5.7 %collective-permute-start.7 = (f32[128,256]{1,0:T(8,128)S(1)}, f32[128,256]{1,0:T(8,128)S(1)}, u32[]{:S(2)}, u32[]{:S(2)}) collective-permute-start(f32[128,256]{1,0:T(8,128)S(1)} %shard_map.131.refs_0_), channel_id=1, source_target_pairs={{0,16},{4,20},{8,24},{12,28},{16,0},{20,4},{24,8},{28,12},{1,17},{... | collective-permute-start | bytes 393224 | tf_op jit(solution)/shard_map/ppermute | solution.py:293
  39.3 5.1 %collective-permute-start.6 = (f32[128,256]{1,0:T(8,128)S(1)}, f32[128,256]{1,0:T(8,128)S(1)}, u32[]{:S(2)}, u32[]{:S(2)}) collective-permute-start(f32[128,256]{1,0:T(8,128)S(1)} %shard_map.131.refs_0_), channel_id=1, source_target_pairs={{0,8},{4,12},{8,0},{12,4},{16,24},{20,28},{24,16},{28,20},{1,9},{5... | collective-permute-start | bytes 393224 | tf_op jit(solution)/shard_map/ppermute | solution.py:293
  40.8 5.9 %collective-permute-start.11 = (f32[128,256]{1,0:T(8,128)S(1)}, f32[128,256]{1,0:T(8,128)S(1)}, u32[]{:S(2)}, u32[]{:S(2)}) collective-permute-start(f32[128,256]{1,0:T(8,128)S(1)} %shard_map.131.refs_0_), channel_id=1, source_target_pairs={{0,24},{4,28},{8,16},{12,20},{16,8},{20,12},{24,0},{28,4},{1,25},{... | collective-permute-start | bytes 393224 | tf_op jit(solution)/shard_map/ppermute | solution.py:293
  42.3 7.4 %collective-permute-start.8 = (f32[128,256]{1,0:T(8,128)S(1)}, f32[128,256]{1,0:T(8,128)S(1)}, u32[]{:S(2)}, u32[]{:S(2)}) collective-permute-start(f32[128,256]{1,0:T(8,128)S(1)} %shard_map.131.refs_0_), channel_id=1, source_target_pairs={{0,4},{4,0},{8,12},{12,8},{16,20},{20,16},{24,28},{28,24},{1,5},{5... | collective-permute-start | bytes 393224 | tf_op jit(solution)/shard_map/ppermute | solution.py:293
  44.4 5.3 %collective-permute-start.10 = (f32[128,256]{1,0:T(8,128)S(1)}, f32[128,256]{1,0:T(8,128)S(1)}, u32[]{:S(2)}, u32[]{:S(2)}) collective-permute-start(f32[128,256]{1,0:T(8,128)S(1)} %collective-permute-done.7.refs_2_), channel_id=1, source_target_pairs={{0,4},{4,0},{8,12},{12,8},{16,20},{20,16},{24,28},{28,24},{1,5},{5... | collective-permute-start | bytes 393224 | tf_op jit(solution)/shard_map/ppermute | solution.py:293
  44.4 5.3 %collective-permute-start.9 = (f32[128,256]{1,0:T(8,128)S(1)}, f32[128,256]{1,0:T(8,128)S(1)}, u32[]{:S(2)}, u32[]{:S(2)}) collective-permute-start(f32[128,256]{1,0:T(8,128)S(1)} %collective-permute-done.6.refs_1_), channel_id=1, source_target_pairs={{0,4},{4,0},{8,12},{12,8},{16,20},{20,16},{24,28},{28,24},{1,5},{5... | collective-permute-start | bytes 393224 | tf_op jit(solution)/shard_map/ppermute | solution.py:293
  46.6 4.2 %collective-permute-start.12 = (f32[128,256]{1,0:T(8,128)S(1)}, f32[128,256]{1,0:T(8,128)S(1)}, u32[]{:S(2)}, u32[]{:S(2)}) collective-permute-start(f32[128,256]{1,0:T(8,128)S(1)} %collective-permute-done.11.refs_3_), channel_id=1, source_target_pairs={{0,4},{4,0},{8,12},{12,8},{16,20},{20,16},{24,28},{28,24},{1,5},{5... | collective-permute-start | bytes 393224 | tf_op jit(solution)/shard_map/ppermute | solution.py:293
  46.6 1.2 %copy-start.2 = (f32[512,512]{1,0:T(8,128)S(1)}, f32[512,512]{1,0:T(8,128)}, u32[]{:S(2)}) copy-start(f32[512,512]{1,0:T(8,128)} %refs_0_.1) | copy-start | bytes 3145732
  47.9 1.2 %copy-start.3 = (f32[512,512]{1,0:T(8,128)S(1)}, f32[512,512]{1,0:T(8,128)}, u32[]{:S(2)}) copy-start(f32[512,512]{1,0:T(8,128)} %refs_1_.1) | copy-start | bytes 3145732
  49.6 26.6 %copy-start.11 = (f32[512]{0:T(512)S(1)}, f32[512]{0:T(512)}, u32[]{:S(2)}) copy-start(f32[512]{0:T(512)} %param.24) | copy-start | bytes 6148
  49.6 26.5 %copy-start.12 = (f32[512]{0:T(512)S(1)}, f32[512]{0:T(512)}, u32[]{:S(2)}) copy-start(f32[512]{0:T(512)} %param.25) | copy-start | bytes 6148
  51.5 5.9 %collective-permute-start.13 = (f32[128,128]{1,0:T(8,128)S(1)}, f32[128,128]{1,0:T(8,128)S(1)}, u32[]{:S(2)}, u32[]{:S(2)}) collective-permute-start(f32[128,128]{1,0:T(8,128)S(1)} %shard_map.133.mixed), channel_id=1, source_target_pairs={{0,1},{1,0},{2,3},{3,2},{4,5},{5,4},{6,7},{7,6},{8,9},{9,8},{10,11... | collective-permute-start | bytes 196616 | tf_op jit(solution)/shard_map/ppermute | solution.py:293
  52.6 7.8 %collective-permute-start.14 = (f32[128,128]{1,0:T(8,128)S(1)}, f32[128,128]{1,0:T(8,128)S(1)}, u32[]{:S(2)}, u32[]{:S(2)}) collective-permute-start(f32[128,128]{1,0:T(8,128)S(1)} %shard_map.133.mixed), channel_id=1, source_target_pairs={{0,2},{1,3},{2,0},{3,1},{4,6},{5,7},{6,4},{7,5},{8,10},{9,11},{10,... | collective-permute-start | bytes 196616 | tf_op jit(solution)/shard_map/ppermute | solution.py:293
  55.1 6.1 %collective-permute-start.15 = (f32[128,128]{1,0:T(8,128)S(1)}, f32[128,128]{1,0:T(8,128)S(1)}, u32[]{:S(2)}, u32[]{:S(2)}) collective-permute-start(f32[128,128]{1,0:T(8,128)S(1)} %shard_map.133.mixed), channel_id=1, source_target_pairs={{0,3},{1,2},{2,1},{3,0},{4,7},{5,6},{6,5},{7,4},{8,11},{9,10},{10,... | collective-permute-start | bytes 196616 | tf_op jit(solution)/shard_map/ppermute | solution.py:293
  62.4 4.5 %collective-permute-start.20 = (f32[128,128]{1,0:T(8,128)S(1)}, f32[128,128]{1,0:T(8,128)S(1)}, u32[]{:S(2)}, u32[]{:S(2)}) collective-permute-start(f32[128,128]{1,0:T(8,128)S(1)} %get-tuple-element.48), channel_id=1, source_target_pairs={{0,1},{1,0},{2,3},{3,2},{4,5},{5,4},{6,7},{7,6},{8,9},{9,8},{10,11... | collective-permute-start | bytes 196616 | tf_op jit(solution)/shard_map/ppermute | solution.py:293
  63.9 7.7 %collective-permute-start.21 = (f32[128,128]{1,0:T(8,128)S(1)}, f32[128,128]{1,0:T(8,128)S(1)}, u32[]{:S(2)}, u32[]{:S(2)}) collective-permute-start(f32[128,128]{1,0:T(8,128)S(1)} %get-tuple-element.49), channel_id=1, source_target_pairs={{0,2},{1,3},{2,0},{3,1},{4,6},{5,7},{6,4},{7,5},{8,10},{9,11},{10,... | collective-permute-start | bytes 196616 | tf_op jit(solution)/shard_map/ppermute | solution.py:293
  65.2 6.4 %collective-permute-start.22 = (f32[128,128]{1,0:T(8,128)S(1)}, f32[128,128]{1,0:T(8,128)S(1)}, u32[]{:S(2)}, u32[]{:S(2)}) collective-permute-start(f32[128,128]{1,0:T(8,128)S(1)} %get-tuple-element.50), channel_id=1, source_target_pairs={{0,3},{1,2},{2,1},{3,0},{4,7},{5,6},{6,5},{7,4},{8,11},{9,10},{10,... | collective-permute-start | bytes 196616 | tf_op jit(solution)/shard_map/ppermute | solution.py:293
  71.7 4.7 %collective-permute-start.23 = (f32[2,128]{1,0:T(2,128)S(1)}, f32[2,128]{1,0:T(2,128)S(1)}, u32[]{:S(2)}, u32[]{:S(2)}) collective-permute-start(f32[2,128]{1,0:T(2,128)S(1)} %get-tuple-element.52.refs_0_), channel_id=1, source_target_pairs={{0,1},{1,0},{2,3},{3,2},{4,5},{5,4},{6,7},{7,6},{8,9},{9,8},{10,11... | collective-permute-start | bytes 3080 | tf_op jit(solution)/shard_map/ppermute | solution.py:293
  73.1 4.5 %collective-permute-start.24 = (f32[2,128]{1,0:T(2,128)S(1)}, f32[2,128]{1,0:T(2,128)S(1)}, u32[]{:S(2)}, u32[]{:S(2)}) collective-permute-start(f32[2,128]{1,0:T(2,128)S(1)} %get-tuple-element.52.refs_0_), channel_id=1, source_target_pairs={{0,2},{1,3},{2,0},{3,1},{4,6},{5,7},{6,4},{7,5},{8,10},{9,11},{10,... | collective-permute-start | bytes 3080 | tf_op jit(solution)/shard_map/ppermute | solution.py:293
  74.4 5.4 %collective-permute-start.25 = (f32[2,128]{1,0:T(2,128)S(1)}, f32[2,128]{1,0:T(2,128)S(1)}, u32[]{:S(2)}, u32[]{:S(2)}) collective-permute-start(f32[2,128]{1,0:T(2,128)S(1)} %get-tuple-element.52.refs_0_), channel_id=1, source_target_pairs={{0,3},{1,2},{2,1},{3,0},{4,7},{5,6},{6,5},{7,4},{8,11},{9,10},{10,... | collective-permute-start | bytes 3080 | tf_op jit(solution)/shard_map/ppermute | solution.py:293
